TPU v7x, 32 devices: a whole 2x2x4 slice. The times are simulated.
32 devices in a mesh: groups: 2 (over y), row: 4 (over x, core), col: 4 (over z).
Axes of the slice: x: 2, y: 2, z: 4, core: 2. Of those that a mesh axis runs over, the one named last changes fastest.
Arguments:
- tokens: bfloat16 [2048, 8192], P('groups', ('row', 'col')), parts along dimension 0, may hold values from -6 to 6
- gate_weight: bfloat16 [8192, 26624], P('row', 'col'), may hold values from -0.0625 to 0.0625
- up_weight: bfloat16 [8192, 26624], P('row', 'col'), may hold values from -0.0625 to 0.0625
- down_weight: bfloat16 [26624, 8192], P('col', 'row'), may hold values from -0.0546875 to 0.0546875
Outputs:
- mixed: bfloat16 [2048, 8192], P('groups', ('row', 'col')), parts along dimension 0
There are 2 independent parts, one for each index of `groups`. A program takes and returns all parts, laid end to end along the dimension named above; an argument that names none is the same for every part. Nothing has to cross between parts.
All inputs are finite; a program needn't handle non-finite values.
Results may differ from a plain program's by a relative error of at most 0.02.
Values may be sent and summed in bfloat16 or wider, within the bound.
No kernel may reach another device: no remote copies, remote signals or barrier semaphores. Data moves between devices by JAX's collectives and lax.ppermute only.
A program may use at most 256 MiB of HBM per device.

v0:
```python
import jax
import jax.numpy as jnp
from jax import lax
from jax.sharding import PartitionSpec as P


def on_device(tokens, gate_weight, up_weight, down_weight):
    gathered = lax.all_gather(tokens, "col", axis=1, tiled=True)
    gate_part = jnp.dot(gathered, gate_weight, preferred_element_type=jnp.float32)
    up_part = jnp.dot(gathered, up_weight, preferred_element_type=jnp.float32)
    gate_part = gate_part.astype(jnp.bfloat16).astype(jnp.float32)
    up_part = up_part.astype(jnp.bfloat16).astype(jnp.float32)
    gate_sum, up_sum = (
        lax.psum(gate_part.astype(jnp.bfloat16), "row").astype(jnp.float32),
        lax.psum(up_part.astype(jnp.bfloat16), "row").astype(jnp.float32),
    )
    hidden = (jax.nn.silu(gate_sum) * up_sum).astype(jnp.bfloat16)
    partial_value = jnp.dot(hidden, down_weight, preferred_element_type=jnp.float32)
    partial_value = partial_value.astype(jnp.bfloat16).astype(jnp.float32)
    total = lax.psum_scatter(
        partial_value.astype(jnp.bfloat16), "col", scatter_dimension=1, tiled=True
    )
    return total


def solution(mesh):
    in_specs = (P("groups", ("row", "col")), P("row", "col"), P("row", "col"), P("col", "row"))
    out_specs = P("groups", ("row", "col"))
    return jax.shard_map(
        on_device, mesh=mesh, in_specs=in_specs, out_specs=out_specs, check_vma=False
    )
```

profile of v0, /device:TPU:0, one launch (start us, length us, event | category | flops | bytes accessed | tf_op | source)
XLA Modules:
  0.0 749.9 jit_solution(18241327143410897063)
XLA Ops:
  6.5 0.0 all-gather.2.cloned.1.call-start
  6.5 0.7 all-gather.2.cloned.1.call-update
  7.3 0.0 all-reduce.3.cloned.1.call-start
  7.3 85.1 %all-gather.2.cloned.1.call-done = bf16[1024,2048]{1,0:T(8,128)(2,1)} async-done(((bf16[1024,512]{1,0:T(8,128)(2,1)}), bf16[1024,2048]{1,0:T(8,128)(2,1)}) %all-gather.2.cloned.1.call-update) | async-done | bytes 4194320 | tf_op jit(solution)/shard_map/all_gather | solution.py:8
  92.4 0.0 copy-start
  92.4 38.7 %convolution_convert_fusion = bf16[1024,6656]{1,0:T(8,128)(2,1)} fusion(bf16[1024,2048]{1,0:T(8,128)(2,1)} %all-gather.2.cloned.1.call-done, bf16[2048,6656]{1,0:T(8,128)(2,1)} %param.6), kind=kOutput, calls=%fused_computation.8 | convolution fusion | flops 27924103168 | bytes 45088768 | tf_op jit(solution)/shard_map/dot_general | solution.py:10
  131.1 0.0 copy-done
  131.1 35.7 %convolution_convert_fusion.1 = bf16[1024,6656]{1,0:T(8,128)(2,1)} fusion(bf16[1024,2048]{1,0:T(8,128)(2,1)S(1)} %copy-done, bf16[2048,6656]{1,0:T(8,128)(2,1)} %param.5), kind=kOutput, calls=%fused_computation.9 | convolution fusion | flops 27924103168 | bytes 45088768 | tf_op jit(solution)/shard_map/dot_general | solution.py:9
  166.8 0.0 all-reduce.3.cloned.1.call-update
  166.9 0.2 reduce-scatter.2.cloned.1.call-start
  167.1 455.9 %all-reduce.3.cloned.1.call-done = (bf16[1024,6656]{1,0:T(8,128)(2,1)}, bf16[1024,6656]{1,0:T(8,128)(2,1)}) async-done(((bf16[1024,6656]{1,0:T(8,128)(2,1)}, bf16[1024,6656]{1,0:T(8,128)(2,1)}), (bf16[1024,6656]{1,0:T(8,128)(2,1)}, bf16[1024,6656]{1,0:T(8,128)(2,1)})) %all-reduce.3.cloned.1.call-update) | async-done | bytes 27262992 | tf_op jit(solution)/shard_map/psum | solution.py:15
  623.0 43.2 %fusion.7 = bf16[1024,2048]{1,0:T(8,128)(2,1)} fusion(bf16[6656,2048]{1,0:T(8,128)(2,1)} %param.7, bf16[1024,6656]{1,0:T(8,128)(2,1)} %get-tuple-element.5, bf16[1024,6656]{1,0:T(8,128)(2,1)} %get-tuple-element.6), kind=kOutput, calls=%fused_computation.10 | convolution fusion | flops 27973910528 | bytes 58720256 | tf_op jit(solution)/shard_map/dot_general | solution.py:18
  666.2 0.0 reduce-scatter.2.cloned.1.call-update
  666.2 77.1 %reduce-scatter.2.cloned.1.call-done = bf16[1024,512]{1,0:T(8,128)(2,1)} async-done(((bf16[1024,2048]{1,0:T(8,128)(2,1)}), bf16[1024,512]{1,0:T(8,128)(2,1)}) %reduce-scatter.2.cloned.1.call-update) | async-done | bytes 1048592 | tf_op jit(solution)/shard_map/reduce_scatter | solution.py:20
Async XLA Ops:
  6.5 85.9 %all-gather.2.cloned.1.call-start = ((), (), s32[]{:S(2)}) async-start(), calls=%async_computation.1 | async-start | bytes 5242880 | tf_op jit(solution)/shard_map/all_gather | solution.py:8
  7.3 615.7 %all-reduce.3.cloned.1.call-start = ((), (), s32[]{:S(2)}) async-start(), calls=%async_computation.3 | async-start | bytes 54525952 | tf_op jit(solution)/shard_map/psum | solution.py:15
  92.4 38.7 %copy-start = (bf16[1024,2048]{1,0:T(8,128)(2,1)S(1)}, bf16[1024,2048]{1,0:T(8,128)(2,1)}, u32[]{:S(2)}) copy-start(bf16[1024,2048]{1,0:T(8,128)(2,1)} %all-gather.2.cloned.1.call-done) | copy-start | bytes 12582916
  166.9 576.5 %reduce-scatter.2.cloned.1.call-start = ((), (), s32[]{:S(2)}) async-start(), calls=%async_computation.2 | async-start | bytes 5242880 | tf_op jit(solution)/shard_map/reduce_scatter | solution.py:20
Sparse Core Ops, SparseCore 0:
  8.9 83.4 all-gather.1
  167.0 455.9 all-reduce.2
  666.3 76.9 reduce-scatter.1
where the time goes:
time: 750 us
  waiting for transfers between devices  619 us (83%)
  matrix products  118 us (16%)
  between operations  13.1 us (2%)
    psum x1, waiting for transfers between devices, on_device(): lax.psum(up_part.astype(jnp.bfloat16), 'row').astype(jnp.float32)  456 us
    all_gather x1, waiting for transfers between devices, on_device(): gathered = lax.all_gather(tokens, 'col', axis=1, tiled=True)  85.1 us
    reduce_scatter x1, waiting for transfers between devices, on_device(): lax.psum_scatter(partial_value.astype(jnp.bfloat16), 'col', scatter_dimen...  77.1 us
    dot_general x1, matrix products, on_device(): jnp.dot(hidden, down_weight, preferred_element_type=jnp.float32)  43.2 us
    dot_general x1, matrix products, on_device(): up_part = jnp.dot(gathered, up_weight, preferred_element_type=jnp.float32)  38.7 us
    dot_general x1, matrix products, on_device(): jnp.dot(gathered, gate_weight, preferred_element_type=jnp.float32)  35.7 us
  transfers between devices with their start and end apart: 3, of which 3 were waited for; matrix products, arithmetic and copies ran while one was open for 0% of the time, Pallas kernels for 0%

commit v1 on v0

v1 whole, which is shorter than its diff:
```python
import functools

import jax
import jax.numpy as jnp
import numpy as np
from jax import lax
from jax.experimental import pallas as pl
from jax.experimental.pallas import tpu as pltpu
from jax.sharding import PartitionSpec as P

BF16, F32 = jnp.bfloat16, jnp.float32
SCALE = 4
VMEM_LIMIT = 52 * 2**20
PARTNER, OWN, X, BLOCKS = 0, 1, 2, 3


def dot(a, b):
    return jnp.dot(a, b, preferred_element_type=F32)


def accumulate(tok_ref, gate_ref, up_ref, acc):
    step = pl.program_id(0)

    @pl.when(step == 0)
    def _():
        acc[0] = dot(tok_ref[...], gate_ref[...])
        acc[1] = dot(tok_ref[...], up_ref[...])

    @pl.when(step > 0)
    def _():
        acc[0] += dot(tok_ref[...], gate_ref[...])
        acc[1] += dot(tok_ref[...], up_ref[...])


def pieces_of(rows):
    half = rows // 2
    return [(which, start) for which in (0, 1) for start in (0, half)], half


def partner_kernel(place, tok_ref, gate_ref, up_ref, *rest):
    out_refs, acc = rest[:-1], rest[-1]
    accumulate(tok_ref, gate_ref, up_ref, acc)

    @pl.when(pl.program_id(0) == pl.num_programs(0) - 1)
    def _():
        pieces, height = pieces_of(acc.shape[1])
        for (which, start), out_ref in zip(pieces, out_refs):
            out_ref[...] = acc[which, start : start + height].astype(BF16)


def own_kernel(place, tok_ref, gate_ref, up_ref, *rest):
    received_refs, (send_ref, keep_ref, acc) = rest[:-3], rest[-3:]
    accumulate(tok_ref, gate_ref, up_ref, acc)
    half = send_ref.shape[1]

    @pl.when(pl.program_id(0) == pl.num_programs(0) - 1)
    def _():
        pieces, height = pieces_of(acc.shape[1])
        for (which, start), ref in zip(pieces, received_refs):
            acc[which, start : start + height] += ref[...].astype(F32)
        for ref, x in ((send_ref, 1 - place[X]), (keep_ref, place[X])):
            ref[...] = acc[:, pl.ds(pl.multiple_of(x * half, half), half), :].astype(BF16)


def down_kernel(place, own_x, other_x, own_x_core, other_x_core, weight_ref, *rest):
    out_refs, total = rest[:-1], rest[-1]
    step, part = pl.program_id(0), pl.program_id(1)

    def rows_of(mine, other):
        top = jnp.where(place[X] == 0, mine, other)
        bottom = jnp.where(place[X] == 0, other, mine)
        return jnp.concatenate([top, bottom], axis=0)

    @pl.when(part == 0)
    def _():
        total[...] = dot(rows_of(own_x[...], other_x[...]), weight_ref[...])

    @pl.when(part == 1)
    def _():
        value = total[...] + dot(rows_of(own_x_core[...], other_x_core[...]), weight_ref[...])
        if len(out_refs) == 1:
            out_refs[0][...] = value.astype(BF16)
            return
        for k, out_ref in enumerate(out_refs):
            @pl.when(step == k)
            def _(out_ref=out_ref):
                out_ref[...] = value.astype(BF16)


def whole(shape):
    return pl.BlockSpec(shape, lambda *_: (0,) * len(shape))


def params(n):
    return pltpu.CompilerParams(dimension_semantics=("arbitrary",) * n, vmem_limit_bytes=VMEM_LIMIT)


def cost(flops, *sizes):
    scale = SCALE
    return pl.CostEstimate(flops=int(flops * scale), bytes_accessed=int(sum(sizes) * scale), transcendentals=0)


def gate_up_call(place, tokens, rows, row_block, weights, n_col, which, span, received=None):
    part, of = span
    full, wide = weights[0].shape[0], weights[0].shape[1] // 2 // of
    depth, half = full // n_col, rows // 2
    weight = pl.BlockSpec((depth, wide), lambda k, place: (place[BLOCKS + k], place[which] * of + part))
    in_specs = [pl.BlockSpec((rows, depth), lambda k, place: (row_block, k)), weight, weight]
    operands = [tokens, *weights]
    if received is None:
        body, name = partner_kernel, "partner"
        out_shape, out_specs = [jax.ShapeDtypeStruct((half, wide), BF16)] * 4, [whole((half, wide))] * 4
    else:
        body, name = own_kernel, "own"
        out_shape, out_specs = [jax.ShapeDtypeStruct((2, half, wide), BF16)] * 2, [whole((2, half, wide))] * 2
        in_specs += [whole((half, wide))] * 4
        operands += received
    return pl.pallas_call(
        body,
        out_shape=out_shape,
        grid_spec=pltpu.PrefetchScalarGridSpec(
            num_scalar_prefetch=1,
            grid=(n_col,),
            in_specs=in_specs,
            out_specs=out_specs,
            scratch_shapes=[pltpu.VMEM((2, rows, wide), F32)],
        ),
        compiler_params=params(1),
        cost_estimate=cost(4 * rows * full * wide, 4 * full * wide, 4 * rows * wide),
        name=name,
    )(place, *operands)


def down_call(place, col, pieces, down_weight, n_col, split):
    half, wide = pieces[0].shape
    rows, block = 2 * half, down_weight.shape[1] // n_col
    if split:
        out_shape = [jax.ShapeDtypeStruct((rows, block), BF16)] * n_col
        out_specs = [whole((rows, block))] * n_col
        column = lambda d, place, col: lax.rem(col[0] + d + 1, n_col)
    else:
        out_shape = jax.ShapeDtypeStruct((rows, block * n_col), BF16)
        out_specs = pl.BlockSpec((rows, block), lambda d, k, place, col: (0, d))
        column = lambda d, place, col: d
    weight = pl.BlockSpec(
        (wide, block), lambda d, k, place, col: (jnp.where(k == 0, place[OWN], place[PARTNER]), column(d, place, col))
    )

    def body(place, col, *refs):
        down_kernel(place, *refs)

    return pl.pallas_call(
        body,
        out_shape=out_shape,
        grid_spec=pltpu.PrefetchScalarGridSpec(
            num_scalar_prefetch=2,
            grid=(n_col, 2),
            in_specs=[whole((half, wide))] * 4 + [weight],
            out_specs=out_specs,
            scratch_shapes=[pltpu.VMEM((rows, block), F32)],
        ),
        compiler_params=params(2),
        cost_estimate=cost(4 * rows * wide * block * n_col, 4 * wide * block * n_col, 8 * half * wide),
        name="down",
    )(place, col, *pieces, down_weight)


def shifted(x, n, shift):
    return lax.ppermute(x, "col", [(i, (i + shift) % n) for i in range(n)])


def swapped(x, mask):
    return lax.ppermute(x, "row", [(i, i ^ mask) for i in range(4)])


def after(x, *deps):
    return lax.optimization_barrier((x,) + deps)[0]


def pipelined(n_col, tokens, gate_weight, up_weight, down_weight):
    eighth = tokens.shape[0] // 8
    weights = (gate_weight, up_weight)
    row, col = lax.axis_index("row"), lax.axis_index("col")
    table = np.array(
        [
            [1 - r % 2, r % 2, r // 2] + [(c - s) % n_col for s in range(n_col)] + list(range(n_col)) + [c]
            for r in range(4)
            for c in range(n_col)
        ],
        np.int32,
    )
    mine = jnp.asarray(table)[row * n_col + col]
    by_shift, col_id = mine[: BLOCKS + n_col], mine[-1:]
    natural = jnp.concatenate([mine[:BLOCKS], mine[BLOCKS + n_col : -1]])

    def direct(piece):
        return [piece] + [shifted(piece, n_col, s) for s in range(1, n_col)]

    bounds = [0, 1, 3, 5, 7, 8]
    first = direct(tokens[:eighth])
    second = direct(after(tokens[eighth : 3 * eighth], *first[1:]))
    third = lax.all_gather(after(tokens[3 * eighth : 5 * eighth], *first[1:]), "col", axis=1, tiled=True)
    rest = lax.all_gather(after(tokens[5 * eighth :], third), "col", axis=1, tiled=True)
    sources = [
        (by_shift, jnp.concatenate(first, axis=1), 0),
        (by_shift, jnp.concatenate(second, axis=1), 0),
        (natural, third, 0),
        (natural, rest, 0),
        (natural, rest, 2),
    ]
    chunk_rows = [(b - a) * eighth for a, b in zip(bounds, bounds[1:])]
    last = [mine]

    def partner(i, span=(0, 1)):
        place, tok, block = sources[i]
        out = gate_up_call(after(place, *last), tok, chunk_rows[i], block, weights, n_col, PARTNER, span)
        last[:] = list(out)
        return [swapped(piece, 1) for piece in out]

    def own(i, received, span=(0, 1)):
        place, tok, block = sources[i]
        send, keep = gate_up_call(after(place, *last), tok, chunk_rows[i], block, weights, n_col, OWN, span, received)
        last[:] = [send]
        return keep, swapped(send, 2)

    def gated(pair):
        keep, arrived = after(pair[0], *last), pair[1]
        gate = keep[0].astype(F32) + arrived[0].astype(F32)
        up = keep[1].astype(F32) + arrived[1].astype(F32)
        hidden = (jax.nn.silu(gate) * up).astype(BF16)
        last[:] = [hidden]
        hidden_x = swapped(hidden, 2)
        return hidden, hidden_x, swapped(hidden, 1), swapped(hidden_x, 1)

    def down(pieces, split=False):
        out = down_call(after(by_shift, *last), col_id, pieces, down_weight, n_col, split)
        last[:] = list(out) if split else [out]
        if not split:
            return lax.psum_scatter(out, "col", scatter_dimension=1, tiled=True)
        total = out[-1].astype(F32)
        for s in range(1, n_col):
            total = total + shifted(out[s - 1], n_col, s).astype(F32)
        return total.astype(BF16)

    r0 = partner(0)
    p0 = own(0, r0)
    r1 = partner(1)
    h0 = gated(p0)
    p1 = own(1, r1)
    r2 = partner(2)
    o0 = down(h0)
    p2 = own(2, r2)
    h1 = gated(p1)
    r3 = partner(3)
    p3 = own(3, r3)
    o1 = down(h1)
    r4 = partner(4)
    h2 = gated(p2)
    p4 = own(4, r4)
    o2 = down(h2)
    h3 = gated(p3)
    h4 = gated(p4)
    o3 = down(h3)
    o4 = down(h4, split=True)
    return jnp.concatenate([o0, o1, o2, o3, o4], axis=0)


def generic(tokens, gate_weight, up_weight, down_weight):
    gathered = lax.all_gather(tokens, "col", axis=1, tiled=True)
    gate = lax.psum_scatter(dot(gathered, gate_weight).astype(BF16), "row", scatter_dimension=0, tiled=True)
    up = lax.psum_scatter(dot(gathered, up_weight).astype(BF16), "row", scatter_dimension=0, tiled=True)
    hidden = (jax.nn.silu(gate.astype(F32)) * up.astype(F32)).astype(BF16)
    hidden = lax.all_gather(hidden, "row", axis=0, tiled=True)
    partial = dot(hidden, down_weight).astype(BF16)
    return lax.psum_scatter(partial, "col", scatter_dimension=1, tiled=True)


def solution(mesh):
    n_row, n_col = mesh.shape["row"], mesh.shape["col"]
    in_specs = (P("groups", ("row", "col")), P("row", "col"), P("row", "col"), P("col", "row"))
    out_specs = P("groups", ("row", "col"))
    step = functools.partial(pipelined, n_col) if n_row == 4 else generic
    return jax.shard_map(step, mesh=mesh, in_specs=in_specs, out_specs=out_specs, check_vma=False)
```

time: 750 us -> 414 us (0.55)
  waiting for transfers between devices: 619 us -> 103 us
  Pallas kernels: 0 us -> 224 us
  matrix products: 118 us -> 0 us
  starting transfers between devices: 0.26 us -> 35.4 us
  local copies, waits for them, and re-layouts: 0.01 us -> 24.6 us
  other arithmetic: 0 us -> 8.72 us
    psum x1 -> x0, waiting for transfers between devices: 456 us -> none  [on_device(): lax.psum(up_part.astype(jnp.bfloat16), 'row').astype(jnp.float32)]
    pallas_call x0 -> x15, Pallas kernels: none -> 224 us  [the longest x10 146 us: gate_up_call(): pl.pallas_call(body, out_shape=out_shape, grid_spec=pltpu.PrefetchScalarG...]
    dot_general x3 -> x0, matrix products: 118 us -> none  [the longest x1 43.2 us: on_device(): jnp.dot(hidden, down_weight, preferred_element_type=jnp.float32)]
    all_gather x1 -> x2, waiting for transfers between devices: 85.1 us -> 6.63 us  [the longest x1 6.63 us: pipelined(): lax.all_gather(after(tokens[5 * eighth:], third), 'col', axis=1, tiled=True)]
    ppermute x0 -> x49, waiting for transfers between devices: none -> 74.3 us  [the longest x40 68.9 us: swapped(): return lax.ppermute(x, 'row', [(i, i ^ mask) for i in range(4)])]
    reduce_scatter x1 -> x4, waiting for transfers between devices: 77.1 us -> 21.9 us  [down(): return lax.psum_scatter(out, 'col', scatter_dimension=1, tiled=True)]
    ppermute x0 -> x49, starting transfers between devices: none -> 35 us  [the longest x40 18.3 us: swapped(): return lax.ppermute(x, 'row', [(i, i ^ mask) for i in range(4)])]
    unnamed x2 -> x41, local copies, waits for them, and re-layouts: 0.01 us -> 17 us
  transfers between devices with their start and end apart: 3 -> 55, of which waited for: 3 -> 13; matrix products, arithmetic and copies ran while one was open for 0% -> 6% of each run, Pallas kernels for 0% -> 55%
where the time goes in v1:
time: 414 us; the launch traced here: 409 us
  Pallas kernels  224 us (54%)
  waiting for transfers between devices  103 us (25%)
  starting transfers between devices  35.4 us (9%)
  local copies, waits for them, and re-layouts  24.6 us (6%)
  between operations  14 us (3%)
  other arithmetic  8.72 us (2%)
    pallas_call x10, Pallas kernels, gate_up_call(): pl.pallas_call(body, out_shape=out_shape, grid_spec=pltpu.PrefetchScalarG...  146 us
    pallas_call x5, Pallas kernels, down_call(): pl.pallas_call(body, out_shape=out_shape, grid_spec=pltpu.PrefetchScalarG...  77.8 us
    ppermute x40, waiting for transfers between devices, swapped(): return lax.ppermute(x, 'row', [(i, i ^ mask) for i in range(4)])  68.9 us
    reduce_scatter x4, waiting for transfers between devices, down(): return lax.psum_scatter(out, 'col', scatter_dimension=1, tiled=True)  21.9 us
    ppermute x40, starting transfers between devices, swapped(): return lax.ppermute(x, 'row', [(i, i ^ mask) for i in range(4)])  18.3 us
    unnamed x41, local copies, waits for them, and re-layouts  17 us
    ppermute x9, starting transfers between devices, shifted(): return lax.ppermute(x, 'col', [(i, (i + shift) % n) for i in range(n)])  16.7 us
  transfers between devices with their start and end apart: 55, of which 13 were waited for; matrix products, arithmetic and copies ran while one was open for 6% of the time, Pallas kernels for 55%

profile of v1, /device:TPU:0, one launch (start us, length us, event | category | flops | bytes accessed | tf_op | source)
XLA Modules:
  0.0 409.5 jit_solution(13366663390663516370)
XLA Ops:
  7.5 3.1 collective-permute-start
  10.5 2.6 collective-permute-start.1
  13.1 1.3 collective-permute-start.2
  14.5 1.9 fusion.21
  17.7 1.8 slice.115
  19.6 2.2 collective-permute-done.1
  21.8 3.3 collective-permute-start.7
  25.0 1.6 collective-permute-start.8
  28.3 11.2 %partner.5 = (bf16[64,3328]{1,0:T(8,128)(2,1)S(1)}, bf16[64,3328]{1,0:T(8,128)(2,1)S(1)}, bf16[64,3328]{1,0:T(8,128)(2,1)S(1)}, bf16[64,3328]{1,0:T(8,128)(2,1)S(1)}) custom-call(s32[7]{0:T(128)S(1)} %slice_bitcast_fusion.2.place, bf16[128,2048]{1,0:T(8,128)(2,1)} %pad_maximum_fusion.tok_ref, bf16[2048,6656]{1,0:T(8,128)(2,1)} %gate_ref.19, ...), custom_call_target="tpu_custom_call" | custom-call | flops 13958643712 | bytes 115867648 | tf_op jit(solution)/shard_map/partner/pallas_call | solution.py:118
  40.1 3.2 collective-permute-done.8
  43.3 1.8 constant_dynamic-update-slice_fusion.3
  45.4 1.7 constant_dynamic-update-slice_fusion.2
  47.0 1.7 constant_dynamic-update-slice_fusion.1
  48.7 1.7 constant_dynamic-update-slice_fusion.tok_ref
  50.4 13.0 %own.5 = (bf16[2,64,3328]{2,1,0:T(8,128)(2,1)}, bf16[2,64,3328]{2,1,0:T(8,128)(2,1)}) custom-call(s32[7]{0:T(128)S(1)} %slice_bitcast_fusion.2.place, bf16[128,2048]{1,0:T(8,128)(2,1)} %pad_maximum_fusion.tok_ref, bf16[2048,6656]{1,0:T(8,128)(2,1)} %gate_ref.19, bf16[2048,6656]{1,0:T(8,128)(2,1)} %up_ref.19, ...), custom_call_target="tpu_custom_call" | custom-call | flops 13958643712 | bytes 115867648 | tf_op jit(solution)/shard_map/own/pallas_call | solution.py:118
  63.4 1.5 collective-permute-start.10
  64.9 14.5 %partner.6 = (bf16[128,3328]{1,0:T(8,128)(2,1)S(1)}, bf16[128,3328]{1,0:T(8,128)(2,1)S(1)}, bf16[128,3328]{1,0:T(8,128)(2,1)}, bf16[128,3328]{1,0:T(8,128)(2,1)}) custom-call(s32[7]{0:T(128)S(1)} %slice_bitcast_fusion.2.place, bf16[256,2048]{1,0:T(8,128)(2,1)} %constant_dynamic-update-slice_fusion.tok_ref, bf16[2048,6656]{1,0:T(8,128)(2,1)} %gate_ref.19, ...), custom_call_target="tpu_custom_call" | custom-call | flops 27917287424 | bytes 122683392 | tf_op jit(solution)/shard_map/partner/pallas_call | solution.py:118
  80.4 4.5 %collective-permute-done.10 = bf16[2,64,3328]{2,1,0:T(8,128)(2,1)S(1)} collective-permute-done((bf16[2,64,3328]{2,1,0:T(8,128)(2,1)}, bf16[2,64,3328]{2,1,0:T(8,128)(2,1)S(1)}, u32[]{:S(2)}, u32[]{:S(2)}) %collective-permute-start.10) | collective-permute-done | bytes 852000 | tf_op jit(solution)/shard_map/ppermute | solution.py:173
  85.2 1.6 collective-permute-start.15
  88.6 17.7 %own.6 = (bf16[2,128,3328]{2,1,0:T(8,128)(2,1)}, bf16[2,128,3328]{2,1,0:T(8,128)(2,1)}) custom-call(s32[7]{0:T(128)S(1)} %slice_bitcast_fusion.2.place, bf16[256,2048]{1,0:T(8,128)(2,1)} %constant_dynamic-update-slice_fusion.tok_ref, bf16[2048,6656]{1,0:T(8,128)(2,1)} %gate_ref.19, bf16[2048,6656]{1,0:T(8,128)(2,1)} %up_ref.19, ...), custom_call_target="tpu_custom_call" | custom-call | flops 27917287424 | bytes 122683392 | tf_op jit(solution)/shard_map/own/pallas_call | solution.py:118
  107.1 14.6 %partner.7 = (bf16[128,3328]{1,0:T(8,128)(2,1)}, bf16[128,3328]{1,0:T(8,128)(2,1)S(1)}, bf16[128,3328]{1,0:T(8,128)(2,1)}, bf16[128,3328]{1,0:T(8,128)(2,1)}) custom-call(s32[7]{0:T(128)S(1)} %pad_add_fusion.place, bf16[256,2048]{1,0:T(8,128)(2,1)} %all-gather.3.cloned.1.call-done.tok_ref, bf16[2048,6656]{1,0:T(8,128)(2,1)} %gate_ref.19, ...), custom_call_target="tpu_custom_call" | custom-call | flops 27917287424 | bytes 122683392 | tf_op jit(solution)/shard_map/partner/pallas_call | solution.py:118
  122.9 14.5 %down.5 = bf16[128,2048]{1,0:T(8,128)(2,1)} custom-call(s32[7]{0:T(128)S(1)} %slice_bitcast_fusion.2.place, s32[1]{0:T(128)} %bitcast.5.col, bf16[64,3328]{1,0:T(8,128)(2,1)S(1)} %fusion.16.refs_0_, bf16[64,3328]{1,0:T(8,128)(2,1)S(1)} %collective-permute-done.15.refs_1_, bf16[64,3328]{1,0:T(8,128)(2,1)} %collective-permute-done.16.refs_2_, ...), custom_call_target="tpu_custom_call" | custom-call | flops 13958643712 | bytes 115867648 | tf_op jit(solution)/shard_map/down/pallas_call | solution.py:152
  137.4 17.3 %own.7 = (bf16[2,128,3328]{2,1,0:T(8,128)(2,1)}, bf16[2,128,3328]{2,1,0:T(8,128)(2,1)}) custom-call(s32[7]{0:T(128)S(1)} %pad_add_fusion.place, bf16[256,2048]{1,0:T(8,128)(2,1)} %all-gather.3.cloned.1.call-done.tok_ref, bf16[2048,6656]{1,0:T(8,128)(2,1)} %gate_ref.19, bf16[2048,6656]{1,0:T(8,128)(2,1)} %up_ref.19, ...), custom_call_target="tpu_custom_call" | custom-call | flops 27917287424 | bytes 122683392 | tf_op jit(solution)/shard_map/own/pallas_call | solution.py:118
  154.7 2.1 fusion.8.refs_0_
  156.8 1.6 collective-permute-start.27
  158.4 6.6 %all-gather.5.cloned.1.call-done.tok_ref = bf16[384,2048]{1,0:T(8,128)(2,1)} async-done(((bf16[384,512]{1,0:T(8,128)(2,1)}), bf16[384,2048]{1,0:T(8,128)(2,1)}) %all-gather.5.cloned.1.call-update) | async-done | bytes 1572880 | tf_op jit(solution)/shard_map/all_gather | solution.py:203
  165.0 14.9 %partner.8 = (bf16[128,3328]{1,0:T(8,128)(2,1)}, bf16[128,3328]{1,0:T(8,128)(2,1)}, bf16[128,3328]{1,0:T(8,128)(2,1)}, bf16[128,3328]{1,0:T(8,128)(2,1)}) custom-call(s32[7]{0:T(128)S(1)} %pad_add_fusion.place, bf16[384,2048]{1,0:T(8,128)(2,1)} %all-gather.5.cloned.1.call-done.tok_ref, bf16[2048,6656]{1,0:T(8,128)(2,1)} %gate_ref.19, bf16[2048,6656]{1,0:T(8,128)(2,1)} %up_ref.19), custom_call_target="tpu_custom_call" | custom-call | flops 27917287424 | bytes 122683392 | tf_op jit(solution)/shard_map/partner/pallas_call | solution.py:118
  181.1 1.5 collective-permute-start.30
  182.7 2.3 collective-permute-done.24.rest_1_
  185.1 2.4 collective-permute-done.26.rest_3_
  187.6 17.4 %own.8 = (bf16[2,128,3328]{2,1,0:T(8,128)(2,1)}, bf16[2,128,3328]{2,1,0:T(8,128)(2,1)}) custom-call(s32[7]{0:T(128)S(1)} %pad_add_fusion.place, bf16[384,2048]{1,0:T(8,128)(2,1)} %all-gather.5.cloned.1.call-done.tok_ref, bf16[2048,6656]{1,0:T(8,128)(2,1)} %gate_ref.19, bf16[2048,6656]{1,0:T(8,128)(2,1)} %up_ref.19, ...), custom_call_target="tpu_custom_call" | custom-call | flops 27917287424 | bytes 122683392 | tf_op jit(solution)/shard_map/own/pallas_call | solution.py:118
  206.8 16.4 %down.6 = bf16[256,2048]{1,0:T(8,128)(2,1)} custom-call(s32[7]{0:T(128)S(1)} %slice_bitcast_fusion.2.place, s32[1]{0:T(128)} %bitcast.5.col, bf16[128,3328]{1,0:T(8,128)(2,1)S(1)} %fusion.8.refs_0_, bf16[128,3328]{1,0:T(8,128)(2,1)S(1)} %collective-permute-done.27.refs_1_, bf16[128,3328]{1,0:T(8,128)(2,1)} %copy-done.13, bf16[128,3328]{1,0:T(8,128)(2,1)} %copy-done.15, ...), custom_call_target="tpu_custom_call" | custom-call | flops 27917287424 | bytes 122683392 | tf_op jit(solution)/shard_map/down/pallas_call | solution.py:152
  223.1 12.4 %partner.9 = (bf16[64,3328]{1,0:T(8,128)(2,1)}, bf16[64,3328]{1,0:T(8,128)(2,1)}, bf16[64,3328]{1,0:T(8,128)(2,1)}, bf16[64,3328]{1,0:T(8,128)(2,1)}) custom-call(s32[7]{0:T(128)S(1)} %pad_add_fusion.place, bf16[384,2048]{1,0:T(8,128)(2,1)} %all-gather.5.cloned.1.call-done.tok_ref, bf16[2048,6656]{1,0:T(8,128)(2,1)} %gate_ref.19, bf16[2048,6656]{1,0:T(8,128)(2,1)} %up_ref.19), custom_call_target="tpu_custom_call" | custom-call | flops 13958643712 | bytes 115867648 | tf_op jit(solution)/shard_map/partner/pallas_call | solution.py:118
  235.5 2.1 fusion.4.refs_0_
  237.6 1.5 collective-permute-start.35
  242.3 17.2 %collective-permute-done.35.refs_1_ = bf16[128,3328]{1,0:T(8,128)(2,1)S(1)} collective-permute-done((bf16[128,3328]{1,0:T(8,128)(2,1)S(1)}, bf16[128,3328]{1,0:T(8,128)(2,1)S(1)}, u32[]{:S(2)}, u32[]{:S(2)}) %collective-permute-start.35) | collective-permute-done | bytes 852000 | tf_op jit(solution)/shard_map/ppermute | solution.py:173
  259.5 13.1 %own.9 = (bf16[2,64,3328]{2,1,0:T(8,128)(2,1)}, bf16[2,64,3328]{2,1,0:T(8,128)(2,1)}) custom-call(s32[7]{0:T(128)S(1)} %pad_add_fusion.place, bf16[384,2048]{1,0:T(8,128)(2,1)} %all-gather.5.cloned.1.call-done.tok_ref, bf16[2048,6656]{1,0:T(8,128)(2,1)} %gate_ref.19, bf16[2048,6656]{1,0:T(8,128)(2,1)} %up_ref.19, ...), custom_call_target="tpu_custom_call" | custom-call | flops 13958643712 | bytes 115867648 | tf_op jit(solution)/shard_map/own/pallas_call | solution.py:118
  274.4 16.4 %down.7 = bf16[256,2048]{1,0:T(8,128)(2,1)} custom-call(s32[7]{0:T(128)S(1)} %slice_bitcast_fusion.2.place, s32[1]{0:T(128)} %bitcast.5.col, bf16[128,3328]{1,0:T(8,128)(2,1)S(1)} %fusion.4.refs_0_, bf16[128,3328]{1,0:T(8,128)(2,1)S(1)} %collective-permute-done.35.refs_1_, bf16[128,3328]{1,0:T(8,128)(2,1)} %copy-done.10, bf16[128,3328]{1,0:T(8,128)(2,1)} %copy-done.14, ...), custom_call_target="tpu_custom_call" | custom-call | flops 27917287424 | bytes 122683392 | tf_op jit(solution)/shard_map/down/pallas_call | solution.py:152
  290.8 4.6 %collective-permute-done.38 = bf16[2,128,3328]{2,1,0:T(8,128)(2,1)} collective-permute-done((bf16[2,128,3328]{2,1,0:T(8,128)(2,1)}, bf16[2,128,3328]{2,1,0:T(8,128)(2,1)}, u32[]{:S(2)}, u32[]{:S(2)}) %collective-permute-start.38) | collective-permute-done | bytes 1703968 | tf_op jit(solution)/shard_map/ppermute | solution.py:173
  295.4 2.1 fusion.refs_0_
  297.5 1.5 collective-permute-start.40
  299.6 19.9 %collective-permute-done.40.refs_1_ = bf16[128,3328]{1,0:T(8,128)(2,1)S(1)} collective-permute-done((bf16[128,3328]{1,0:T(8,128)(2,1)S(1)}, bf16[128,3328]{1,0:T(8,128)(2,1)S(1)}, u32[]{:S(2)}, u32[]{:S(2)}) %collective-permute-start.40) | collective-permute-done | bytes 852000 | tf_op jit(solution)/shard_map/ppermute | solution.py:173
  319.5 16.7 %collective-permute-done.39 = bf16[2,64,3328]{2,1,0:T(8,128)(2,1)S(1)} collective-permute-done((bf16[2,64,3328]{2,1,0:T(8,128)(2,1)S(1)}, bf16[2,64,3328]{2,1,0:T(8,128)(2,1)S(1)}, u32[]{:S(2)}, u32[]{:S(2)}) %collective-permute-start.39) | collective-permute-done | bytes 852000 | tf_op jit(solution)/shard_map/ppermute | solution.py:173
  336.5 1.5 collective-permute-start.43
  339.1 16.7 %down.8 = bf16[256,2048]{1,0:T(8,128)(2,1)} custom-call(s32[7]{0:T(128)S(1)} %slice_bitcast_fusion.2.place, s32[1]{0:T(128)} %bitcast.5.col, bf16[128,3328]{1,0:T(8,128)(2,1)S(1)} %fusion.refs_0_, bf16[128,3328]{1,0:T(8,128)(2,1)S(1)} %collective-permute-done.40.refs_1_, bf16[128,3328]{1,0:T(8,128)(2,1)} %copy-done.12, ...), custom_call_target="tpu_custom_call" | custom-call | flops 27917287424 | bytes 122683392 | tf_op jit(solution)/shard_map/down/pallas_call | solution.py:152
  359.1 13.7 %down.9 = (bf16[128,512]{1,0:T(8,128)(2,1)S(1)}, bf16[128,512]{1,0:T(8,128)(2,1)S(1)}, bf16[128,512]{1,0:T(8,128)(2,1)S(1)}, bf16[128,512]{1,0:T(8,128)(2,1)S(1)}) custom-call(s32[7]{0:T(128)S(1)} %slice_bitcast_fusion.2.place, s32[1]{0:T(128)} %bitcast.5.col, bf16[64,3328]{1,0:T(8,128)(2,1)S(1)} %fusion.12.refs_0_, ...), custom_call_target="tpu_custom_call" | custom-call | flops 13958643712 | bytes 115867648 | tf_op jit(solution)/shard_map/down/pallas_call | solution.py:152
  374.0 2.8 collective-permute-start.48
  377.8 21.9 %reduce-scatter.11.cloned.1.call-done = bf16[256,512]{1,0:T(8,128)(2,1)} async-done(((bf16[256,2048]{1,0:T(8,128)(2,1)}), bf16[256,512]{1,0:T(8,128)(2,1)}) %reduce-scatter.11.cloned.1.call-update) | async-done | bytes 262160 | tf_op jit(solution)/shard_map/reduce_scatter | solution.py:239
  (141 shorter events, 28.0 us)
Async XLA Ops:
  6.5 100.5 %all-gather.3.cloned.1.call-start = ((), (), s32[]{:S(2)}) async-start(), calls=%async_computation.4 | async-start | bytes 1310720 | tf_op jit(solution)/shard_map/all_gather | solution.py:202
  7.5 12.1 %collective-permute-start = (bf16[128,512]{1,0:T(8,128)(2,1)S(1)}, bf16[128,512]{1,0:T(8,128)(2,1)S(1)}, u32[]{:S(2)}, u32[]{:S(2)}) collective-permute-start(bf16[128,512]{1,0:T(8,128)(2,1)S(1)} %slice.102), channel_id=1, source_target_pairs={{0,1},{1,2},{2,3},{3,0},{4,5},{5,6},{6,7},{7,4},{8,9},{9,10},{10,1... | collective-permute-start | bytes 393224 | tf_op jit(solution)/shard_map/ppermute | solution.py:169
  10.5 11.2 %collective-permute-start.1 = (bf16[128,512]{1,0:T(8,128)(2,1)S(1)}, bf16[128,512]{1,0:T(8,128)(2,1)S(1)}, u32[]{:S(2)}, u32[]{:S(2)}) collective-permute-start(bf16[128,512]{1,0:T(8,128)(2,1)S(1)} %slice.102), channel_id=1, source_target_pairs={{0,2},{1,3},{2,0},{3,1},{4,6},{5,7},{6,4},{7,5},{8,10},{9,11},{10,... | collective-permute-start | bytes 393224 | tf_op jit(solution)/shard_map/ppermute | solution.py:169
  13.1 8.6 %collective-permute-start.2 = (bf16[128,512]{1,0:T(8,128)(2,1)S(1)}, bf16[128,512]{1,0:T(8,128)(2,1)S(1)}, u32[]{:S(2)}, u32[]{:S(2)}) collective-permute-start(bf16[128,512]{1,0:T(8,128)(2,1)S(1)} %slice.102), channel_id=1, source_target_pairs={{0,3},{1,0},{2,1},{3,2},{4,7},{5,4},{6,5},{7,6},{8,11},{9,8},{10,9... | collective-permute-start | bytes 393224 | tf_op jit(solution)/shard_map/ppermute | solution.py:169
  21.8 18.3 %collective-permute-start.7 = (bf16[256,512]{1,0:T(8,128)(2,1)}, bf16[256,512]{1,0:T(8,128)(2,1)S(1)}, u32[]{:S(2)}, u32[]{:S(2)}) collective-permute-start(bf16[256,512]{1,0:T(8,128)(2,1)} %get-tuple-element.69), channel_id=1, source_target_pairs={{0,1},{1,2},{2,3},{3,0},{4,5},{5,6},{6,7},{7,4},{8,9},{9,10},{10,1... | collective-permute-start | bytes 786440 | tf_op jit(solution)/shard_map/ppermute | solution.py:169
  25.0 18.2 %collective-permute-start.8 = (bf16[256,512]{1,0:T(8,128)(2,1)}, bf16[256,512]{1,0:T(8,128)(2,1)S(1)}, u32[]{:S(2)}, u32[]{:S(2)}) collective-permute-start(bf16[256,512]{1,0:T(8,128)(2,1)} %get-tuple-element.69), channel_id=1, source_target_pairs={{0,2},{1,3},{2,0},{3,1},{4,6},{5,7},{6,4},{7,5},{8,10},{9,11},{10,... | collective-permute-start | bytes 786440 | tf_op jit(solution)/shard_map/ppermute | solution.py:169
  26.7 22.0 %collective-permute-start.9 = (bf16[256,512]{1,0:T(8,128)(2,1)}, bf16[256,512]{1,0:T(8,128)(2,1)}, u32[]{:S(2)}, u32[]{:S(2)}) collective-permute-start(bf16[256,512]{1,0:T(8,128)(2,1)} %get-tuple-element.69), channel_id=1, source_target_pairs={{0,3},{1,0},{2,1},{3,2},{4,7},{5,4},{6,5},{7,6},{8,11},{9,8},{10,9... | collective-permute-start | bytes 786440 | tf_op jit(solution)/shard_map/ppermute | solution.py:169
  39.4 10.9 %collective-permute-start.3 = (bf16[64,3328]{1,0:T(8,128)(2,1)S(1)}, bf16[64,3328]{1,0:T(8,128)(2,1)S(1)}, u32[]{:S(2)}, u32[]{:S(2)}) collective-permute-start(bf16[64,3328]{1,0:T(8,128)(2,1)S(1)} %get-tuple-element.61), channel_id=1, source_target_pairs={{0,4},{4,0},{8,12},{12,8},{1,5},{5,1},{9,13},{13,9},{2,6},{6,2},{1... | collective-permute-start | bytes 1277960 | tf_op jit(solution)/shard_map/ppermute | solution.py:173
  39.5 10.9 %collective-permute-start.4 = (bf16[64,3328]{1,0:T(8,128)(2,1)S(1)}, bf16[64,3328]{1,0:T(8,128)(2,1)S(1)}, u32[]{:S(2)}, u32[]{:S(2)}) collective-permute-start(bf16[64,3328]{1,0:T(8,128)(2,1)S(1)} %get-tuple-element.62), channel_id=1, source_target_pairs={{0,4},{4,0},{8,12},{12,8},{1,5},{5,1},{9,13},{13,9},{2,6},{6,2},{1... | collective-permute-start | bytes 1277960 | tf_op jit(solution)/shard_map/ppermute | solution.py:173
  40.0 10.4 %collective-permute-start.5 = (bf16[64,3328]{1,0:T(8,128)(2,1)S(1)}, bf16[64,3328]{1,0:T(8,128)(2,1)S(1)}, u32[]{:S(2)}, u32[]{:S(2)}) collective-permute-start(bf16[64,3328]{1,0:T(8,128)(2,1)S(1)} %get-tuple-element.63), channel_id=1, source_target_pairs={{0,4},{4,0},{8,12},{12,8},{1,5},{5,1},{9,13},{13,9},{2,6},{6,2},{1... | collective-permute-start | bytes 1277960 | tf_op jit(solution)/shard_map/ppermute | solution.py:173
  43.3 7.1 %collective-permute-start.6 = (bf16[64,3328]{1,0:T(8,128)(2,1)S(1)}, bf16[64,3328]{1,0:T(8,128)(2,1)S(1)}, u32[]{:S(2)}, u32[]{:S(2)}) collective-permute-start(bf16[64,3328]{1,0:T(8,128)(2,1)S(1)} %get-tuple-element.64), channel_id=1, source_target_pairs={{0,4},{4,0},{8,12},{12,8},{1,5},{5,1},{9,13},{13,9},{2,6},{6,2},{1... | collective-permute-start | bytes 1277960 | tf_op jit(solution)/shard_map/ppermute | solution.py:173
  45.1 120.0 %all-gather.5.cloned.1.call-start = ((), (), s32[]{:S(2)}) async-start(), calls=%async_computation.6 | async-start | bytes 1966080 | tf_op jit(solution)/shard_map/all_gather | solution.py:203
  63.4 21.5 %collective-permute-start.10 = (bf16[2,64,3328]{2,1,0:T(8,128)(2,1)}, bf16[2,64,3328]{2,1,0:T(8,128)(2,1)S(1)}, u32[]{:S(2)}, u32[]{:S(2)}) collective-permute-start(bf16[2,64,3328]{2,1,0:T(8,128)(2,1)} %get-tuple-element.67), channel_id=1, source_target_pairs={{0,8},{4,12},{8,0},{12,4},{1,9},{5,13},{9,1},{13,5},{2,10},{6,14},... | collective-permute-start | bytes 2555912 | tf_op jit(solution)/shard_map/ppermute | solution.py:173
  79.3 7.5 %collective-permute-start.11 = (bf16[128,3328]{1,0:T(8,128)(2,1)S(1)}, bf16[128,3328]{1,0:T(8,128)(2,1)S(1)}, u32[]{:S(2)}, u32[]{:S(2)}) collective-permute-start(bf16[128,3328]{1,0:T(8,128)(2,1)S(1)} %get-tuple-element.70), channel_id=1, source_target_pairs={{0,4},{4,0},{8,12},{12,8},{1,5},{5,1},{9,13},{13,9},{2,6},{6,2},{1... | collective-permute-start | bytes 2555912 | tf_op jit(solution)/shard_map/ppermute | solution.py:173
  79.5 7.3 %collective-permute-start.12 = (bf16[128,3328]{1,0:T(8,128)(2,1)S(1)}, bf16[128,3328]{1,0:T(8,128)(2,1)S(1)}, u32[]{:S(2)}, u32[]{:S(2)}) collective-permute-start(bf16[128,3328]{1,0:T(8,128)(2,1)S(1)} %get-tuple-element.71), channel_id=1, source_target_pairs={{0,4},{4,0},{8,12},{12,8},{1,5},{5,1},{9,13},{13,9},{2,6},{6,2},{1... | collective-permute-start | bytes 2555912 | tf_op jit(solution)/shard_map/ppermute | solution.py:173
  79.8 7.0 %collective-permute-start.13 = (bf16[128,3328]{1,0:T(8,128)(2,1)}, bf16[128,3328]{1,0:T(8,128)(2,1)S(1)}, u32[]{:S(2)}, u32[]{:S(2)}) collective-permute-start(bf16[128,3328]{1,0:T(8,128)(2,1)} %get-tuple-element.72), channel_id=1, source_target_pairs={{0,4},{4,0},{8,12},{12,8},{1,5},{5,1},{9,13},{13,9},{2,6},{6,2},{1... | collective-permute-start | bytes 2555912 | tf_op jit(solution)/shard_map/ppermute | solution.py:173
  80.0 6.8 %collective-permute-start.14 = (bf16[128,3328]{1,0:T(8,128)(2,1)}, bf16[128,3328]{1,0:T(8,128)(2,1)S(1)}, u32[]{:S(2)}, u32[]{:S(2)}) collective-permute-start(bf16[128,3328]{1,0:T(8,128)(2,1)} %get-tuple-element.73), channel_id=1, source_target_pairs={{0,4},{4,0},{8,12},{12,8},{1,5},{5,1},{9,13},{13,9},{2,6},{6,2},{1... | collective-permute-start | bytes 2555912 | tf_op jit(solution)/shard_map/ppermute | solution.py:173
  85.2 21.8 %collective-permute-start.15 = (bf16[64,3328]{1,0:T(8,128)(2,1)S(1)}, bf16[64,3328]{1,0:T(8,128)(2,1)S(1)}, u32[]{:S(2)}, u32[]{:S(2)}) collective-permute-start(bf16[64,3328]{1,0:T(8,128)(2,1)S(1)} %fusion.16.refs_0_), channel_id=1, source_target_pairs={{0,8},{4,12},{8,0},{12,4},{1,9},{5,13},{9,1},{13,5},{2,10},{6,14},... | collective-permute-start | bytes 1277960 | tf_op jit(solution)/shard_map/ppermute | solution.py:173
  86.8 35.5 %collective-permute-start.16 = (bf16[64,3328]{1,0:T(8,128)(2,1)S(1)}, bf16[64,3328]{1,0:T(8,128)(2,1)}, u32[]{:S(2)}, u32[]{:S(2)}) collective-permute-start(bf16[64,3328]{1,0:T(8,128)(2,1)S(1)} %fusion.16.refs_0_), channel_id=1, source_target_pairs={{0,4},{4,0},{8,12},{12,8},{1,5},{5,1},{9,13},{13,9},{2,6},{6,2},{1... | collective-permute-start | bytes 1277960 | tf_op jit(solution)/shard_map/ppermute | solution.py:173
  106.4 48.3 %collective-permute-start.22 = (bf16[2,128,3328]{2,1,0:T(8,128)(2,1)}, bf16[2,128,3328]{2,1,0:T(8,128)(2,1)}, u32[]{:S(2)}, u32[]{:S(2)}) collective-permute-start(bf16[2,128,3328]{2,1,0:T(8,128)(2,1)} %get-tuple-element.76), channel_id=1, source_target_pairs={{0,8},{4,12},{8,0},{12,4},{1,9},{5,13},{9,1},{13,5},{2,10},{6,14},... | collective-permute-start | bytes 5111816 | tf_op jit(solution)/shard_map/ppermute | solution.py:173
  107.0 15.8 %collective-permute-start.17 = (bf16[64,3328]{1,0:T(8,128)(2,1)S(1)}, bf16[64,3328]{1,0:T(8,128)(2,1)}, u32[]{:S(2)}, u32[]{:S(2)}) collective-permute-start(bf16[64,3328]{1,0:T(8,128)(2,1)S(1)} %collective-permute-done.15.refs_1_), channel_id=1, source_target_pairs={{0,4},{4,0},{8,12},{12,8},{1,5},{5,1},{9,13},{13,9},{2,6},{6,2},{1... | collective-permute-start | bytes 1277960 | tf_op jit(solution)/shard_map/ppermute | solution.py:173
  121.7 15.7 %collective-permute-start.18 = (bf16[128,3328]{1,0:T(8,128)(2,1)}, bf16[128,3328]{1,0:T(8,128)(2,1)S(1)}, u32[]{:S(2)}, u32[]{:S(2)}) collective-permute-start(bf16[128,3328]{1,0:T(8,128)(2,1)} %get-tuple-element.79), channel_id=1, source_target_pairs={{0,4},{4,0},{8,12},{12,8},{1,5},{5,1},{9,13},{13,9},{2,6},{6,2},{1... | collective-permute-start | bytes 2555912 | tf_op jit(solution)/shard_map/ppermute | solution.py:173
  122.1 15.3 %collective-permute-start.19 = (bf16[128,3328]{1,0:T(8,128)(2,1)S(1)}, bf16[128,3328]{1,0:T(8,128)(2,1)S(1)}, u32[]{:S(2)}, u32[]{:S(2)}) collective-permute-start(bf16[128,3328]{1,0:T(8,128)(2,1)S(1)} %get-tuple-element.80), channel_id=1, source_target_pairs={{0,4},{4,0},{8,12},{12,8},{1,5},{5,1},{9,13},{13,9},{2,6},{6,2},{1... | collective-permute-start | bytes 2555912 | tf_op jit(solution)/shard_map/ppermute | solution.py:173
  122.2 234.2 %reduce-scatter.5.cloned.1.call-start = ((), (), s32[]{:S(2)}) async-start(), calls=%async_computation.5 | async-start | bytes 655360 | tf_op jit(solution)/shard_map/reduce_scatter | solution.py:239
  122.3 15.2 %collective-permute-start.20 = (bf16[128,3328]{1,0:T(8,128)(2,1)}, bf16[128,3328]{1,0:T(8,128)(2,1)}, u32[]{:S(2)}, u32[]{:S(2)}) collective-permute-start(bf16[128,3328]{1,0:T(8,128)(2,1)} %get-tuple-element.81), channel_id=1, source_target_pairs={{0,4},{4,0},{8,12},{12,8},{1,5},{5,1},{9,13},{13,9},{2,6},{6,2},{1... | collective-permute-start | bytes 2555912 | tf_op jit(solution)/shard_map/ppermute | solution.py:173
  122.8 14.7 %collective-permute-start.21 = (bf16[128,3328]{1,0:T(8,128)(2,1)}, bf16[128,3328]{1,0:T(8,128)(2,1)}, u32[]{:S(2)}, u32[]{:S(2)}) collective-permute-start(bf16[128,3328]{1,0:T(8,128)(2,1)} %get-tuple-element.82), channel_id=1, source_target_pairs={{0,4},{4,0},{8,12},{12,8},{1,5},{5,1},{9,13},{13,9},{2,6},{6,2},{1... | collective-permute-start | bytes 2555912 | tf_op jit(solution)/shard_map/ppermute | solution.py:173
  156.8 24.2 %collective-permute-start.27 = (bf16[128,3328]{1,0:T(8,128)(2,1)S(1)}, bf16[128,3328]{1,0:T(8,128)(2,1)S(1)}, u32[]{:S(2)}, u32[]{:S(2)}) collective-permute-start(bf16[128,3328]{1,0:T(8,128)(2,1)S(1)} %fusion.8.refs_0_), channel_id=1, source_target_pairs={{0,8},{4,12},{8,0},{12,4},{1,9},{5,13},{9,1},{13,5},{2,10},{6,14},... | collective-permute-start | bytes 2555912 | tf_op jit(solution)/shard_map/ppermute | solution.py:173
  180.5 7.1 %collective-permute-start.26 = (bf16[128,3328]{1,0:T(8,128)(2,1)}, bf16[128,3328]{1,0:T(8,128)(2,1)}, u32[]{:S(2)}, u32[]{:S(2)}) collective-permute-start(bf16[128,3328]{1,0:T(8,128)(2,1)} %get-tuple-element.93), channel_id=1, source_target_pairs={{0,4},{4,0},{8,12},{12,8},{1,5},{5,1},{9,13},{13,9},{2,6},{6,2},{1... | collective-permute-start | bytes 2555912 | tf_op jit(solution)/shard_map/ppermute | solution.py:173
  181.0 176.3 %reduce-scatter.7.cloned.1.call-start = ((), (), s32[]{:S(2)}) async-start(), calls=%async_computation.7 | async-start | bytes 1310720 | tf_op jit(solution)/shard_map/reduce_scatter | solution.py:239
  181.1 54.4 %collective-permute-start.30 = (bf16[2,128,3328]{2,1,0:T(8,128)(2,1)}, bf16[2,128,3328]{2,1,0:T(8,128)(2,1)}, u32[]{:S(2)}, u32[]{:S(2)}) collective-permute-start(bf16[2,128,3328]{2,1,0:T(8,128)(2,1)} %get-tuple-element.86), channel_id=1, source_target_pairs={{0,8},{4,12},{8,0},{12,4},{1,9},{5,13},{9,1},{13,5},{2,10},{6,14},... | collective-permute-start | bytes 5111816 | tf_op jit(solution)/shard_map/ppermute | solution.py:173
  182.6 22.3 %collective-permute-start.28 = (bf16[128,3328]{1,0:T(8,128)(2,1)S(1)}, bf16[128,3328]{1,0:T(8,128)(2,1)S(1)}, u32[]{:S(2)}, u32[]{:S(2)}) collective-permute-start(bf16[128,3328]{1,0:T(8,128)(2,1)S(1)} %fusion.8.refs_0_), channel_id=1, source_target_pairs={{0,4},{4,0},{8,12},{12,8},{1,5},{5,1},{9,13},{13,9},{2,6},{6,2},{1... | collective-permute-start | bytes 2555912 | tf_op jit(solution)/shard_map/ppermute | solution.py:173
  185.0 19.9 %collective-permute-start.29 = (bf16[128,3328]{1,0:T(8,128)(2,1)S(1)}, bf16[128,3328]{1,0:T(8,128)(2,1)S(1)}, u32[]{:S(2)}, u32[]{:S(2)}) collective-permute-start(bf16[128,3328]{1,0:T(8,128)(2,1)S(1)} %collective-permute-done.27.refs_1_), channel_id=1, source_target_pairs={{0,4},{4,0},{8,12},{12,8},{1,5},{5,1},{9,13},{13,9},{2,6},{6,2},{1... | collective-permute-start | bytes 2555912 | tf_op jit(solution)/shard_map/ppermute | solution.py:173
  237.6 21.8 %collective-permute-start.35 = (bf16[128,3328]{1,0:T(8,128)(2,1)S(1)}, bf16[128,3328]{1,0:T(8,128)(2,1)S(1)}, u32[]{:S(2)}, u32[]{:S(2)}) collective-permute-start(bf16[128,3328]{1,0:T(8,128)(2,1)S(1)} %fusion.4.refs_0_), channel_id=1, source_target_pairs={{0,8},{4,12},{8,0},{12,4},{1,9},{5,13},{9,1},{13,5},{2,10},{6,14},... | collective-permute-start | bytes 2555912 | tf_op jit(solution)/shard_map/ppermute | solution.py:173
  239.7 19.8 %collective-permute-start.33 = (bf16[64,3328]{1,0:T(8,128)(2,1)}, bf16[64,3328]{1,0:T(8,128)(2,1)S(1)}, u32[]{:S(2)}, u32[]{:S(2)}) collective-permute-start(bf16[64,3328]{1,0:T(8,128)(2,1)} %get-tuple-element.101), channel_id=1, source_target_pairs={{0,4},{4,0},{8,12},{12,8},{1,5},{5,1},{9,13},{13,9},{2,6},{6,2},{1... | collective-permute-start | bytes 1277960 | tf_op jit(solution)/shard_map/ppermute | solution.py:173
  239.7 19.8 %collective-permute-start.34 = (bf16[64,3328]{1,0:T(8,128)(2,1)}, bf16[64,3328]{1,0:T(8,128)(2,1)S(1)}, u32[]{:S(2)}, u32[]{:S(2)}) collective-permute-start(bf16[64,3328]{1,0:T(8,128)(2,1)} %get-tuple-element.102), channel_id=1, source_target_pairs={{0,4},{4,0},{8,12},{12,8},{1,5},{5,1},{9,13},{13,9},{2,6},{6,2},{1... | collective-permute-start | bytes 1277960 | tf_op jit(solution)/shard_map/ppermute | solution.py:173
  240.2 136.6 %reduce-scatter.9.cloned.1.call-start = ((), (), s32[]{:S(2)}) async-start(), calls=%async_computation.8 | async-start | bytes 1310720 | tf_op jit(solution)/shard_map/reduce_scatter | solution.py:239
  241.1 31.4 %collective-permute-start.36 = (bf16[128,3328]{1,0:T(8,128)(2,1)S(1)}, bf16[128,3328]{1,0:T(8,128)(2,1)S(1)}, u32[]{:S(2)}, u32[]{:S(2)}) collective-permute-start(bf16[128,3328]{1,0:T(8,128)(2,1)S(1)} %fusion.4.refs_0_), channel_id=1, source_target_pairs={{0,4},{4,0},{8,12},{12,8},{1,5},{5,1},{9,13},{13,9},{2,6},{6,2},{1... | collective-permute-start | bytes 2555912 | tf_op jit(solution)/shard_map/ppermute | solution.py:173
  241.8 53.7 %collective-permute-start.38 = (bf16[2,128,3328]{2,1,0:T(8,128)(2,1)}, bf16[2,128,3328]{2,1,0:T(8,128)(2,1)}, u32[]{:S(2)}, u32[]{:S(2)}) collective-permute-start(bf16[2,128,3328]{2,1,0:T(8,128)(2,1)} %get-tuple-element.95), channel_id=1, source_target_pairs={{0,8},{4,12},{8,0},{12,4},{1,9},{5,13},{9,1},{13,5},{2,10},{6,14},... | collective-permute-start | bytes 5111816 | tf_op jit(solution)/shard_map/ppermute | solution.py:173
  259.5 13.1 %collective-permute-start.37 = (bf16[128,3328]{1,0:T(8,128)(2,1)S(1)}, bf16[128,3328]{1,0:T(8,128)(2,1)S(1)}, u32[]{:S(2)}, u32[]{:S(2)}) collective-permute-start(bf16[128,3328]{1,0:T(8,128)(2,1)S(1)} %collective-permute-done.35.refs_1_), channel_id=1, source_target_pairs={{0,4},{4,0},{8,12},{12,8},{1,5},{5,1},{9,13},{13,9},{2,6},{6,2},{1... | collective-permute-start | bytes 2555912 | tf_op jit(solution)/shard_map/ppermute | solution.py:173
  297.5 21.9 %collective-permute-start.40 = (bf16[128,3328]{1,0:T(8,128)(2,1)S(1)}, bf16[128,3328]{1,0:T(8,128)(2,1)S(1)}, u32[]{:S(2)}, u32[]{:S(2)}) collective-permute-start(bf16[128,3328]{1,0:T(8,128)(2,1)S(1)} %fusion.refs_0_), channel_id=1, source_target_pairs={{0,8},{4,12},{8,0},{12,4},{1,9},{5,13},{9,1},{13,5},{2,10},{6,14},... | collective-permute-start | bytes 2555912 | tf_op jit(solution)/shard_map/ppermute | solution.py:173
  299.1 37.1 %collective-permute-start.39 = (bf16[2,64,3328]{2,1,0:T(8,128)(2,1)S(1)}, bf16[2,64,3328]{2,1,0:T(8,128)(2,1)S(1)}, u32[]{:S(2)}, u32[]{:S(2)}) collective-permute-start(bf16[2,64,3328]{2,1,0:T(8,128)(2,1)S(1)} %copy-done.8), channel_id=1, source_target_pairs={{0,8},{4,12},{8,0},{12,4},{1,9},{5,13},{9,1},{13,5},{2,10},{6,14},... | collective-permute-start | bytes 2555912 | tf_op jit(solution)/shard_map/ppermute | solution.py:173
  299.6 38.5 %collective-permute-start.41 = (bf16[128,3328]{1,0:T(8,128)(2,1)S(1)}, bf16[128,3328]{1,0:T(8,128)(2,1)S(1)}, u32[]{:S(2)}, u32[]{:S(2)}) collective-permute-start(bf16[128,3328]{1,0:T(8,128)(2,1)S(1)} %fusion.refs_0_), channel_id=1, source_target_pairs={{0,4},{4,0},{8,12},{12,8},{1,5},{5,1},{9,13},{13,9},{2,6},{6,2},{1... | collective-permute-start | bytes 2555912 | tf_op jit(solution)/shard_map/ppermute | solution.py:173
  319.5 18.7 %collective-permute-start.42 = (bf16[128,3328]{1,0:T(8,128)(2,1)S(1)}, bf16[128,3328]{1,0:T(8,128)(2,1)}, u32[]{:S(2)}, u32[]{:S(2)}) collective-permute-start(bf16[128,3328]{1,0:T(8,128)(2,1)S(1)} %collective-permute-done.40.refs_1_), channel_id=1, source_target_pairs={{0,4},{4,0},{8,12},{12,8},{1,5},{5,1},{9,13},{13,9},{2,6},{6,2},{1... | collective-permute-start | bytes 2555912 | tf_op jit(solution)/shard_map/ppermute | solution.py:173
  336.5 19.4 %collective-permute-start.43 = (bf16[64,3328]{1,0:T(8,128)(2,1)S(1)}, bf16[64,3328]{1,0:T(8,128)(2,1)S(1)}, u32[]{:S(2)}, u32[]{:S(2)}) collective-permute-start(bf16[64,3328]{1,0:T(8,128)(2,1)S(1)} %fusion.12.refs_0_), channel_id=1, source_target_pairs={{0,8},{4,12},{8,0},{12,4},{1,9},{5,13},{9,1},{13,5},{2,10},{6,14},... | collective-permute-start | bytes 1277960 | tf_op jit(solution)/shard_map/ppermute | solution.py:173
  338.1 61.7 %reduce-scatter.11.cloned.1.call-start = ((), (), s32[]{:S(2)}) async-start(), calls=%async_computation.9 | async-start | bytes 1310720 | tf_op jit(solution)/shard_map/reduce_scatter | solution.py:239
  372.8 27.9 %collective-permute-start.46 = (bf16[128,512]{1,0:T(8,128)(2,1)S(1)}, bf16[128,512]{1,0:T(8,128)(2,1)S(1)}, u32[]{:S(2)}, u32[]{:S(2)}) collective-permute-start(bf16[128,512]{1,0:T(8,128)(2,1)S(1)} %get-tuple-element.114), channel_id=1, source_target_pairs={{0,1},{1,2},{2,3},{3,0},{4,5},{5,6},{6,7},{7,4},{8,9},{9,10},{10,1... | collective-permute-start | bytes 393224 | tf_op jit(solution)/shard_map/ppermute | solution.py:169
  373.1 27.6 %collective-permute-start.47 = (bf16[128,512]{1,0:T(8,128)(2,1)S(1)}, bf16[128,512]{1,0:T(8,128)(2,1)S(1)}, u32[]{:S(2)}, u32[]{:S(2)}) collective-permute-start(bf16[128,512]{1,0:T(8,128)(2,1)S(1)} %get-tuple-element.115), channel_id=1, source_target_pairs={{0,2},{1,3},{2,0},{3,1},{4,6},{5,7},{6,4},{7,5},{8,10},{9,11},{10,... | collective-permute-start | bytes 393224 | tf_op jit(solution)/shard_map/ppermute | solution.py:169
  374.0 26.7 %collective-permute-start.48 = (bf16[128,512]{1,0:T(8,128)(2,1)S(1)}, bf16[128,512]{1,0:T(8,128)(2,1)S(1)}, u32[]{:S(2)}, u32[]{:S(2)}) collective-permute-start(bf16[128,512]{1,0:T(8,128)(2,1)S(1)} %get-tuple-element.116), channel_id=1, source_target_pairs={{0,3},{1,0},{2,1},{3,2},{4,7},{5,4},{6,5},{7,6},{8,11},{9,8},{10,9... | collective-permute-start | bytes 393224 | tf_op jit(solution)/shard_map/ppermute | solution.py:169
  (24 other events, 162.6 us)
Sparse Core Ops, SparseCore 0:
  45.2 33.3 all-gather.2
  122.3 42.6 all-gather.4
  181.1 20.3 reduce-scatter.4
  240.3 25.0 reduce-scatter.6
  338.2 25.0 reduce-scatter.8
  365.5 34.2 reduce-scatter.10

commit v2 on v1

v2 whole, which is shorter than its diff:
```python
import functools

import jax
import jax.numpy as jnp
import numpy as np
from jax import lax
from jax.experimental import pallas as pl
from jax.experimental.pallas import tpu as pltpu
from jax.sharding import PartitionSpec as P

BF16, F32 = jnp.bfloat16, jnp.float32
GATE_UP_COST, DOWN_COST = 0.3, 4
SPLIT = (0, 1)
VMEM_LIMIT = 32 * 2**20
PARTNER, OWN, X, BLOCKS = 0, 1, 2, 3


def dot(a, b):
    return jnp.dot(a, b, preferred_element_type=F32)


def accumulate(place, token_refs, gate_ref, up_ref, stage, acc):
    step, depth = pl.program_id(0), gate_ref.shape[0]

    @pl.when(step == 0)
    def _():
        acc[...] = jnp.zeros_like(acc)
        for k in range(stage.shape[0]):
            if len(token_refs) == 1:
                stage[k] = token_refs[0][:, k * depth : (k + 1) * depth]
            else:
                stage[k] = token_refs[k][...]

    tok = stage[step]
    acc[0] += dot(tok, gate_ref[...])
    acc[1] += dot(tok, up_ref[...])


def pieces_of(rows, split):
    half = rows // 2
    if not split:
        return [(slice(0, 2), slice(0, rows))]
    return [(slice(w, w + 1), slice(at, at + half)) for w in (0, 1) for at in (0, half)]


def partner_kernel(n_tok, split, place, *refs):
    token_refs, (gate_ref, up_ref, *out_refs), (stage, acc) = refs[:n_tok], refs[n_tok:-2], refs[-2:]
    accumulate(place, token_refs, gate_ref, up_ref, stage, acc)

    @pl.when(pl.program_id(0) == pl.num_programs(0) - 1)
    def _():
        for (which, rows), out_ref in zip(pieces_of(acc.shape[1], split), out_refs):
            out_ref[...] = acc[which, rows].astype(BF16)


def own_kernel(n_tok, split, place, *refs):
    token_refs, (gate_ref, up_ref, *received_refs) = refs[:n_tok], refs[n_tok:-4]
    send_ref, keep_ref, stage, acc = refs[-4:]
    accumulate(place, token_refs, gate_ref, up_ref, stage, acc)
    half = send_ref.shape[1]

    @pl.when(pl.program_id(0) == pl.num_programs(0) - 1)
    def _():
        for (which, rows), ref in zip(pieces_of(acc.shape[1], split), received_refs):
            acc[which, rows] += ref[...].astype(F32)
        for ref, x in ((send_ref, 1 - place[X]), (keep_ref, place[X])):
            ref[...] = acc[:, pl.ds(pl.multiple_of(x * half, half), half), :].astype(BF16)


def down_kernel(n_col, split, place, col, own_x, other_x, own_x_core, other_x_core, weight_ref, *rest):
    out_refs, (own_half, partner_half) = rest[:-2], rest[-2:]
    step = pl.program_id(0)
    height, wide = own_x.shape

    @pl.when(step == 0)
    def _():
        for target, mine, other in ((own_half, own_x, other_x), (partner_half, own_x_core, other_x_core)):
            target[pl.ds(pl.multiple_of(place[X] * height, height), height), :] = mine[...]
            target[pl.ds(pl.multiple_of((1 - place[X]) * height, height), height), :] = other[...]

    block = weight_ref.shape[1] // n_col
    at = lax.rem(col[0] + step + 1, n_col) if split else step
    columns = pl.ds(pl.multiple_of(at * block, block), block)
    total = dot(own_half[...], weight_ref[pl.ds(pl.multiple_of(place[OWN] * wide, wide), wide), columns])
    total += dot(partner_half[...], weight_ref[pl.ds(pl.multiple_of(place[PARTNER] * wide, wide), wide), columns])
    value = total.astype(BF16)
    if not split:
        out_refs[0][...] = value
        return
    for k, out_ref in enumerate(out_refs):
        @pl.when(step == k)
        def _(out_ref=out_ref):
            out_ref[...] = value


def whole(shape):
    return pl.BlockSpec(shape, lambda *_: (0,) * len(shape), pipeline_mode=pl.Buffered(1))


def params(n):
    return pltpu.CompilerParams(dimension_semantics=("arbitrary",) * n, vmem_limit_bytes=VMEM_LIMIT)


def cost(scale, flops, *sizes):
    return pl.CostEstimate(flops=int(flops * scale), bytes_accessed=int(sum(sizes) * scale), transcendentals=0)


def gate_up_call(place, tokens, rows, row_block, weights, n_col, which, split, received=None):
    full, wide = weights[0].shape[0], weights[0].shape[1] // 2
    depth, half = full // n_col, rows // 2
    weight = pl.BlockSpec((depth, wide), lambda k, place: (place[BLOCKS + k], place[which]))
    token = pl.BlockSpec(
        (rows, tokens[0].shape[1]), lambda k, place: (row_block, 0), pipeline_mode=pl.Buffered(1)
    )
    in_specs = [token] * len(tokens) + [weight, weight]
    operands = [*tokens, *weights]
    shapes = [(w.stop - w.start, r.stop - r.start, wide) for w, r in pieces_of(rows, split)]
    if received is None:
        body, name = partner_kernel, "partner"
        out_shape, out_specs = [jax.ShapeDtypeStruct(a, BF16) for a in shapes], [whole(a) for a in shapes]
    else:
        body, name = own_kernel, "own"
        out_shape, out_specs = [jax.ShapeDtypeStruct((2, half, wide), BF16)] * 2, [whole((2, half, wide))] * 2
        in_specs += [whole(a) for a in shapes]
        operands += received
    return pl.pallas_call(
        functools.partial(body, len(tokens), split),
        out_shape=out_shape,
        grid_spec=pltpu.PrefetchScalarGridSpec(
            num_scalar_prefetch=1,
            grid=(n_col,),
            in_specs=in_specs,
            out_specs=out_specs,
            scratch_shapes=[pltpu.VMEM((n_col, rows, depth), BF16), pltpu.VMEM((2, rows, wide), F32)],
        ),
        compiler_params=params(1),
        cost_estimate=cost(GATE_UP_COST, 4 * rows * full * wide, 4 * full * wide, 4 * rows * wide),
        name=name,
    )(place, *operands)


def down_call(place, col, pieces, down_weight, n_col, split):
    half, wide = pieces[0].shape
    rows, block = 2 * half, down_weight.shape[1] // n_col
    if split:
        out_shape = [jax.ShapeDtypeStruct((rows, block), BF16)] * n_col
        out_specs = [whole((rows, block))] * n_col
    else:
        out_shape = jax.ShapeDtypeStruct((rows, block * n_col), BF16)
        out_specs = pl.BlockSpec((rows, block), lambda d, place, col: (0, d))
    return pl.pallas_call(
        functools.partial(down_kernel, n_col, split),
        out_shape=out_shape,
        grid_spec=pltpu.PrefetchScalarGridSpec(
            num_scalar_prefetch=2,
            grid=(n_col,),
            in_specs=[whole((half, wide))] * 4 + [pl.BlockSpec(memory_space=pltpu.VMEM)],
            out_specs=out_specs,
            scratch_shapes=[pltpu.VMEM((rows, wide), BF16)] * 2,
        ),
        compiler_params=params(1),
        cost_estimate=cost(DOWN_COST, 4 * rows * wide * block * n_col, 8 * half * wide),
        name="down",
    )(place, col, *pieces, down_weight)


def shifted(x, n, shift):
    return lax.ppermute(x, "col", [(i, (i + shift) % n) for i in range(n)])


def swapped(x, mask):
    return lax.ppermute(x, "row", [(i, i ^ mask) for i in range(4)])


def after(x, *deps):
    return lax.optimization_barrier((x,) + deps)[0]


def pipelined(n_col, tokens, gate_weight, up_weight, down_weight):
    eighth = tokens.shape[0] // 8
    weights = (gate_weight, up_weight)
    down_weight = pltpu.with_memory_space_constraint(down_weight, pltpu.VMEM)
    row, col = lax.axis_index("row"), lax.axis_index("col")
    table = np.array(
        [
            [1 - r % 2, r % 2, r // 2] + [(c - s) % n_col for s in range(n_col)] + list(range(n_col)) + [c]
            for r in range(4)
            for c in range(n_col)
        ],
        np.int32,
    )
    mine = jnp.asarray(table)[row * n_col + col]
    by_shift, col_id = mine[: BLOCKS + n_col], mine[-1:]
    natural = jnp.concatenate([mine[:BLOCKS], mine[BLOCKS + n_col : -1]])

    def direct(piece):
        return [piece] + [shifted(piece, n_col, s) for s in range(1, n_col)]

    bounds = [0, 1, 3, 5, 7, 8]
    def gathered(lo, hi, *behind):
        piece = after(tokens[lo * eighth : hi * eighth], *behind)
        return lax.all_gather(piece, "col", axis=1, tiled=True)

    def gathered(lo, hi, *behind):
        piece = after(tokens[lo * eighth : hi * eighth], *behind)
        return lax.all_gather(piece, "col", axis=1, tiled=True)

    first = direct(tokens[:eighth])
    second = lax.all_gather(tokens[eighth : 3 * eighth], "col", axis=1, tiled=True)
    sources = [(by_shift, first, 0), (natural, [second], 0)]
    chunk_rows = [(b - a) * eighth for a, b in zip(bounds, bounds[1:])]
    last = [mine]

    def partner(i):
        place, tok, block = sources[i]
        out = gate_up_call(after(place, *last), tok, chunk_rows[i], block, weights, n_col, PARTNER, i in SPLIT)
        last[:] = list(out)
        return [swapped(piece, 1) for piece in out]

    def own(i, received):
        place, tok, block = sources[i]
        send, keep = gate_up_call(after(place, *last), tok, chunk_rows[i], block, weights, n_col, OWN, i in SPLIT, received)
        last[:] = [send]
        return keep, swapped(send, 2)

    def gated(pair):
        keep, arrived = after(pair[0], *last), pair[1]
        gate = keep[0].astype(F32) + arrived[0].astype(F32)
        up = keep[1].astype(F32) + arrived[1].astype(F32)
        hidden = (jax.nn.silu(gate) * up).astype(BF16)
        last[:] = [hidden]
        hidden_x = swapped(hidden, 2)
        return hidden, hidden_x, swapped(hidden, 1), swapped(hidden_x, 1)

    def down(pieces, split=False):
        out = down_call(after(by_shift, *last), col_id, pieces, down_weight, n_col, split)
        last[:] = list(out) if split else [out]
        if not split:
            return lax.psum_scatter(out, "col", scatter_dimension=1, tiled=True)
        total = out[-1].astype(F32)
        for s in range(1, n_col):
            total = total + shifted(out[s - 1], n_col, s).astype(F32)
        return total.astype(BF16)

    r0 = partner(0)
    p0 = own(0, r0)
    r1 = partner(1)
    third = gathered(3, 5, second, *last)
    sources.append((natural, [third], 0))
    h0 = gated(p0)
    p1 = own(1, r1)
    r2 = partner(2)
    rest = gathered(5, 8, third, *last)
    sources += [(natural, [rest], 0), (natural, [rest], 2)]
    r3 = partner(3)
    p2 = own(2, r2)
    h1 = gated(p1)
    o0 = down(h0)
    r4 = partner(4)
    p3 = own(3, r3)
    h2 = gated(p2)
    o1 = down(h1)
    p4 = own(4, r4)
    h3 = gated(p3)
    o2 = down(h2)
    h4 = gated(p4)
    o3 = down(h3)
    o4 = down(h4, split=True)
    return jnp.concatenate([o0, o1, o2, o3, o4], axis=0)


def generic(tokens, gate_weight, up_weight, down_weight):
    gathered = lax.all_gather(tokens, "col", axis=1, tiled=True)
    gate = lax.psum_scatter(dot(gathered, gate_weight).astype(BF16), "row", scatter_dimension=0, tiled=True)
    up = lax.psum_scatter(dot(gathered, up_weight).astype(BF16), "row", scatter_dimension=0, tiled=True)
    hidden = (jax.nn.silu(gate.astype(F32)) * up.astype(F32)).astype(BF16)
    hidden = lax.all_gather(hidden, "row", axis=0, tiled=True)
    partial = dot(hidden, down_weight).astype(BF16)
    return lax.psum_scatter(partial, "col", scatter_dimension=1, tiled=True)


def solution(mesh):
    n_row, n_col = mesh.shape["row"], mesh.shape["col"]
    in_specs = (P("groups", ("row", "col")), P("row", "col"), P("row", "col"), P("col", "row"))
    out_specs = P("groups", ("row", "col"))
    step = functools.partial(pipelined, n_col) if n_row == 4 else generic
    return jax.shard_map(step, mesh=mesh, in_specs=in_specs, out_specs=out_specs, check_vma=False)
```

time: 414 us -> 459 us (1.11)
  local copies, waits for them, and re-layouts: 24.6 us -> 69.9 us
  Pallas kernels: 224 us -> 192 us
  waiting for transfers between devices: 103 us -> 133 us
  starting transfers between devices: 35.4 us -> 28.6 us
  other arithmetic: 8.72 us -> 14.8 us
    unnamed x41 -> x78, local copies, waits for them, and re-layouts: 17 us -> 64 us
    all_gather x2 -> x3, waiting for transfers between devices: 6.63 us -> 47.8 us  [the longest x2 47.8 us: gathered(): return lax.all_gather(piece, 'col', axis=1, tiled=True)]
    pallas_call x15, Pallas kernels: 224 us -> 192 us  [the longest x10 139 us: gate_up_call(): pl.pallas_call(functools.partial(body, len(tokens), split), out_shape=out...]
    reduce_scatter x4, waiting for transfers between devices: 21.9 us -> 10.8 us  [down(): return lax.psum_scatter(out, 'col', scatter_dimension=1, tiled=True)]
    ppermute x9 -> x6, waiting for transfers between devices: 5.36 us -> 12 us  [shifted(): return lax.ppermute(x, 'col', [(i, (i + shift) % n) for i in range(n)])]
    ppermute x9 -> x6, starting transfers between devices: 16.7 us -> 10.3 us  [shifted(): return lax.ppermute(x, 'col', [(i, (i + shift) % n) for i in range(n)])]
    ppermute x40 -> x31, waiting for transfers between devices: 68.9 us -> 62.7 us  [swapped(): return lax.ppermute(x, 'row', [(i, i ^ mask) for i in range(4)])]
    convert_element_type x5, other arithmetic: 7.05 us -> 13.1 us  [gated(): hidden = (jax.nn.silu(gate) * up).astype(BF16)]
  transfers between devices with their start and end apart: 55 -> 44, of which waited for: 13 -> 17; matrix products, arithmetic and copies ran while one was open for 6% -> 5% of each run, Pallas kernels for 55% -> 39%
where the time goes in v2:
time: 459 us; the launch traced here: 453 us
  Pallas kernels  192 us (42%)
  waiting for transfers between devices  133 us (29%)
  local copies, waits for them, and re-layouts  69.9 us (15%)
  starting transfers between devices  28.6 us (6%)
  other arithmetic  14.8 us (3%)
  between operations  14.1 us (3%)
    pallas_call x10, Pallas kernels, gate_up_call(): pl.pallas_call(functools.partial(body, len(tokens), split), out_shape=out...  139 us
    unnamed x78, local copies, waits for them, and re-layouts  64 us
    ppermute x31, waiting for transfers between devices, swapped(): return lax.ppermute(x, 'row', [(i, i ^ mask) for i in range(4)])  62.7 us
    pallas_call x5, Pallas kernels, down_call(): pl.pallas_call(functools.partial(down_kernel, n_col, split), out_shape=ou...  52.8 us
    all_gather x2, waiting for transfers between devices, gathered(): return lax.all_gather(piece, 'col', axis=1, tiled=True)  47.8 us
    ppermute x31, starting transfers between devices, swapped(): return lax.ppermute(x, 'row', [(i, i ^ mask) for i in range(4)])  16.9 us
    convert_element_type x5, other arithmetic, gated(): hidden = (jax.nn.silu(gate) * up).astype(BF16)  13.1 us
    ppermute x6, waiting for transfers between devices, shifted(): return lax.ppermute(x, 'col', [(i, (i + shift) % n) for i in range(n)])  12 us
  transfers between devices with their start and end apart: 44, of which 17 were waited for; matrix products, arithmetic and copies ran while one was open for 5% of the time, Pallas kernels for 39%

profile of v2, /device:TPU:0, one launch (start us, length us, event | category | flops | bytes accessed | tf_op | source)
XLA Modules:
  0.0 453.1 jit_solution(4483504080217949571)
XLA Ops:
  6.5 1.9 fusion.21
  9.4 3.1 collective-permute-start
  12.5 2.6 collective-permute-start.1
  17.1 1.8 collective-permute-done.refs_1_
  18.9 6.4 %collective-permute-done.1.refs_2_ = bf16[128,512]{1,0:T(8,128)(2,1)S(1)} collective-permute-done((bf16[128,512]{1,0:T(8,128)(2,1)S(1)}, bf16[128,512]{1,0:T(8,128)(2,1)S(1)}, u32[]{:S(2)}, u32[]{:S(2)}) %collective-permute-start.1) | collective-permute-done | bytes 131104 | tf_op jit(solution)/shard_map/ppermute | solution.py:168
  25.3 11.3 %partner.5 = (bf16[1,64,3328]{2,1,0:T(8,128)(2,1)S(1)}, bf16[1,64,3328]{2,1,0:T(8,128)(2,1)S(1)}, bf16[1,64,3328]{2,1,0:T(8,128)(2,1)S(1)}, bf16[1,64,3328]{2,1,0:T(8,128)(2,1)S(1)}) custom-call(s32[7]{0:T(128)S(1)} %slice_bitcast_fusion.2.place, bf16[128,512]{1,0:T(8,128)(2,1)S(1)} %slice.102.refs_0_, bf16[128,512]{1,0:T(8,128)(2,1)S(1)} %collective-permute-done.refs_1_, ...), custom_call_target="tpu_custom_call" | custom-call | flops 1046898304 | bytes 8690073 | tf_op jit(solution)/shard_map/partner/pallas_call | solution.py:126
  40.3 11.7 %own.5 = (bf16[2,64,3328]{2,1,0:T(8,128)(2,1)S(1)}, bf16[2,64,3328]{2,1,0:T(8,128)(2,1)S(1)}) custom-call(s32[7]{0:T(128)S(1)} %slice_bitcast_fusion.2.place, bf16[128,512]{1,0:T(8,128)(2,1)S(1)} %slice.102.refs_0_, bf16[128,512]{1,0:T(8,128)(2,1)S(1)} %collective-permute-done.refs_1_, bf16[128,512]{1,0:T(8,128)(2,1)S(1)} %collective-permute-done.1.refs_2_, ...), custom_call_target="tpu_custom_call" | custom-call | flops 1046898304 | bytes 8690073 | tf_op jit(solution)/shard_map/own/pallas_call | solution.py:126
  51.9 1.6 collective-permute-start.7
  54.8 13.5 %partner.6 = (bf16[1,128,3328]{2,1,0:T(8,128)(2,1)S(1)}, bf16[1,128,3328]{2,1,0:T(8,128)(2,1)S(1)}, bf16[1,128,3328]{2,1,0:T(8,128)(2,1)S(1)}, bf16[1,128,3328]{2,1,0:T(8,128)(2,1)S(1)}) custom-call(s32[7]{0:T(128)S(1)} %pad_add_fusion.place, bf16[256,2048]{1,0:T(8,128)(2,1)S(1)} %copy-done.4, bf16[2048,6656]{1,0:T(8,128)(2,1)} %refs_1_.15, ...), custom_call_target="tpu_custom_call" | custom-call | flops 2093796608 | bytes 9201254 | tf_op jit(solution)/shard_map/partner/pallas_call | solution.py:126
  73.7 2.3 fusion.16.own_x
  78.9 14.6 %own.6 = (bf16[2,128,3328]{2,1,0:T(8,128)(2,1)S(1)}, bf16[2,128,3328]{2,1,0:T(8,128)(2,1)S(1)}) custom-call(s32[7]{0:T(128)S(1)} %pad_add_fusion.place, bf16[256,2048]{1,0:T(8,128)(2,1)S(1)} %copy-done.5, bf16[2048,6656]{1,0:T(8,128)(2,1)} %refs_1_.15, bf16[2048,6656]{1,0:T(8,128)(2,1)} %refs_2_.15, ...), custom_call_target="tpu_custom_call" | custom-call | flops 2093796608 | bytes 9201254 | tf_op jit(solution)/shard_map/own/pallas_call | solution.py:126
  95.9 12.7 %all-gather.6.cloned.1.call-done.refs_0_ = bf16[256,2048]{1,0:T(8,128)(2,1)} async-done(((bf16[256,512]{1,0:T(8,128)(2,1)}), bf16[256,2048]{1,0:T(8,128)(2,1)}) %all-gather.6.cloned.1.call-update) | async-done | bytes 1048592 | tf_op jit(solution)/shard_map/all_gather | solution.py:206
  109.8 15.3 %partner.7 = bf16[2,256,3328]{2,1,0:T(8,128)(2,1)} custom-call(s32[7]{0:T(128)S(1)} %pad_add_fusion.place, bf16[256,2048]{1,0:T(8,128)(2,1)S(1)} %copy-done.2, bf16[2048,6656]{1,0:T(8,128)(2,1)} %refs_1_.15, bf16[2048,6656]{1,0:T(8,128)(2,1)} %refs_2_.15), custom_call_target="tpu_custom_call" | custom-call | flops 2093796608 | bytes 9201254 | tf_op jit(solution)/shard_map/partner/pallas_call | solution.py:126
  125.1 1.8 slice.109
  127.1 1.5 collective-permute-start.13
  128.7 35.1 %all-gather.8.cloned.1.call-done.refs_0_ = bf16[384,2048]{1,0:T(8,128)(2,1)} async-done(((bf16[384,512]{1,0:T(8,128)(2,1)}), bf16[384,2048]{1,0:T(8,128)(2,1)}) %all-gather.8.cloned.1.call-update) | async-done | bytes 1572880 | tf_op jit(solution)/shard_map/all_gather | solution.py:206
  165.2 15.2 %partner.8 = bf16[2,256,3328]{2,1,0:T(8,128)(2,1)} custom-call(s32[7]{0:T(128)S(1)} %pad_add_fusion.place, bf16[384,2048]{1,0:T(8,128)(2,1)S(1)} %copy-done, bf16[2048,6656]{1,0:T(8,128)(2,1)} %refs_1_.15, bf16[2048,6656]{1,0:T(8,128)(2,1)} %refs_2_.15), custom_call_target="tpu_custom_call" | custom-call | flops 2093796608 | bytes 9201254 | tf_op jit(solution)/shard_map/partner/pallas_call | solution.py:126
  180.4 1.5 collective-permute-start.14
  182.8 9.9 %collective-permute-done.14.other_x = bf16[64,3328]{1,0:T(8,128)(2,1)S(1)} collective-permute-done((bf16[64,3328]{1,0:T(8,128)(2,1)S(1)}, bf16[64,3328]{1,0:T(8,128)(2,1)S(1)}, u32[]{:S(2)}, u32[]{:S(2)}) %collective-permute-start.14) | collective-permute-done | bytes 426016 | tf_op jit(solution)/shard_map/ppermute | solution.py:172
  192.7 15.6 %own.7 = (bf16[2,128,3328]{2,1,0:T(8,128)(2,1)}, bf16[2,128,3328]{2,1,0:T(8,128)(2,1)S(1)}) custom-call(s32[7]{0:T(128)S(1)} %pad_add_fusion.place, bf16[256,2048]{1,0:T(8,128)(2,1)S(1)} %copy-done.3, bf16[2048,6656]{1,0:T(8,128)(2,1)} %refs_1_.15, bf16[2048,6656]{1,0:T(8,128)(2,1)} %refs_2_.15, bf16[2,256,3328]{2,1,0:T(8,128)(2,1)S(1)} %collective-permute-done.12.refs_3_), custom_call_target="tpu_custom_call" | custom-call | flops 2093796608 | bytes 9201254 | tf_op jit(solution)/shard_map/own/pallas_call | solution.py:126
  208.3 1.5 collective-permute-start.18
  209.8 3.0 fusion.8.own_x
  214.3 8.8 %copy-done.13 = bf16[6656,2048]{1,0:T(8,128)(2,1)S(1)} copy-done((bf16[6656,2048]{1,0:T(8,128)(2,1)S(1)}, bf16[6656,2048]{1,0:T(8,128)(2,1)}, u32[]{:S(2)}) %copy-start.13) | copy-done | bytes 27263000
  223.1 8.1 %down.5 = bf16[128,2048]{1,0:T(8,128)(2,1)} custom-call(s32[7]{0:T(128)} %copy-done.12, s32[1]{0:T(128)} %bitcast.7.col, bf16[64,3328]{1,0:T(8,128)(2,1)} %fusion.16.own_x, bf16[64,3328]{1,0:T(8,128)(2,1)} %copy-done.32, bf16[64,3328]{1,0:T(8,128)(2,1)} %copy-done.33, bf16[64,3328]{1,0:T(8,128)(2,1)} %copy-done.34, bf16[6656,2048]{1,0:T(8,128)(2,1)S(1)} %copy-done.13), custom_call_target="tpu_custom_call" | custom-call | flops 13958643712 | bytes 6815744 | tf_op jit(solution)/shard_map/down/pallas_call | solution.py:151
  231.8 12.4 %partner.9 = bf16[2,128,3328]{2,1,0:T(8,128)(2,1)} custom-call(s32[7]{0:T(128)S(1)} %pad_add_fusion.place, bf16[384,2048]{1,0:T(8,128)(2,1)S(1)} %copy-done.1, bf16[2048,6656]{1,0:T(8,128)(2,1)} %refs_1_.15, bf16[2048,6656]{1,0:T(8,128)(2,1)} %refs_2_.15), custom_call_target="tpu_custom_call" | custom-call | flops 1046898304 | bytes 8690073 | tf_op jit(solution)/shard_map/partner/pallas_call | solution.py:126
  244.5 22.0 %collective-permute-done.19.other_x = bf16[128,3328]{1,0:T(8,128)(2,1)} collective-permute-done((bf16[128,3328]{1,0:T(8,128)(2,1)}, bf16[128,3328]{1,0:T(8,128)(2,1)}, u32[]{:S(2)}, u32[]{:S(2)}) %collective-permute-start.19) | collective-permute-done | bytes 852000 | tf_op jit(solution)/shard_map/ppermute | solution.py:172
  266.5 16.7 %own.8 = (bf16[2,128,3328]{2,1,0:T(8,128)(2,1)}, bf16[2,128,3328]{2,1,0:T(8,128)(2,1)S(1)}) custom-call(s32[7]{0:T(128)S(1)} %pad_add_fusion.place, bf16[384,2048]{1,0:T(8,128)(2,1)S(1)} %copy-done.1, bf16[2048,6656]{1,0:T(8,128)(2,1)} %refs_1_.15, bf16[2048,6656]{1,0:T(8,128)(2,1)} %refs_2_.15, bf16[2,256,3328]{2,1,0:T(8,128)(2,1)} %collective-permute-done.17.refs_3_), custom_call_target="tpu_custom_call" | custom-call | flops 2093796608 | bytes 9201254 | tf_op jit(solution)/shard_map/own/pallas_call | solution.py:126
  283.2 1.5 collective-permute-start.23
  284.6 3.0 fusion.4.own_x
  290.0 8.8 %copy-done.14 = bf16[6656,2048]{1,0:T(8,128)(2,1)S(1)} copy-done((bf16[6656,2048]{1,0:T(8,128)(2,1)S(1)}, bf16[6656,2048]{1,0:T(8,128)(2,1)}, u32[]{:S(2)}) %copy-start.14) | copy-done | bytes 27263000
  298.8 12.1 %down.6 = bf16[256,2048]{1,0:T(8,128)(2,1)} custom-call(s32[7]{0:T(128)} %copy-done.12, s32[1]{0:T(128)} %bitcast.7.col, bf16[128,3328]{1,0:T(8,128)(2,1)} %fusion.8.own_x, bf16[128,3328]{1,0:T(8,128)(2,1)} %collective-permute-done.19.other_x, bf16[128,3328]{1,0:T(8,128)(2,1)} %copy-done.27, bf16[128,3328]{1,0:T(8,128)(2,1)} %copy-done.29, ...), custom_call_target="tpu_custom_call" | custom-call | flops 27917287424 | bytes 13631488 | tf_op jit(solution)/shard_map/down/pallas_call | solution.py:151
  311.3 13.1 %own.9 = (bf16[2,64,3328]{2,1,0:T(8,128)(2,1)}, bf16[2,64,3328]{2,1,0:T(8,128)(2,1)S(1)}) custom-call(s32[7]{0:T(128)S(1)} %pad_add_fusion.place, bf16[384,2048]{1,0:T(8,128)(2,1)S(1)} %copy-done.1, bf16[2048,6656]{1,0:T(8,128)(2,1)} %refs_1_.15, bf16[2048,6656]{1,0:T(8,128)(2,1)} %refs_2_.15, bf16[2,128,3328]{2,1,0:T(8,128)(2,1)} %collective-permute-done.22.refs_3_), custom_call_target="tpu_custom_call" | custom-call | flops 1046898304 | bytes 8690073 | tf_op jit(solution)/shard_map/own/pallas_call | solution.py:126
  324.4 1.5 collective-permute-start.27
  325.8 15.9 %collective-permute-done.24.other_x = bf16[128,3328]{1,0:T(8,128)(2,1)} collective-permute-done((bf16[128,3328]{1,0:T(8,128)(2,1)}, bf16[128,3328]{1,0:T(8,128)(2,1)}, u32[]{:S(2)}, u32[]{:S(2)}) %collective-permute-start.24) | collective-permute-done | bytes 852000 | tf_op jit(solution)/shard_map/ppermute | solution.py:172
  341.7 3.0 fusion.own_x
  344.8 1.5 collective-permute-start.28
  347.4 8.8 %copy-done.15 = bf16[6656,2048]{1,0:T(8,128)(2,1)S(1)} copy-done((bf16[6656,2048]{1,0:T(8,128)(2,1)S(1)}, bf16[6656,2048]{1,0:T(8,128)(2,1)}, u32[]{:S(2)}) %copy-start.15) | copy-done | bytes 27263000
  356.2 12.2 %down.7 = bf16[256,2048]{1,0:T(8,128)(2,1)} custom-call(s32[7]{0:T(128)} %copy-done.12, s32[1]{0:T(128)} %bitcast.7.col, bf16[128,3328]{1,0:T(8,128)(2,1)} %fusion.4.own_x, bf16[128,3328]{1,0:T(8,128)(2,1)} %collective-permute-done.24.other_x, bf16[128,3328]{1,0:T(8,128)(2,1)} %collective-permute-done.25.own_x_core, bf16[128,3328]{1,0:T(8,128)(2,1)} %copy-done.30, ...), custom_call_target="tpu_custom_call" | custom-call | flops 27917287424 | bytes 13631488 | tf_op jit(solution)/shard_map/down/pallas_call | solution.py:151
  368.3 9.4 %collective-permute-done.28.other_x = bf16[128,3328]{1,0:T(8,128)(2,1)S(1)} collective-permute-done((bf16[128,3328]{1,0:T(8,128)(2,1)}, bf16[128,3328]{1,0:T(8,128)(2,1)S(1)}, u32[]{:S(2)}, u32[]{:S(2)}) %collective-permute-start.28) | collective-permute-done | bytes 852000 | tf_op jit(solution)/shard_map/ppermute | solution.py:172
  377.8 1.8 fusion.12.own_x
  379.6 1.5 collective-permute-start.31
  382.1 9.0 %copy-done.16 = bf16[6656,2048]{1,0:T(8,128)(2,1)S(1)} copy-done((bf16[6656,2048]{1,0:T(8,128)(2,1)S(1)}, bf16[6656,2048]{1,0:T(8,128)(2,1)}, u32[]{:S(2)}) %copy-start.16) | copy-done | bytes 27263000
  391.1 12.2 %down.8 = bf16[256,2048]{1,0:T(8,128)(2,1)} custom-call(s32[7]{0:T(128)} %copy-done.12, s32[1]{0:T(128)} %bitcast.7.col, bf16[128,3328]{1,0:T(8,128)(2,1)} %fusion.own_x, bf16[128,3328]{1,0:T(8,128)(2,1)} %copy-done.26, bf16[128,3328]{1,0:T(8,128)(2,1)} %copy-done.28, bf16[128,3328]{1,0:T(8,128)(2,1)} %collective-permute-done.30.other_x_core, ...), custom_call_target="tpu_custom_call" | custom-call | flops 27917287424 | bytes 13631488 | tf_op jit(solution)/shard_map/down/pallas_call | solution.py:151
  407.3 9.0 %copy-done.17 = bf16[6656,2048]{1,0:T(8,128)(2,1)S(1)} copy-done((bf16[6656,2048]{1,0:T(8,128)(2,1)S(1)}, bf16[6656,2048]{1,0:T(8,128)(2,1)}, u32[]{:S(2)}) %copy-start.17) | copy-done | bytes 27263000
  416.3 8.2 %down.9 = (bf16[128,512]{1,0:T(8,128)(2,1)}, bf16[128,512]{1,0:T(8,128)(2,1)}, bf16[128,512]{1,0:T(8,128)(2,1)}, bf16[128,512]{1,0:T(8,128)(2,1)}) custom-call(s32[7]{0:T(128)} %copy-done.12, s32[1]{0:T(128)} %bitcast.7.col, bf16[64,3328]{1,0:T(8,128)(2,1)} %copy-done.24, bf16[64,3328]{1,0:T(8,128)(2,1)} %copy-done.31, bf16[64,3328]{1,0:T(8,128)(2,1)} %copy-done.35, ...), custom_call_target="tpu_custom_call" | custom-call | flops 13958643712 | bytes 6815744 | tf_op jit(solution)/shard_map/down/pallas_call | solution.py:151
  428.7 10.8 %reduce-scatter.11.cloned.1.call-done = bf16[256,512]{1,0:T(8,128)(2,1)} async-done(((bf16[256,2048]{1,0:T(8,128)(2,1)}), bf16[256,512]{1,0:T(8,128)(2,1)}) %reduce-scatter.11.cloned.1.call-update) | async-done | bytes 262160 | tf_op jit(solution)/shard_map/reduce_scatter | solution.py:239
  440.5 3.8 collective-permute-done.35
  444.4 1.6 fusion.20
  (155 shorter events, 38.8 us)
Async XLA Ops:
  6.5 47.1 %all-gather.4.cloned.1.call-start = ((), (), s32[]{:S(2)}) async-start(), calls=%async_computation.4 | async-start | bytes 1310720 | tf_op jit(solution)/shard_map/all_gather | solution.py:209
  8.4 100.2 %all-gather.6.cloned.1.call-start = ((), (), s32[]{:S(2)}) async-start(), calls=%async_computation.5 | async-start | bytes 1310720 | tf_op jit(solution)/shard_map/all_gather | solution.py:206
  9.4 9.5 %collective-permute-start = (bf16[128,512]{1,0:T(8,128)(2,1)S(1)}, bf16[128,512]{1,0:T(8,128)(2,1)S(1)}, u32[]{:S(2)}, u32[]{:S(2)}) collective-permute-start(bf16[128,512]{1,0:T(8,128)(2,1)S(1)} %slice.102.refs_0_), channel_id=1, source_target_pairs={{0,1},{1,2},{2,3},{3,0},{4,5},{5,6},{6,7},{7,4},{8,9},{9,10},{10,1... | collective-permute-start | bytes 393224 | tf_op jit(solution)/shard_map/ppermute | solution.py:168
  12.5 12.8 %collective-permute-start.1 = (bf16[128,512]{1,0:T(8,128)(2,1)S(1)}, bf16[128,512]{1,0:T(8,128)(2,1)S(1)}, u32[]{:S(2)}, u32[]{:S(2)}) collective-permute-start(bf16[128,512]{1,0:T(8,128)(2,1)S(1)} %slice.102.refs_0_), channel_id=1, source_target_pairs={{0,2},{1,3},{2,0},{3,1},{4,6},{5,7},{6,4},{7,5},{8,10},{9,11},{10,... | collective-permute-start | bytes 393224 | tf_op jit(solution)/shard_map/ppermute | solution.py:168
  15.0 10.2 %collective-permute-start.2 = (bf16[128,512]{1,0:T(8,128)(2,1)S(1)}, bf16[128,512]{1,0:T(8,128)(2,1)S(1)}, u32[]{:S(2)}, u32[]{:S(2)}) collective-permute-start(bf16[128,512]{1,0:T(8,128)(2,1)S(1)} %slice.102.refs_0_), channel_id=1, source_target_pairs={{0,3},{1,0},{2,1},{3,2},{4,7},{5,4},{6,5},{7,6},{8,11},{9,8},{10,9... | collective-permute-start | bytes 393224 | tf_op jit(solution)/shard_map/ppermute | solution.py:168
  36.6 1.8 collective-permute-start.3
  36.7 2.4 collective-permute-start.4
  37.2 2.5 collective-permute-start.5
  37.2 3.0 collective-permute-start.6
  51.9 21.8 %collective-permute-start.7 = (bf16[2,64,3328]{2,1,0:T(8,128)(2,1)S(1)}, bf16[2,64,3328]{2,1,0:T(8,128)(2,1)}, u32[]{:S(2)}, u32[]{:S(2)}) collective-permute-start(bf16[2,64,3328]{2,1,0:T(8,128)(2,1)S(1)} %get-tuple-element.54), channel_id=1, source_target_pairs={{0,8},{4,12},{8,0},{12,4},{1,9},{5,13},{9,1},{13,5},{2,10},{6,14},... | collective-permute-start | bytes 2555912 | tf_op jit(solution)/shard_map/ppermute | solution.py:172
  72.0 91.8 %all-gather.8.cloned.1.call-start = ((), (), s32[]{:S(2)}) async-start(), calls=%async_computation.6 | async-start | bytes 1966080 | tf_op jit(solution)/shard_map/all_gather | solution.py:206
  72.6 3.3 collective-permute-start.8
  72.7 3.8 collective-permute-start.9
  73.2 4.5 collective-permute-start.10
  73.3 5.7 %collective-permute-start.11 = (bf16[1,128,3328]{2,1,0:T(8,128)(2,1)}, bf16[1,128,3328]{2,1,0:T(8,128)(2,1)S(1)}, u32[]{:S(2)}, u32[]{:S(2)}) collective-permute-start(bf16[1,128,3328]{2,1,0:T(8,128)(2,1)} %copy-done.19), channel_id=1, source_target_pairs={{0,4},{4,0},{8,12},{12,8},{1,5},{5,1},{9,13},{13,9},{2,6},{6,2},{1... | collective-permute-start | bytes 2555912 | tf_op jit(solution)/shard_map/ppermute | solution.py:172
  125.1 67.5 %collective-permute-start.12 = (bf16[2,256,3328]{2,1,0:T(8,128)(2,1)}, bf16[2,256,3328]{2,1,0:T(8,128)(2,1)S(1)}, u32[]{:S(2)}, u32[]{:S(2)}) collective-permute-start(bf16[2,256,3328]{2,1,0:T(8,128)(2,1)} %partner.7), channel_id=1, source_target_pairs={{0,4},{4,0},{8,12},{12,8},{1,5},{5,1},{9,13},{13,9},{2,6},{6,2},{1... | collective-permute-start | bytes 10223624 | tf_op jit(solution)/shard_map/ppermute | solution.py:172
  126.9 276.9 %reduce-scatter.5.cloned.1.call-start = ((), (), s32[]{:S(2)}) async-start(), calls=%async_computation.7 | async-start | bytes 655360 | tf_op jit(solution)/shard_map/reduce_scatter | solution.py:239
  127.1 82.6 %collective-permute-start.13 = (bf16[2,128,3328]{2,1,0:T(8,128)(2,1)}, bf16[2,128,3328]{2,1,0:T(8,128)(2,1)}, u32[]{:S(2)}, u32[]{:S(2)}) collective-permute-start(bf16[2,128,3328]{2,1,0:T(8,128)(2,1)} %copy-done.18), channel_id=1, source_target_pairs={{0,8},{4,12},{8,0},{12,4},{1,9},{5,13},{9,1},{13,5},{2,10},{6,14},... | collective-permute-start | bytes 5111816 | tf_op jit(solution)/shard_map/ppermute | solution.py:172
  165.2 27.4 %copy-start.3 = (bf16[256,2048]{1,0:T(8,128)(2,1)S(1)}, bf16[256,2048]{1,0:T(8,128)(2,1)}, u32[]{:S(2)}) copy-start(bf16[256,2048]{1,0:T(8,128)(2,1)} %all-gather.6.cloned.1.call-done.refs_0_) | copy-start | bytes 3145732
  180.4 86.1 %collective-permute-start.17 = (bf16[2,256,3328]{2,1,0:T(8,128)(2,1)}, bf16[2,256,3328]{2,1,0:T(8,128)(2,1)}, u32[]{:S(2)}, u32[]{:S(2)}) collective-permute-start(bf16[2,256,3328]{2,1,0:T(8,128)(2,1)} %partner.8), channel_id=1, source_target_pairs={{0,4},{4,0},{8,12},{12,8},{1,5},{5,1},{9,13},{13,9},{2,6},{6,2},{1... | collective-permute-start | bytes 10223624 | tf_op jit(solution)/shard_map/ppermute | solution.py:172
  180.4 12.2 %collective-permute-start.14 = (bf16[64,3328]{1,0:T(8,128)(2,1)S(1)}, bf16[64,3328]{1,0:T(8,128)(2,1)S(1)}, u32[]{:S(2)}, u32[]{:S(2)}) collective-permute-start(bf16[64,3328]{1,0:T(8,128)(2,1)S(1)} %copy-done.23), channel_id=1, source_target_pairs={{0,8},{4,12},{8,0},{12,4},{1,9},{5,13},{9,1},{13,5},{2,10},{6,14},... | collective-permute-start | bytes 1277960 | tf_op jit(solution)/shard_map/ppermute | solution.py:172
  182.6 27.2 %copy-start.7 = (bf16[2,128,3328]{2,1,0:T(8,128)(2,1)S(1)}, bf16[2,128,3328]{2,1,0:T(8,128)(2,1)}, u32[]{:S(2)}) copy-start(bf16[2,128,3328]{2,1,0:T(8,128)(2,1)} %copy-done.6) | copy-start | bytes 5111812
  182.6 30.8 %collective-permute-start.15 = (bf16[64,3328]{1,0:T(8,128)(2,1)S(1)}, bf16[64,3328]{1,0:T(8,128)(2,1)S(1)}, u32[]{:S(2)}, u32[]{:S(2)}) collective-permute-start(bf16[64,3328]{1,0:T(8,128)(2,1)S(1)} %copy-done.23), channel_id=1, source_target_pairs={{0,4},{4,0},{8,12},{12,8},{1,5},{5,1},{9,13},{13,9},{2,6},{6,2},{1... | collective-permute-start | bytes 1277960 | tf_op jit(solution)/shard_map/ppermute | solution.py:172
  192.7 20.7 %collective-permute-start.16 = (bf16[64,3328]{1,0:T(8,128)(2,1)S(1)}, bf16[64,3328]{1,0:T(8,128)(2,1)S(1)}, u32[]{:S(2)}, u32[]{:S(2)}) collective-permute-start(bf16[64,3328]{1,0:T(8,128)(2,1)S(1)} %collective-permute-done.14.other_x), channel_id=1, source_target_pairs={{0,4},{4,0},{8,12},{12,8},{1,5},{5,1},{9,13},{13,9},{2,6},{6,2},{1... | collective-permute-start | bytes 1277960 | tf_op jit(solution)/shard_map/ppermute | solution.py:172
  208.3 76.3 %collective-permute-start.18 = (bf16[2,128,3328]{2,1,0:T(8,128)(2,1)}, bf16[2,128,3328]{2,1,0:T(8,128)(2,1)}, u32[]{:S(2)}, u32[]{:S(2)}) collective-permute-start(bf16[2,128,3328]{2,1,0:T(8,128)(2,1)} %get-tuple-element.69), channel_id=1, source_target_pairs={{0,8},{4,12},{8,0},{12,4},{1,9},{5,13},{9,1},{13,5},{2,10},{6,14},... | collective-permute-start | bytes 5111816 | tf_op jit(solution)/shard_map/ppermute | solution.py:172
  212.8 53.7 %collective-permute-start.19 = (bf16[128,3328]{1,0:T(8,128)(2,1)}, bf16[128,3328]{1,0:T(8,128)(2,1)}, u32[]{:S(2)}, u32[]{:S(2)}) collective-permute-start(bf16[128,3328]{1,0:T(8,128)(2,1)} %fusion.8.own_x), channel_id=1, source_target_pairs={{0,8},{4,12},{8,0},{12,4},{1,9},{5,13},{9,1},{13,5},{2,10},{6,14},... | collective-permute-start | bytes 2555912 | tf_op jit(solution)/shard_map/ppermute | solution.py:172
  231.2 173.6 %reduce-scatter.7.cloned.1.call-start = ((), (), s32[]{:S(2)}) async-start(), calls=%async_computation.8 | async-start | bytes 1310720 | tf_op jit(solution)/shard_map/reduce_scatter | solution.py:239
  231.5 56.7 %collective-permute-start.20 = (bf16[128,3328]{1,0:T(8,128)(2,1)}, bf16[128,3328]{1,0:T(8,128)(2,1)S(1)}, u32[]{:S(2)}, u32[]{:S(2)}) collective-permute-start(bf16[128,3328]{1,0:T(8,128)(2,1)} %fusion.8.own_x), channel_id=1, source_target_pairs={{0,4},{4,0},{8,12},{12,8},{1,5},{5,1},{9,13},{13,9},{2,6},{6,2},{1... | collective-permute-start | bytes 2555912 | tf_op jit(solution)/shard_map/ppermute | solution.py:172
  244.2 40.4 %copy-start.9 = (bf16[2,128,3328]{2,1,0:T(8,128)(2,1)S(1)}, bf16[2,128,3328]{2,1,0:T(8,128)(2,1)}, u32[]{:S(2)}) copy-start(bf16[2,128,3328]{2,1,0:T(8,128)(2,1)} %copy-done.8) | copy-start | bytes 5111812
  244.2 67.1 %collective-permute-start.22 = (bf16[2,128,3328]{2,1,0:T(8,128)(2,1)}, bf16[2,128,3328]{2,1,0:T(8,128)(2,1)}, u32[]{:S(2)}, u32[]{:S(2)}) collective-permute-start(bf16[2,128,3328]{2,1,0:T(8,128)(2,1)} %partner.9), channel_id=1, source_target_pairs={{0,4},{4,0},{8,12},{12,8},{1,5},{5,1},{9,13},{13,9},{2,6},{6,2},{1... | collective-permute-start | bytes 5111816 | tf_op jit(solution)/shard_map/ppermute | solution.py:172
  266.5 21.7 %collective-permute-start.21 = (bf16[128,3328]{1,0:T(8,128)(2,1)}, bf16[128,3328]{1,0:T(8,128)(2,1)S(1)}, u32[]{:S(2)}, u32[]{:S(2)}) collective-permute-start(bf16[128,3328]{1,0:T(8,128)(2,1)} %collective-permute-done.19.other_x), channel_id=1, source_target_pairs={{0,4},{4,0},{8,12},{12,8},{1,5},{5,1},{9,13},{13,9},{2,6},{6,2},{1... | collective-permute-start | bytes 2555912 | tf_op jit(solution)/shard_map/ppermute | solution.py:172
  283.2 58.6 %collective-permute-start.23 = (bf16[2,128,3328]{2,1,0:T(8,128)(2,1)}, bf16[2,128,3328]{2,1,0:T(8,128)(2,1)}, u32[]{:S(2)}, u32[]{:S(2)}) collective-permute-start(bf16[2,128,3328]{2,1,0:T(8,128)(2,1)} %get-tuple-element.75), channel_id=1, source_target_pairs={{0,8},{4,12},{8,0},{12,4},{1,9},{5,13},{9,1},{13,5},{2,10},{6,14},... | collective-permute-start | bytes 5111816 | tf_op jit(solution)/shard_map/ppermute | solution.py:172
  287.6 54.1 %collective-permute-start.24 = (bf16[128,3328]{1,0:T(8,128)(2,1)}, bf16[128,3328]{1,0:T(8,128)(2,1)}, u32[]{:S(2)}, u32[]{:S(2)}) collective-permute-start(bf16[128,3328]{1,0:T(8,128)(2,1)} %fusion.4.own_x), channel_id=1, source_target_pairs={{0,8},{4,12},{8,0},{12,4},{1,9},{5,13},{9,1},{13,5},{2,10},{6,14},... | collective-permute-start | bytes 2555912 | tf_op jit(solution)/shard_map/ppermute | solution.py:172
  288.2 58.3 %collective-permute-start.25 = (bf16[128,3328]{1,0:T(8,128)(2,1)}, bf16[128,3328]{1,0:T(8,128)(2,1)}, u32[]{:S(2)}, u32[]{:S(2)}) collective-permute-start(bf16[128,3328]{1,0:T(8,128)(2,1)} %fusion.4.own_x), channel_id=1, source_target_pairs={{0,4},{4,0},{8,12},{12,8},{1,5},{5,1},{9,13},{13,9},{2,6},{6,2},{1... | collective-permute-start | bytes 2555912 | tf_op jit(solution)/shard_map/ppermute | solution.py:172
  310.9 116.8 %reduce-scatter.9.cloned.1.call-start = ((), (), s32[]{:S(2)}) async-start(), calls=%async_computation.9 | async-start | bytes 1310720 | tf_op jit(solution)/shard_map/reduce_scatter | solution.py:239
  324.4 53.4 %collective-permute-start.27 = (bf16[2,64,3328]{2,1,0:T(8,128)(2,1)}, bf16[2,64,3328]{2,1,0:T(8,128)(2,1)}, u32[]{:S(2)}, u32[]{:S(2)}) collective-permute-start(bf16[2,64,3328]{2,1,0:T(8,128)(2,1)} %get-tuple-element.80), channel_id=1, source_target_pairs={{0,8},{4,12},{8,0},{12,4},{1,9},{5,13},{9,1},{13,5},{2,10},{6,14},... | collective-permute-start | bytes 2555912 | tf_op jit(solution)/shard_map/ppermute | solution.py:172
  341.7 4.7 %collective-permute-start.26 = (bf16[128,3328]{1,0:T(8,128)(2,1)}, bf16[128,3328]{1,0:T(8,128)(2,1)S(1)}, u32[]{:S(2)}, u32[]{:S(2)}) collective-permute-start(bf16[128,3328]{1,0:T(8,128)(2,1)} %collective-permute-done.24.other_x), channel_id=1, source_target_pairs={{0,4},{4,0},{8,12},{12,8},{1,5},{5,1},{9,13},{13,9},{2,6},{6,2},{1... | collective-permute-start | bytes 2555912 | tf_op jit(solution)/shard_map/ppermute | solution.py:172
  344.8 33.0 %collective-permute-start.28 = (bf16[128,3328]{1,0:T(8,128)(2,1)}, bf16[128,3328]{1,0:T(8,128)(2,1)S(1)}, u32[]{:S(2)}, u32[]{:S(2)}) collective-permute-start(bf16[128,3328]{1,0:T(8,128)(2,1)} %fusion.own_x), channel_id=1, source_target_pairs={{0,8},{4,12},{8,0},{12,4},{1,9},{5,13},{9,1},{13,5},{2,10},{6,14},... | collective-permute-start | bytes 2555912 | tf_op jit(solution)/shard_map/ppermute | solution.py:172
  346.2 31.5 %copy-start.11 = (bf16[2,64,3328]{2,1,0:T(8,128)(2,1)S(1)}, bf16[2,64,3328]{2,1,0:T(8,128)(2,1)}, u32[]{:S(2)}) copy-start(bf16[2,64,3328]{2,1,0:T(8,128)(2,1)} %copy-done.10) | copy-start | bytes 2555908
  346.2 34.9 %collective-permute-start.29 = (bf16[128,3328]{1,0:T(8,128)(2,1)}, bf16[128,3328]{1,0:T(8,128)(2,1)S(1)}, u32[]{:S(2)}, u32[]{:S(2)}) collective-permute-start(bf16[128,3328]{1,0:T(8,128)(2,1)} %fusion.own_x), channel_id=1, source_target_pairs={{0,4},{4,0},{8,12},{12,8},{1,5},{5,1},{9,13},{13,9},{2,6},{6,2},{1... | collective-permute-start | bytes 2555912 | tf_op jit(solution)/shard_map/ppermute | solution.py:172
  377.8 3.5 collective-permute-start.30
  379.6 23.8 %collective-permute-start.31 = (bf16[64,3328]{1,0:T(8,128)(2,1)S(1)}, bf16[64,3328]{1,0:T(8,128)(2,1)S(1)}, u32[]{:S(2)}, u32[]{:S(2)}) collective-permute-start(bf16[64,3328]{1,0:T(8,128)(2,1)S(1)} %fusion.12.own_x), channel_id=1, source_target_pairs={{0,8},{4,12},{8,0},{12,4},{1,9},{5,13},{9,1},{13,5},{2,10},{6,14},... | collective-permute-start | bytes 1277960 | tf_op jit(solution)/shard_map/ppermute | solution.py:172
  381.1 58.4 %reduce-scatter.11.cloned.1.call-start = ((), (), s32[]{:S(2)}) async-start(), calls=%async_computation.10 | async-start | bytes 1310720 | tf_op jit(solution)/shard_map/reduce_scatter | solution.py:239
  403.3 2.5 collective-permute-start.32
  403.4 2.4 collective-permute-start.33
  424.5 16.0 %collective-permute-start.36 = (bf16[128,512]{1,0:T(8,128)(2,1)}, bf16[128,512]{1,0:T(8,128)(2,1)S(1)}, u32[]{:S(2)}, u32[]{:S(2)}) collective-permute-start(bf16[128,512]{1,0:T(8,128)(2,1)} %get-tuple-element.90), channel_id=1, source_target_pairs={{0,3},{1,0},{2,1},{3,2},{4,7},{5,4},{6,5},{7,6},{8,11},{9,8},{10,9... | collective-permute-start | bytes 393224 | tf_op jit(solution)/shard_map/ppermute | solution.py:168
  425.6 18.7 %collective-permute-start.35 = (bf16[128,512]{1,0:T(8,128)(2,1)}, bf16[128,512]{1,0:T(8,128)(2,1)S(1)}, u32[]{:S(2)}, u32[]{:S(2)}) collective-permute-start(bf16[128,512]{1,0:T(8,128)(2,1)} %get-tuple-element.89), channel_id=1, source_target_pairs={{0,2},{1,3},{2,0},{3,1},{4,6},{5,7},{6,4},{7,5},{8,10},{9,11},{10,... | collective-permute-start | bytes 393224 | tf_op jit(solution)/shard_map/ppermute | solution.py:168
  426.4 17.9 %collective-permute-start.34 = (bf16[128,512]{1,0:T(8,128)(2,1)}, bf16[128,512]{1,0:T(8,128)(2,1)S(1)}, u32[]{:S(2)}, u32[]{:S(2)}) collective-permute-start(bf16[128,512]{1,0:T(8,128)(2,1)} %get-tuple-element.88), channel_id=1, source_target_pairs={{0,1},{1,2},{2,3},{3,0},{4,5},{5,6},{6,7},{7,4},{8,9},{9,10},{10,1... | collective-permute-start | bytes 393224 | tf_op jit(solution)/shard_map/ppermute | solution.py:168
  (33 other events, 189.0 us)
Sparse Core Ops, SparseCore 0:
  8.9 34.7 all-gather.3
  72.2 36.4 all-gather.5
  127.0 36.7 all-gather.7
  231.3 20.3 reduce-scatter.4
  311.1 25.9 reduce-scatter.6
  381.3 25.0 reduce-scatter.8
  408.7 30.8 reduce-scatter.10

commit v3 on v2

--- a/solution.py
+++ b/solution.py
@@ -9,9 +9,9 @@
 from jax.sharding import PartitionSpec as P
 
 BF16, F32 = jnp.bfloat16, jnp.float32
-GATE_UP_COST, DOWN_COST = 0.3, 4
-SPLIT = (0, 1)
-VMEM_LIMIT = 32 * 2**20
+GATE_UP_COST, DOWN_COST = 1, 1
+SPLIT = (0, 1, 2, 3)
+VMEM_LIMIT = 29 * 2**20
 PARTNER, OWN, X, BLOCKS = 0, 1, 2, 3
 
 
@@ -67,7 +67,7 @@
             ref[...] = acc[:, pl.ds(pl.multiple_of(x * half, half), half), :].astype(BF16)
 
 
-def down_kernel(n_col, split, place, col, own_x, other_x, own_x_core, other_x_core, weight_ref, *rest):
+def down_kernel(n_col, direct, place, order, own_x, other_x, own_x_core, other_x_core, weight_ref, *rest):
     out_refs, (own_half, partner_half) = rest[:-2], rest[-2:]
     step = pl.program_id(0)
     height, wide = own_x.shape
@@ -79,16 +79,13 @@
             target[pl.ds(pl.multiple_of((1 - place[X]) * height, height), height), :] = other[...]
 
     block = weight_ref.shape[1] // n_col
-    at = lax.rem(col[0] + step + 1, n_col) if split else step
-    columns = pl.ds(pl.multiple_of(at * block, block), block)
+    columns = pl.ds(pl.multiple_of(order[step] * block, block), block)
     total = dot(own_half[...], weight_ref[pl.ds(pl.multiple_of(place[OWN] * wide, wide), wide), columns])
     total += dot(partner_half[...], weight_ref[pl.ds(pl.multiple_of(place[PARTNER] * wide, wide), wide), columns])
     value = total.astype(BF16)
-    if not split:
-        out_refs[0][...] = value
-        return
+    each = n_col // len(out_refs)
     for k, out_ref in enumerate(out_refs):
-        @pl.when(step == k)
+        @pl.when(step // each == k)
         def _(out_ref=out_ref):
             out_ref[...] = value
 
@@ -139,17 +136,20 @@
     )(place, *operands)
 
 
-def down_call(place, col, pieces, down_weight, n_col, split):
+def down_call(place, order, pieces, down_weight, n_col, direct):
     half, wide = pieces[0].shape
     rows, block = 2 * half, down_weight.shape[1] // n_col
-    if split:
+    if direct:
         out_shape = [jax.ShapeDtypeStruct((rows, block), BF16)] * n_col
         out_specs = [whole((rows, block))] * n_col
     else:
-        out_shape = jax.ShapeDtypeStruct((rows, block * n_col), BF16)
-        out_specs = pl.BlockSpec((rows, block), lambda d, place, col: (0, d))
+        out_shape = [jax.ShapeDtypeStruct((rows, 2 * block), BF16)] * 2
+        out_specs = [
+            pl.BlockSpec((rows, block), lambda d, place, order: (0, jnp.minimum(d, 1))),
+            pl.BlockSpec((rows, block), lambda d, place, order: (0, jnp.maximum(d - 2, 0))),
+        ]
     return pl.pallas_call(
-        functools.partial(down_kernel, n_col, split),
+        functools.partial(down_kernel, n_col, direct),
         out_shape=out_shape,
         grid_spec=pltpu.PrefetchScalarGridSpec(
             num_scalar_prefetch=2,
@@ -161,7 +161,7 @@
         compiler_params=params(1),
         cost_estimate=cost(DOWN_COST, 4 * rows * wide * block * n_col, 8 * half * wide),
         name="down",
-    )(place, col, *pieces, down_weight)
+    )(place, order, *pieces, down_weight)
 
 
 def shifted(x, n, shift):
@@ -176,50 +176,37 @@
     return lax.optimization_barrier((x,) + deps)[0]
 
 
-def pipelined(n_col, tokens, gate_weight, up_weight, down_weight):
+def pipelined(tokens, gate_weight, up_weight, down_weight):
+    n_col = 4
     eighth = tokens.shape[0] // 8
     weights = (gate_weight, up_weight)
     down_weight = pltpu.with_memory_space_constraint(down_weight, pltpu.VMEM)
-    row, col = lax.axis_index("row"), lax.axis_index("col")
     table = np.array(
         [
-            [1 - r % 2, r % 2, r // 2] + [(c - s) % n_col for s in range(n_col)] + list(range(n_col)) + [c]
+            [[1 - r % 2, r % 2, r // 2] + [(c - s) % n_col for s in range(n_col)] + [0]]
+            + [[c ^ 1, c ^ 3, c, c ^ 2] * 2, [(c + 1) % n_col, (c + 2) % n_col, (c + 3) % n_col, c] * 2]
             for r in range(4)
             for c in range(n_col)
         ],
         np.int32,
     )
-    mine = jnp.asarray(table)[row * n_col + col]
-    by_shift, col_id = mine[: BLOCKS + n_col], mine[-1:]
-    natural = jnp.concatenate([mine[:BLOCKS], mine[BLOCKS + n_col : -1]])
-
-    def direct(piece):
+    mine = jnp.asarray(table)[lax.axis_index("row") * n_col + lax.axis_index("col")]
+    place, halving, straight = mine[0], mine[1], mine[2]
+    last = [place]
+
+    def send_tokens(lo, hi):
+        piece = after(tokens[lo * eighth : hi * eighth], *last)
         return [piece] + [shifted(piece, n_col, s) for s in range(1, n_col)]
 
-    bounds = [0, 1, 3, 5, 7, 8]
-    def gathered(lo, hi, *behind):
-        piece = after(tokens[lo * eighth : hi * eighth], *behind)
-        return lax.all_gather(piece, "col", axis=1, tiled=True)
-
-    def gathered(lo, hi, *behind):
-        piece = after(tokens[lo * eighth : hi * eighth], *behind)
-        return lax.all_gather(piece, "col", axis=1, tiled=True)
-
-    first = direct(tokens[:eighth])
-    second = lax.all_gather(tokens[eighth : 3 * eighth], "col", axis=1, tiled=True)
-    sources = [(by_shift, first, 0), (natural, [second], 0)]
-    chunk_rows = [(b - a) * eighth for a, b in zip(bounds, bounds[1:])]
-    last = [mine]
-
     def partner(i):
-        place, tok, block = sources[i]
-        out = gate_up_call(after(place, *last), tok, chunk_rows[i], block, weights, n_col, PARTNER, i in SPLIT)
+        tok, rows, block = sources[i]
+        out = gate_up_call(after(place, *last), tok, rows, block, weights, n_col, PARTNER, i in SPLIT)
         last[:] = list(out)
         return [swapped(piece, 1) for piece in out]
 
     def own(i, received):
-        place, tok, block = sources[i]
-        send, keep = gate_up_call(after(place, *last), tok, chunk_rows[i], block, weights, n_col, OWN, i in SPLIT, received)
+        tok, rows, block = sources[i]
+        send, keep = gate_up_call(after(place, *last), tok, rows, block, weights, n_col, OWN, i in SPLIT, received)
         last[:] = [send]
         return keep, swapped(send, 2)
 
@@ -229,44 +216,70 @@
         up = keep[1].astype(F32) + arrived[1].astype(F32)
         hidden = (jax.nn.silu(gate) * up).astype(BF16)
         last[:] = [hidden]
-        hidden_x = swapped(hidden, 2)
-        return hidden, hidden_x, swapped(hidden, 1), swapped(hidden_x, 1)
-
-    def down(pieces, split=False):
-        out = down_call(after(by_shift, *last), col_id, pieces, down_weight, n_col, split)
-        last[:] = list(out) if split else [out]
-        if not split:
-            return lax.psum_scatter(out, "col", scatter_dimension=1, tiled=True)
+        return hidden, swapped(hidden, 2), swapped(hidden, 1)
+
+    def relay(pieces):
+        hidden, hidden_x, hidden_core = pieces
+        return hidden, hidden_x, hidden_core, swapped(after(hidden_x, *last), 1)
+
+    def down(pieces):
+        send, keep = down_call(after(place, *last), halving, pieces, down_weight, n_col, False)
+        last[:] = [send]
+        return keep, lax.ppermute(send, "col", [(c, c ^ 1) for c in range(n_col)])
+
+    def halve(pair):
+        keep, arrived = after(pair[0], *last), pair[1]
+        block = keep.shape[1] // 2
+        total = [keep[:, at : at + block].astype(F32) + arrived[:, at : at + block].astype(F32) for at in (0, block)]
+        send = total[1].astype(BF16)
+        last[:] = [send]
+        return total[0], lax.ppermute(send, "col", [(c, c ^ 2) for c in range(n_col)])
+
+    def down_direct(pieces):
+        out = down_call(after(place, *last), straight, pieces, down_weight, n_col, True)
         total = out[-1].astype(F32)
         for s in range(1, n_col):
             total = total + shifted(out[s - 1], n_col, s).astype(F32)
         return total.astype(BF16)
 
+    def finish(pair):
+        return (pair[0] + pair[1].astype(F32)).astype(BF16)
+
+    t0, t1 = send_tokens(0, 1), send_tokens(1, 3)
+    sources = [(t0, eighth, 0), (t1, 2 * eighth, 0)]
     r0 = partner(0)
+    t2 = send_tokens(3, 5)
     p0 = own(0, r0)
     r1 = partner(1)
-    third = gathered(3, 5, second, *last)
-    sources.append((natural, [third], 0))
     h0 = gated(p0)
     p1 = own(1, r1)
+    t3 = send_tokens(5, 8)
+    sources += [(t2, 2 * eighth, 0), (t3, 2 * eighth, 0), (t3, eighth, 2)]
     r2 = partner(2)
-    rest = gathered(5, 8, third, *last)
-    sources += [(natural, [rest], 0), (natural, [rest], 2)]
-    r3 = partner(3)
+    h0 = relay(h0)
+    d0 = down(h0)
     p2 = own(2, r2)
     h1 = gated(p1)
-    o0 = down(h0)
+    r3 = partner(3)
+    z0 = halve(d0)
+    p3 = own(3, r3)
+    h1 = relay(h1)
+    h2 = gated(p2)
     r4 = partner(4)
-    p3 = own(3, r3)
-    h2 = gated(p2)
-    o1 = down(h1)
+    d1 = down(h1)
     p4 = own(4, r4)
+    z1 = halve(d1)
+    h2 = relay(h2)
     h3 = gated(p3)
-    o2 = down(h2)
+    d2 = down(h2)
+    h3 = relay(h3)
     h4 = gated(p4)
-    o3 = down(h3)
-    o4 = down(h4, split=True)
-    return jnp.concatenate([o0, o1, o2, o3, o4], axis=0)
+    z2 = halve(d2)
+    d3 = down(h3)
+    h4 = relay(h4)
+    z3 = halve(d3)
+    o4 = down_direct(h4)
+    return jnp.concatenate([finish(z0), finish(z1), finish(z2), finish(z3), o4], axis=0)
 
 
 def generic(tokens, gate_weight, up_weight, down_weight):
@@ -283,5 +296,5 @@
     n_row, n_col = mesh.shape["row"], mesh.shape["col"]
     in_specs = (P("groups", ("row", "col")), P("row", "col"), P("row", "col"), P("col", "row"))
     out_specs = P("groups", ("row", "col"))
-    step = functools.partial(pipelined, n_col) if n_row == 4 else generic
+    step = pipelined if (n_row, n_col) == (4, 4) else generic
     return jax.shard_map(step, mesh=mesh, in_specs=in_specs, out_specs=out_specs, check_vma=False)

time: 459 us -> 373 us (0.81)
  local copies, waits for them, and re-layouts: 69.9 us -> 16.1 us
  waiting for transfers between devices: 133 us -> 86.8 us
  starting transfers between devices: 28.6 us -> 67.3 us
  between operations: 14.1 us -> 1.13 us
  Pallas kernels: 192 us -> 185 us
  other arithmetic: 14.8 us -> 9.85 us
    unnamed x78 -> x88, local copies, waits for them, and re-layouts: 64 us -> 12.8 us
    all_gather x3 -> x0, waiting for transfers between devices: 47.8 us -> none  [the longest x2 47.8 us: gathered(): return lax.all_gather(piece, 'col', axis=1, tiled=True)]
    ppermute x6 -> x15, starting transfers between devices: 10.3 us -> 35.8 us  [shifted(): return lax.ppermute(x, 'col', [(i, (i + shift) % n) for i in range(n)])]
    ppermute x0 -> x8, starting transfers between devices: none -> 15.5 us  [the longest x4 9.33 us: down(): return (keep, lax.ppermute(send, 'col', [(c, c ^ 1) for c in range(n_col)]))]
    ppermute x0 -> x8, waiting for transfers between devices: none -> 12.8 us  [the longest x4 12.8 us: down(): return (keep, lax.ppermute(send, 'col', [(c, c ^ 1) for c in range(n_col)]))]
    reduce_scatter x4 -> x0, waiting for transfers between devices: 10.8 us -> none  [down(): return lax.psum_scatter(out, 'col', scatter_dimension=1, tiled=True)]
    ppermute x31 -> x37, waiting for transfers between devices: 62.7 us -> 56.7 us  [swapped(): return lax.ppermute(x, 'row', [(i, i ^ mask) for i in range(4)])]
    convert_element_type x5, other arithmetic: 13.1 us -> 7.47 us  [gated(): hidden = (jax.nn.silu(gate) * up).astype(BF16)]
  transfers between devices with their start and end apart: 44 -> 60, of which waited for: 17 -> 19; matrix products, arithmetic and copies ran while one was open for 5% -> 3% of each run, Pallas kernels for 39% -> 47%
where the time goes in v3:
time: 373 us; the launch traced here: 366 us
  Pallas kernels  185 us (50%)
  waiting for transfers between devices  86.8 us (23%)
  starting transfers between devices  67.3 us (18%)
  local copies, waits for them, and re-layouts  16.1 us (4%)
  other arithmetic  9.85 us (3%)
    pallas_call x10, Pallas kernels, gate_up_call(): pl.pallas_call(functools.partial(body, len(tokens), split), out_shape=out...  134 us
    ppermute x37, waiting for transfers between devices, swapped(): return lax.ppermute(x, 'row', [(i, i ^ mask) for i in range(4)])  56.7 us
    pallas_call x5, Pallas kernels, down_call(): pl.pallas_call(functools.partial(down_kernel, n_col, direct), out_shape=o...  50.8 us
    ppermute x15, starting transfers between devices, shifted(): return lax.ppermute(x, 'col', [(i, (i + shift) % n) for i in range(n)])  35.8 us
    ppermute x15, waiting for transfers between devices, shifted(): return lax.ppermute(x, 'col', [(i, (i + shift) % n) for i in range(n)])  17.3 us
    ppermute x37, starting transfers between devices, swapped(): return lax.ppermute(x, 'row', [(i, i ^ mask) for i in range(4)])  16.1 us
    unnamed x88, local copies, waits for them, and re-layouts  12.8 us
    ppermute x4, waiting for transfers between devices, down(): return (keep, lax.ppermute(send, 'col', [(c, c ^ 1) for c in range(n_col)]))  12.8 us
  transfers between devices with their start and end apart: 60, of which 19 were waited for; matrix products, arithmetic and copies ran while one was open for 3% of the time, Pallas kernels for 47%

profile of v3, /device:TPU:0, one launch (start us, length us, event | category | flops | bytes accessed | tf_op | source)
XLA Modules:
  0.0 366.3 jit_solution(14110716247714286181)
XLA Ops:
  2.2 3.1 collective-permute-start
  5.3 2.6 collective-permute-start.1
  9.2 2.5 collective-permute-done.refs_1_
  11.7 4.8 %collective-permute-done.1.refs_2_ = bf16[128,512]{1,0:T(8,128)(2,1)S(1)} collective-permute-done((bf16[128,512]{1,0:T(8,128)(2,1)S(1)}, bf16[128,512]{1,0:T(8,128)(2,1)S(1)}, u32[]{:S(2)}, u32[]{:S(2)}) %collective-permute-start.1) | collective-permute-done | bytes 131104 | tf_op jit(solution)/shard_map/ppermute | solution.py:168
  16.5 11.3 %partner.5 = (bf16[1,64,3328]{2,1,0:T(8,128)(2,1)S(1)}, bf16[1,64,3328]{2,1,0:T(8,128)(2,1)S(1)}, bf16[1,64,3328]{2,1,0:T(8,128)(2,1)S(1)}, bf16[1,64,3328]{2,1,0:T(8,128)(2,1)S(1)}) custom-call(s32[8]{0:T(128)S(1)} %get-tuple-element.141.place, bf16[128,512]{1,0:T(8,128)(2,1)S(1)} %slice.133.refs_0_, bf16[128,512]{1,0:T(8,128)(2,1)S(1)} %collective-permute-done.refs_1_, ...), custom_call_target="tpu_custom_call" | custom-call | flops 3489660928 | bytes 28966912 | tf_op jit(solution)/shard_map/partner/pallas_call | solution.py:123
  28.9 3.3 collective-permute-start.7
  32.3 1.7 collective-permute-start.8
  35.3 11.7 %own.5 = (bf16[2,64,3328]{2,1,0:T(8,128)(2,1)S(1)}, bf16[2,64,3328]{2,1,0:T(8,128)(2,1)S(1)}) custom-call(s32[8]{0:T(128)S(1)} %get-tuple-element.141.place, bf16[128,512]{1,0:T(8,128)(2,1)S(1)} %slice.133.refs_0_, bf16[128,512]{1,0:T(8,128)(2,1)S(1)} %collective-permute-done.refs_1_, bf16[128,512]{1,0:T(8,128)(2,1)S(1)} %collective-permute-done.1.refs_2_, ...), custom_call_target="tpu_custom_call" | custom-call | flops 3489660928 | bytes 28966912 | tf_op jit(solution)/shard_map/own/pallas_call | solution.py:123
  47.0 1.6 collective-permute-start.10
  49.2 2.1 collective-permute-done.8.refs_2_
  51.3 13.5 %partner.6 = (bf16[1,128,3328]{2,1,0:T(8,128)(2,1)S(1)}, bf16[1,128,3328]{2,1,0:T(8,128)(2,1)S(1)}, bf16[1,128,3328]{2,1,0:T(8,128)(2,1)S(1)}, bf16[1,128,3328]{2,1,0:T(8,128)(2,1)S(1)}) custom-call(s32[8]{0:T(128)S(1)} %get-tuple-element.141.place, bf16[256,512]{1,0:T(8,128)(2,1)S(1)} %get-tuple-element.86.refs_0_, ...), custom_call_target="tpu_custom_call" | custom-call | flops 6979321856 | bytes 30670848 | tf_op jit(solution)/shard_map/partner/pallas_call | solution.py:123
  65.4 2.0 collective-permute-done.10
  67.9 10.0 %collective-permute-start.16 = (bf16[256,512]{1,0:T(8,128)(2,1)S(1)}, bf16[256,512]{1,0:T(8,128)(2,1)S(1)}, u32[]{:S(2)}, u32[]{:S(2)}) collective-permute-start(bf16[256,512]{1,0:T(8,128)(2,1)S(1)} %get-tuple-element.95.refs_0_), channel_id=1, source_target_pairs={{0,2},{1,3},{2,0},{3,1},{4,6},{5,7},{6,4},{7,5},{8,10},{9,11},{10,... | collective-permute-start | bytes 786440 | tf_op jit(solution)/shard_map/ppermute | solution.py:168
  77.9 3.5 collective-permute-start.17
  82.9 15.6 %own.6 = (bf16[2,128,3328]{2,1,0:T(8,128)(2,1)}, bf16[2,128,3328]{2,1,0:T(8,128)(2,1)S(1)}) custom-call(s32[8]{0:T(128)S(1)} %get-tuple-element.141.place, bf16[256,512]{1,0:T(8,128)(2,1)S(1)} %get-tuple-element.86.refs_0_, bf16[256,512]{1,0:T(8,128)(2,1)S(1)} %collective-permute-done.7.refs_1_, bf16[256,512]{1,0:T(8,128)(2,1)S(1)} %collective-permute-done.8.refs_2_, ...), custom_call_target="tpu_custom_call" | custom-call | flops 6979321856 | bytes 30670848 | tf_op jit(solution)/shard_map/own/pallas_call | solution.py:123
  98.6 15.8 %partner.7 = (bf16[1,128,3328]{2,1,0:T(8,128)(2,1)S(1)}, bf16[1,128,3328]{2,1,0:T(8,128)(2,1)}, bf16[1,128,3328]{2,1,0:T(8,128)(2,1)}, bf16[1,128,3328]{2,1,0:T(8,128)(2,1)S(1)}) custom-call(s32[8]{0:T(128)S(1)} %get-tuple-element.141.place, bf16[256,512]{1,0:T(8,128)(2,1)S(1)} %get-tuple-element.95.refs_0_, ...), custom_call_target="tpu_custom_call" | custom-call | flops 6979321856 | bytes 30670848 | tf_op jit(solution)/shard_map/partner/pallas_call | solution.py:123
  118.6 7.7 %down.5 = (bf16[128,1024]{1,0:T(8,128)(2,1)}, bf16[128,1024]{1,0:T(8,128)(2,1)}) custom-call(s32[8]{0:T(128)} %copy-done.1, s32[8]{0:T(128)} %get-tuple-element.150.order, bf16[64,3328]{1,0:T(8,128)(2,1)} %copy-done.5, bf16[64,3328]{1,0:T(8,128)(2,1)} %copy-done.20, bf16[64,3328]{1,0:T(8,128)(2,1)} %copy-done.21, bf16[64,3328]{1,0:T(8,128)(2,1)} %copy-done.24, ...), custom_call_target="tpu_custom_call" | custom-call | flops 3489660928 | bytes 1703936 | tf_op jit(solution)/shard_map/down/pallas_call | solution.py:151
  126.8 1.7 collective-permute-start.27
  128.5 1.9 collective-permute-start.28
  131.0 14.4 %own.7 = (bf16[2,128,3328]{2,1,0:T(8,128)(2,1)S(1)}, bf16[2,128,3328]{2,1,0:T(8,128)(2,1)S(1)}) custom-call(s32[8]{0:T(128)S(1)} %copy-done.2, bf16[256,512]{1,0:T(8,128)(2,1)S(1)} %get-tuple-element.95.refs_0_, bf16[256,512]{1,0:T(8,128)(2,1)S(1)} %collective-permute-done.15.refs_1_, bf16[256,512]{1,0:T(8,128)(2,1)S(1)} %collective-permute-done.16.refs_2_, ...), custom_call_target="tpu_custom_call" | custom-call | flops 6979321856 | bytes 30670848 | tf_op jit(solution)/shard_map/own/pallas_call | solution.py:123
  145.4 9.1 %collective-permute-done.25 = bf16[2,128,3328]{2,1,0:T(8,128)(2,1)} collective-permute-done((bf16[2,128,3328]{2,1,0:T(8,128)(2,1)}, bf16[2,128,3328]{2,1,0:T(8,128)(2,1)}, u32[]{:S(2)}, u32[]{:S(2)}) %collective-permute-start.25) | collective-permute-done | bytes 1703968 | tf_op jit(solution)/shard_map/ppermute | solution.py:172
  155.0 3.0 fusion.8.own_x
  158.0 13.5 %partner.8 = (bf16[1,128,3328]{2,1,0:T(8,128)(2,1)S(1)}, bf16[1,128,3328]{2,1,0:T(8,128)(2,1)S(1)}, bf16[1,128,3328]{2,1,0:T(8,128)(2,1)S(1)}, bf16[1,128,3328]{2,1,0:T(8,128)(2,1)S(1)}) custom-call(s32[8]{0:T(128)S(1)} %copy-done.2, bf16[384,512]{1,0:T(8,128)(2,1)S(1)} %slice.145.refs_0_, bf16[384,512]{1,0:T(8,128)(2,1)S(1)} %collective-permute-done.26.refs_1_, ...), custom_call_target="tpu_custom_call" | custom-call | flops 6979321856 | bytes 30670848 | tf_op jit(solution)/shard_map/partner/pallas_call | solution.py:123
  177.6 14.4 %own.8 = (bf16[2,128,3328]{2,1,0:T(8,128)(2,1)S(1)}, bf16[2,128,3328]{2,1,0:T(8,128)(2,1)S(1)}) custom-call(s32[8]{0:T(128)S(1)} %copy-done.2, bf16[384,512]{1,0:T(8,128)(2,1)S(1)} %slice.145.refs_0_, bf16[384,512]{1,0:T(8,128)(2,1)S(1)} %collective-permute-done.26.refs_1_, bf16[384,512]{1,0:T(8,128)(2,1)S(1)} %collective-permute-done.27.refs_2_, ...), custom_call_target="tpu_custom_call" | custom-call | flops 6979321856 | bytes 30670848 | tf_op jit(solution)/shard_map/own/pallas_call | solution.py:123
  192.0 2.6 collective-permute-done.35
  194.6 1.6 fusion.4.own_x
  196.2 12.6 %partner.9 = bf16[2,128,3328]{2,1,0:T(8,128)(2,1)S(1)} custom-call(s32[8]{0:T(128)S(1)} %copy-done.2, bf16[384,512]{1,0:T(8,128)(2,1)S(1)} %slice.145.refs_0_, bf16[384,512]{1,0:T(8,128)(2,1)S(1)} %collective-permute-done.26.refs_1_, bf16[384,512]{1,0:T(8,128)(2,1)S(1)} %collective-permute-done.27.refs_2_, ...), custom_call_target="tpu_custom_call" | custom-call | flops 3489660928 | bytes 28966912 | tf_op jit(solution)/shard_map/partner/pallas_call | solution.py:123
  209.4 1.8 collective-permute-done.36.other_x
  213.7 1.6 collective-permute-done.38.other_x_core
  215.3 11.9 %down.6 = (bf16[256,1024]{1,0:T(8,128)(2,1)}, bf16[256,1024]{1,0:T(8,128)(2,1)}) custom-call(s32[8]{0:T(128)} %copy-done.1, s32[8]{0:T(128)} %get-tuple-element.150.order, bf16[128,3328]{1,0:T(8,128)(2,1)} %fusion.8.own_x, bf16[128,3328]{1,0:T(8,128)(2,1)} %collective-permute-done.36.other_x, bf16[128,3328]{1,0:T(8,128)(2,1)} %collective-permute-done.37.own_x_core, ...), custom_call_target="tpu_custom_call" | custom-call | flops 6979321856 | bytes 3407872 | tf_op jit(solution)/shard_map/down/pallas_call | solution.py:151
  227.2 4.4 %collective-permute-start.40 = (bf16[256,1024]{1,0:T(8,128)(2,1)}, bf16[256,1024]{1,0:T(8,128)(2,1)S(1)}, u32[]{:S(2)}, u32[]{:S(2)}) collective-permute-start(bf16[256,1024]{1,0:T(8,128)(2,1)} %get-tuple-element.123), channel_id=1, source_target_pairs={{0,1},{1,0},{2,3},{3,2},{4,5},{5,4},{6,7},{7,6},{8,9},{9,8},{10,11... | collective-permute-start | bytes 1572872 | tf_op jit(solution)/shard_map/ppermute | solution.py:228
  231.6 11.7 %own.9 = (bf16[2,64,3328]{2,1,0:T(8,128)(2,1)S(1)}, bf16[2,64,3328]{2,1,0:T(8,128)(2,1)S(1)}) custom-call(s32[8]{0:T(128)S(1)} %copy-done.3, bf16[384,512]{1,0:T(8,128)(2,1)S(1)} %slice.145.refs_0_, bf16[384,512]{1,0:T(8,128)(2,1)S(1)} %collective-permute-done.26.refs_1_, bf16[384,512]{1,0:T(8,128)(2,1)S(1)} %collective-permute-done.27.refs_2_, ...), custom_call_target="tpu_custom_call" | custom-call | flops 3489660928 | bytes 28966912 | tf_op jit(solution)/shard_map/own/pallas_call | solution.py:123
  244.8 24.3 %collective-permute-done.43.other_x = bf16[128,3328]{1,0:T(8,128)(2,1)} collective-permute-done((bf16[128,3328]{1,0:T(8,128)(2,1)}, bf16[128,3328]{1,0:T(8,128)(2,1)}, u32[]{:S(2)}, u32[]{:S(2)}) %collective-permute-start.43) | collective-permute-done | bytes 852000 | tf_op jit(solution)/shard_map/ppermute | solution.py:172
  269.2 2.1 fusion.own_x
  273.4 1.6 collective-permute-start.30
  276.4 8.8 %copy-done = bf16[6656,2048]{1,0:T(8,128)(2,1)S(1)} copy-done((bf16[6656,2048]{1,0:T(8,128)(2,1)S(1)}, bf16[6656,2048]{1,0:T(8,128)(2,1)}, u32[]{:S(2)}) %copy-start) | copy-done | bytes 27263000
  285.2 11.8 %down.7 = (bf16[256,1024]{1,0:T(8,128)(2,1)}, bf16[256,1024]{1,0:T(8,128)(2,1)}) custom-call(s32[8]{0:T(128)} %copy-done.1, s32[8]{0:T(128)} %get-tuple-element.150.order, bf16[128,3328]{1,0:T(8,128)(2,1)} %fusion.4.own_x, bf16[128,3328]{1,0:T(8,128)(2,1)} %collective-permute-done.43.other_x, bf16[128,3328]{1,0:T(8,128)(2,1)} %copy-done.9, ...), custom_call_target="tpu_custom_call" | custom-call | flops 6979321856 | bytes 3407872 | tf_op jit(solution)/shard_map/down/pallas_call | solution.py:151
  297.0 2.7 collective-permute-start.47
  299.7 11.3 %collective-permute-done.46 = bf16[2,64,3328]{2,1,0:T(8,128)(2,1)S(1)} collective-permute-done((bf16[2,64,3328]{2,1,0:T(8,128)(2,1)S(1)}, bf16[2,64,3328]{2,1,0:T(8,128)(2,1)S(1)}, u32[]{:S(2)}, u32[]{:S(2)}) %collective-permute-start.46) | collective-permute-done | bytes 852000 | tf_op jit(solution)/shard_map/ppermute | solution.py:172
  315.8 11.8 %down.8 = (bf16[256,1024]{1,0:T(8,128)(2,1)}, bf16[256,1024]{1,0:T(8,128)(2,1)}) custom-call(s32[8]{0:T(128)} %copy-done.1, s32[8]{0:T(128)} %get-tuple-element.150.order, bf16[128,3328]{1,0:T(8,128)(2,1)} %copy-done.4, bf16[128,3328]{1,0:T(8,128)(2,1)} %copy-done.8, bf16[128,3328]{1,0:T(8,128)(2,1)} %copy-done.10, bf16[128,3328]{1,0:T(8,128)(2,1)} %copy-done.12, ...), custom_call_target="tpu_custom_call" | custom-call | flops 6979321856 | bytes 3407872 | tf_op jit(solution)/shard_map/down/pallas_call | solution.py:151
  327.6 1.7 collective-permute-start.52
  330.3 11.3 %collective-permute-done.52 = bf16[256,1024]{1,0:T(8,128)(2,1)S(1)} collective-permute-done((bf16[256,1024]{1,0:T(8,128)(2,1)}, bf16[256,1024]{1,0:T(8,128)(2,1)S(1)}, u32[]{:S(2)}, u32[]{:S(2)}) %collective-permute-start.52) | collective-permute-done | bytes 524320 | tf_op jit(solution)/shard_map/ppermute | solution.py:228
  341.7 1.9 collective-permute-start.53
  344.6 7.6 %down.9 = (bf16[128,512]{1,0:T(8,128)(2,1)}, bf16[128,512]{1,0:T(8,128)(2,1)}, bf16[128,512]{1,0:T(8,128)(2,1)}, bf16[128,512]{1,0:T(8,128)(2,1)}) custom-call(s32[8]{0:T(128)} %copy-done.1, s32[8]{0:T(128)} %get-tuple-element.149.order, bf16[64,3328]{1,0:T(8,128)(2,1)} %copy-done.6, bf16[64,3328]{1,0:T(8,128)(2,1)} %copy-done.19, ...), custom_call_target="tpu_custom_call" | custom-call | flops 3489660928 | bytes 1703936 | tf_op jit(solution)/shard_map/down/pallas_call | solution.py:151
  352.1 1.7 collective-permute-start.57
  356.4 4.3 %collective-permute-done.57 = bf16[128,512]{1,0:T(8,128)(2,1)S(1)} collective-permute-done((bf16[128,512]{1,0:T(8,128)(2,1)}, bf16[128,512]{1,0:T(8,128)(2,1)S(1)}, u32[]{:S(2)}, u32[]{:S(2)}) %collective-permute-start.57) | collective-permute-done | bytes 131104 | tf_op jit(solution)/shard_map/ppermute | solution.py:168
  360.6 3.6 collective-permute-done.58
  364.2 1.6 fusion.24
  (196 shorter events, 38.4 us)
Async XLA Ops:
  2.2 9.5 %collective-permute-start = (bf16[128,512]{1,0:T(8,128)(2,1)S(1)}, bf16[128,512]{1,0:T(8,128)(2,1)S(1)}, u32[]{:S(2)}, u32[]{:S(2)}) collective-permute-start(bf16[128,512]{1,0:T(8,128)(2,1)S(1)} %slice.133.refs_0_), channel_id=1, source_target_pairs={{0,1},{1,2},{2,3},{3,0},{4,5},{5,6},{6,7},{7,4},{8,9},{9,10},{10,1... | collective-permute-start | bytes 393224 | tf_op jit(solution)/shard_map/ppermute | solution.py:168
  5.3 11.2 %collective-permute-start.1 = (bf16[128,512]{1,0:T(8,128)(2,1)S(1)}, bf16[128,512]{1,0:T(8,128)(2,1)S(1)}, u32[]{:S(2)}, u32[]{:S(2)}) collective-permute-start(bf16[128,512]{1,0:T(8,128)(2,1)S(1)} %slice.133.refs_0_), channel_id=1, source_target_pairs={{0,2},{1,3},{2,0},{3,1},{4,6},{5,7},{6,4},{7,5},{8,10},{9,11},{10,... | collective-permute-start | bytes 393224 | tf_op jit(solution)/shard_map/ppermute | solution.py:168
  7.9 8.6 %collective-permute-start.2 = (bf16[128,512]{1,0:T(8,128)(2,1)S(1)}, bf16[128,512]{1,0:T(8,128)(2,1)S(1)}, u32[]{:S(2)}, u32[]{:S(2)}) collective-permute-start(bf16[128,512]{1,0:T(8,128)(2,1)S(1)} %slice.133.refs_0_), channel_id=1, source_target_pairs={{0,3},{1,0},{2,1},{3,2},{4,7},{5,4},{6,5},{7,6},{8,11},{9,8},{10,9... | collective-permute-start | bytes 393224 | tf_op jit(solution)/shard_map/ppermute | solution.py:168
  28.4 6.9 %collective-permute-start.5 = (bf16[1,64,3328]{2,1,0:T(8,128)(2,1)S(1)}, bf16[1,64,3328]{2,1,0:T(8,128)(2,1)S(1)}, u32[]{:S(2)}, u32[]{:S(2)}) collective-permute-start(bf16[1,64,3328]{2,1,0:T(8,128)(2,1)S(1)} %get-tuple-element.80), channel_id=1, source_target_pairs={{0,4},{4,0},{8,12},{12,8},{1,5},{5,1},{9,13},{13,9},{2,6},{6,2},{1... | collective-permute-start | bytes 1277960 | tf_op jit(solution)/shard_map/ppermute | solution.py:172
  28.5 6.8 %collective-permute-start.6 = (bf16[1,64,3328]{2,1,0:T(8,128)(2,1)S(1)}, bf16[1,64,3328]{2,1,0:T(8,128)(2,1)S(1)}, u32[]{:S(2)}, u32[]{:S(2)}) collective-permute-start(bf16[1,64,3328]{2,1,0:T(8,128)(2,1)S(1)} %get-tuple-element.81), channel_id=1, source_target_pairs={{0,4},{4,0},{8,12},{12,8},{1,5},{5,1},{9,13},{13,9},{2,6},{6,2},{1... | collective-permute-start | bytes 1277960 | tf_op jit(solution)/shard_map/ppermute | solution.py:172
  28.9 20.3 %collective-permute-start.7 = (bf16[256,512]{1,0:T(8,128)(2,1)S(1)}, bf16[256,512]{1,0:T(8,128)(2,1)S(1)}, u32[]{:S(2)}, u32[]{:S(2)}) collective-permute-start(bf16[256,512]{1,0:T(8,128)(2,1)S(1)} %get-tuple-element.86.refs_0_), channel_id=1, source_target_pairs={{0,1},{1,2},{2,3},{3,0},{4,5},{5,6},{6,7},{7,4},{8,9},{9,10},{10,1... | collective-permute-start | bytes 786440 | tf_op jit(solution)/shard_map/ppermute | solution.py:168
  32.3 19.0 %collective-permute-start.8 = (bf16[256,512]{1,0:T(8,128)(2,1)S(1)}, bf16[256,512]{1,0:T(8,128)(2,1)S(1)}, u32[]{:S(2)}, u32[]{:S(2)}) collective-permute-start(bf16[256,512]{1,0:T(8,128)(2,1)S(1)} %get-tuple-element.86.refs_0_), channel_id=1, source_target_pairs={{0,2},{1,3},{2,0},{3,1},{4,6},{5,7},{6,4},{7,5},{8,10},{9,11},{10,... | collective-permute-start | bytes 786440 | tf_op jit(solution)/shard_map/ppermute | solution.py:168
  33.9 17.4 %collective-permute-start.9 = (bf16[256,512]{1,0:T(8,128)(2,1)S(1)}, bf16[256,512]{1,0:T(8,128)(2,1)S(1)}, u32[]{:S(2)}, u32[]{:S(2)}) collective-permute-start(bf16[256,512]{1,0:T(8,128)(2,1)S(1)} %get-tuple-element.86.refs_0_), channel_id=1, source_target_pairs={{0,3},{1,0},{2,1},{3,2},{4,7},{5,4},{6,5},{7,6},{8,11},{9,8},{10,9... | collective-permute-start | bytes 786440 | tf_op jit(solution)/shard_map/ppermute | solution.py:168
  47.0 20.5 %collective-permute-start.10 = (bf16[2,64,3328]{2,1,0:T(8,128)(2,1)S(1)}, bf16[2,64,3328]{2,1,0:T(8,128)(2,1)S(1)}, u32[]{:S(2)}, u32[]{:S(2)}) collective-permute-start(bf16[2,64,3328]{2,1,0:T(8,128)(2,1)S(1)} %get-tuple-element.84), channel_id=1, source_target_pairs={{0,8},{4,12},{8,0},{12,4},{1,9},{5,13},{9,1},{13,5},{2,10},{6,14},... | collective-permute-start | bytes 2555912 | tf_op jit(solution)/shard_map/ppermute | solution.py:172
  48.5 50.0 %collective-permute-start.15 = (bf16[256,512]{1,0:T(8,128)(2,1)S(1)}, bf16[256,512]{1,0:T(8,128)(2,1)S(1)}, u32[]{:S(2)}, u32[]{:S(2)}) collective-permute-start(bf16[256,512]{1,0:T(8,128)(2,1)S(1)} %get-tuple-element.95.refs_0_), channel_id=1, source_target_pairs={{0,1},{1,2},{2,3},{3,0},{4,5},{5,6},{6,7},{7,4},{8,9},{9,10},{10,1... | collective-permute-start | bytes 786440 | tf_op jit(solution)/shard_map/ppermute | solution.py:168
  64.8 13.1 %collective-permute-start.12 = (bf16[1,128,3328]{2,1,0:T(8,128)(2,1)S(1)}, bf16[1,128,3328]{2,1,0:T(8,128)(2,1)S(1)}, u32[]{:S(2)}, u32[]{:S(2)}) collective-permute-start(bf16[1,128,3328]{2,1,0:T(8,128)(2,1)S(1)} %get-tuple-element.88), channel_id=1, source_target_pairs={{0,4},{4,0},{8,12},{12,8},{1,5},{5,1},{9,13},{13,9},{2,6},{6,2},{1... | collective-permute-start | bytes 2555912 | tf_op jit(solution)/shard_map/ppermute | solution.py:172
  65.3 16.1 %collective-permute-start.13 = (bf16[1,128,3328]{2,1,0:T(8,128)(2,1)S(1)}, bf16[1,128,3328]{2,1,0:T(8,128)(2,1)S(1)}, u32[]{:S(2)}, u32[]{:S(2)}) collective-permute-start(bf16[1,128,3328]{2,1,0:T(8,128)(2,1)S(1)} %get-tuple-element.89), channel_id=1, source_target_pairs={{0,4},{4,0},{8,12},{12,8},{1,5},{5,1},{9,13},{13,9},{2,6},{6,2},{1... | collective-permute-start | bytes 2555912 | tf_op jit(solution)/shard_map/ppermute | solution.py:172
  67.5 15.5 %collective-permute-start.14 = (bf16[1,128,3328]{2,1,0:T(8,128)(2,1)S(1)}, bf16[1,128,3328]{2,1,0:T(8,128)(2,1)S(1)}, u32[]{:S(2)}, u32[]{:S(2)}) collective-permute-start(bf16[1,128,3328]{2,1,0:T(8,128)(2,1)S(1)} %get-tuple-element.90), channel_id=1, source_target_pairs={{0,4},{4,0},{8,12},{12,8},{1,5},{5,1},{9,13},{13,9},{2,6},{6,2},{1... | collective-permute-start | bytes 2555912 | tf_op jit(solution)/shard_map/ppermute | solution.py:172
  67.9 30.7 %collective-permute-start.16 = (bf16[256,512]{1,0:T(8,128)(2,1)S(1)}, bf16[256,512]{1,0:T(8,128)(2,1)S(1)}, u32[]{:S(2)}, u32[]{:S(2)}) collective-permute-start(bf16[256,512]{1,0:T(8,128)(2,1)S(1)} %get-tuple-element.95.refs_0_), channel_id=1, source_target_pairs={{0,2},{1,3},{2,0},{3,1},{4,6},{5,7},{6,4},{7,5},{8,10},{9,11},{10,... | collective-permute-start | bytes 786440 | tf_op jit(solution)/shard_map/ppermute | solution.py:168
  77.9 20.7 %collective-permute-start.17 = (bf16[256,512]{1,0:T(8,128)(2,1)S(1)}, bf16[256,512]{1,0:T(8,128)(2,1)S(1)}, u32[]{:S(2)}, u32[]{:S(2)}) collective-permute-start(bf16[256,512]{1,0:T(8,128)(2,1)S(1)} %get-tuple-element.95.refs_0_), channel_id=1, source_target_pairs={{0,3},{1,0},{2,1},{3,2},{4,7},{5,4},{6,5},{7,6},{8,11},{9,8},{10,9... | collective-permute-start | bytes 786440 | tf_op jit(solution)/shard_map/ppermute | solution.py:168
  81.4 33.0 %collective-permute-start.18 = (bf16[64,3328]{1,0:T(8,128)(2,1)S(1)}, bf16[64,3328]{1,0:T(8,128)(2,1)S(1)}, u32[]{:S(2)}, u32[]{:S(2)}) collective-permute-start(bf16[64,3328]{1,0:T(8,128)(2,1)S(1)} %fusion.16.own_x), channel_id=1, source_target_pairs={{0,8},{4,12},{8,0},{12,4},{1,9},{5,13},{9,1},{13,5},{2,10},{6,14},... | collective-permute-start | bytes 1277960 | tf_op jit(solution)/shard_map/ppermute | solution.py:172
  82.9 33.1 %collective-permute-start.19 = (bf16[64,3328]{1,0:T(8,128)(2,1)S(1)}, bf16[64,3328]{1,0:T(8,128)(2,1)S(1)}, u32[]{:S(2)}, u32[]{:S(2)}) collective-permute-start(bf16[64,3328]{1,0:T(8,128)(2,1)S(1)} %fusion.16.own_x), channel_id=1, source_target_pairs={{0,4},{4,0},{8,12},{12,8},{1,5},{5,1},{9,13},{13,9},{2,6},{6,2},{1... | collective-permute-start | bytes 1277960 | tf_op jit(solution)/shard_map/ppermute | solution.py:172
  115.0 39.5 %collective-permute-start.25 = (bf16[2,128,3328]{2,1,0:T(8,128)(2,1)}, bf16[2,128,3328]{2,1,0:T(8,128)(2,1)}, u32[]{:S(2)}, u32[]{:S(2)}) collective-permute-start(bf16[2,128,3328]{2,1,0:T(8,128)(2,1)} %get-tuple-element.93), channel_id=1, source_target_pairs={{0,8},{4,12},{8,0},{12,4},{1,9},{5,13},{9,1},{13,5},{2,10},{6,14},... | collective-permute-start | bytes 5111816 | tf_op jit(solution)/shard_map/ppermute | solution.py:172
  115.5 10.8 %collective-permute-start.21 = (bf16[1,128,3328]{2,1,0:T(8,128)(2,1)S(1)}, bf16[1,128,3328]{2,1,0:T(8,128)(2,1)S(1)}, u32[]{:S(2)}, u32[]{:S(2)}) collective-permute-start(bf16[1,128,3328]{2,1,0:T(8,128)(2,1)S(1)} %get-tuple-element.96), channel_id=1, source_target_pairs={{0,4},{4,0},{8,12},{12,8},{1,5},{5,1},{9,13},{13,9},{2,6},{6,2},{1... | collective-permute-start | bytes 2555912 | tf_op jit(solution)/shard_map/ppermute | solution.py:172
  115.5 11.3 %collective-permute-start.22 = (bf16[1,128,3328]{2,1,0:T(8,128)(2,1)}, bf16[1,128,3328]{2,1,0:T(8,128)(2,1)S(1)}, u32[]{:S(2)}, u32[]{:S(2)}) collective-permute-start(bf16[1,128,3328]{2,1,0:T(8,128)(2,1)} %get-tuple-element.97), channel_id=1, source_target_pairs={{0,4},{4,0},{8,12},{12,8},{1,5},{5,1},{9,13},{13,9},{2,6},{6,2},{1... | collective-permute-start | bytes 2555912 | tf_op jit(solution)/shard_map/ppermute | solution.py:172
  116.0 12.5 %collective-permute-start.23 = (bf16[1,128,3328]{2,1,0:T(8,128)(2,1)}, bf16[1,128,3328]{2,1,0:T(8,128)(2,1)S(1)}, u32[]{:S(2)}, u32[]{:S(2)}) collective-permute-start(bf16[1,128,3328]{2,1,0:T(8,128)(2,1)} %get-tuple-element.98), channel_id=1, source_target_pairs={{0,4},{4,0},{8,12},{12,8},{1,5},{5,1},{9,13},{13,9},{2,6},{6,2},{1... | collective-permute-start | bytes 2555912 | tf_op jit(solution)/shard_map/ppermute | solution.py:172
  117.5 12.9 %collective-permute-start.24 = (bf16[1,128,3328]{2,1,0:T(8,128)(2,1)S(1)}, bf16[1,128,3328]{2,1,0:T(8,128)(2,1)S(1)}, u32[]{:S(2)}, u32[]{:S(2)}) collective-permute-start(bf16[1,128,3328]{2,1,0:T(8,128)(2,1)S(1)} %get-tuple-element.99), channel_id=1, source_target_pairs={{0,4},{4,0},{8,12},{12,8},{1,5},{5,1},{9,13},{13,9},{2,6},{6,2},{1... | collective-permute-start | bytes 2555912 | tf_op jit(solution)/shard_map/ppermute | solution.py:172
  126.3 31.7 %collective-permute-start.26 = (bf16[384,512]{1,0:T(8,128)(2,1)S(1)}, bf16[384,512]{1,0:T(8,128)(2,1)S(1)}, u32[]{:S(2)}, u32[]{:S(2)}) collective-permute-start(bf16[384,512]{1,0:T(8,128)(2,1)S(1)} %slice.145.refs_0_), channel_id=1, source_target_pairs={{0,1},{1,2},{2,3},{3,0},{4,5},{5,6},{6,7},{7,4},{8,9},{9,10},{10,1... | collective-permute-start | bytes 1179656 | tf_op jit(solution)/shard_map/ppermute | solution.py:168
  126.8 31.2 %collective-permute-start.27 = (bf16[384,512]{1,0:T(8,128)(2,1)S(1)}, bf16[384,512]{1,0:T(8,128)(2,1)S(1)}, u32[]{:S(2)}, u32[]{:S(2)}) collective-permute-start(bf16[384,512]{1,0:T(8,128)(2,1)S(1)} %slice.145.refs_0_), channel_id=1, source_target_pairs={{0,2},{1,3},{2,0},{3,1},{4,6},{5,7},{6,4},{7,5},{8,10},{9,11},{10,... | collective-permute-start | bytes 1179656 | tf_op jit(solution)/shard_map/ppermute | solution.py:168
  128.5 29.5 %collective-permute-start.28 = (bf16[384,512]{1,0:T(8,128)(2,1)S(1)}, bf16[384,512]{1,0:T(8,128)(2,1)S(1)}, u32[]{:S(2)}, u32[]{:S(2)}) collective-permute-start(bf16[384,512]{1,0:T(8,128)(2,1)S(1)} %slice.145.refs_0_), channel_id=1, source_target_pairs={{0,3},{1,0},{2,1},{3,2},{4,7},{5,4},{6,5},{7,6},{8,11},{9,8},{10,9... | collective-permute-start | bytes 1179656 | tf_op jit(solution)/shard_map/ppermute | solution.py:168
  130.4 41.8 %collective-permute-start.29 = (bf16[128,1024]{1,0:T(8,128)(2,1)}, bf16[128,1024]{1,0:T(8,128)(2,1)S(1)}, u32[]{:S(2)}, u32[]{:S(2)}) collective-permute-start(bf16[128,1024]{1,0:T(8,128)(2,1)} %get-tuple-element.104), channel_id=1, source_target_pairs={{0,1},{1,0},{2,3},{3,2},{4,5},{5,4},{6,7},{7,6},{8,9},{9,8},{10,11... | collective-permute-start | bytes 786440 | tf_op jit(solution)/shard_map/ppermute | solution.py:228
  154.5 40.1 %collective-permute-start.35 = (bf16[2,128,3328]{2,1,0:T(8,128)(2,1)S(1)}, bf16[2,128,3328]{2,1,0:T(8,128)(2,1)S(1)}, u32[]{:S(2)}, u32[]{:S(2)}) collective-permute-start(bf16[2,128,3328]{2,1,0:T(8,128)(2,1)S(1)} %get-tuple-element.106), channel_id=1, source_target_pairs={{0,8},{4,12},{8,0},{12,4},{1,9},{5,13},{9,1},{13,5},{2,10},{6,14},... | collective-permute-start | bytes 5111816 | tf_op jit(solution)/shard_map/ppermute | solution.py:172
  174.0 37.2 %collective-permute-start.36 = (bf16[128,3328]{1,0:T(8,128)(2,1)}, bf16[128,3328]{1,0:T(8,128)(2,1)}, u32[]{:S(2)}, u32[]{:S(2)}) collective-permute-start(bf16[128,3328]{1,0:T(8,128)(2,1)} %fusion.8.own_x), channel_id=1, source_target_pairs={{0,8},{4,12},{8,0},{12,4},{1,9},{5,13},{9,1},{13,5},{2,10},{6,14},... | collective-permute-start | bytes 2555912 | tf_op jit(solution)/shard_map/ppermute | solution.py:172
  208.8 22.8 %collective-permute-start.39 = (bf16[2,128,3328]{2,1,0:T(8,128)(2,1)S(1)}, bf16[2,128,3328]{2,1,0:T(8,128)(2,1)S(1)}, u32[]{:S(2)}, u32[]{:S(2)}) collective-permute-start(bf16[2,128,3328]{2,1,0:T(8,128)(2,1)S(1)} %partner.9), channel_id=1, source_target_pairs={{0,4},{4,0},{8,12},{12,8},{1,5},{5,1},{9,13},{13,9},{2,6},{6,2},{1... | collective-permute-start | bytes 5111816 | tf_op jit(solution)/shard_map/ppermute | solution.py:172
  211.2 58.0 %collective-permute-start.42 = (bf16[2,128,3328]{2,1,0:T(8,128)(2,1)S(1)}, bf16[2,128,3328]{2,1,0:T(8,128)(2,1)}, u32[]{:S(2)}, u32[]{:S(2)}) collective-permute-start(bf16[2,128,3328]{2,1,0:T(8,128)(2,1)S(1)} %get-tuple-element.117), channel_id=1, source_target_pairs={{0,8},{4,12},{8,0},{12,4},{1,9},{5,13},{9,1},{13,5},{2,10},{6,14},... | collective-permute-start | bytes 5111816 | tf_op jit(solution)/shard_map/ppermute | solution.py:172
  211.7 57.4 %collective-permute-start.43 = (bf16[128,3328]{1,0:T(8,128)(2,1)}, bf16[128,3328]{1,0:T(8,128)(2,1)}, u32[]{:S(2)}, u32[]{:S(2)}) collective-permute-start(bf16[128,3328]{1,0:T(8,128)(2,1)} %fusion.4.own_x), channel_id=1, source_target_pairs={{0,8},{4,12},{8,0},{12,4},{1,9},{5,13},{9,1},{13,5},{2,10},{6,14},... | collective-permute-start | bytes 2555912 | tf_op jit(solution)/shard_map/ppermute | solution.py:172
  227.2 16.8 %collective-permute-start.40 = (bf16[256,1024]{1,0:T(8,128)(2,1)}, bf16[256,1024]{1,0:T(8,128)(2,1)S(1)}, u32[]{:S(2)}, u32[]{:S(2)}) collective-permute-start(bf16[256,1024]{1,0:T(8,128)(2,1)} %get-tuple-element.123), channel_id=1, source_target_pairs={{0,1},{1,0},{2,3},{3,2},{4,5},{5,4},{6,7},{7,6},{8,9},{9,8},{10,11... | collective-permute-start | bytes 1572872 | tf_op jit(solution)/shard_map/ppermute | solution.py:228
  231.6 43.4 %collective-permute-start.44 = (bf16[128,3328]{1,0:T(8,128)(2,1)}, bf16[128,3328]{1,0:T(8,128)(2,1)S(1)}, u32[]{:S(2)}, u32[]{:S(2)}) collective-permute-start(bf16[128,3328]{1,0:T(8,128)(2,1)} %fusion.4.own_x), channel_id=1, source_target_pairs={{0,4},{4,0},{8,12},{12,8},{1,5},{5,1},{9,13},{13,9},{2,6},{6,2},{1... | collective-permute-start | bytes 2555912 | tf_op jit(solution)/shard_map/ppermute | solution.py:172
  271.3 25.7 %collective-permute-start.49 = (bf16[128,3328]{1,0:T(8,128)(2,1)S(1)}, bf16[128,3328]{1,0:T(8,128)(2,1)S(1)}, u32[]{:S(2)}, u32[]{:S(2)}) collective-permute-start(bf16[128,3328]{1,0:T(8,128)(2,1)S(1)} %fusion.own_x), channel_id=1, source_target_pairs={{0,8},{4,12},{8,0},{12,4},{1,9},{5,13},{9,1},{13,5},{2,10},{6,14},... | collective-permute-start | bytes 2555912 | tf_op jit(solution)/shard_map/ppermute | solution.py:172
  271.9 39.1 %collective-permute-start.46 = (bf16[2,64,3328]{2,1,0:T(8,128)(2,1)S(1)}, bf16[2,64,3328]{2,1,0:T(8,128)(2,1)S(1)}, u32[]{:S(2)}, u32[]{:S(2)}) collective-permute-start(bf16[2,64,3328]{2,1,0:T(8,128)(2,1)S(1)} %get-tuple-element.125), channel_id=1, source_target_pairs={{0,8},{4,12},{8,0},{12,4},{1,9},{5,13},{9,1},{13,5},{2,10},{6,14},... | collective-permute-start | bytes 2555912 | tf_op jit(solution)/shard_map/ppermute | solution.py:172
  273.4 56.0 %collective-permute-start.30 = (bf16[128,512]{1,0:T(8,128)(2,1)S(1)}, bf16[128,512]{1,0:T(8,128)(2,1)S(1)}, u32[]{:S(2)}, u32[]{:S(2)}) collective-permute-start(bf16[128,512]{1,0:T(8,128)(2,1)S(1)} %add_convert_fusion.8), channel_id=1, source_target_pairs={{0,2},{1,3},{2,0},{3,1},{4,6},{5,7},{6,4},{7,5},{8,10},{9,11},{10,... | collective-permute-start | bytes 393224 | tf_op jit(solution)/shard_map/ppermute | solution.py:236
  275.0 38.6 %collective-permute-start.50 = (bf16[128,3328]{1,0:T(8,128)(2,1)S(1)}, bf16[128,3328]{1,0:T(8,128)(2,1)S(1)}, u32[]{:S(2)}, u32[]{:S(2)}) collective-permute-start(bf16[128,3328]{1,0:T(8,128)(2,1)S(1)} %fusion.own_x), channel_id=1, source_target_pairs={{0,4},{4,0},{8,12},{12,8},{1,5},{5,1},{9,13},{13,9},{2,6},{6,2},{1... | collective-permute-start | bytes 2555912 | tf_op jit(solution)/shard_map/ppermute | solution.py:172
  275.0 54.4 %collective-permute-start.41 = (bf16[256,512]{1,0:T(8,128)(2,1)S(1)}, bf16[256,512]{1,0:T(8,128)(2,1)S(1)}, u32[]{:S(2)}, u32[]{:S(2)}) collective-permute-start(bf16[256,512]{1,0:T(8,128)(2,1)S(1)} %add_convert_fusion.5), channel_id=1, source_target_pairs={{0,2},{1,3},{2,0},{3,1},{4,6},{5,7},{6,4},{7,5},{8,10},{9,11},{10,... | collective-permute-start | bytes 786440 | tf_op jit(solution)/shard_map/ppermute | solution.py:236
  297.0 15.1 %collective-permute-start.47 = (bf16[256,1024]{1,0:T(8,128)(2,1)}, bf16[256,1024]{1,0:T(8,128)(2,1)S(1)}, u32[]{:S(2)}, u32[]{:S(2)}) collective-permute-start(bf16[256,1024]{1,0:T(8,128)(2,1)} %get-tuple-element.133), channel_id=1, source_target_pairs={{0,1},{1,0},{2,3},{3,2},{4,5},{5,4},{6,7},{7,6},{8,9},{9,8},{10,11... | collective-permute-start | bytes 1572872 | tf_op jit(solution)/shard_map/ppermute | solution.py:228
  312.2 17.5 %collective-permute-start.54 = (bf16[64,3328]{1,0:T(8,128)(2,1)S(1)}, bf16[64,3328]{1,0:T(8,128)(2,1)S(1)}, u32[]{:S(2)}, u32[]{:S(2)}) collective-permute-start(bf16[64,3328]{1,0:T(8,128)(2,1)S(1)} %fusion.12.own_x), channel_id=1, source_target_pairs={{0,8},{4,12},{8,0},{12,4},{1,9},{5,13},{9,1},{13,5},{2,10},{6,14},... | collective-permute-start | bytes 1277960 | tf_op jit(solution)/shard_map/ppermute | solution.py:172
  313.6 16.6 %collective-permute-start.48 = (bf16[256,512]{1,0:T(8,128)(2,1)S(1)}, bf16[256,512]{1,0:T(8,128)(2,1)S(1)}, u32[]{:S(2)}, u32[]{:S(2)}) collective-permute-start(bf16[256,512]{1,0:T(8,128)(2,1)S(1)} %add_convert_fusion.3), channel_id=1, source_target_pairs={{0,2},{1,3},{2,0},{3,1},{4,6},{5,7},{6,4},{7,5},{8,10},{9,11},{10,... | collective-permute-start | bytes 786440 | tf_op jit(solution)/shard_map/ppermute | solution.py:236
  327.6 14.0 %collective-permute-start.52 = (bf16[256,1024]{1,0:T(8,128)(2,1)}, bf16[256,1024]{1,0:T(8,128)(2,1)S(1)}, u32[]{:S(2)}, u32[]{:S(2)}) collective-permute-start(bf16[256,1024]{1,0:T(8,128)(2,1)} %get-tuple-element.139), channel_id=1, source_target_pairs={{0,1},{1,0},{2,3},{3,2},{4,5},{5,4},{6,7},{7,6},{8,9},{9,8},{10,11... | collective-permute-start | bytes 1572872 | tf_op jit(solution)/shard_map/ppermute | solution.py:228
  329.6 14.0 %collective-permute-start.55 = (bf16[64,3328]{1,0:T(8,128)(2,1)S(1)}, bf16[64,3328]{1,0:T(8,128)(2,1)S(1)}, u32[]{:S(2)}, u32[]{:S(2)}) collective-permute-start(bf16[64,3328]{1,0:T(8,128)(2,1)S(1)} %fusion.12.own_x), channel_id=1, source_target_pairs={{0,4},{4,0},{8,12},{12,8},{1,5},{5,1},{9,13},{13,9},{2,6},{6,2},{1... | collective-permute-start | bytes 1277960 | tf_op jit(solution)/shard_map/ppermute | solution.py:172
  329.7 13.9 %collective-permute-start.56 = (bf16[64,3328]{1,0:T(8,128)(2,1)S(1)}, bf16[64,3328]{1,0:T(8,128)(2,1)S(1)}, u32[]{:S(2)}, u32[]{:S(2)}) collective-permute-start(bf16[64,3328]{1,0:T(8,128)(2,1)S(1)} %collective-permute-done.54.other_x), channel_id=1, source_target_pairs={{0,4},{4,0},{8,12},{12,8},{1,5},{5,1},{9,13},{13,9},{2,6},{6,2},{1... | collective-permute-start | bytes 1277960 | tf_op jit(solution)/shard_map/ppermute | solution.py:172
  341.7 14.5 %collective-permute-start.53 = (bf16[256,512]{1,0:T(8,128)(2,1)S(1)}, bf16[256,512]{1,0:T(8,128)(2,1)S(1)}, u32[]{:S(2)}, u32[]{:S(2)}) collective-permute-start(bf16[256,512]{1,0:T(8,128)(2,1)S(1)} %add_convert_fusion.1), channel_id=1, source_target_pairs={{0,2},{1,3},{2,0},{3,1},{4,6},{5,7},{6,4},{7,5},{8,10},{9,11},{10,... | collective-permute-start | bytes 786440 | tf_op jit(solution)/shard_map/ppermute | solution.py:236
  352.1 8.5 %collective-permute-start.57 = (bf16[128,512]{1,0:T(8,128)(2,1)}, bf16[128,512]{1,0:T(8,128)(2,1)S(1)}, u32[]{:S(2)}, u32[]{:S(2)}) collective-permute-start(bf16[128,512]{1,0:T(8,128)(2,1)} %get-tuple-element.144), channel_id=1, source_target_pairs={{0,1},{1,2},{2,3},{3,0},{4,5},{5,6},{6,7},{7,4},{8,9},{9,10},{10,1... | collective-permute-start | bytes 393224 | tf_op jit(solution)/shard_map/ppermute | solution.py:168
  353.8 10.4 %collective-permute-start.58 = (bf16[128,512]{1,0:T(8,128)(2,1)}, bf16[128,512]{1,0:T(8,128)(2,1)S(1)}, u32[]{:S(2)}, u32[]{:S(2)}) collective-permute-start(bf16[128,512]{1,0:T(8,128)(2,1)} %get-tuple-element.145), channel_id=1, source_target_pairs={{0,2},{1,3},{2,0},{3,1},{4,6},{5,7},{6,4},{7,5},{8,10},{9,11},{10,... | collective-permute-start | bytes 393224 | tf_op jit(solution)/shard_map/ppermute | solution.py:168
  354.9 9.3 %collective-permute-start.59 = (bf16[128,512]{1,0:T(8,128)(2,1)}, bf16[128,512]{1,0:T(8,128)(2,1)S(1)}, u32[]{:S(2)}, u32[]{:S(2)}) collective-permute-start(bf16[128,512]{1,0:T(8,128)(2,1)} %get-tuple-element.146), channel_id=1, source_target_pairs={{0,3},{1,0},{2,1},{3,2},{4,7},{5,4},{6,5},{7,6},{8,11},{9,8},{10,9... | collective-permute-start | bytes 393224 | tf_op jit(solution)/shard_map/ppermute | solution.py:168
  (56 other events, 764.3 us)

commit v4 on v3

--- a/solution.py
+++ b/solution.py
@@ -9,8 +9,8 @@
 from jax.sharding import PartitionSpec as P
 
 BF16, F32 = jnp.bfloat16, jnp.float32
-GATE_UP_COST, DOWN_COST = 1, 1
-SPLIT = (0, 1, 2, 3)
+FIRST_COST, GATE_UP_COST, DOWN_COST = 0.2, 0.2, 0.2
+SPLIT = (4, 4, 4, 2, 2)
 VMEM_LIMIT = 29 * 2**20
 PARTNER, OWN, X, BLOCKS = 0, 1, 2, 3
 
@@ -37,10 +37,10 @@
 
 
 def pieces_of(rows, split):
-    half = rows // 2
-    if not split:
+    if split == 1:
         return [(slice(0, 2), slice(0, rows))]
-    return [(slice(w, w + 1), slice(at, at + half)) for w in (0, 1) for at in (0, half)]
+    height = 2 * rows // split
+    return [(slice(w, w + 1), slice(at, at + height)) for w in (0, 1) for at in range(0, rows, height)]
 
 
 def partner_kernel(n_tok, split, place, *refs):
@@ -102,7 +102,7 @@
     return pl.CostEstimate(flops=int(flops * scale), bytes_accessed=int(sum(sizes) * scale), transcendentals=0)
 
 
-def gate_up_call(place, tokens, rows, row_block, weights, n_col, which, split, received=None):
+def gate_up_call(place, tokens, rows, row_block, weights, n_col, which, split, scale, received=None):
     full, wide = weights[0].shape[0], weights[0].shape[1] // 2
     depth, half = full // n_col, rows // 2
     weight = pl.BlockSpec((depth, wide), lambda k, place: (place[BLOCKS + k], place[which]))
@@ -131,7 +131,7 @@
             scratch_shapes=[pltpu.VMEM((n_col, rows, depth), BF16), pltpu.VMEM((2, rows, wide), F32)],
         ),
         compiler_params=params(1),
-        cost_estimate=cost(GATE_UP_COST, 4 * rows * full * wide, 4 * full * wide, 4 * rows * wide),
+        cost_estimate=cost(scale, 4 * rows * full * wide, 4 * full * wide, 4 * rows * wide),
         name=name,
     )(place, *operands)
 
@@ -184,6 +184,7 @@
     table = np.array(
         [
             [[1 - r % 2, r % 2, r // 2] + [(c - s) % n_col for s in range(n_col)] + [0]]
+            + [[1 - r % 2, r % 2, r // 2] + list(range(n_col)) + [0]]
             + [[c ^ 1, c ^ 3, c, c ^ 2] * 2, [(c + 1) % n_col, (c + 2) % n_col, (c + 3) % n_col, c] * 2]
             for r in range(4)
             for c in range(n_col)
@@ -191,22 +192,22 @@
         np.int32,
     )
     mine = jnp.asarray(table)[lax.axis_index("row") * n_col + lax.axis_index("col")]
-    place, halving, straight = mine[0], mine[1], mine[2]
+    by_shift, natural, halving, straight = (mine[k] for k in range(4))
+    place = natural
     last = [place]
 
-    def send_tokens(lo, hi):
-        piece = after(tokens[lo * eighth : hi * eighth], *last)
-        return [piece] + [shifted(piece, n_col, s) for s in range(1, n_col)]
+    def scale(i):
+        return FIRST_COST if i == 0 else GATE_UP_COST
 
     def partner(i):
-        tok, rows, block = sources[i]
-        out = gate_up_call(after(place, *last), tok, rows, block, weights, n_col, PARTNER, i in SPLIT)
+        where, tok, rows, block = sources[i]
+        out = gate_up_call(after(where, *last), tok, rows, block, weights, n_col, PARTNER, SPLIT[i], scale(i))
         last[:] = list(out)
         return [swapped(piece, 1) for piece in out]
 
     def own(i, received):
-        tok, rows, block = sources[i]
-        send, keep = gate_up_call(after(place, *last), tok, rows, block, weights, n_col, OWN, i in SPLIT, received)
+        where, tok, rows, block = sources[i]
+        send, keep = gate_up_call(after(where, *last), tok, rows, block, weights, n_col, OWN, SPLIT[i], scale(i), received)
         last[:] = [send]
         return keep, swapped(send, 2)
 
@@ -237,49 +238,60 @@
 
     def down_direct(pieces):
         out = down_call(after(place, *last), straight, pieces, down_weight, n_col, True)
+        last[:] = out
         total = out[-1].astype(F32)
         for s in range(1, n_col):
             total = total + shifted(out[s - 1], n_col, s).astype(F32)
         return total.astype(BF16)
 
     def finish(pair):
-        return (pair[0] + pair[1].astype(F32)).astype(BF16)
-
-    t0, t1 = send_tokens(0, 1), send_tokens(1, 3)
-    sources = [(t0, eighth, 0), (t1, 2 * eighth, 0)]
+        out = (after(pair[0], *last) + pair[1].astype(F32)).astype(BF16)
+        last[:] = [out]
+        return out
+
+    first = [tokens[: 2 * eighth]]
+    first += [shifted(first[0], n_col, s) for s in range(1, n_col)]
+    rest = [lax.all_gather(tokens[2 * eighth :], "col", axis=1, tiled=True)]
+    sources = [
+        (by_shift, first, 2 * eighth, 0),
+        (natural, rest, 2 * eighth, 0),
+        (natural, rest, 2 * eighth, 1),
+        (natural, rest, eighth, 4),
+        (natural, rest, eighth, 5),
+    ]
     r0 = partner(0)
-    t2 = send_tokens(3, 5)
     p0 = own(0, r0)
     r1 = partner(1)
     h0 = gated(p0)
     p1 = own(1, r1)
-    t3 = send_tokens(5, 8)
-    sources += [(t2, 2 * eighth, 0), (t3, 2 * eighth, 0), (t3, eighth, 2)]
-    r2 = partner(2)
     h0 = relay(h0)
     d0 = down(h0)
+    r2 = partner(2)
+    z0 = halve(d0)
+    h1 = gated(p1)
     p2 = own(2, r2)
-    h1 = gated(p1)
+    h1 = relay(h1)
+    d1 = down(h1)
     r3 = partner(3)
-    z0 = halve(d0)
+    o0 = finish(z0)
+    r4 = partner(4)
+    z1 = halve(d1)
+    h2 = gated(p2)
     p3 = own(3, r3)
-    h1 = relay(h1)
-    h2 = gated(p2)
-    r4 = partner(4)
-    d1 = down(h1)
     p4 = own(4, r4)
-    z1 = halve(d1)
+    o1 = finish(z1)
     h2 = relay(h2)
+    d2 = down(h2)
     h3 = gated(p3)
-    d2 = down(h2)
+    h4 = gated(p4)
     h3 = relay(h3)
-    h4 = gated(p4)
     z2 = halve(d2)
     d3 = down(h3)
     h4 = relay(h4)
+    o4 = down_direct(h4)
+    o2 = finish(z2)
     z3 = halve(d3)
-    o4 = down_direct(h4)
-    return jnp.concatenate([finish(z0), finish(z1), finish(z2), finish(z3), o4], axis=0)
+    return jnp.concatenate([o0, o1, o2, finish(z3), o4], axis=0)
 
 
 def generic(tokens, gate_weight, up_weight, down_weight):

time: 373 us -> 421 us (1.13)
  the two profiles are of different devices: /device:TPU:0 before, /device:TPU:13 now
where the time goes in v4:
time: 421 us; the launch traced here: 413 us
  Pallas kernels  184 us (44%)
  waiting for transfers between devices  120 us (29%)
  starting transfers between devices  50.7 us (12%)
  local copies, waits for them, and re-layouts  29.2 us (7%)
  other arithmetic  14.9 us (4%)
  between operations  14.3 us (3%)
    pallas_call x10, Pallas kernels, gate_up_call(): pl.pallas_call(functools.partial(body, len(tokens), split), out_shape=out...  133 us
    ppermute x36, waiting for transfers between devices, swapped(): return lax.ppermute(x, 'row', [(i, i ^ mask) for i in range(4)])  61.1 us
    ppermute x6, waiting for transfers between devices, shifted(): return lax.ppermute(x, 'col', [(i, (i + shift) % n) for i in range(n)])  52.3 us
    pallas_call x5, Pallas kernels, down_call(): pl.pallas_call(functools.partial(down_kernel, n_col, direct), out_shape=o...  51.1 us
    ppermute x36, starting transfers between devices, swapped(): return lax.ppermute(x, 'row', [(i, i ^ mask) for i in range(4)])  34 us
    unnamed x82, local copies, waits for them, and re-layouts  24.9 us
  transfers between devices with their start and end apart: 51, of which 25 were waited for; matrix products, arithmetic and copies ran while one was open for 4% of the time, Pallas kernels for 45%

profile of v4, /device:TPU:13, one launch (start us, length us, event | category | flops | bytes accessed | tf_op | source)
XLA Modules:
  0.0 412.9 jit_solution(8036561255636845381)
XLA Ops:
  6.5 2.1 slice.133
  9.8 2.3 collective-permute-start.1
  12.1 2.2 collective-permute-start
  16.8 19.5 %collective-permute-done.1.refs_2_ = bf16[256,512]{1,0:T(8,128)(2,1)S(1)} collective-permute-done((bf16[256,512]{1,0:T(8,128)(2,1)S(1)}, bf16[256,512]{1,0:T(8,128)(2,1)S(1)}, u32[]{:S(2)}, u32[]{:S(2)}) %collective-permute-start.1) | collective-permute-done | bytes 262176 | tf_op jit(solution)/shard_map/ppermute | solution.py:168
  36.3 19.6 %collective-permute-done.refs_1_ = bf16[256,512]{1,0:T(8,128)(2,1)S(1)} collective-permute-done((bf16[256,512]{1,0:T(8,128)(2,1)S(1)}, bf16[256,512]{1,0:T(8,128)(2,1)S(1)}, u32[]{:S(2)}, u32[]{:S(2)}) %collective-permute-start) | collective-permute-done | bytes 262176 | tf_op jit(solution)/shard_map/ppermute | solution.py:168
  55.9 13.6 %partner.5 = (bf16[1,128,3328]{2,1,0:T(8,128)(2,1)S(1)}, bf16[1,128,3328]{2,1,0:T(8,128)(2,1)S(1)}, bf16[1,128,3328]{2,1,0:T(8,128)(2,1)S(1)}, bf16[1,128,3328]{2,1,0:T(8,128)(2,1)S(1)}) custom-call(s32[8]{0:T(128)S(1)} %get-tuple-element.81.place, bf16[256,512]{1,0:T(8,128)(2,1)S(1)} %slice.132.refs_0_, bf16[256,512]{1,0:T(8,128)(2,1)S(1)} %collective-permute-done.refs_1_, ...), custom_call_target="tpu_custom_call" | custom-call | flops 1395864320 | bytes 6134169 | tf_op jit(solution)/shard_map/partner/pallas_call | solution.py:123
  69.5 7.7 %collective-permute-start.3 = (bf16[1,128,3328]{2,1,0:T(8,128)(2,1)S(1)}, bf16[1,128,3328]{2,1,0:T(8,128)(2,1)S(1)}, u32[]{:S(2)}, u32[]{:S(2)}) collective-permute-start(bf16[1,128,3328]{2,1,0:T(8,128)(2,1)S(1)} %get-tuple-element.77), channel_id=1, source_target_pairs={{0,4},{4,0},{8,12},{12,8},{1,5},{5,1},{9,13},{13,9},{2,6},{6,2},{1... | collective-permute-start | bytes 2555912 | tf_op jit(solution)/shard_map/ppermute | solution.py:172
  77.8 1.4 collective-permute-done.3.refs_6_
  82.8 15.6 %own.5 = (bf16[2,128,3328]{2,1,0:T(8,128)(2,1)}, bf16[2,128,3328]{2,1,0:T(8,128)(2,1)S(1)}) custom-call(s32[8]{0:T(128)S(1)} %get-tuple-element.81.place, bf16[256,512]{1,0:T(8,128)(2,1)S(1)} %slice.132.refs_0_, bf16[256,512]{1,0:T(8,128)(2,1)S(1)} %collective-permute-done.refs_1_, bf16[256,512]{1,0:T(8,128)(2,1)S(1)} %collective-permute-done.1.refs_2_, ...), custom_call_target="tpu_custom_call" | custom-call | flops 1395864320 | bytes 6134169 | tf_op jit(solution)/shard_map/own/pallas_call | solution.py:123
  99.7 1.9 copy-done.2
  101.5 13.5 %partner.6 = (bf16[1,128,3328]{2,1,0:T(8,128)(2,1)S(1)}, bf16[1,128,3328]{2,1,0:T(8,128)(2,1)S(1)}, bf16[1,128,3328]{2,1,0:T(8,128)(2,1)S(1)}, bf16[1,128,3328]{2,1,0:T(8,128)(2,1)S(1)}) custom-call(s32[8]{0:T(128)S(1)} %get-tuple-element.137.place, bf16[768,2048]{1,0:T(8,128)(2,1)S(1)} %copy-done.2, bf16[2048,6656]{1,0:T(8,128)(2,1)} %refs_1_.15, ...), custom_call_target="tpu_custom_call" | custom-call | flops 1395864320 | bytes 6134169 | tf_op jit(solution)/shard_map/partner/pallas_call | solution.py:123
  116.4 20.8 %collective-permute-done.7 = bf16[2,128,3328]{2,1,0:T(8,128)(2,1)} collective-permute-done((bf16[2,128,3328]{2,1,0:T(8,128)(2,1)}, bf16[2,128,3328]{2,1,0:T(8,128)(2,1)}, u32[]{:S(2)}, u32[]{:S(2)}) %collective-permute-start.7) | collective-permute-done | bytes 1703968 | tf_op jit(solution)/shard_map/ppermute | solution.py:172
  137.2 2.1 fusion.8.own_x
  140.5 1.5 collective-permute-start.13
  142.1 14.6 %own.6 = (bf16[2,128,3328]{2,1,0:T(8,128)(2,1)S(1)}, bf16[2,128,3328]{2,1,0:T(8,128)(2,1)S(1)}) custom-call(s32[8]{0:T(128)S(1)} %get-tuple-element.137.place, bf16[768,2048]{1,0:T(8,128)(2,1)S(1)} %copy-done.2, bf16[2048,6656]{1,0:T(8,128)(2,1)} %refs_1_.15, bf16[2048,6656]{1,0:T(8,128)(2,1)} %refs_2_.15, ...), custom_call_target="tpu_custom_call" | custom-call | flops 1395864320 | bytes 6134169 | tf_op jit(solution)/shard_map/own/pallas_call | solution.py:123
  156.7 1.9 collective-permute-done.12.other_x
  158.6 2.1 collective-permute-start.14
  163.8 8.8 %copy-done = bf16[6656,2048]{1,0:T(8,128)(2,1)S(1)} copy-done((bf16[6656,2048]{1,0:T(8,128)(2,1)S(1)}, bf16[6656,2048]{1,0:T(8,128)(2,1)}, u32[]{:S(2)}) %copy-start) | copy-done | bytes 27263000
  172.6 12.1 %down.5 = (bf16[256,1024]{1,0:T(8,128)(2,1)}, bf16[256,1024]{1,0:T(8,128)(2,1)}) custom-call(s32[8]{0:T(128)} %copy-done.5, s32[8]{0:T(128)} %get-tuple-element.162.order, bf16[128,3328]{1,0:T(8,128)(2,1)} %copy-done.9, bf16[128,3328]{1,0:T(8,128)(2,1)} %copy-done.14, bf16[128,3328]{1,0:T(8,128)(2,1)} %copy-done.16, bf16[128,3328]{1,0:T(8,128)(2,1)} %copy-done.18, ...), custom_call_target="tpu_custom_call" | custom-call | flops 1395864320 | bytes 681574 | tf_op jit(solution)/shard_map/down/pallas_call | solution.py:151
  184.7 13.5 %partner.7 = (bf16[1,128,3328]{2,1,0:T(8,128)(2,1)S(1)}, bf16[1,128,3328]{2,1,0:T(8,128)(2,1)S(1)}, bf16[1,128,3328]{2,1,0:T(8,128)(2,1)S(1)}, bf16[1,128,3328]{2,1,0:T(8,128)(2,1)S(1)}) custom-call(s32[8]{0:T(128)S(1)} %copy-done.6, bf16[768,2048]{1,0:T(8,128)(2,1)S(1)} %copy-done.3, bf16[2048,6656]{1,0:T(8,128)(2,1)} %refs_1_.15, bf16[2048,6656]{1,0:T(8,128)(2,1)} %refs_2_.15), custom_call_target="tpu_custom_call" | custom-call | flops 1395864320 | bytes 6134169 | tf_op jit(solution)/shard_map/partner/pallas_call | solution.py:123
  199.6 2.1 fusion.4.own_x
  204.3 14.6 %own.7 = (bf16[2,128,3328]{2,1,0:T(8,128)(2,1)S(1)}, bf16[2,128,3328]{2,1,0:T(8,128)(2,1)S(1)}) custom-call(s32[8]{0:T(128)S(1)} %copy-done.6, bf16[768,2048]{1,0:T(8,128)(2,1)S(1)} %copy-done.3, bf16[2048,6656]{1,0:T(8,128)(2,1)} %refs_1_.15, bf16[2048,6656]{1,0:T(8,128)(2,1)} %refs_2_.15, bf16[1,128,3328]{2,1,0:T(8,128)(2,1)S(1)} %collective-permute-done.17.refs_3_, ...), custom_call_target="tpu_custom_call" | custom-call | flops 1395864320 | bytes 6134169 | tf_op jit(solution)/shard_map/own/pallas_call | solution.py:123
  218.9 2.6 collective-permute-done.21.other_x
  221.5 1.7 collective-permute-start.23
  224.4 3.2 collective-permute-start.24
  228.6 8.8 %copy-done.1 = bf16[6656,2048]{1,0:T(8,128)(2,1)S(1)} copy-done((bf16[6656,2048]{1,0:T(8,128)(2,1)S(1)}, bf16[6656,2048]{1,0:T(8,128)(2,1)}, u32[]{:S(2)}) %copy-start.1) | copy-done | bytes 27263000
  237.3 11.8 %down.6 = (bf16[256,1024]{1,0:T(8,128)(2,1)}, bf16[256,1024]{1,0:T(8,128)(2,1)}) custom-call(s32[8]{0:T(128)} %copy-done.5, s32[8]{0:T(128)} %get-tuple-element.162.order, bf16[128,3328]{1,0:T(8,128)(2,1)} %copy-done.8, bf16[128,3328]{1,0:T(8,128)(2,1)} %copy-done.13, bf16[128,3328]{1,0:T(8,128)(2,1)} %copy-done.15, ...), custom_call_target="tpu_custom_call" | custom-call | flops 1395864320 | bytes 681574 | tf_op jit(solution)/shard_map/down/pallas_call | solution.py:151
  249.4 11.3 %partner.8 = (bf16[1,128,3328]{2,1,0:T(8,128)(2,1)S(1)}, bf16[1,128,3328]{2,1,0:T(8,128)(2,1)S(1)}) custom-call(s32[8]{0:T(128)S(1)} %copy-done.7, bf16[768,2048]{1,0:T(8,128)(2,1)S(1)} %copy-done.3, bf16[2048,6656]{1,0:T(8,128)(2,1)} %refs_1_.15, bf16[2048,6656]{1,0:T(8,128)(2,1)} %refs_2_.15), custom_call_target="tpu_custom_call" | custom-call | flops 697932160 | bytes 5793382 | tf_op jit(solution)/shard_map/partner/pallas_call | solution.py:123
  262.5 11.3 %partner.9 = (bf16[1,128,3328]{2,1,0:T(8,128)(2,1)S(1)}, bf16[1,128,3328]{2,1,0:T(8,128)(2,1)S(1)}) custom-call(s32[8]{0:T(128)S(1)} %copy-done.7, bf16[768,2048]{1,0:T(8,128)(2,1)S(1)} %copy-done.3, bf16[2048,6656]{1,0:T(8,128)(2,1)} %refs_1_.15, bf16[2048,6656]{1,0:T(8,128)(2,1)} %refs_2_.15), custom_call_target="tpu_custom_call" | custom-call | flops 697932160 | bytes 5793382 | tf_op jit(solution)/shard_map/partner/pallas_call | solution.py:123
  275.4 3.0 fusion.own_x
  280.3 12.0 %own.8 = (bf16[2,64,3328]{2,1,0:T(8,128)(2,1)S(1)}, bf16[2,64,3328]{2,1,0:T(8,128)(2,1)S(1)}) custom-call(s32[8]{0:T(128)S(1)} %copy-done.7, bf16[768,2048]{1,0:T(8,128)(2,1)S(1)} %copy-done.3, bf16[2048,6656]{1,0:T(8,128)(2,1)} %refs_1_.15, bf16[2048,6656]{1,0:T(8,128)(2,1)} %refs_2_.15, bf16[1,128,3328]{2,1,0:T(8,128)(2,1)S(1)} %collective-permute-done.27.refs_3_, ...), custom_call_target="tpu_custom_call" | custom-call | flops 697932160 | bytes 5793382 | tf_op jit(solution)/shard_map/own/pallas_call | solution.py:123
  292.4 13.2 %own.9 = (bf16[2,64,3328]{2,1,0:T(8,128)(2,1)S(1)}, bf16[2,64,3328]{2,1,0:T(8,128)(2,1)S(1)}) custom-call(s32[8]{0:T(128)S(1)} %copy-done.7, bf16[768,2048]{1,0:T(8,128)(2,1)S(1)} %copy-done.4, bf16[2048,6656]{1,0:T(8,128)(2,1)} %refs_1_.15, bf16[2048,6656]{1,0:T(8,128)(2,1)} %refs_2_.15, bf16[1,128,3328]{2,1,0:T(8,128)(2,1)S(1)} %collective-permute-done.29.refs_3_, ...), custom_call_target="tpu_custom_call" | custom-call | flops 697932160 | bytes 5793382 | tf_op jit(solution)/shard_map/own/pallas_call | solution.py:123
  305.6 2.6 constant_dynamic-update-slice_fusion.1
  311.8 11.9 %down.7 = (bf16[256,1024]{1,0:T(8,128)(2,1)}, bf16[256,1024]{1,0:T(8,128)(2,1)}) custom-call(s32[8]{0:T(128)} %copy-done.5, s32[8]{0:T(128)} %get-tuple-element.162.order, bf16[128,3328]{1,0:T(8,128)(2,1)} %fusion.own_x, bf16[128,3328]{1,0:T(8,128)(2,1)} %collective-permute-done.32.other_x, bf16[128,3328]{1,0:T(8,128)(2,1)} %collective-permute-done.33.own_x_core, ...), custom_call_target="tpu_custom_call" | custom-call | flops 1395864320 | bytes 681574 | tf_op jit(solution)/shard_map/down/pallas_call | solution.py:151
  323.7 4.6 %collective-permute-done.35 = bf16[2,64,3328]{2,1,0:T(8,128)(2,1)S(1)} collective-permute-done((bf16[2,64,3328]{2,1,0:T(8,128)(2,1)S(1)}, bf16[2,64,3328]{2,1,0:T(8,128)(2,1)S(1)}, u32[]{:S(2)}, u32[]{:S(2)}) %collective-permute-start.35) | collective-permute-done | bytes 852000 | tf_op jit(solution)/shard_map/ppermute | solution.py:172
  328.6 2.4 collective-permute-start.39
  332.6 13.9 %collective-permute-done.36 = bf16[2,64,3328]{2,1,0:T(8,128)(2,1)S(1)} collective-permute-done((bf16[2,64,3328]{2,1,0:T(8,128)(2,1)S(1)}, bf16[2,64,3328]{2,1,0:T(8,128)(2,1)S(1)}, u32[]{:S(2)}, u32[]{:S(2)}) %collective-permute-start.36) | collective-permute-done | bytes 852000 | tf_op jit(solution)/shard_map/ppermute | solution.py:172
  346.9 8.8 %collective-permute-done.38.other_x = bf16[64,3328]{1,0:T(8,128)(2,1)S(1)} collective-permute-done((bf16[64,3328]{1,0:T(8,128)(2,1)S(1)}, bf16[64,3328]{1,0:T(8,128)(2,1)S(1)}, u32[]{:S(2)}, u32[]{:S(2)}) %collective-permute-start.38) | collective-permute-done | bytes 426016 | tf_op jit(solution)/shard_map/ppermute | solution.py:172
  355.7 1.3 collective-permute-start.40
  359.8 7.6 %down.8 = (bf16[128,1024]{1,0:T(8,128)(2,1)}, bf16[128,1024]{1,0:T(8,128)(2,1)}) custom-call(s32[8]{0:T(128)} %copy-done.5, s32[8]{0:T(128)} %get-tuple-element.162.order, bf16[64,3328]{1,0:T(8,128)(2,1)} %copy-done.12, bf16[64,3328]{1,0:T(8,128)(2,1)} %copy-done.25, bf16[64,3328]{1,0:T(8,128)(2,1)} %copy-done.24, bf16[64,3328]{1,0:T(8,128)(2,1)} %copy-done.26, ...), custom_call_target="tpu_custom_call" | custom-call | flops 697932160 | bytes 340787 | tf_op jit(solution)/shard_map/down/pallas_call | solution.py:151
  369.2 1.7 collective-permute-start.44
  373.2 7.7 %down.9 = (bf16[128,512]{1,0:T(8,128)(2,1)}, bf16[128,512]{1,0:T(8,128)(2,1)}, bf16[128,512]{1,0:T(8,128)(2,1)}, bf16[128,512]{1,0:T(8,128)(2,1)}) custom-call(s32[8]{0:T(128)} %copy-done.5, s32[8]{0:T(128)} %get-tuple-element.161.order, bf16[64,3328]{1,0:T(8,128)(2,1)} %copy-done.11, bf16[64,3328]{1,0:T(8,128)(2,1)} %copy-done.22, ...), custom_call_target="tpu_custom_call" | custom-call | flops 697932160 | bytes 340787 | tf_op jit(solution)/shard_map/down/pallas_call | solution.py:151
  380.9 1.4 collective-permute-done.44
  384.5 1.9 collective-permute-start.46
  388.6 3.7 collective-permute-done.46
  393.0 7.4 %collective-permute-done.47 = bf16[128,512]{1,0:T(8,128)(2,1)S(1)} collective-permute-done((bf16[128,512]{1,0:T(8,128)(2,1)S(1)}, bf16[128,512]{1,0:T(8,128)(2,1)S(1)}, u32[]{:S(2)}, u32[]{:S(2)}) %collective-permute-start.47) | collective-permute-done | bytes 131104 | tf_op jit(solution)/shard_map/ppermute | solution.py:168
  400.4 2.8 collective-permute-done.48
  403.2 1.7 collective-permute-done.49
  (171 shorter events, 45.2 us)
Async XLA Ops:
  6.5 93.1 %all-gather.2.cloned.1.call-start = ((), (), s32[]{:S(2)}) async-start(), calls=%async_computation | async-start | bytes 3932160 | tf_op jit(solution)/shard_map/all_gather | solution.py:254
  9.6 7.2 %collective-permute-start.2 = (bf16[256,512]{1,0:T(8,128)(2,1)S(1)}, bf16[256,512]{1,0:T(8,128)(2,1)S(1)}, u32[]{:S(2)}, u32[]{:S(2)}) collective-permute-start(bf16[256,512]{1,0:T(8,128)(2,1)S(1)} %slice.132.refs_0_), channel_id=1, source_target_pairs={{0,3},{1,0},{2,1},{3,2},{4,7},{5,4},{6,5},{7,6},{8,11},{9,8},{10,9... | collective-permute-start | bytes 786440 | tf_op jit(solution)/shard_map/ppermute | solution.py:168
  9.8 26.5 %collective-permute-start.1 = (bf16[256,512]{1,0:T(8,128)(2,1)S(1)}, bf16[256,512]{1,0:T(8,128)(2,1)S(1)}, u32[]{:S(2)}, u32[]{:S(2)}) collective-permute-start(bf16[256,512]{1,0:T(8,128)(2,1)S(1)} %slice.132.refs_0_), channel_id=1, source_target_pairs={{0,2},{1,3},{2,0},{3,1},{4,6},{5,7},{6,4},{7,5},{8,10},{9,11},{10,... | collective-permute-start | bytes 786440 | tf_op jit(solution)/shard_map/ppermute | solution.py:168
  12.1 43.8 %collective-permute-start = (bf16[256,512]{1,0:T(8,128)(2,1)S(1)}, bf16[256,512]{1,0:T(8,128)(2,1)S(1)}, u32[]{:S(2)}, u32[]{:S(2)}) collective-permute-start(bf16[256,512]{1,0:T(8,128)(2,1)S(1)} %slice.132.refs_0_), channel_id=1, source_target_pairs={{0,1},{1,2},{2,3},{3,0},{4,5},{5,6},{6,7},{7,4},{8,9},{9,10},{10,1... | collective-permute-start | bytes 786440 | tf_op jit(solution)/shard_map/ppermute | solution.py:168
  69.5 9.7 %collective-permute-start.3 = (bf16[1,128,3328]{2,1,0:T(8,128)(2,1)S(1)}, bf16[1,128,3328]{2,1,0:T(8,128)(2,1)S(1)}, u32[]{:S(2)}, u32[]{:S(2)}) collective-permute-start(bf16[1,128,3328]{2,1,0:T(8,128)(2,1)S(1)} %get-tuple-element.77), channel_id=1, source_target_pairs={{0,4},{4,0},{8,12},{12,8},{1,5},{5,1},{9,13},{13,9},{2,6},{6,2},{1... | collective-permute-start | bytes 2555912 | tf_op jit(solution)/shard_map/ppermute | solution.py:172
  77.3 4.4 %collective-permute-start.5 = (bf16[1,128,3328]{2,1,0:T(8,128)(2,1)S(1)}, bf16[1,128,3328]{2,1,0:T(8,128)(2,1)S(1)}, u32[]{:S(2)}, u32[]{:S(2)}) collective-permute-start(bf16[1,128,3328]{2,1,0:T(8,128)(2,1)S(1)} %get-tuple-element.79), channel_id=1, source_target_pairs={{0,4},{4,0},{8,12},{12,8},{1,5},{5,1},{9,13},{13,9},{2,6},{6,2},{1... | collective-permute-start | bytes 2555912 | tf_op jit(solution)/shard_map/ppermute | solution.py:172
  77.7 5.2 %collective-permute-start.6 = (bf16[1,128,3328]{2,1,0:T(8,128)(2,1)S(1)}, bf16[1,128,3328]{2,1,0:T(8,128)(2,1)S(1)}, u32[]{:S(2)}, u32[]{:S(2)}) collective-permute-start(bf16[1,128,3328]{2,1,0:T(8,128)(2,1)S(1)} %get-tuple-element.80), channel_id=1, source_target_pairs={{0,4},{4,0},{8,12},{12,8},{1,5},{5,1},{9,13},{13,9},{2,6},{6,2},{1... | collective-permute-start | bytes 2555912 | tf_op jit(solution)/shard_map/ppermute | solution.py:172
  98.4 38.7 %collective-permute-start.7 = (bf16[2,128,3328]{2,1,0:T(8,128)(2,1)}, bf16[2,128,3328]{2,1,0:T(8,128)(2,1)}, u32[]{:S(2)}, u32[]{:S(2)}) collective-permute-start(bf16[2,128,3328]{2,1,0:T(8,128)(2,1)} %get-tuple-element.83), channel_id=1, source_target_pairs={{0,8},{4,12},{8,0},{12,4},{1,9},{5,13},{9,1},{13,5},{2,10},{6,14},... | collective-permute-start | bytes 5111816 | tf_op jit(solution)/shard_map/ppermute | solution.py:172
  115.0 25.5 %collective-permute-start.8 = (bf16[1,128,3328]{2,1,0:T(8,128)(2,1)S(1)}, bf16[1,128,3328]{2,1,0:T(8,128)(2,1)S(1)}, u32[]{:S(2)}, u32[]{:S(2)}) collective-permute-start(bf16[1,128,3328]{2,1,0:T(8,128)(2,1)S(1)} %get-tuple-element.85), channel_id=1, source_target_pairs={{0,4},{4,0},{8,12},{12,8},{1,5},{5,1},{9,13},{13,9},{2,6},{6,2},{1... | collective-permute-start | bytes 2555912 | tf_op jit(solution)/shard_map/ppermute | solution.py:172
  115.8 26.3 %collective-permute-start.9 = (bf16[1,128,3328]{2,1,0:T(8,128)(2,1)S(1)}, bf16[1,128,3328]{2,1,0:T(8,128)(2,1)S(1)}, u32[]{:S(2)}, u32[]{:S(2)}) collective-permute-start(bf16[1,128,3328]{2,1,0:T(8,128)(2,1)S(1)} %get-tuple-element.86), channel_id=1, source_target_pairs={{0,4},{4,0},{8,12},{12,8},{1,5},{5,1},{9,13},{13,9},{2,6},{6,2},{1... | collective-permute-start | bytes 2555912 | tf_op jit(solution)/shard_map/ppermute | solution.py:172
  115.8 26.2 %collective-permute-start.10 = (bf16[1,128,3328]{2,1,0:T(8,128)(2,1)S(1)}, bf16[1,128,3328]{2,1,0:T(8,128)(2,1)S(1)}, u32[]{:S(2)}, u32[]{:S(2)}) collective-permute-start(bf16[1,128,3328]{2,1,0:T(8,128)(2,1)S(1)} %get-tuple-element.87), channel_id=1, source_target_pairs={{0,4},{4,0},{8,12},{12,8},{1,5},{5,1},{9,13},{13,9},{2,6},{6,2},{1... | collective-permute-start | bytes 2555912 | tf_op jit(solution)/shard_map/ppermute | solution.py:172
  116.3 25.8 %collective-permute-start.11 = (bf16[1,128,3328]{2,1,0:T(8,128)(2,1)S(1)}, bf16[1,128,3328]{2,1,0:T(8,128)(2,1)S(1)}, u32[]{:S(2)}, u32[]{:S(2)}) collective-permute-start(bf16[1,128,3328]{2,1,0:T(8,128)(2,1)S(1)} %get-tuple-element.88), channel_id=1, source_target_pairs={{0,4},{4,0},{8,12},{12,8},{1,5},{5,1},{9,13},{13,9},{2,6},{6,2},{1... | collective-permute-start | bytes 2555912 | tf_op jit(solution)/shard_map/ppermute | solution.py:172
  139.3 19.3 %collective-permute-start.12 = (bf16[128,3328]{1,0:T(8,128)(2,1)S(1)}, bf16[128,3328]{1,0:T(8,128)(2,1)S(1)}, u32[]{:S(2)}, u32[]{:S(2)}) collective-permute-start(bf16[128,3328]{1,0:T(8,128)(2,1)S(1)} %fusion.8.own_x), channel_id=1, source_target_pairs={{0,8},{4,12},{8,0},{12,4},{1,9},{5,13},{9,1},{13,5},{2,10},{6,14},... | collective-permute-start | bytes 2555912 | tf_op jit(solution)/shard_map/ppermute | solution.py:172
  140.5 21.4 %collective-permute-start.13 = (bf16[128,3328]{1,0:T(8,128)(2,1)S(1)}, bf16[128,3328]{1,0:T(8,128)(2,1)S(1)}, u32[]{:S(2)}, u32[]{:S(2)}) collective-permute-start(bf16[128,3328]{1,0:T(8,128)(2,1)S(1)} %fusion.8.own_x), channel_id=1, source_target_pairs={{0,4},{4,0},{8,12},{12,8},{1,5},{5,1},{9,13},{13,9},{2,6},{6,2},{1... | collective-permute-start | bytes 2555912 | tf_op jit(solution)/shard_map/ppermute | solution.py:172
  158.6 4.1 %collective-permute-start.14 = (bf16[128,3328]{1,0:T(8,128)(2,1)S(1)}, bf16[128,3328]{1,0:T(8,128)(2,1)S(1)}, u32[]{:S(2)}, u32[]{:S(2)}) collective-permute-start(bf16[128,3328]{1,0:T(8,128)(2,1)S(1)} %collective-permute-done.12.other_x), channel_id=1, source_target_pairs={{0,4},{4,0},{8,12},{12,8},{1,5},{5,1},{9,13},{13,9},{2,6},{6,2},{1... | collective-permute-start | bytes 2555912 | tf_op jit(solution)/shard_map/ppermute | solution.py:172
  160.7 38.9 %collective-permute-start.16 = (bf16[2,128,3328]{2,1,0:T(8,128)(2,1)S(1)}, bf16[2,128,3328]{2,1,0:T(8,128)(2,1)}, u32[]{:S(2)}, u32[]{:S(2)}) collective-permute-start(bf16[2,128,3328]{2,1,0:T(8,128)(2,1)S(1)} %get-tuple-element.91), channel_id=1, source_target_pairs={{0,8},{4,12},{8,0},{12,4},{1,9},{5,13},{9,1},{13,5},{2,10},{6,14},... | collective-permute-start | bytes 5111816 | tf_op jit(solution)/shard_map/ppermute | solution.py:172
  184.7 14.4 %collective-permute-start.15 = (bf16[256,1024]{1,0:T(8,128)(2,1)}, bf16[256,1024]{1,0:T(8,128)(2,1)S(1)}, u32[]{:S(2)}, u32[]{:S(2)}) collective-permute-start(bf16[256,1024]{1,0:T(8,128)(2,1)} %get-tuple-element.95), channel_id=1, source_target_pairs={{0,1},{1,0},{2,3},{3,2},{4,5},{5,4},{6,7},{7,6},{8,9},{9,8},{10,11... | collective-permute-start | bytes 1572872 | tf_op jit(solution)/shard_map/ppermute | solution.py:229
  198.2 4.9 %collective-permute-start.17 = (bf16[1,128,3328]{2,1,0:T(8,128)(2,1)S(1)}, bf16[1,128,3328]{2,1,0:T(8,128)(2,1)S(1)}, u32[]{:S(2)}, u32[]{:S(2)}) collective-permute-start(bf16[1,128,3328]{2,1,0:T(8,128)(2,1)S(1)} %get-tuple-element.97), channel_id=1, source_target_pairs={{0,4},{4,0},{8,12},{12,8},{1,5},{5,1},{9,13},{13,9},{2,6},{6,2},{1... | collective-permute-start | bytes 2555912 | tf_op jit(solution)/shard_map/ppermute | solution.py:172
  198.5 5.6 %collective-permute-start.18 = (bf16[1,128,3328]{2,1,0:T(8,128)(2,1)S(1)}, bf16[1,128,3328]{2,1,0:T(8,128)(2,1)S(1)}, u32[]{:S(2)}, u32[]{:S(2)}) collective-permute-start(bf16[1,128,3328]{2,1,0:T(8,128)(2,1)S(1)} %get-tuple-element.98), channel_id=1, source_target_pairs={{0,4},{4,0},{8,12},{12,8},{1,5},{5,1},{9,13},{13,9},{2,6},{6,2},{1... | collective-permute-start | bytes 2555912 | tf_op jit(solution)/shard_map/ppermute | solution.py:172
  198.8 5.4 %collective-permute-start.19 = (bf16[1,128,3328]{2,1,0:T(8,128)(2,1)S(1)}, bf16[1,128,3328]{2,1,0:T(8,128)(2,1)S(1)}, u32[]{:S(2)}, u32[]{:S(2)}) collective-permute-start(bf16[1,128,3328]{2,1,0:T(8,128)(2,1)S(1)} %get-tuple-element.99), channel_id=1, source_target_pairs={{0,4},{4,0},{8,12},{12,8},{1,5},{5,1},{9,13},{13,9},{2,6},{6,2},{1... | collective-permute-start | bytes 2555912 | tf_op jit(solution)/shard_map/ppermute | solution.py:172
  199.1 5.2 %collective-permute-start.20 = (bf16[1,128,3328]{2,1,0:T(8,128)(2,1)S(1)}, bf16[1,128,3328]{2,1,0:T(8,128)(2,1)S(1)}, u32[]{:S(2)}, u32[]{:S(2)}) collective-permute-start(bf16[1,128,3328]{2,1,0:T(8,128)(2,1)S(1)} %get-tuple-element.100), channel_id=1, source_target_pairs={{0,4},{4,0},{8,12},{12,8},{1,5},{5,1},{9,13},{13,9},{2,6},{6,2},{1... | collective-permute-start | bytes 2555912 | tf_op jit(solution)/shard_map/ppermute | solution.py:172
  201.8 19.8 %collective-permute-start.21 = (bf16[128,3328]{1,0:T(8,128)(2,1)S(1)}, bf16[128,3328]{1,0:T(8,128)(2,1)S(1)}, u32[]{:S(2)}, u32[]{:S(2)}) collective-permute-start(bf16[128,3328]{1,0:T(8,128)(2,1)S(1)} %fusion.4.own_x), channel_id=1, source_target_pairs={{0,8},{4,12},{8,0},{12,4},{1,9},{5,13},{9,1},{13,5},{2,10},{6,14},... | collective-permute-start | bytes 2555912 | tf_op jit(solution)/shard_map/ppermute | solution.py:172
  203.0 24.6 %collective-permute-start.22 = (bf16[128,3328]{1,0:T(8,128)(2,1)S(1)}, bf16[128,3328]{1,0:T(8,128)(2,1)S(1)}, u32[]{:S(2)}, u32[]{:S(2)}) collective-permute-start(bf16[128,3328]{1,0:T(8,128)(2,1)S(1)} %fusion.4.own_x), channel_id=1, source_target_pairs={{0,4},{4,0},{8,12},{12,8},{1,5},{5,1},{9,13},{13,9},{2,6},{6,2},{1... | collective-permute-start | bytes 2555912 | tf_op jit(solution)/shard_map/ppermute | solution.py:172
  221.5 7.1 %collective-permute-start.23 = (bf16[128,3328]{1,0:T(8,128)(2,1)S(1)}, bf16[128,3328]{1,0:T(8,128)(2,1)}, u32[]{:S(2)}, u32[]{:S(2)}) collective-permute-start(bf16[128,3328]{1,0:T(8,128)(2,1)S(1)} %collective-permute-done.21.other_x), channel_id=1, source_target_pairs={{0,4},{4,0},{8,12},{12,8},{1,5},{5,1},{9,13},{13,9},{2,6},{6,2},{1... | collective-permute-start | bytes 2555912 | tf_op jit(solution)/shard_map/ppermute | solution.py:172
  223.2 52.2 %collective-permute-start.26 = (bf16[2,128,3328]{2,1,0:T(8,128)(2,1)S(1)}, bf16[2,128,3328]{2,1,0:T(8,128)(2,1)}, u32[]{:S(2)}, u32[]{:S(2)}) collective-permute-start(bf16[2,128,3328]{2,1,0:T(8,128)(2,1)S(1)} %get-tuple-element.105), channel_id=1, source_target_pairs={{0,8},{4,12},{8,0},{12,4},{1,9},{5,13},{9,1},{13,5},{2,10},{6,14},... | collective-permute-start | bytes 5111816 | tf_op jit(solution)/shard_map/ppermute | solution.py:172
  224.4 37.3 %collective-permute-start.24 = (bf16[256,512]{1,0:T(8,128)(2,1)S(1)}, bf16[256,512]{1,0:T(8,128)(2,1)S(1)}, u32[]{:S(2)}, u32[]{:S(2)}) collective-permute-start(bf16[256,512]{1,0:T(8,128)(2,1)S(1)} %get-tuple-element.157), channel_id=1, source_target_pairs={{0,2},{1,3},{2,0},{3,1},{4,6},{5,7},{6,4},{7,5},{8,10},{9,11},{10,... | collective-permute-start | bytes 786440 | tf_op jit(solution)/shard_map/ppermute | solution.py:237
  249.2 25.1 %collective-permute-start.25 = (bf16[256,1024]{1,0:T(8,128)(2,1)}, bf16[256,1024]{1,0:T(8,128)(2,1)S(1)}, u32[]{:S(2)}, u32[]{:S(2)}) collective-permute-start(bf16[256,1024]{1,0:T(8,128)(2,1)} %get-tuple-element.108), channel_id=1, source_target_pairs={{0,1},{1,0},{2,3},{3,2},{4,5},{5,4},{6,7},{7,6},{8,9},{9,8},{10,11... | collective-permute-start | bytes 1572872 | tf_op jit(solution)/shard_map/ppermute | solution.py:229
  260.7 18.0 %collective-permute-start.27 = (bf16[1,128,3328]{2,1,0:T(8,128)(2,1)S(1)}, bf16[1,128,3328]{2,1,0:T(8,128)(2,1)S(1)}, u32[]{:S(2)}, u32[]{:S(2)}) collective-permute-start(bf16[1,128,3328]{2,1,0:T(8,128)(2,1)S(1)} %get-tuple-element.110), channel_id=1, source_target_pairs={{0,4},{4,0},{8,12},{12,8},{1,5},{5,1},{9,13},{13,9},{2,6},{6,2},{1... | collective-permute-start | bytes 2555912 | tf_op jit(solution)/shard_map/ppermute | solution.py:172
  261.6 17.7 %collective-permute-start.28 = (bf16[1,128,3328]{2,1,0:T(8,128)(2,1)S(1)}, bf16[1,128,3328]{2,1,0:T(8,128)(2,1)S(1)}, u32[]{:S(2)}, u32[]{:S(2)}) collective-permute-start(bf16[1,128,3328]{2,1,0:T(8,128)(2,1)S(1)} %get-tuple-element.111), channel_id=1, source_target_pairs={{0,4},{4,0},{8,12},{12,8},{1,5},{5,1},{9,13},{13,9},{2,6},{6,2},{1... | collective-permute-start | bytes 2555912 | tf_op jit(solution)/shard_map/ppermute | solution.py:172
  273.8 18.6 %collective-permute-start.29 = (bf16[1,128,3328]{2,1,0:T(8,128)(2,1)S(1)}, bf16[1,128,3328]{2,1,0:T(8,128)(2,1)S(1)}, u32[]{:S(2)}, u32[]{:S(2)}) collective-permute-start(bf16[1,128,3328]{2,1,0:T(8,128)(2,1)S(1)} %get-tuple-element.115), channel_id=1, source_target_pairs={{0,4},{4,0},{8,12},{12,8},{1,5},{5,1},{9,13},{13,9},{2,6},{6,2},{1... | collective-permute-start | bytes 2555912 | tf_op jit(solution)/shard_map/ppermute | solution.py:172
  274.3 18.1 %collective-permute-start.30 = (bf16[1,128,3328]{2,1,0:T(8,128)(2,1)S(1)}, bf16[1,128,3328]{2,1,0:T(8,128)(2,1)S(1)}, u32[]{:S(2)}, u32[]{:S(2)}) collective-permute-start(bf16[1,128,3328]{2,1,0:T(8,128)(2,1)S(1)} %get-tuple-element.116), channel_id=1, source_target_pairs={{0,4},{4,0},{8,12},{12,8},{1,5},{5,1},{9,13},{13,9},{2,6},{6,2},{1... | collective-permute-start | bytes 2555912 | tf_op jit(solution)/shard_map/ppermute | solution.py:172
  278.4 29.8 %collective-permute-start.32 = (bf16[128,3328]{1,0:T(8,128)(2,1)}, bf16[128,3328]{1,0:T(8,128)(2,1)}, u32[]{:S(2)}, u32[]{:S(2)}) collective-permute-start(bf16[128,3328]{1,0:T(8,128)(2,1)} %fusion.own_x), channel_id=1, source_target_pairs={{0,8},{4,12},{8,0},{12,4},{1,9},{5,13},{9,1},{13,5},{2,10},{6,14},... | collective-permute-start | bytes 2555912 | tf_op jit(solution)/shard_map/ppermute | solution.py:172
  278.7 26.9 %collective-permute-start.31 = (bf16[256,512]{1,0:T(8,128)(2,1)}, bf16[256,512]{1,0:T(8,128)(2,1)}, u32[]{:S(2)}, u32[]{:S(2)}) collective-permute-start(bf16[256,512]{1,0:T(8,128)(2,1)} %get-tuple-element.155), channel_id=1, source_target_pairs={{0,2},{1,3},{2,0},{3,1},{4,6},{5,7},{6,4},{7,5},{8,10},{9,11},{10,... | collective-permute-start | bytes 786440 | tf_op jit(solution)/shard_map/ppermute | solution.py:237
  279.3 30.4 %collective-permute-start.33 = (bf16[128,3328]{1,0:T(8,128)(2,1)}, bf16[128,3328]{1,0:T(8,128)(2,1)}, u32[]{:S(2)}, u32[]{:S(2)}) collective-permute-start(bf16[128,3328]{1,0:T(8,128)(2,1)} %fusion.own_x), channel_id=1, source_target_pairs={{0,4},{4,0},{8,12},{12,8},{1,5},{5,1},{9,13},{13,9},{2,6},{6,2},{1... | collective-permute-start | bytes 2555912 | tf_op jit(solution)/shard_map/ppermute | solution.py:172
  308.2 20.0 %collective-permute-start.35 = (bf16[2,64,3328]{2,1,0:T(8,128)(2,1)S(1)}, bf16[2,64,3328]{2,1,0:T(8,128)(2,1)S(1)}, u32[]{:S(2)}, u32[]{:S(2)}) collective-permute-start(bf16[2,64,3328]{2,1,0:T(8,128)(2,1)S(1)} %get-tuple-element.121), channel_id=1, source_target_pairs={{0,8},{4,12},{8,0},{12,4},{1,9},{5,13},{9,1},{13,5},{2,10},{6,14},... | collective-permute-start | bytes 2555912 | tf_op jit(solution)/shard_map/ppermute | solution.py:172
  309.1 37.5 %collective-permute-start.36 = (bf16[2,64,3328]{2,1,0:T(8,128)(2,1)S(1)}, bf16[2,64,3328]{2,1,0:T(8,128)(2,1)S(1)}, u32[]{:S(2)}, u32[]{:S(2)}) collective-permute-start(bf16[2,64,3328]{2,1,0:T(8,128)(2,1)S(1)} %get-tuple-element.123), channel_id=1, source_target_pairs={{0,8},{4,12},{8,0},{12,4},{1,9},{5,13},{9,1},{13,5},{2,10},{6,14},... | collective-permute-start | bytes 2555912 | tf_op jit(solution)/shard_map/ppermute | solution.py:172
  328.6 29.6 %collective-permute-start.39 = (bf16[64,3328]{1,0:T(8,128)(2,1)S(1)}, bf16[64,3328]{1,0:T(8,128)(2,1)S(1)}, u32[]{:S(2)}, u32[]{:S(2)}) collective-permute-start(bf16[64,3328]{1,0:T(8,128)(2,1)S(1)} %fusion.16.own_x), channel_id=1, source_target_pairs={{0,4},{4,0},{8,12},{12,8},{1,5},{5,1},{9,13},{13,9},{2,6},{6,2},{1... | collective-permute-start | bytes 1277960 | tf_op jit(solution)/shard_map/ppermute | solution.py:172
  331.0 24.7 %collective-permute-start.38 = (bf16[64,3328]{1,0:T(8,128)(2,1)S(1)}, bf16[64,3328]{1,0:T(8,128)(2,1)S(1)}, u32[]{:S(2)}, u32[]{:S(2)}) collective-permute-start(bf16[64,3328]{1,0:T(8,128)(2,1)S(1)} %fusion.16.own_x), channel_id=1, source_target_pairs={{0,8},{4,12},{8,0},{12,4},{1,9},{5,13},{9,1},{13,5},{2,10},{6,14},... | collective-permute-start | bytes 1277960 | tf_op jit(solution)/shard_map/ppermute | solution.py:172
  331.8 26.3 %collective-permute-start.37 = (bf16[256,1024]{1,0:T(8,128)(2,1)S(1)}, bf16[256,1024]{1,0:T(8,128)(2,1)S(1)}, u32[]{:S(2)}, u32[]{:S(2)}) collective-permute-start(bf16[256,1024]{1,0:T(8,128)(2,1)S(1)} %copy-done.30), channel_id=1, source_target_pairs={{0,1},{1,0},{2,3},{3,2},{4,5},{5,4},{6,7},{7,6},{8,9},{9,8},{10,11... | collective-permute-start | bytes 1572872 | tf_op jit(solution)/shard_map/ppermute | solution.py:229
  357.0 11.4 %collective-permute-start.41 = (bf16[64,3328]{1,0:T(8,128)(2,1)S(1)}, bf16[64,3328]{1,0:T(8,128)(2,1)S(1)}, u32[]{:S(2)}, u32[]{:S(2)}) collective-permute-start(bf16[64,3328]{1,0:T(8,128)(2,1)S(1)} %fusion.12.own_x), channel_id=1, source_target_pairs={{0,8},{4,12},{8,0},{12,4},{1,9},{5,13},{9,1},{13,5},{2,10},{6,14},... | collective-permute-start | bytes 1277960 | tf_op jit(solution)/shard_map/ppermute | solution.py:172
  357.8 14.5 %collective-permute-start.42 = (bf16[64,3328]{1,0:T(8,128)(2,1)S(1)}, bf16[64,3328]{1,0:T(8,128)(2,1)S(1)}, u32[]{:S(2)}, u32[]{:S(2)}) collective-permute-start(bf16[64,3328]{1,0:T(8,128)(2,1)S(1)} %fusion.12.own_x), channel_id=1, source_target_pairs={{0,4},{4,0},{8,12},{12,8},{1,5},{5,1},{9,13},{13,9},{2,6},{6,2},{1... | collective-permute-start | bytes 1277960 | tf_op jit(solution)/shard_map/ppermute | solution.py:172
  368.4 3.8 collective-permute-start.43
  369.2 13.1 %collective-permute-start.44 = (bf16[256,512]{1,0:T(8,128)(2,1)S(1)}, bf16[256,512]{1,0:T(8,128)(2,1)S(1)}, u32[]{:S(2)}, u32[]{:S(2)}) collective-permute-start(bf16[256,512]{1,0:T(8,128)(2,1)S(1)} %get-tuple-element.153), channel_id=1, source_target_pairs={{0,2},{1,3},{2,0},{3,1},{4,6},{5,7},{6,4},{7,5},{8,10},{9,11},{10,... | collective-permute-start | bytes 786440 | tf_op jit(solution)/shard_map/ppermute | solution.py:237
  371.0 13.5 %collective-permute-start.45 = (bf16[128,1024]{1,0:T(8,128)(2,1)}, bf16[128,1024]{1,0:T(8,128)(2,1)S(1)}, u32[]{:S(2)}, u32[]{:S(2)}) collective-permute-start(bf16[128,1024]{1,0:T(8,128)(2,1)} %get-tuple-element.136), channel_id=1, source_target_pairs={{0,1},{1,0},{2,3},{3,2},{4,5},{5,4},{6,7},{7,6},{8,9},{9,8},{10,11... | collective-permute-start | bytes 786440 | tf_op jit(solution)/shard_map/ppermute | solution.py:229
  384.5 7.8 %collective-permute-start.46 = (bf16[128,512]{1,0:T(8,128)(2,1)S(1)}, bf16[128,512]{1,0:T(8,128)(2,1)S(1)}, u32[]{:S(2)}, u32[]{:S(2)}) collective-permute-start(bf16[128,512]{1,0:T(8,128)(2,1)S(1)} %get-tuple-element.159), channel_id=1, source_target_pairs={{0,2},{1,3},{2,0},{3,1},{4,6},{5,7},{6,4},{7,5},{8,10},{9,11},{10,... | collective-permute-start | bytes 393224 | tf_op jit(solution)/shard_map/ppermute | solution.py:237
  386.4 14.0 %collective-permute-start.47 = (bf16[128,512]{1,0:T(8,128)(2,1)S(1)}, bf16[128,512]{1,0:T(8,128)(2,1)S(1)}, u32[]{:S(2)}, u32[]{:S(2)}) collective-permute-start(bf16[128,512]{1,0:T(8,128)(2,1)S(1)} %copy-done.33), channel_id=1, source_target_pairs={{0,1},{1,2},{2,3},{3,0},{4,5},{5,6},{6,7},{7,4},{8,9},{9,10},{10,1... | collective-permute-start | bytes 393224 | tf_op jit(solution)/shard_map/ppermute | solution.py:168
  387.4 15.8 %collective-permute-start.48 = (bf16[128,512]{1,0:T(8,128)(2,1)S(1)}, bf16[128,512]{1,0:T(8,128)(2,1)S(1)}, u32[]{:S(2)}, u32[]{:S(2)}) collective-permute-start(bf16[128,512]{1,0:T(8,128)(2,1)S(1)} %copy-done.32), channel_id=1, source_target_pairs={{0,2},{1,3},{2,0},{3,1},{4,6},{5,7},{6,4},{7,5},{8,10},{9,11},{10,... | collective-permute-start | bytes 393224 | tf_op jit(solution)/shard_map/ppermute | solution.py:168
  388.3 16.6 %collective-permute-start.49 = (bf16[128,512]{1,0:T(8,128)(2,1)S(1)}, bf16[128,512]{1,0:T(8,128)(2,1)S(1)}, u32[]{:S(2)}, u32[]{:S(2)}) collective-permute-start(bf16[128,512]{1,0:T(8,128)(2,1)S(1)} %copy-done.31), channel_id=1, source_target_pairs={{0,3},{1,0},{2,1},{3,2},{4,7},{5,4},{6,5},{7,6},{8,11},{9,8},{10,9... | collective-permute-start | bytes 393224 | tf_op jit(solution)/shard_map/ppermute | solution.py:168
  (44 other events, 601.1 us)
Sparse Core Ops, SparseCore 0:
  8.9 76.8 all-gather.1

commit v5 on v3

--- a/solution.py
+++ b/solution.py
@@ -9,8 +9,8 @@
 from jax.sharding import PartitionSpec as P
 
 BF16, F32 = jnp.bfloat16, jnp.float32
-GATE_UP_COST, DOWN_COST = 1, 1
-SPLIT = (0, 1, 2, 3)
+FIRST_COST, GATE_UP_COST, DOWN_COST = 1, 0.2, 0.2
+SPLIT = (4, 4, 4, 4, 1)
 VMEM_LIMIT = 29 * 2**20
 PARTNER, OWN, X, BLOCKS = 0, 1, 2, 3
 
@@ -37,10 +37,10 @@
 
 
 def pieces_of(rows, split):
-    half = rows // 2
-    if not split:
+    if split == 1:
         return [(slice(0, 2), slice(0, rows))]
-    return [(slice(w, w + 1), slice(at, at + half)) for w in (0, 1) for at in (0, half)]
+    height = 2 * rows // split
+    return [(slice(w, w + 1), slice(at, at + height)) for w in (0, 1) for at in range(0, rows, height)]
 
 
 def partner_kernel(n_tok, split, place, *refs):
@@ -102,7 +102,7 @@
     return pl.CostEstimate(flops=int(flops * scale), bytes_accessed=int(sum(sizes) * scale), transcendentals=0)
 
 
-def gate_up_call(place, tokens, rows, row_block, weights, n_col, which, split, received=None):
+def gate_up_call(place, tokens, rows, row_block, weights, n_col, which, split, scale, received=None):
     full, wide = weights[0].shape[0], weights[0].shape[1] // 2
     depth, half = full // n_col, rows // 2
     weight = pl.BlockSpec((depth, wide), lambda k, place: (place[BLOCKS + k], place[which]))
@@ -131,7 +131,7 @@
             scratch_shapes=[pltpu.VMEM((n_col, rows, depth), BF16), pltpu.VMEM((2, rows, wide), F32)],
         ),
         compiler_params=params(1),
-        cost_estimate=cost(GATE_UP_COST, 4 * rows * full * wide, 4 * full * wide, 4 * rows * wide),
+        cost_estimate=cost(scale, 4 * rows * full * wide, 4 * full * wide, 4 * rows * wide),
         name=name,
     )(place, *operands)
 
@@ -198,15 +198,18 @@
         piece = after(tokens[lo * eighth : hi * eighth], *last)
         return [piece] + [shifted(piece, n_col, s) for s in range(1, n_col)]
 
+    def scale(i, which):
+        return FIRST_COST if i == 0 or (i, which) == (1, PARTNER) else GATE_UP_COST
+
     def partner(i):
         tok, rows, block = sources[i]
-        out = gate_up_call(after(place, *last), tok, rows, block, weights, n_col, PARTNER, i in SPLIT)
+        out = gate_up_call(after(place, *last), tok, rows, block, weights, n_col, PARTNER, SPLIT[i], scale(i, PARTNER))
         last[:] = list(out)
         return [swapped(piece, 1) for piece in out]
 
     def own(i, received):
         tok, rows, block = sources[i]
-        send, keep = gate_up_call(after(place, *last), tok, rows, block, weights, n_col, OWN, i in SPLIT, received)
+        send, keep = gate_up_call(after(place, *last), tok, rows, block, weights, n_col, OWN, SPLIT[i], scale(i, OWN), received)
         last[:] = [send]
         return keep, swapped(send, 2)
 
@@ -237,13 +240,16 @@
 
     def down_direct(pieces):
         out = down_call(after(place, *last), straight, pieces, down_weight, n_col, True)
+        last[:] = out
         total = out[-1].astype(F32)
         for s in range(1, n_col):
             total = total + shifted(out[s - 1], n_col, s).astype(F32)
         return total.astype(BF16)
 
     def finish(pair):
-        return (pair[0] + pair[1].astype(F32)).astype(BF16)
+        out = (after(pair[0], *last) + pair[1].astype(F32)).astype(BF16)
+        last[:] = [out]
+        return out
 
     t0, t1 = send_tokens(0, 1), send_tokens(1, 3)
     sources = [(t0, eighth, 0), (t1, 2 * eighth, 0)]
@@ -266,20 +272,23 @@
     h1 = relay(h1)
     h2 = gated(p2)
     r4 = partner(4)
+    o0 = finish(z0)
     d1 = down(h1)
     p4 = own(4, r4)
     z1 = halve(d1)
     h2 = relay(h2)
     h3 = gated(p3)
     d2 = down(h2)
+    o1 = finish(z1)
     h3 = relay(h3)
     h4 = gated(p4)
     z2 = halve(d2)
     d3 = down(h3)
     h4 = relay(h4)
+    o4 = down_direct(h4)
+    o2 = finish(z2)
     z3 = halve(d3)
-    o4 = down_direct(h4)
-    return jnp.concatenate([finish(z0), finish(z1), finish(z2), finish(z3), o4], axis=0)
+    return jnp.concatenate([o0, o1, o2, finish(z3), o4], axis=0)
 
 
 def generic(tokens, gate_weight, up_weight, down_weight):

time: 373 us -> 376 us (level)
  starting transfers between devices: 67.3 us -> 79.9 us
  waiting for transfers between devices: 86.8 us -> 75.4 us
    ppermute x37, waiting for transfers between devices: 56.7 us -> 26.1 us  [swapped(): return lax.ppermute(x, 'row', [(i, i ^ mask) for i in range(4)])]
    ppermute x4, waiting for transfers between devices: 0.01 us -> 25.3 us  [halve(): lax.ppermute(send, 'col', [(c, c ^ 2) for c in range(n_col)])]
    ppermute x4, starting transfers between devices: 6.12 us -> 20 us  [halve(): lax.ppermute(send, 'col', [(c, c ^ 2) for c in range(n_col)])]
    ppermute x4, waiting for transfers between devices: 12.8 us -> 6.13 us  [down(): return (keep, lax.ppermute(send, 'col', [(c, c ^ 1) for c in range(n_col)]))]
    ppermute x15, starting transfers between devices: 35.8 us -> 30.5 us  [shifted(): return lax.ppermute(x, 'col', [(i, (i + shift) % n) for i in range(n)])]
    unnamed x88 -> x86, local copies, waits for them, and re-layouts: 12.8 us -> 14.8 us
  transfers between devices with their start and end apart: 60 -> 60, of which waited for: 19 -> 18; matrix products, arithmetic and copies ran while one was open for 3% -> 3% of each run, Pallas kernels for 47% -> 47%
where the time goes in v5:
time: 376 us; the launch traced here: 370 us
  Pallas kernels  186 us (49%)
  starting transfers between devices  79.9 us (21%)
  waiting for transfers between devices  75.4 us (20%)
  local copies, waits for them, and re-layouts  18 us (5%)
  other arithmetic  9.62 us (3%)
    pallas_call x10, Pallas kernels, gate_up_call(): pl.pallas_call(functools.partial(body, len(tokens), split), out_shape=out...  135 us
    pallas_call x5, Pallas kernels, down_call(): pl.pallas_call(functools.partial(down_kernel, n_col, direct), out_shape=o...  51 us
    ppermute x15, starting transfers between devices, shifted(): return lax.ppermute(x, 'col', [(i, (i + shift) % n) for i in range(n)])  30.5 us
    ppermute x37, waiting for transfers between devices, swapped(): return lax.ppermute(x, 'row', [(i, i ^ mask) for i in range(4)])  26.1 us
    ppermute x4, waiting for transfers between devices, halve(): lax.ppermute(send, 'col', [(c, c ^ 2) for c in range(n_col)])  25.3 us
    ppermute x4, starting transfers between devices, halve(): lax.ppermute(send, 'col', [(c, c ^ 2) for c in range(n_col)])  20 us
    ppermute x37, starting transfers between devices, swapped(): return lax.ppermute(x, 'row', [(i, i ^ mask) for i in range(4)])  18.4 us
    ppermute x15, waiting for transfers between devices, shifted(): return lax.ppermute(x, 'col', [(i, (i + shift) % n) for i in range(n)])  17.9 us
  transfers between devices with their start and end apart: 60, of which 18 were waited for; matrix products, arithmetic and copies ran while one was open for 3% of the time, Pallas kernels for 47%

profile of v5, /device:TPU:0, one launch (start us, length us, event | category | flops | bytes accessed | tf_op | source)
XLA Modules:
  0.0 369.8 jit_solution(611101287461266088)
XLA Ops:
  2.2 3.1 collective-permute-start
  5.2 2.6 collective-permute-start.1
  9.2 2.5 collective-permute-done.refs_1_
  11.7 4.8 %collective-permute-done.1.refs_2_ = bf16[128,512]{1,0:T(8,128)(2,1)S(1)} collective-permute-done((bf16[128,512]{1,0:T(8,128)(2,1)S(1)}, bf16[128,512]{1,0:T(8,128)(2,1)S(1)}, u32[]{:S(2)}, u32[]{:S(2)}) %collective-permute-start.1) | collective-permute-done | bytes 131104 | tf_op jit(solution)/shard_map/ppermute | solution.py:168
  16.5 11.3 %partner.5 = (bf16[1,64,3328]{2,1,0:T(8,128)(2,1)S(1)}, bf16[1,64,3328]{2,1,0:T(8,128)(2,1)S(1)}, bf16[1,64,3328]{2,1,0:T(8,128)(2,1)S(1)}, bf16[1,64,3328]{2,1,0:T(8,128)(2,1)S(1)}) custom-call(s32[8]{0:T(128)S(1)} %get-tuple-element.145.place, bf16[128,512]{1,0:T(8,128)(2,1)S(1)} %slice.133.refs_0_, bf16[128,512]{1,0:T(8,128)(2,1)S(1)} %collective-permute-done.refs_1_, ...), custom_call_target="tpu_custom_call" | custom-call | flops 3489660928 | bytes 28966912 | tf_op jit(solution)/shard_map/partner/pallas_call | solution.py:123
  28.9 3.3 collective-permute-start.7
  32.2 1.7 collective-permute-start.8
  35.2 11.7 %own.5 = (bf16[2,64,3328]{2,1,0:T(8,128)(2,1)S(1)}, bf16[2,64,3328]{2,1,0:T(8,128)(2,1)S(1)}) custom-call(s32[8]{0:T(128)S(1)} %get-tuple-element.145.place, bf16[128,512]{1,0:T(8,128)(2,1)S(1)} %slice.133.refs_0_, bf16[128,512]{1,0:T(8,128)(2,1)S(1)} %collective-permute-done.refs_1_, bf16[128,512]{1,0:T(8,128)(2,1)S(1)} %collective-permute-done.1.refs_2_, ...), custom_call_target="tpu_custom_call" | custom-call | flops 3489660928 | bytes 28966912 | tf_op jit(solution)/shard_map/own/pallas_call | solution.py:123
  46.9 1.6 collective-permute-start.10
  48.5 2.7 collective-permute-done.8.refs_2_
  51.2 13.5 %partner.6 = (bf16[1,128,3328]{2,1,0:T(8,128)(2,1)S(1)}, bf16[1,128,3328]{2,1,0:T(8,128)(2,1)S(1)}, bf16[1,128,3328]{2,1,0:T(8,128)(2,1)S(1)}, bf16[1,128,3328]{2,1,0:T(8,128)(2,1)S(1)}) custom-call(s32[8]{0:T(128)S(1)} %get-tuple-element.145.place, bf16[256,512]{1,0:T(8,128)(2,1)S(1)} %get-tuple-element.90.refs_0_, ...), custom_call_target="tpu_custom_call" | custom-call | flops 6979321856 | bytes 30670848 | tf_op jit(solution)/shard_map/partner/pallas_call | solution.py:123
  65.8 1.6 collective-permute-done.10
  69.3 4.5 %collective-permute-start.15 = (bf16[256,512]{1,0:T(8,128)(2,1)S(1)}, bf16[256,512]{1,0:T(8,128)(2,1)S(1)}, u32[]{:S(2)}, u32[]{:S(2)}) collective-permute-start(bf16[256,512]{1,0:T(8,128)(2,1)S(1)} %get-tuple-element.99.refs_0_), channel_id=1, source_target_pairs={{0,1},{1,2},{2,3},{3,0},{4,5},{5,6},{6,7},{7,4},{8,9},{9,10},{10,1... | collective-permute-start | bytes 786440 | tf_op jit(solution)/shard_map/ppermute | solution.py:168
  75.1 1.9 collective-permute-start.17
  77.0 15.6 %own.6 = (bf16[2,128,3328]{2,1,0:T(8,128)(2,1)}, bf16[2,128,3328]{2,1,0:T(8,128)(2,1)S(1)}) custom-call(s32[8]{0:T(128)S(1)} %get-tuple-element.145.place, bf16[256,512]{1,0:T(8,128)(2,1)S(1)} %get-tuple-element.90.refs_0_, bf16[256,512]{1,0:T(8,128)(2,1)S(1)} %collective-permute-done.7.refs_1_, bf16[256,512]{1,0:T(8,128)(2,1)S(1)} %collective-permute-done.8.refs_2_, ...), custom_call_target="tpu_custom_call" | custom-call | flops 1395864320 | bytes 6134169 | tf_op jit(solution)/shard_map/own/pallas_call | solution.py:123
  92.6 1.6 collective-permute-start.25
  94.2 16.3 %partner.7 = (bf16[1,128,3328]{2,1,0:T(8,128)(2,1)S(1)}, bf16[1,128,3328]{2,1,0:T(8,128)(2,1)}, bf16[1,128,3328]{2,1,0:T(8,128)(2,1)}, bf16[1,128,3328]{2,1,0:T(8,128)(2,1)S(1)}) custom-call(s32[8]{0:T(128)S(1)} %get-tuple-element.145.place, bf16[256,512]{1,0:T(8,128)(2,1)S(1)} %get-tuple-element.99.refs_0_, ...), custom_call_target="tpu_custom_call" | custom-call | flops 1395864320 | bytes 6134169 | tf_op jit(solution)/shard_map/partner/pallas_call | solution.py:123
  114.7 7.7 %down.5 = (bf16[128,1024]{1,0:T(8,128)(2,1)}, bf16[128,1024]{1,0:T(8,128)(2,1)}) custom-call(s32[8]{0:T(128)} %copy-done.1, s32[8]{0:T(128)} %get-tuple-element.172.order, bf16[64,3328]{1,0:T(8,128)(2,1)} %copy-done.5, bf16[64,3328]{1,0:T(8,128)(2,1)} %copy-done.16, bf16[64,3328]{1,0:T(8,128)(2,1)} %copy-done.19, bf16[64,3328]{1,0:T(8,128)(2,1)} %copy-done.20, ...), custom_call_target="tpu_custom_call" | custom-call | flops 697932160 | bytes 340787 | tf_op jit(solution)/shard_map/down/pallas_call | solution.py:151
  122.4 2.8 collective-permute-start.26
  125.2 1.6 collective-permute-start.27
  129.0 14.4 %own.7 = (bf16[2,128,3328]{2,1,0:T(8,128)(2,1)S(1)}, bf16[2,128,3328]{2,1,0:T(8,128)(2,1)S(1)}) custom-call(s32[8]{0:T(128)S(1)} %copy-done.2, bf16[256,512]{1,0:T(8,128)(2,1)S(1)} %get-tuple-element.99.refs_0_, bf16[256,512]{1,0:T(8,128)(2,1)S(1)} %collective-permute-done.15.refs_1_, bf16[256,512]{1,0:T(8,128)(2,1)S(1)} %collective-permute-done.16.refs_2_, ...), custom_call_target="tpu_custom_call" | custom-call | flops 1395864320 | bytes 6134169 | tf_op jit(solution)/shard_map/own/pallas_call | solution.py:123
  144.8 3.0 fusion.8.own_x
  147.8 5.1 %collective-permute-done.27.refs_2_ = bf16[384,512]{1,0:T(8,128)(2,1)S(1)} collective-permute-done((bf16[384,512]{1,0:T(8,128)(2,1)S(1)}, bf16[384,512]{1,0:T(8,128)(2,1)S(1)}, u32[]{:S(2)}, u32[]{:S(2)}) %collective-permute-start.27) | collective-permute-done | bytes 393248 | tf_op jit(solution)/shard_map/ppermute | solution.py:168
  152.9 13.5 %partner.8 = (bf16[1,128,3328]{2,1,0:T(8,128)(2,1)S(1)}, bf16[1,128,3328]{2,1,0:T(8,128)(2,1)S(1)}, bf16[1,128,3328]{2,1,0:T(8,128)(2,1)S(1)}, bf16[1,128,3328]{2,1,0:T(8,128)(2,1)S(1)}) custom-call(s32[8]{0:T(128)S(1)} %copy-done.2, bf16[384,512]{1,0:T(8,128)(2,1)S(1)} %slice.145.refs_0_, bf16[384,512]{1,0:T(8,128)(2,1)S(1)} %collective-permute-done.26.refs_1_, ...), custom_call_target="tpu_custom_call" | custom-call | flops 1395864320 | bytes 6134169 | tf_op jit(solution)/shard_map/partner/pallas_call | solution.py:123
  172.5 14.4 %own.8 = (bf16[2,128,3328]{2,1,0:T(8,128)(2,1)S(1)}, bf16[2,128,3328]{2,1,0:T(8,128)(2,1)S(1)}) custom-call(s32[8]{0:T(128)S(1)} %copy-done.2, bf16[384,512]{1,0:T(8,128)(2,1)S(1)} %slice.145.refs_0_, bf16[384,512]{1,0:T(8,128)(2,1)S(1)} %collective-permute-done.26.refs_1_, bf16[384,512]{1,0:T(8,128)(2,1)S(1)} %collective-permute-done.27.refs_2_, ...), custom_call_target="tpu_custom_call" | custom-call | flops 1395864320 | bytes 6134169 | tf_op jit(solution)/shard_map/own/pallas_call | solution.py:123
  186.9 1.6 fusion.4.own_x
  188.5 12.6 %partner.9 = bf16[2,128,3328]{2,1,0:T(8,128)(2,1)S(1)} custom-call(s32[8]{0:T(128)S(1)} %copy-done.2, bf16[384,512]{1,0:T(8,128)(2,1)S(1)} %slice.145.refs_0_, bf16[384,512]{1,0:T(8,128)(2,1)S(1)} %collective-permute-done.26.refs_1_, bf16[384,512]{1,0:T(8,128)(2,1)S(1)} %collective-permute-done.27.refs_2_, ...), custom_call_target="tpu_custom_call" | custom-call | flops 697932160 | bytes 5793382 | tf_op jit(solution)/shard_map/partner/pallas_call | solution.py:123
  203.1 7.9 %collective-permute-start.35 = (bf16[128,512]{1,0:T(8,128)(2,1)S(1)}, bf16[128,512]{1,0:T(8,128)(2,1)S(1)}, u32[]{:S(2)}, u32[]{:S(2)}) collective-permute-start(bf16[128,512]{1,0:T(8,128)(2,1)S(1)} %get-tuple-element.169), channel_id=1, source_target_pairs={{0,2},{1,3},{2,0},{3,1},{4,6},{5,7},{6,4},{7,5},{8,10},{9,11},{10,... | collective-permute-start | bytes 393224 | tf_op jit(solution)/shard_map/ppermute | solution.py:239
  211.0 3.7 %collective-permute-done.35 = bf16[128,512]{1,0:T(8,128)(2,1)S(1)} collective-permute-done((bf16[128,512]{1,0:T(8,128)(2,1)S(1)}, bf16[128,512]{1,0:T(8,128)(2,1)S(1)}, u32[]{:S(2)}, u32[]{:S(2)}) %collective-permute-start.35) | collective-permute-done | bytes 131104 | tf_op jit(solution)/shard_map/ppermute | solution.py:239
  216.3 11.9 %down.6 = (bf16[256,1024]{1,0:T(8,128)(2,1)}, bf16[256,1024]{1,0:T(8,128)(2,1)}) custom-call(s32[8]{0:T(128)} %copy-done.1, s32[8]{0:T(128)} %get-tuple-element.172.order, bf16[128,3328]{1,0:T(8,128)(2,1)} %fusion.8.own_x, bf16[128,3328]{1,0:T(8,128)(2,1)} %collective-permute-done.36.other_x, bf16[128,3328]{1,0:T(8,128)(2,1)} %collective-permute-done.37.own_x_core, ...), custom_call_target="tpu_custom_call" | custom-call | flops 1395864320 | bytes 681574 | tf_op jit(solution)/shard_map/down/pallas_call | solution.py:151
  228.2 3.7 collective-permute-start.40
  231.9 11.7 %own.9 = (bf16[2,64,3328]{2,1,0:T(8,128)(2,1)S(1)}, bf16[2,64,3328]{2,1,0:T(8,128)(2,1)S(1)}) custom-call(s32[8]{0:T(128)S(1)} %copy-done.3, bf16[384,512]{1,0:T(8,128)(2,1)S(1)} %slice.145.refs_0_, bf16[384,512]{1,0:T(8,128)(2,1)S(1)} %collective-permute-done.26.refs_1_, bf16[384,512]{1,0:T(8,128)(2,1)S(1)} %collective-permute-done.27.refs_2_, ...), custom_call_target="tpu_custom_call" | custom-call | flops 697932160 | bytes 5793382 | tf_op jit(solution)/shard_map/own/pallas_call | solution.py:123
  243.9 15.8 %collective-permute-done.42.other_x = bf16[128,3328]{1,0:T(8,128)(2,1)} collective-permute-done((bf16[128,3328]{1,0:T(8,128)(2,1)}, bf16[128,3328]{1,0:T(8,128)(2,1)}, u32[]{:S(2)}, u32[]{:S(2)}) %collective-permute-start.42) | collective-permute-done | bytes 852000 | tf_op jit(solution)/shard_map/ppermute | solution.py:172
  259.7 2.2 fusion.own_x
  264.0 7.9 %collective-permute-start.45 = (bf16[256,512]{1,0:T(8,128)(2,1)S(1)}, bf16[256,512]{1,0:T(8,128)(2,1)S(1)}, u32[]{:S(2)}, u32[]{:S(2)}) collective-permute-start(bf16[256,512]{1,0:T(8,128)(2,1)S(1)} %get-tuple-element.165), channel_id=1, source_target_pairs={{0,2},{1,3},{2,0},{3,1},{4,6},{5,7},{6,4},{7,5},{8,10},{9,11},{10,... | collective-permute-start | bytes 786440 | tf_op jit(solution)/shard_map/ppermute | solution.py:239
  273.8 8.8 %copy-done = bf16[6656,2048]{1,0:T(8,128)(2,1)S(1)} copy-done((bf16[6656,2048]{1,0:T(8,128)(2,1)S(1)}, bf16[6656,2048]{1,0:T(8,128)(2,1)}, u32[]{:S(2)}) %copy-start) | copy-done | bytes 27263000
  282.5 11.9 %down.7 = (bf16[256,1024]{1,0:T(8,128)(2,1)}, bf16[256,1024]{1,0:T(8,128)(2,1)}) custom-call(s32[8]{0:T(128)} %copy-done.1, s32[8]{0:T(128)} %get-tuple-element.172.order, bf16[128,3328]{1,0:T(8,128)(2,1)} %fusion.4.own_x, bf16[128,3328]{1,0:T(8,128)(2,1)} %collective-permute-done.42.other_x, bf16[128,3328]{1,0:T(8,128)(2,1)} %copy-done.10, ...), custom_call_target="tpu_custom_call" | custom-call | flops 1395864320 | bytes 681574 | tf_op jit(solution)/shard_map/down/pallas_call | solution.py:151
  294.4 2.3 collective-permute-start.47
  296.8 4.8 %collective-permute-done.46 = bf16[2,64,3328]{2,1,0:T(8,128)(2,1)S(1)} collective-permute-done((bf16[2,64,3328]{2,1,0:T(8,128)(2,1)S(1)}, bf16[2,64,3328]{2,1,0:T(8,128)(2,1)S(1)}, u32[]{:S(2)}, u32[]{:S(2)}) %collective-permute-start.46) | collective-permute-done | bytes 852000 | tf_op jit(solution)/shard_map/ppermute | solution.py:172
  303.3 5.3 %collective-permute-done.47 = bf16[256,1024]{1,0:T(8,128)(2,1)S(1)} collective-permute-done((bf16[256,1024]{1,0:T(8,128)(2,1)}, bf16[256,1024]{1,0:T(8,128)(2,1)S(1)}, u32[]{:S(2)}, u32[]{:S(2)}) %collective-permute-start.47) | collective-permute-done | bytes 524320 | tf_op jit(solution)/shard_map/ppermute | solution.py:231
  310.6 11.8 %down.8 = (bf16[256,1024]{1,0:T(8,128)(2,1)}, bf16[256,1024]{1,0:T(8,128)(2,1)}) custom-call(s32[8]{0:T(128)} %copy-done.1, s32[8]{0:T(128)} %get-tuple-element.172.order, bf16[128,3328]{1,0:T(8,128)(2,1)} %copy-done.4, bf16[128,3328]{1,0:T(8,128)(2,1)} %copy-done.8, bf16[128,3328]{1,0:T(8,128)(2,1)} %copy-done.9, bf16[128,3328]{1,0:T(8,128)(2,1)} %copy-done.11, ...), custom_call_target="tpu_custom_call" | custom-call | flops 1395864320 | bytes 681574 | tf_op jit(solution)/shard_map/down/pallas_call | solution.py:151
  322.6 4.1 %collective-permute-start.55 = (bf16[256,1024]{1,0:T(8,128)(2,1)}, bf16[256,1024]{1,0:T(8,128)(2,1)S(1)}, u32[]{:S(2)}, u32[]{:S(2)}) collective-permute-start(bf16[256,1024]{1,0:T(8,128)(2,1)} %get-tuple-element.144), channel_id=1, source_target_pairs={{0,1},{1,0},{2,3},{3,2},{4,5},{5,4},{6,7},{7,6},{8,9},{9,8},{10,11... | collective-permute-start | bytes 1572872 | tf_op jit(solution)/shard_map/ppermute | solution.py:231
  329.0 7.7 %down.9 = (bf16[128,512]{1,0:T(8,128)(2,1)}, bf16[128,512]{1,0:T(8,128)(2,1)}, bf16[128,512]{1,0:T(8,128)(2,1)}, bf16[128,512]{1,0:T(8,128)(2,1)}) custom-call(s32[8]{0:T(128)} %copy-done.1, s32[8]{0:T(128)} %get-tuple-element.171.order, bf16[64,3328]{1,0:T(8,128)(2,1)} %copy-done.6, bf16[64,3328]{1,0:T(8,128)(2,1)} %copy-done.17, ...), custom_call_target="tpu_custom_call" | custom-call | flops 697932160 | bytes 340787 | tf_op jit(solution)/shard_map/down/pallas_call | solution.py:151
  336.7 7.2 %collective-permute-done.54 = bf16[256,512]{1,0:T(8,128)(2,1)S(1)} collective-permute-done((bf16[256,512]{1,0:T(8,128)(2,1)S(1)}, bf16[256,512]{1,0:T(8,128)(2,1)S(1)}, u32[]{:S(2)}, u32[]{:S(2)}) %collective-permute-start.54) | collective-permute-done | bytes 262176 | tf_op jit(solution)/shard_map/ppermute | solution.py:239
  344.8 2.8 collective-permute-start.56
  349.3 2.2 collective-permute-start.59
  351.5 14.4 %collective-permute-done.56 = bf16[256,512]{1,0:T(8,128)(2,1)S(1)} collective-permute-done((bf16[256,512]{1,0:T(8,128)(2,1)S(1)}, bf16[256,512]{1,0:T(8,128)(2,1)S(1)}, u32[]{:S(2)}, u32[]{:S(2)}) %collective-permute-start.56) | collective-permute-done | bytes 262176 | tf_op jit(solution)/shard_map/ppermute | solution.py:239
  365.9 2.7 collective-permute-done.58
  (194 shorter events, 41.3 us)
Async XLA Ops:
  2.2 9.5 %collective-permute-start = (bf16[128,512]{1,0:T(8,128)(2,1)S(1)}, bf16[128,512]{1,0:T(8,128)(2,1)S(1)}, u32[]{:S(2)}, u32[]{:S(2)}) collective-permute-start(bf16[128,512]{1,0:T(8,128)(2,1)S(1)} %slice.133.refs_0_), channel_id=1, source_target_pairs={{0,1},{1,2},{2,3},{3,0},{4,5},{5,6},{6,7},{7,4},{8,9},{9,10},{10,1... | collective-permute-start | bytes 393224 | tf_op jit(solution)/shard_map/ppermute | solution.py:168
  5.2 11.2 %collective-permute-start.1 = (bf16[128,512]{1,0:T(8,128)(2,1)S(1)}, bf16[128,512]{1,0:T(8,128)(2,1)S(1)}, u32[]{:S(2)}, u32[]{:S(2)}) collective-permute-start(bf16[128,512]{1,0:T(8,128)(2,1)S(1)} %slice.133.refs_0_), channel_id=1, source_target_pairs={{0,2},{1,3},{2,0},{3,1},{4,6},{5,7},{6,4},{7,5},{8,10},{9,11},{10,... | collective-permute-start | bytes 393224 | tf_op jit(solution)/shard_map/ppermute | solution.py:168
  28.9 19.6 %collective-permute-start.7 = (bf16[256,512]{1,0:T(8,128)(2,1)S(1)}, bf16[256,512]{1,0:T(8,128)(2,1)S(1)}, u32[]{:S(2)}, u32[]{:S(2)}) collective-permute-start(bf16[256,512]{1,0:T(8,128)(2,1)S(1)} %get-tuple-element.90.refs_0_), channel_id=1, source_target_pairs={{0,1},{1,2},{2,3},{3,0},{4,5},{5,6},{6,7},{7,4},{8,9},{9,10},{10,1... | collective-permute-start | bytes 786440 | tf_op jit(solution)/shard_map/ppermute | solution.py:168
  32.2 19.0 %collective-permute-start.8 = (bf16[256,512]{1,0:T(8,128)(2,1)S(1)}, bf16[256,512]{1,0:T(8,128)(2,1)S(1)}, u32[]{:S(2)}, u32[]{:S(2)}) collective-permute-start(bf16[256,512]{1,0:T(8,128)(2,1)S(1)} %get-tuple-element.90.refs_0_), channel_id=1, source_target_pairs={{0,2},{1,3},{2,0},{3,1},{4,6},{5,7},{6,4},{7,5},{8,10},{9,11},{10,... | collective-permute-start | bytes 786440 | tf_op jit(solution)/shard_map/ppermute | solution.py:168
  33.9 17.4 %collective-permute-start.9 = (bf16[256,512]{1,0:T(8,128)(2,1)S(1)}, bf16[256,512]{1,0:T(8,128)(2,1)S(1)}, u32[]{:S(2)}, u32[]{:S(2)}) collective-permute-start(bf16[256,512]{1,0:T(8,128)(2,1)S(1)} %get-tuple-element.90.refs_0_), channel_id=1, source_target_pairs={{0,3},{1,0},{2,1},{3,2},{4,7},{5,4},{6,5},{7,6},{8,11},{9,8},{10,9... | collective-permute-start | bytes 786440 | tf_op jit(solution)/shard_map/ppermute | solution.py:168
  46.9 20.5 %collective-permute-start.10 = (bf16[2,64,3328]{2,1,0:T(8,128)(2,1)S(1)}, bf16[2,64,3328]{2,1,0:T(8,128)(2,1)S(1)}, u32[]{:S(2)}, u32[]{:S(2)}) collective-permute-start(bf16[2,64,3328]{2,1,0:T(8,128)(2,1)S(1)} %get-tuple-element.88), channel_id=1, source_target_pairs={{0,8},{4,12},{8,0},{12,4},{1,9},{5,13},{9,1},{13,5},{2,10},{6,14},... | collective-permute-start | bytes 2555912 | tf_op jit(solution)/shard_map/ppermute | solution.py:172
  64.8 9.0 %collective-permute-start.12 = (bf16[1,128,3328]{2,1,0:T(8,128)(2,1)S(1)}, bf16[1,128,3328]{2,1,0:T(8,128)(2,1)S(1)}, u32[]{:S(2)}, u32[]{:S(2)}) collective-permute-start(bf16[1,128,3328]{2,1,0:T(8,128)(2,1)S(1)} %get-tuple-element.92), channel_id=1, source_target_pairs={{0,4},{4,0},{8,12},{12,8},{1,5},{5,1},{9,13},{13,9},{2,6},{6,2},{1... | collective-permute-start | bytes 2555912 | tf_op jit(solution)/shard_map/ppermute | solution.py:172
  65.3 9.8 %collective-permute-start.13 = (bf16[1,128,3328]{2,1,0:T(8,128)(2,1)S(1)}, bf16[1,128,3328]{2,1,0:T(8,128)(2,1)S(1)}, u32[]{:S(2)}, u32[]{:S(2)}) collective-permute-start(bf16[1,128,3328]{2,1,0:T(8,128)(2,1)S(1)} %get-tuple-element.93), channel_id=1, source_target_pairs={{0,4},{4,0},{8,12},{12,8},{1,5},{5,1},{9,13},{13,9},{2,6},{6,2},{1... | collective-permute-start | bytes 2555912 | tf_op jit(solution)/shard_map/ppermute | solution.py:172
  65.4 11.6 %collective-permute-start.14 = (bf16[1,128,3328]{2,1,0:T(8,128)(2,1)S(1)}, bf16[1,128,3328]{2,1,0:T(8,128)(2,1)S(1)}, u32[]{:S(2)}, u32[]{:S(2)}) collective-permute-start(bf16[1,128,3328]{2,1,0:T(8,128)(2,1)S(1)} %get-tuple-element.94), channel_id=1, source_target_pairs={{0,4},{4,0},{8,12},{12,8},{1,5},{5,1},{9,13},{13,9},{2,6},{6,2},{1... | collective-permute-start | bytes 2555912 | tf_op jit(solution)/shard_map/ppermute | solution.py:172
  67.8 42.7 %collective-permute-start.18 = (bf16[64,3328]{1,0:T(8,128)(2,1)S(1)}, bf16[64,3328]{1,0:T(8,128)(2,1)S(1)}, u32[]{:S(2)}, u32[]{:S(2)}) collective-permute-start(bf16[64,3328]{1,0:T(8,128)(2,1)S(1)} %fusion.16.own_x), channel_id=1, source_target_pairs={{0,8},{4,12},{8,0},{12,4},{1,9},{5,13},{9,1},{13,5},{2,10},{6,14},... | collective-permute-start | bytes 1277960 | tf_op jit(solution)/shard_map/ppermute | solution.py:172
  69.3 24.9 %collective-permute-start.15 = (bf16[256,512]{1,0:T(8,128)(2,1)S(1)}, bf16[256,512]{1,0:T(8,128)(2,1)S(1)}, u32[]{:S(2)}, u32[]{:S(2)}) collective-permute-start(bf16[256,512]{1,0:T(8,128)(2,1)S(1)} %get-tuple-element.99.refs_0_), channel_id=1, source_target_pairs={{0,1},{1,2},{2,3},{3,0},{4,5},{5,6},{6,7},{7,4},{8,9},{9,10},{10,1... | collective-permute-start | bytes 786440 | tf_op jit(solution)/shard_map/ppermute | solution.py:168
  73.8 20.4 %collective-permute-start.16 = (bf16[256,512]{1,0:T(8,128)(2,1)S(1)}, bf16[256,512]{1,0:T(8,128)(2,1)S(1)}, u32[]{:S(2)}, u32[]{:S(2)}) collective-permute-start(bf16[256,512]{1,0:T(8,128)(2,1)S(1)} %get-tuple-element.99.refs_0_), channel_id=1, source_target_pairs={{0,2},{1,3},{2,0},{3,1},{4,6},{5,7},{6,4},{7,5},{8,10},{9,11},{10,... | collective-permute-start | bytes 786440 | tf_op jit(solution)/shard_map/ppermute | solution.py:168
  75.1 19.1 %collective-permute-start.17 = (bf16[256,512]{1,0:T(8,128)(2,1)S(1)}, bf16[256,512]{1,0:T(8,128)(2,1)S(1)}, u32[]{:S(2)}, u32[]{:S(2)}) collective-permute-start(bf16[256,512]{1,0:T(8,128)(2,1)S(1)} %get-tuple-element.99.refs_0_), channel_id=1, source_target_pairs={{0,3},{1,0},{2,1},{3,2},{4,7},{5,4},{6,5},{7,6},{8,11},{9,8},{10,9... | collective-permute-start | bytes 786440 | tf_op jit(solution)/shard_map/ppermute | solution.py:168
  92.6 50.8 %collective-permute-start.25 = (bf16[2,128,3328]{2,1,0:T(8,128)(2,1)}, bf16[2,128,3328]{2,1,0:T(8,128)(2,1)}, u32[]{:S(2)}, u32[]{:S(2)}) collective-permute-start(bf16[2,128,3328]{2,1,0:T(8,128)(2,1)} %get-tuple-element.97), channel_id=1, source_target_pairs={{0,8},{4,12},{8,0},{12,4},{1,9},{5,13},{9,1},{13,5},{2,10},{6,14},... | collective-permute-start | bytes 5111816 | tf_op jit(solution)/shard_map/ppermute | solution.py:172
  94.2 17.4 %collective-permute-start.19 = (bf16[64,3328]{1,0:T(8,128)(2,1)S(1)}, bf16[64,3328]{1,0:T(8,128)(2,1)S(1)}, u32[]{:S(2)}, u32[]{:S(2)}) collective-permute-start(bf16[64,3328]{1,0:T(8,128)(2,1)S(1)} %fusion.16.own_x), channel_id=1, source_target_pairs={{0,4},{4,0},{8,12},{12,8},{1,5},{5,1},{9,13},{13,9},{2,6},{6,2},{1... | collective-permute-start | bytes 1277960 | tf_op jit(solution)/shard_map/ppermute | solution.py:172
  111.1 11.3 %collective-permute-start.21 = (bf16[1,128,3328]{2,1,0:T(8,128)(2,1)S(1)}, bf16[1,128,3328]{2,1,0:T(8,128)(2,1)S(1)}, u32[]{:S(2)}, u32[]{:S(2)}) collective-permute-start(bf16[1,128,3328]{2,1,0:T(8,128)(2,1)S(1)} %get-tuple-element.100), channel_id=1, source_target_pairs={{0,4},{4,0},{8,12},{12,8},{1,5},{5,1},{9,13},{13,9},{2,6},{6,2},{1... | collective-permute-start | bytes 2555912 | tf_op jit(solution)/shard_map/ppermute | solution.py:172
  111.1 14.1 %collective-permute-start.22 = (bf16[1,128,3328]{2,1,0:T(8,128)(2,1)}, bf16[1,128,3328]{2,1,0:T(8,128)(2,1)S(1)}, u32[]{:S(2)}, u32[]{:S(2)}) collective-permute-start(bf16[1,128,3328]{2,1,0:T(8,128)(2,1)} %get-tuple-element.101), channel_id=1, source_target_pairs={{0,4},{4,0},{8,12},{12,8},{1,5},{5,1},{9,13},{13,9},{2,6},{6,2},{1... | collective-permute-start | bytes 2555912 | tf_op jit(solution)/shard_map/ppermute | solution.py:172
  111.6 15.2 %collective-permute-start.23 = (bf16[1,128,3328]{2,1,0:T(8,128)(2,1)}, bf16[1,128,3328]{2,1,0:T(8,128)(2,1)S(1)}, u32[]{:S(2)}, u32[]{:S(2)}) collective-permute-start(bf16[1,128,3328]{2,1,0:T(8,128)(2,1)} %get-tuple-element.102), channel_id=1, source_target_pairs={{0,4},{4,0},{8,12},{12,8},{1,5},{5,1},{9,13},{13,9},{2,6},{6,2},{1... | collective-permute-start | bytes 2555912 | tf_op jit(solution)/shard_map/ppermute | solution.py:172
  113.2 14.7 %collective-permute-start.24 = (bf16[1,128,3328]{2,1,0:T(8,128)(2,1)S(1)}, bf16[1,128,3328]{2,1,0:T(8,128)(2,1)S(1)}, u32[]{:S(2)}, u32[]{:S(2)}) collective-permute-start(bf16[1,128,3328]{2,1,0:T(8,128)(2,1)S(1)} %get-tuple-element.103), channel_id=1, source_target_pairs={{0,4},{4,0},{8,12},{12,8},{1,5},{5,1},{9,13},{13,9},{2,6},{6,2},{1... | collective-permute-start | bytes 2555912 | tf_op jit(solution)/shard_map/ppermute | solution.py:172
  122.4 25.4 %collective-permute-start.26 = (bf16[384,512]{1,0:T(8,128)(2,1)S(1)}, bf16[384,512]{1,0:T(8,128)(2,1)S(1)}, u32[]{:S(2)}, u32[]{:S(2)}) collective-permute-start(bf16[384,512]{1,0:T(8,128)(2,1)S(1)} %slice.145.refs_0_), channel_id=1, source_target_pairs={{0,1},{1,2},{2,3},{3,0},{4,5},{5,6},{6,7},{7,4},{8,9},{9,10},{10,1... | collective-permute-start | bytes 1179656 | tf_op jit(solution)/shard_map/ppermute | solution.py:168
  125.2 27.7 %collective-permute-start.27 = (bf16[384,512]{1,0:T(8,128)(2,1)S(1)}, bf16[384,512]{1,0:T(8,128)(2,1)S(1)}, u32[]{:S(2)}, u32[]{:S(2)}) collective-permute-start(bf16[384,512]{1,0:T(8,128)(2,1)S(1)} %slice.145.refs_0_), channel_id=1, source_target_pairs={{0,2},{1,3},{2,0},{3,1},{4,6},{5,7},{6,4},{7,5},{8,10},{9,11},{10,... | collective-permute-start | bytes 1179656 | tf_op jit(solution)/shard_map/ppermute | solution.py:168
  126.8 26.1 %collective-permute-start.28 = (bf16[384,512]{1,0:T(8,128)(2,1)S(1)}, bf16[384,512]{1,0:T(8,128)(2,1)S(1)}, u32[]{:S(2)}, u32[]{:S(2)}) collective-permute-start(bf16[384,512]{1,0:T(8,128)(2,1)S(1)} %slice.145.refs_0_), channel_id=1, source_target_pairs={{0,3},{1,0},{2,1},{3,2},{4,7},{5,4},{6,5},{7,6},{8,11},{9,8},{10,9... | collective-permute-start | bytes 1179656 | tf_op jit(solution)/shard_map/ppermute | solution.py:168
  128.0 39.1 %collective-permute-start.29 = (bf16[128,1024]{1,0:T(8,128)(2,1)}, bf16[128,1024]{1,0:T(8,128)(2,1)S(1)}, u32[]{:S(2)}, u32[]{:S(2)}) collective-permute-start(bf16[128,1024]{1,0:T(8,128)(2,1)} %get-tuple-element.108), channel_id=1, source_target_pairs={{0,1},{1,0},{2,3},{3,2},{4,5},{5,4},{6,7},{7,6},{8,9},{9,8},{10,11... | collective-permute-start | bytes 786440 | tf_op jit(solution)/shard_map/ppermute | solution.py:231
  143.4 43.5 %collective-permute-start.34 = (bf16[2,128,3328]{2,1,0:T(8,128)(2,1)S(1)}, bf16[2,128,3328]{2,1,0:T(8,128)(2,1)S(1)}, u32[]{:S(2)}, u32[]{:S(2)}) collective-permute-start(bf16[2,128,3328]{2,1,0:T(8,128)(2,1)S(1)} %get-tuple-element.110), channel_id=1, source_target_pairs={{0,8},{4,12},{8,0},{12,4},{1,9},{5,13},{9,1},{13,5},{2,10},{6,14},... | collective-permute-start | bytes 5111816 | tf_op jit(solution)/shard_map/ppermute | solution.py:172
  168.8 32.9 %collective-permute-start.36 = (bf16[128,3328]{1,0:T(8,128)(2,1)}, bf16[128,3328]{1,0:T(8,128)(2,1)}, u32[]{:S(2)}, u32[]{:S(2)}) collective-permute-start(bf16[128,3328]{1,0:T(8,128)(2,1)} %fusion.8.own_x), channel_id=1, source_target_pairs={{0,8},{4,12},{8,0},{12,4},{1,9},{5,13},{9,1},{13,5},{2,10},{6,14},... | collective-permute-start | bytes 2555912 | tf_op jit(solution)/shard_map/ppermute | solution.py:172
  201.1 30.7 %collective-permute-start.39 = (bf16[2,128,3328]{2,1,0:T(8,128)(2,1)S(1)}, bf16[2,128,3328]{2,1,0:T(8,128)(2,1)S(1)}, u32[]{:S(2)}, u32[]{:S(2)}) collective-permute-start(bf16[2,128,3328]{2,1,0:T(8,128)(2,1)S(1)} %partner.9), channel_id=1, source_target_pairs={{0,4},{4,0},{8,12},{12,8},{1,5},{5,1},{9,13},{13,9},{2,6},{6,2},{1... | collective-permute-start | bytes 5111816 | tf_op jit(solution)/shard_map/ppermute | solution.py:172
  201.3 14.9 %collective-permute-start.37 = (bf16[128,3328]{1,0:T(8,128)(2,1)}, bf16[128,3328]{1,0:T(8,128)(2,1)}, u32[]{:S(2)}, u32[]{:S(2)}) collective-permute-start(bf16[128,3328]{1,0:T(8,128)(2,1)} %fusion.8.own_x), channel_id=1, source_target_pairs={{0,4},{4,0},{8,12},{12,8},{1,5},{5,1},{9,13},{13,9},{2,6},{6,2},{1... | collective-permute-start | bytes 2555912 | tf_op jit(solution)/shard_map/ppermute | solution.py:172
  201.7 14.5 %collective-permute-start.38 = (bf16[128,3328]{1,0:T(8,128)(2,1)}, bf16[128,3328]{1,0:T(8,128)(2,1)}, u32[]{:S(2)}, u32[]{:S(2)}) collective-permute-start(bf16[128,3328]{1,0:T(8,128)(2,1)} %collective-permute-done.36.other_x), channel_id=1, source_target_pairs={{0,4},{4,0},{8,12},{12,8},{1,5},{5,1},{9,13},{13,9},{2,6},{6,2},{1... | collective-permute-start | bytes 2555912 | tf_op jit(solution)/shard_map/ppermute | solution.py:172
  201.9 57.8 %collective-permute-start.41 = (bf16[2,128,3328]{2,1,0:T(8,128)(2,1)S(1)}, bf16[2,128,3328]{2,1,0:T(8,128)(2,1)}, u32[]{:S(2)}, u32[]{:S(2)}) collective-permute-start(bf16[2,128,3328]{2,1,0:T(8,128)(2,1)S(1)} %get-tuple-element.121), channel_id=1, source_target_pairs={{0,8},{4,12},{8,0},{12,4},{1,9},{5,13},{9,1},{13,5},{2,10},{6,14},... | collective-permute-start | bytes 5111816 | tf_op jit(solution)/shard_map/ppermute | solution.py:172
  203.1 11.6 %collective-permute-start.35 = (bf16[128,512]{1,0:T(8,128)(2,1)S(1)}, bf16[128,512]{1,0:T(8,128)(2,1)S(1)}, u32[]{:S(2)}, u32[]{:S(2)}) collective-permute-start(bf16[128,512]{1,0:T(8,128)(2,1)S(1)} %get-tuple-element.169), channel_id=1, source_target_pairs={{0,2},{1,3},{2,0},{3,1},{4,6},{5,7},{6,4},{7,5},{8,10},{9,11},{10,... | collective-permute-start | bytes 393224 | tf_op jit(solution)/shard_map/ppermute | solution.py:239
  214.8 44.9 %collective-permute-start.42 = (bf16[128,3328]{1,0:T(8,128)(2,1)}, bf16[128,3328]{1,0:T(8,128)(2,1)}, u32[]{:S(2)}, u32[]{:S(2)}) collective-permute-start(bf16[128,3328]{1,0:T(8,128)(2,1)} %fusion.4.own_x), channel_id=1, source_target_pairs={{0,8},{4,12},{8,0},{12,4},{1,9},{5,13},{9,1},{13,5},{2,10},{6,14},... | collective-permute-start | bytes 2555912 | tf_op jit(solution)/shard_map/ppermute | solution.py:172
  228.2 15.6 %collective-permute-start.40 = (bf16[256,1024]{1,0:T(8,128)(2,1)}, bf16[256,1024]{1,0:T(8,128)(2,1)S(1)}, u32[]{:S(2)}, u32[]{:S(2)}) collective-permute-start(bf16[256,1024]{1,0:T(8,128)(2,1)} %get-tuple-element.128), channel_id=1, source_target_pairs={{0,1},{1,0},{2,3},{3,2},{4,5},{5,4},{6,7},{7,6},{8,9},{9,8},{10,11... | collective-permute-start | bytes 1572872 | tf_op jit(solution)/shard_map/ppermute | solution.py:231
  231.8 40.1 %collective-permute-start.43 = (bf16[128,3328]{1,0:T(8,128)(2,1)}, bf16[128,3328]{1,0:T(8,128)(2,1)S(1)}, u32[]{:S(2)}, u32[]{:S(2)}) collective-permute-start(bf16[128,3328]{1,0:T(8,128)(2,1)} %fusion.4.own_x), channel_id=1, source_target_pairs={{0,4},{4,0},{8,12},{12,8},{1,5},{5,1},{9,13},{13,9},{2,6},{6,2},{1... | collective-permute-start | bytes 2555912 | tf_op jit(solution)/shard_map/ppermute | solution.py:172
  259.7 12.2 %collective-permute-start.44 = (bf16[128,3328]{1,0:T(8,128)(2,1)}, bf16[128,3328]{1,0:T(8,128)(2,1)S(1)}, u32[]{:S(2)}, u32[]{:S(2)}) collective-permute-start(bf16[128,3328]{1,0:T(8,128)(2,1)} %collective-permute-done.42.other_x), channel_id=1, source_target_pairs={{0,4},{4,0},{8,12},{12,8},{1,5},{5,1},{9,13},{13,9},{2,6},{6,2},{1... | collective-permute-start | bytes 2555912 | tf_op jit(solution)/shard_map/ppermute | solution.py:172
  261.9 34.8 %collective-permute-start.48 = (bf16[128,3328]{1,0:T(8,128)(2,1)S(1)}, bf16[128,3328]{1,0:T(8,128)(2,1)S(1)}, u32[]{:S(2)}, u32[]{:S(2)}) collective-permute-start(bf16[128,3328]{1,0:T(8,128)(2,1)S(1)} %fusion.own_x), channel_id=1, source_target_pairs={{0,8},{4,12},{8,0},{12,4},{1,9},{5,13},{9,1},{13,5},{2,10},{6,14},... | collective-permute-start | bytes 2555912 | tf_op jit(solution)/shard_map/ppermute | solution.py:172
  263.3 38.3 %collective-permute-start.46 = (bf16[2,64,3328]{2,1,0:T(8,128)(2,1)S(1)}, bf16[2,64,3328]{2,1,0:T(8,128)(2,1)S(1)}, u32[]{:S(2)}, u32[]{:S(2)}) collective-permute-start(bf16[2,64,3328]{2,1,0:T(8,128)(2,1)S(1)} %get-tuple-element.130), channel_id=1, source_target_pairs={{0,8},{4,12},{8,0},{12,4},{1,9},{5,13},{9,1},{13,5},{2,10},{6,14},... | collective-permute-start | bytes 2555912 | tf_op jit(solution)/shard_map/ppermute | solution.py:172
  264.0 32.6 %collective-permute-start.45 = (bf16[256,512]{1,0:T(8,128)(2,1)S(1)}, bf16[256,512]{1,0:T(8,128)(2,1)S(1)}, u32[]{:S(2)}, u32[]{:S(2)}) collective-permute-start(bf16[256,512]{1,0:T(8,128)(2,1)S(1)} %get-tuple-element.165), channel_id=1, source_target_pairs={{0,2},{1,3},{2,0},{3,1},{4,6},{5,7},{6,4},{7,5},{8,10},{9,11},{10,... | collective-permute-start | bytes 786440 | tf_op jit(solution)/shard_map/ppermute | solution.py:239
  271.9 36.9 %collective-permute-start.49 = (bf16[128,3328]{1,0:T(8,128)(2,1)S(1)}, bf16[128,3328]{1,0:T(8,128)(2,1)S(1)}, u32[]{:S(2)}, u32[]{:S(2)}) collective-permute-start(bf16[128,3328]{1,0:T(8,128)(2,1)S(1)} %fusion.own_x), channel_id=1, source_target_pairs={{0,4},{4,0},{8,12},{12,8},{1,5},{5,1},{9,13},{13,9},{2,6},{6,2},{1... | collective-permute-start | bytes 2555912 | tf_op jit(solution)/shard_map/ppermute | solution.py:172
  294.4 14.3 %collective-permute-start.47 = (bf16[256,1024]{1,0:T(8,128)(2,1)}, bf16[256,1024]{1,0:T(8,128)(2,1)S(1)}, u32[]{:S(2)}, u32[]{:S(2)}) collective-permute-start(bf16[256,1024]{1,0:T(8,128)(2,1)} %get-tuple-element.136), channel_id=1, source_target_pairs={{0,1},{1,0},{2,3},{3,2},{4,5},{5,4},{6,7},{7,6},{8,9},{9,8},{10,11... | collective-permute-start | bytes 1572872 | tf_op jit(solution)/shard_map/ppermute | solution.py:231
  296.8 12.0 %collective-permute-start.50 = (bf16[128,3328]{1,0:T(8,128)(2,1)S(1)}, bf16[128,3328]{1,0:T(8,128)(2,1)S(1)}, u32[]{:S(2)}, u32[]{:S(2)}) collective-permute-start(bf16[128,3328]{1,0:T(8,128)(2,1)S(1)} %collective-permute-done.48.other_x), channel_id=1, source_target_pairs={{0,4},{4,0},{8,12},{12,8},{1,5},{5,1},{9,13},{13,9},{2,6},{6,2},{1... | collective-permute-start | bytes 2555912 | tf_op jit(solution)/shard_map/ppermute | solution.py:172
  302.0 20.5 %collective-permute-start.51 = (bf16[64,3328]{1,0:T(8,128)(2,1)S(1)}, bf16[64,3328]{1,0:T(8,128)(2,1)S(1)}, u32[]{:S(2)}, u32[]{:S(2)}) collective-permute-start(bf16[64,3328]{1,0:T(8,128)(2,1)S(1)} %fusion.12.own_x), channel_id=1, source_target_pairs={{0,8},{4,12},{8,0},{12,4},{1,9},{5,13},{9,1},{13,5},{2,10},{6,14},... | collective-permute-start | bytes 1277960 | tf_op jit(solution)/shard_map/ppermute | solution.py:172
  303.3 24.7 %collective-permute-start.52 = (bf16[64,3328]{1,0:T(8,128)(2,1)S(1)}, bf16[64,3328]{1,0:T(8,128)(2,1)S(1)}, u32[]{:S(2)}, u32[]{:S(2)}) collective-permute-start(bf16[64,3328]{1,0:T(8,128)(2,1)S(1)} %fusion.12.own_x), channel_id=1, source_target_pairs={{0,4},{4,0},{8,12},{12,8},{1,5},{5,1},{9,13},{13,9},{2,6},{6,2},{1... | collective-permute-start | bytes 1277960 | tf_op jit(solution)/shard_map/ppermute | solution.py:172
  322.6 22.1 %collective-permute-start.55 = (bf16[256,1024]{1,0:T(8,128)(2,1)}, bf16[256,1024]{1,0:T(8,128)(2,1)S(1)}, u32[]{:S(2)}, u32[]{:S(2)}) collective-permute-start(bf16[256,1024]{1,0:T(8,128)(2,1)} %get-tuple-element.144), channel_id=1, source_target_pairs={{0,1},{1,0},{2,3},{3,2},{4,5},{5,4},{6,7},{7,6},{8,9},{9,8},{10,11... | collective-permute-start | bytes 1572872 | tf_op jit(solution)/shard_map/ppermute | solution.py:231
  326.6 17.3 %collective-permute-start.54 = (bf16[256,512]{1,0:T(8,128)(2,1)S(1)}, bf16[256,512]{1,0:T(8,128)(2,1)S(1)}, u32[]{:S(2)}, u32[]{:S(2)}) collective-permute-start(bf16[256,512]{1,0:T(8,128)(2,1)S(1)} %get-tuple-element.163), channel_id=1, source_target_pairs={{0,2},{1,3},{2,0},{3,1},{4,6},{5,7},{6,4},{7,5},{8,10},{9,11},{10,... | collective-permute-start | bytes 786440 | tf_op jit(solution)/shard_map/ppermute | solution.py:239
  344.8 21.1 %collective-permute-start.56 = (bf16[256,512]{1,0:T(8,128)(2,1)S(1)}, bf16[256,512]{1,0:T(8,128)(2,1)S(1)}, u32[]{:S(2)}, u32[]{:S(2)}) collective-permute-start(bf16[256,512]{1,0:T(8,128)(2,1)S(1)} %get-tuple-element.161), channel_id=1, source_target_pairs={{0,2},{1,3},{2,0},{3,1},{4,6},{5,7},{6,4},{7,5},{8,10},{9,11},{10,... | collective-permute-start | bytes 786440 | tf_op jit(solution)/shard_map/ppermute | solution.py:239
  347.6 18.4 %collective-permute-start.57 = (bf16[128,512]{1,0:T(8,128)(2,1)S(1)}, bf16[128,512]{1,0:T(8,128)(2,1)S(1)}, u32[]{:S(2)}, u32[]{:S(2)}) collective-permute-start(bf16[128,512]{1,0:T(8,128)(2,1)S(1)} %copy-done.28), channel_id=1, source_target_pairs={{0,1},{1,2},{2,3},{3,0},{4,5},{5,6},{6,7},{7,4},{8,9},{9,10},{10,1... | collective-permute-start | bytes 393224 | tf_op jit(solution)/shard_map/ppermute | solution.py:168
  348.0 20.7 %collective-permute-start.58 = (bf16[128,512]{1,0:T(8,128)(2,1)S(1)}, bf16[128,512]{1,0:T(8,128)(2,1)S(1)}, u32[]{:S(2)}, u32[]{:S(2)}) collective-permute-start(bf16[128,512]{1,0:T(8,128)(2,1)S(1)} %copy-done.27), channel_id=1, source_target_pairs={{0,2},{1,3},{2,0},{3,1},{4,6},{5,7},{6,4},{7,5},{8,10},{9,11},{10,... | collective-permute-start | bytes 393224 | tf_op jit(solution)/shard_map/ppermute | solution.py:168
  349.3 19.4 %collective-permute-start.59 = (bf16[128,512]{1,0:T(8,128)(2,1)S(1)}, bf16[128,512]{1,0:T(8,128)(2,1)S(1)}, u32[]{:S(2)}, u32[]{:S(2)}) collective-permute-start(bf16[128,512]{1,0:T(8,128)(2,1)S(1)} %copy-done.26), channel_id=1, source_target_pairs={{0,3},{1,0},{2,1},{3,2},{4,7},{5,4},{6,5},{7,6},{8,11},{9,8},{10,9... | collective-permute-start | bytes 393224 | tf_op jit(solution)/shard_map/ppermute | solution.py:168
  (55 other events, 838.9 us)

commit v6 on v5

--- a/solution.py
+++ b/solution.py
@@ -11,7 +11,7 @@
 BF16, F32 = jnp.bfloat16, jnp.float32
 FIRST_COST, GATE_UP_COST, DOWN_COST = 1, 0.2, 0.2
 SPLIT = (4, 4, 4, 4, 1)
-VMEM_LIMIT = 29 * 2**20
+MIB, GATE_UP_VMEM, DOWN_VMEM = 2**20, 29, 29
 PARTNER, OWN, X, BLOCKS = 0, 1, 2, 3
 
 
@@ -94,8 +94,8 @@
     return pl.BlockSpec(shape, lambda *_: (0,) * len(shape), pipeline_mode=pl.Buffered(1))
 
 
-def params(n):
-    return pltpu.CompilerParams(dimension_semantics=("arbitrary",) * n, vmem_limit_bytes=VMEM_LIMIT)
+def params(limit):
+    return pltpu.CompilerParams(dimension_semantics=("arbitrary",), vmem_limit_bytes=int(limit))
 
 
 def cost(scale, flops, *sizes):
@@ -130,7 +130,7 @@
             out_specs=out_specs,
             scratch_shapes=[pltpu.VMEM((n_col, rows, depth), BF16), pltpu.VMEM((2, rows, wide), F32)],
         ),
-        compiler_params=params(1),
+        compiler_params=params(GATE_UP_VMEM * MIB),
         cost_estimate=cost(scale, 4 * rows * full * wide, 4 * full * wide, 4 * rows * wide),
         name=name,
     )(place, *operands)
@@ -158,7 +158,7 @@
             out_specs=out_specs,
             scratch_shapes=[pltpu.VMEM((rows, wide), BF16)] * 2,
         ),
-        compiler_params=params(1),
+        compiler_params=params(DOWN_VMEM * MIB),
         cost_estimate=cost(DOWN_COST, 4 * rows * wide * block * n_col, 8 * half * wide),
         name="down",
     )(place, order, *pieces, down_weight)
@@ -241,10 +241,15 @@
     def down_direct(pieces):
         out = down_call(after(place, *last), straight, pieces, down_weight, n_col, True)
         last[:] = out
-        total = out[-1].astype(F32)
-        for s in range(1, n_col):
-            total = total + shifted(out[s - 1], n_col, s).astype(F32)
-        return total.astype(BF16)
+        return [shifted(part, n_col, s + 1) for s, part in enumerate(out[:-1])] + [out[-1]]
+
+    def sum_direct(out):
+        total = after(out[-1], *last).astype(F32)
+        for part in out[:-1]:
+            total = total + part.astype(F32)
+        out = total.astype(BF16)
+        last[:] = [out]
+        return out
 
     def finish(pair):
         out = (after(pair[0], *last) + pair[1].astype(F32)).astype(BF16)
@@ -285,10 +290,12 @@
     z2 = halve(d2)
     d3 = down(h3)
     h4 = relay(h4)
-    o4 = down_direct(h4)
     o2 = finish(z2)
+    d4 = down_direct(h4)
     z3 = halve(d3)
-    return jnp.concatenate([o0, o1, o2, finish(z3), o4], axis=0)
+    o4 = sum_direct(d4)
+    o3 = finish(z3)
+    return jnp.concatenate([o0, o1, o2, o3, o4], axis=0)
 
 
 def generic(tokens, gate_weight, up_weight, down_weight):

time: 376 us -> 373 us (level)
    ppermute x4, waiting for transfers between devices: 25.3 us -> 16.2 us  [halve(): lax.ppermute(send, 'col', [(c, c ^ 2) for c in range(n_col)])]
    ppermute x15, waiting for transfers between devices: 17.9 us -> 23 us  [shifted(): return lax.ppermute(x, 'col', [(i, (i + shift) % n) for i in range(n)])]
    unnamed x86 -> x80, local copies, waits for them, and re-layouts: 14.8 us -> 15.6 us
  transfers between devices with their start and end apart: 60 -> 60, of which waited for: 18 -> 19; matrix products, arithmetic and copies ran while one was open for 3% -> 3% of each run, Pallas kernels for 47% -> 48%
where the time goes in v6:
time: 373 us; the launch traced here: 367 us
  Pallas kernels  186 us (50%)
  starting transfers between devices  79.2 us (21%)
  waiting for transfers between devices  72.4 us (19%)
  local copies, waits for them, and re-layouts  19.5 us (5%)
  other arithmetic  8.95 us (2%)
    pallas_call x10, Pallas kernels, gate_up_call(): pl.pallas_call(functools.partial(body, len(tokens), split), out_shape=out...  135 us
    pallas_call x5, Pallas kernels, down_call(): pl.pallas_call(functools.partial(down_kernel, n_col, direct), out_shape=o...  50.9 us
    ppermute x15, starting transfers between devices, shifted(): return lax.ppermute(x, 'col', [(i, (i + shift) % n) for i in range(n)])  31.1 us
    ppermute x37, waiting for transfers between devices, swapped(): return lax.ppermute(x, 'row', [(i, i ^ mask) for i in range(4)])  27.9 us
    ppermute x15, waiting for transfers between devices, shifted(): return lax.ppermute(x, 'col', [(i, (i + shift) % n) for i in range(n)])  23 us
    ppermute x4, starting transfers between devices, halve(): lax.ppermute(send, 'col', [(c, c ^ 2) for c in range(n_col)])  19.9 us
    ppermute x37, starting transfers between devices, swapped(): return lax.ppermute(x, 'row', [(i, i ^ mask) for i in range(4)])  18.8 us
    ppermute x4, waiting for transfers between devices, halve(): lax.ppermute(send, 'col', [(c, c ^ 2) for c in range(n_col)])  16.2 us
  transfers between devices with their start and end apart: 60, of which 19 were waited for; matrix products, arithmetic and copies ran while one was open for 3% of the time, Pallas kernels for 48%

profile of v6, /device:TPU:0, one launch (start us, length us, event | category | flops | bytes accessed | tf_op | source)
XLA Modules:
  0.0 366.8 jit_solution(11844381353778142571)
XLA Ops:
  2.1 3.1 collective-permute-start
  5.2 2.6 collective-permute-start.1
  9.1 2.5 collective-permute-done.refs_1_
  11.7 4.8 %collective-permute-done.1.refs_2_ = bf16[128,512]{1,0:T(8,128)(2,1)S(1)} collective-permute-done((bf16[128,512]{1,0:T(8,128)(2,1)S(1)}, bf16[128,512]{1,0:T(8,128)(2,1)S(1)}, u32[]{:S(2)}, u32[]{:S(2)}) %collective-permute-start.1) | collective-permute-done | bytes 131104 | tf_op jit(solution)/shard_map/ppermute | solution.py:168
  16.4 11.3 %partner.5 = (bf16[1,64,3328]{2,1,0:T(8,128)(2,1)S(1)}, bf16[1,64,3328]{2,1,0:T(8,128)(2,1)S(1)}, bf16[1,64,3328]{2,1,0:T(8,128)(2,1)S(1)}, bf16[1,64,3328]{2,1,0:T(8,128)(2,1)S(1)}) custom-call(s32[8]{0:T(128)S(1)} %get-tuple-element.148.place, bf16[128,512]{1,0:T(8,128)(2,1)S(1)} %slice.133.refs_0_, bf16[128,512]{1,0:T(8,128)(2,1)S(1)} %collective-permute-done.refs_1_, ...), custom_call_target="tpu_custom_call" | custom-call | flops 3489660928 | bytes 28966912 | tf_op jit(solution)/shard_map/partner/pallas_call | solution.py:123
  28.8 3.3 collective-permute-start.7
  32.2 1.7 collective-permute-start.8
  35.2 11.7 %own.5 = (bf16[2,64,3328]{2,1,0:T(8,128)(2,1)S(1)}, bf16[2,64,3328]{2,1,0:T(8,128)(2,1)S(1)}) custom-call(s32[8]{0:T(128)S(1)} %get-tuple-element.148.place, bf16[128,512]{1,0:T(8,128)(2,1)S(1)} %slice.133.refs_0_, bf16[128,512]{1,0:T(8,128)(2,1)S(1)} %collective-permute-done.refs_1_, bf16[128,512]{1,0:T(8,128)(2,1)S(1)} %collective-permute-done.1.refs_2_, ...), custom_call_target="tpu_custom_call" | custom-call | flops 3489660928 | bytes 28966912 | tf_op jit(solution)/shard_map/own/pallas_call | solution.py:123
  48.4 2.7 collective-permute-done.8.refs_2_
  51.2 13.5 %partner.6 = (bf16[1,128,3328]{2,1,0:T(8,128)(2,1)S(1)}, bf16[1,128,3328]{2,1,0:T(8,128)(2,1)S(1)}, bf16[1,128,3328]{2,1,0:T(8,128)(2,1)S(1)}, bf16[1,128,3328]{2,1,0:T(8,128)(2,1)S(1)}) custom-call(s32[8]{0:T(128)S(1)} %get-tuple-element.148.place, bf16[256,512]{1,0:T(8,128)(2,1)S(1)} %get-tuple-element.91.refs_0_, ...), custom_call_target="tpu_custom_call" | custom-call | flops 6979321856 | bytes 30670848 | tf_op jit(solution)/shard_map/partner/pallas_call | solution.py:123
  65.8 1.6 collective-permute-done.10
  67.7 1.6 collective-permute-start.18
  69.3 4.5 %collective-permute-start.15 = (bf16[256,512]{1,0:T(8,128)(2,1)S(1)}, bf16[256,512]{1,0:T(8,128)(2,1)S(1)}, u32[]{:S(2)}, u32[]{:S(2)}) collective-permute-start(bf16[256,512]{1,0:T(8,128)(2,1)S(1)} %get-tuple-element.100.refs_0_), channel_id=1, source_target_pairs={{0,1},{1,2},{2,3},{3,0},{4,5},{5,6},{6,7},{7,4},{8,9},{9,10},{10,1... | collective-permute-start | bytes 786440 | tf_op jit(solution)/shard_map/ppermute | solution.py:168
  75.0 1.9 collective-permute-start.17
  76.9 15.6 %own.6 = (bf16[2,128,3328]{2,1,0:T(8,128)(2,1)}, bf16[2,128,3328]{2,1,0:T(8,128)(2,1)S(1)}) custom-call(s32[8]{0:T(128)S(1)} %get-tuple-element.148.place, bf16[256,512]{1,0:T(8,128)(2,1)S(1)} %get-tuple-element.91.refs_0_, bf16[256,512]{1,0:T(8,128)(2,1)S(1)} %collective-permute-done.7.refs_1_, bf16[256,512]{1,0:T(8,128)(2,1)S(1)} %collective-permute-done.8.refs_2_, ...), custom_call_target="tpu_custom_call" | custom-call | flops 1395864320 | bytes 6134169 | tf_op jit(solution)/shard_map/own/pallas_call | solution.py:123
  94.2 16.3 %partner.7 = (bf16[1,128,3328]{2,1,0:T(8,128)(2,1)S(1)}, bf16[1,128,3328]{2,1,0:T(8,128)(2,1)}, bf16[1,128,3328]{2,1,0:T(8,128)(2,1)}, bf16[1,128,3328]{2,1,0:T(8,128)(2,1)S(1)}) custom-call(s32[8]{0:T(128)S(1)} %get-tuple-element.148.place, bf16[256,512]{1,0:T(8,128)(2,1)S(1)} %get-tuple-element.100.refs_0_, ...), custom_call_target="tpu_custom_call" | custom-call | flops 1395864320 | bytes 6134169 | tf_op jit(solution)/shard_map/partner/pallas_call | solution.py:123
  114.6 7.7 %down.5 = (bf16[128,1024]{1,0:T(8,128)(2,1)}, bf16[128,1024]{1,0:T(8,128)(2,1)}) custom-call(s32[8]{0:T(128)} %copy-done.1, s32[8]{0:T(128)} %get-tuple-element.174.order, bf16[64,3328]{1,0:T(8,128)(2,1)} %copy-done.5, bf16[64,3328]{1,0:T(8,128)(2,1)} %copy-done.16, bf16[64,3328]{1,0:T(8,128)(2,1)} %copy-done.18, bf16[64,3328]{1,0:T(8,128)(2,1)} %copy-done.20, ...), custom_call_target="tpu_custom_call" | custom-call | flops 697932160 | bytes 340787 | tf_op jit(solution)/shard_map/down/pallas_call | solution.py:151
  122.3 2.9 collective-permute-start.26
  125.2 1.6 collective-permute-start.27
  129.0 14.4 %own.7 = (bf16[2,128,3328]{2,1,0:T(8,128)(2,1)S(1)}, bf16[2,128,3328]{2,1,0:T(8,128)(2,1)S(1)}) custom-call(s32[8]{0:T(128)S(1)} %copy-done.2, bf16[256,512]{1,0:T(8,128)(2,1)S(1)} %get-tuple-element.100.refs_0_, bf16[256,512]{1,0:T(8,128)(2,1)S(1)} %collective-permute-done.15.refs_1_, bf16[256,512]{1,0:T(8,128)(2,1)S(1)} %collective-permute-done.16.refs_2_, ...), custom_call_target="tpu_custom_call" | custom-call | flops 1395864320 | bytes 6134169 | tf_op jit(solution)/shard_map/own/pallas_call | solution.py:123
  144.8 3.0 fusion.8.own_x
  147.8 5.1 %collective-permute-done.27.refs_2_ = bf16[384,512]{1,0:T(8,128)(2,1)S(1)} collective-permute-done((bf16[384,512]{1,0:T(8,128)(2,1)S(1)}, bf16[384,512]{1,0:T(8,128)(2,1)S(1)}, u32[]{:S(2)}, u32[]{:S(2)}) %collective-permute-start.27) | collective-permute-done | bytes 393248 | tf_op jit(solution)/shard_map/ppermute | solution.py:168
  152.9 13.5 %partner.8 = (bf16[1,128,3328]{2,1,0:T(8,128)(2,1)S(1)}, bf16[1,128,3328]{2,1,0:T(8,128)(2,1)S(1)}, bf16[1,128,3328]{2,1,0:T(8,128)(2,1)S(1)}, bf16[1,128,3328]{2,1,0:T(8,128)(2,1)S(1)}) custom-call(s32[8]{0:T(128)S(1)} %copy-done.2, bf16[384,512]{1,0:T(8,128)(2,1)S(1)} %slice.145.refs_0_, bf16[384,512]{1,0:T(8,128)(2,1)S(1)} %collective-permute-done.26.refs_1_, ...), custom_call_target="tpu_custom_call" | custom-call | flops 1395864320 | bytes 6134169 | tf_op jit(solution)/shard_map/partner/pallas_call | solution.py:123
  172.5 14.4 %own.8 = (bf16[2,128,3328]{2,1,0:T(8,128)(2,1)S(1)}, bf16[2,128,3328]{2,1,0:T(8,128)(2,1)S(1)}) custom-call(s32[8]{0:T(128)S(1)} %copy-done.2, bf16[384,512]{1,0:T(8,128)(2,1)S(1)} %slice.145.refs_0_, bf16[384,512]{1,0:T(8,128)(2,1)S(1)} %collective-permute-done.26.refs_1_, bf16[384,512]{1,0:T(8,128)(2,1)S(1)} %collective-permute-done.27.refs_2_, ...), custom_call_target="tpu_custom_call" | custom-call | flops 1395864320 | bytes 6134169 | tf_op jit(solution)/shard_map/own/pallas_call | solution.py:123
  186.9 1.6 fusion.4.own_x
  188.5 12.6 %partner.9 = bf16[2,128,3328]{2,1,0:T(8,128)(2,1)S(1)} custom-call(s32[8]{0:T(128)S(1)} %copy-done.2, bf16[384,512]{1,0:T(8,128)(2,1)S(1)} %slice.145.refs_0_, bf16[384,512]{1,0:T(8,128)(2,1)S(1)} %collective-permute-done.26.refs_1_, bf16[384,512]{1,0:T(8,128)(2,1)S(1)} %collective-permute-done.27.refs_2_, ...), custom_call_target="tpu_custom_call" | custom-call | flops 697932160 | bytes 5793382 | tf_op jit(solution)/shard_map/partner/pallas_call | solution.py:123
  203.1 7.9 %collective-permute-start.35 = (bf16[128,512]{1,0:T(8,128)(2,1)S(1)}, bf16[128,512]{1,0:T(8,128)(2,1)S(1)}, u32[]{:S(2)}, u32[]{:S(2)}) collective-permute-start(bf16[128,512]{1,0:T(8,128)(2,1)S(1)} %get-tuple-element.171), channel_id=1, source_target_pairs={{0,2},{1,3},{2,0},{3,1},{4,6},{5,7},{6,4},{7,5},{8,10},{9,11},{10,... | collective-permute-start | bytes 393224 | tf_op jit(solution)/shard_map/ppermute | solution.py:239
  211.0 3.7 %collective-permute-done.35 = bf16[128,512]{1,0:T(8,128)(2,1)S(1)} collective-permute-done((bf16[128,512]{1,0:T(8,128)(2,1)S(1)}, bf16[128,512]{1,0:T(8,128)(2,1)S(1)}, u32[]{:S(2)}, u32[]{:S(2)}) %collective-permute-start.35) | collective-permute-done | bytes 131104 | tf_op jit(solution)/shard_map/ppermute | solution.py:239
  216.3 11.9 %down.6 = (bf16[256,1024]{1,0:T(8,128)(2,1)}, bf16[256,1024]{1,0:T(8,128)(2,1)}) custom-call(s32[8]{0:T(128)} %copy-done.1, s32[8]{0:T(128)} %get-tuple-element.174.order, bf16[128,3328]{1,0:T(8,128)(2,1)} %fusion.8.own_x, bf16[128,3328]{1,0:T(8,128)(2,1)} %collective-permute-done.36.other_x, bf16[128,3328]{1,0:T(8,128)(2,1)} %collective-permute-done.37.own_x_core, ...), custom_call_target="tpu_custom_call" | custom-call | flops 1395864320 | bytes 681574 | tf_op jit(solution)/shard_map/down/pallas_call | solution.py:151
  228.2 3.7 collective-permute-start.40
  231.8 11.8 %own.9 = (bf16[2,64,3328]{2,1,0:T(8,128)(2,1)S(1)}, bf16[2,64,3328]{2,1,0:T(8,128)(2,1)S(1)}) custom-call(s32[8]{0:T(128)S(1)} %copy-done.3, bf16[384,512]{1,0:T(8,128)(2,1)S(1)} %slice.145.refs_0_, bf16[384,512]{1,0:T(8,128)(2,1)S(1)} %collective-permute-done.26.refs_1_, bf16[384,512]{1,0:T(8,128)(2,1)S(1)} %collective-permute-done.27.refs_2_, ...), custom_call_target="tpu_custom_call" | custom-call | flops 697932160 | bytes 5793382 | tf_op jit(solution)/shard_map/own/pallas_call | solution.py:123
  243.9 15.8 %collective-permute-done.42.other_x = bf16[128,3328]{1,0:T(8,128)(2,1)} collective-permute-done((bf16[128,3328]{1,0:T(8,128)(2,1)}, bf16[128,3328]{1,0:T(8,128)(2,1)}, u32[]{:S(2)}, u32[]{:S(2)}) %collective-permute-start.42) | collective-permute-done | bytes 852000 | tf_op jit(solution)/shard_map/ppermute | solution.py:172
  259.7 2.2 fusion.own_x
  264.0 7.9 %collective-permute-start.45 = (bf16[256,512]{1,0:T(8,128)(2,1)S(1)}, bf16[256,512]{1,0:T(8,128)(2,1)S(1)}, u32[]{:S(2)}, u32[]{:S(2)}) collective-permute-start(bf16[256,512]{1,0:T(8,128)(2,1)S(1)} %get-tuple-element.167), channel_id=1, source_target_pairs={{0,2},{1,3},{2,0},{3,1},{4,6},{5,7},{6,4},{7,5},{8,10},{9,11},{10,... | collective-permute-start | bytes 786440 | tf_op jit(solution)/shard_map/ppermute | solution.py:239
  273.7 8.8 %copy-done = bf16[6656,2048]{1,0:T(8,128)(2,1)S(1)} copy-done((bf16[6656,2048]{1,0:T(8,128)(2,1)S(1)}, bf16[6656,2048]{1,0:T(8,128)(2,1)}, u32[]{:S(2)}) %copy-start) | copy-done | bytes 27263000
  282.5 11.8 %down.7 = (bf16[256,1024]{1,0:T(8,128)(2,1)}, bf16[256,1024]{1,0:T(8,128)(2,1)}) custom-call(s32[8]{0:T(128)} %copy-done.1, s32[8]{0:T(128)} %get-tuple-element.174.order, bf16[128,3328]{1,0:T(8,128)(2,1)} %fusion.4.own_x, bf16[128,3328]{1,0:T(8,128)(2,1)} %collective-permute-done.42.other_x, bf16[128,3328]{1,0:T(8,128)(2,1)} %copy-done.10, ...), custom_call_target="tpu_custom_call" | custom-call | flops 1395864320 | bytes 681574 | tf_op jit(solution)/shard_map/down/pallas_call | solution.py:151
  294.3 2.3 collective-permute-start.47
  296.8 4.8 %collective-permute-done.46 = bf16[2,64,3328]{2,1,0:T(8,128)(2,1)S(1)} collective-permute-done((bf16[2,64,3328]{2,1,0:T(8,128)(2,1)S(1)}, bf16[2,64,3328]{2,1,0:T(8,128)(2,1)S(1)}, u32[]{:S(2)}, u32[]{:S(2)}) %collective-permute-start.46) | collective-permute-done | bytes 852000 | tf_op jit(solution)/shard_map/ppermute | solution.py:172
  303.3 5.3 %collective-permute-done.47 = bf16[256,1024]{1,0:T(8,128)(2,1)S(1)} collective-permute-done((bf16[256,1024]{1,0:T(8,128)(2,1)}, bf16[256,1024]{1,0:T(8,128)(2,1)S(1)}, u32[]{:S(2)}, u32[]{:S(2)}) %collective-permute-start.47) | collective-permute-done | bytes 524320 | tf_op jit(solution)/shard_map/ppermute | solution.py:231
  308.7 2.7 collective-permute-start.51
  313.2 11.8 %down.8 = (bf16[256,1024]{1,0:T(8,128)(2,1)}, bf16[256,1024]{1,0:T(8,128)(2,1)}) custom-call(s32[8]{0:T(128)} %copy-done.1, s32[8]{0:T(128)} %get-tuple-element.174.order, bf16[128,3328]{1,0:T(8,128)(2,1)} %copy-done.4, bf16[128,3328]{1,0:T(8,128)(2,1)} %copy-done.8, bf16[128,3328]{1,0:T(8,128)(2,1)} %copy-done.9, bf16[128,3328]{1,0:T(8,128)(2,1)} %copy-done.11, ...), custom_call_target="tpu_custom_call" | custom-call | flops 1395864320 | bytes 681574 | tf_op jit(solution)/shard_map/down/pallas_call | solution.py:151
  325.0 2.4 collective-permute-start.55
  330.6 7.7 %down.9 = (bf16[128,512]{1,0:T(8,128)(2,1)}, bf16[128,512]{1,0:T(8,128)(2,1)}, bf16[128,512]{1,0:T(8,128)(2,1)}, bf16[128,512]{1,0:T(8,128)(2,1)}) custom-call(s32[8]{0:T(128)} %copy-done.1, s32[8]{0:T(128)} %get-tuple-element.173.order, bf16[64,3328]{1,0:T(8,128)(2,1)} %copy-done.6, bf16[64,3328]{1,0:T(8,128)(2,1)} %copy-done.17, ...), custom_call_target="tpu_custom_call" | custom-call | flops 697932160 | bytes 340787 | tf_op jit(solution)/shard_map/down/pallas_call | solution.py:151
  338.3 1.6 collective-permute-start.57
  339.9 2.9 collective-permute-start.58
  344.3 2.4 collective-permute-done.56
  346.8 5.4 %collective-permute-done.57 = bf16[128,512]{1,0:T(8,128)(2,1)S(1)} collective-permute-done((bf16[128,512]{1,0:T(8,128)(2,1)}, bf16[128,512]{1,0:T(8,128)(2,1)S(1)}, u32[]{:S(2)}, u32[]{:S(2)}) %collective-permute-start.57) | collective-permute-done | bytes 131104 | tf_op jit(solution)/shard_map/ppermute | solution.py:168
  352.3 12.4 %collective-permute-done.59 = bf16[256,512]{1,0:T(8,128)(2,1)S(1)} collective-permute-done((bf16[256,512]{1,0:T(8,128)(2,1)S(1)}, bf16[256,512]{1,0:T(8,128)(2,1)S(1)}, u32[]{:S(2)}, u32[]{:S(2)}) %collective-permute-start.59) | collective-permute-done | bytes 262176 | tf_op jit(solution)/shard_map/ppermute | solution.py:239
  (189 shorter events, 43.5 us)
Async XLA Ops:
  2.1 9.5 %collective-permute-start = (bf16[128,512]{1,0:T(8,128)(2,1)S(1)}, bf16[128,512]{1,0:T(8,128)(2,1)S(1)}, u32[]{:S(2)}, u32[]{:S(2)}) collective-permute-start(bf16[128,512]{1,0:T(8,128)(2,1)S(1)} %slice.133.refs_0_), channel_id=1, source_target_pairs={{0,1},{1,2},{2,3},{3,0},{4,5},{5,6},{6,7},{7,4},{8,9},{9,10},{10,1... | collective-permute-start | bytes 393224 | tf_op jit(solution)/shard_map/ppermute | solution.py:168
  5.2 11.2 %collective-permute-start.1 = (bf16[128,512]{1,0:T(8,128)(2,1)S(1)}, bf16[128,512]{1,0:T(8,128)(2,1)S(1)}, u32[]{:S(2)}, u32[]{:S(2)}) collective-permute-start(bf16[128,512]{1,0:T(8,128)(2,1)S(1)} %slice.133.refs_0_), channel_id=1, source_target_pairs={{0,2},{1,3},{2,0},{3,1},{4,6},{5,7},{6,4},{7,5},{8,10},{9,11},{10,... | collective-permute-start | bytes 393224 | tf_op jit(solution)/shard_map/ppermute | solution.py:168
  7.8 8.6 %collective-permute-start.2 = (bf16[128,512]{1,0:T(8,128)(2,1)S(1)}, bf16[128,512]{1,0:T(8,128)(2,1)S(1)}, u32[]{:S(2)}, u32[]{:S(2)}) collective-permute-start(bf16[128,512]{1,0:T(8,128)(2,1)S(1)} %slice.133.refs_0_), channel_id=1, source_target_pairs={{0,3},{1,0},{2,1},{3,2},{4,7},{5,4},{6,5},{7,6},{8,11},{9,8},{10,9... | collective-permute-start | bytes 393224 | tf_op jit(solution)/shard_map/ppermute | solution.py:168
  28.8 19.6 %collective-permute-start.7 = (bf16[256,512]{1,0:T(8,128)(2,1)S(1)}, bf16[256,512]{1,0:T(8,128)(2,1)S(1)}, u32[]{:S(2)}, u32[]{:S(2)}) collective-permute-start(bf16[256,512]{1,0:T(8,128)(2,1)S(1)} %get-tuple-element.91.refs_0_), channel_id=1, source_target_pairs={{0,1},{1,2},{2,3},{3,0},{4,5},{5,6},{6,7},{7,4},{8,9},{9,10},{10,1... | collective-permute-start | bytes 786440 | tf_op jit(solution)/shard_map/ppermute | solution.py:168
  32.2 19.0 %collective-permute-start.8 = (bf16[256,512]{1,0:T(8,128)(2,1)S(1)}, bf16[256,512]{1,0:T(8,128)(2,1)S(1)}, u32[]{:S(2)}, u32[]{:S(2)}) collective-permute-start(bf16[256,512]{1,0:T(8,128)(2,1)S(1)} %get-tuple-element.91.refs_0_), channel_id=1, source_target_pairs={{0,2},{1,3},{2,0},{3,1},{4,6},{5,7},{6,4},{7,5},{8,10},{9,11},{10,... | collective-permute-start | bytes 786440 | tf_op jit(solution)/shard_map/ppermute | solution.py:168
  33.8 17.4 %collective-permute-start.9 = (bf16[256,512]{1,0:T(8,128)(2,1)S(1)}, bf16[256,512]{1,0:T(8,128)(2,1)S(1)}, u32[]{:S(2)}, u32[]{:S(2)}) collective-permute-start(bf16[256,512]{1,0:T(8,128)(2,1)S(1)} %get-tuple-element.91.refs_0_), channel_id=1, source_target_pairs={{0,3},{1,0},{2,1},{3,2},{4,7},{5,4},{6,5},{7,6},{8,11},{9,8},{10,9... | collective-permute-start | bytes 786440 | tf_op jit(solution)/shard_map/ppermute | solution.py:168
  46.9 20.5 %collective-permute-start.10 = (bf16[2,64,3328]{2,1,0:T(8,128)(2,1)S(1)}, bf16[2,64,3328]{2,1,0:T(8,128)(2,1)S(1)}, u32[]{:S(2)}, u32[]{:S(2)}) collective-permute-start(bf16[2,64,3328]{2,1,0:T(8,128)(2,1)S(1)} %get-tuple-element.89), channel_id=1, source_target_pairs={{0,8},{4,12},{8,0},{12,4},{1,9},{5,13},{9,1},{13,5},{2,10},{6,14},... | collective-permute-start | bytes 2555912 | tf_op jit(solution)/shard_map/ppermute | solution.py:172
  64.8 9.0 %collective-permute-start.12 = (bf16[1,128,3328]{2,1,0:T(8,128)(2,1)S(1)}, bf16[1,128,3328]{2,1,0:T(8,128)(2,1)S(1)}, u32[]{:S(2)}, u32[]{:S(2)}) collective-permute-start(bf16[1,128,3328]{2,1,0:T(8,128)(2,1)S(1)} %get-tuple-element.93), channel_id=1, source_target_pairs={{0,4},{4,0},{8,12},{12,8},{1,5},{5,1},{9,13},{13,9},{2,6},{6,2},{1... | collective-permute-start | bytes 2555912 | tf_op jit(solution)/shard_map/ppermute | solution.py:172
  65.3 9.8 %collective-permute-start.13 = (bf16[1,128,3328]{2,1,0:T(8,128)(2,1)S(1)}, bf16[1,128,3328]{2,1,0:T(8,128)(2,1)S(1)}, u32[]{:S(2)}, u32[]{:S(2)}) collective-permute-start(bf16[1,128,3328]{2,1,0:T(8,128)(2,1)S(1)} %get-tuple-element.94), channel_id=1, source_target_pairs={{0,4},{4,0},{8,12},{12,8},{1,5},{5,1},{9,13},{13,9},{2,6},{6,2},{1... | collective-permute-start | bytes 2555912 | tf_op jit(solution)/shard_map/ppermute | solution.py:172
  65.3 11.6 %collective-permute-start.14 = (bf16[1,128,3328]{2,1,0:T(8,128)(2,1)S(1)}, bf16[1,128,3328]{2,1,0:T(8,128)(2,1)S(1)}, u32[]{:S(2)}, u32[]{:S(2)}) collective-permute-start(bf16[1,128,3328]{2,1,0:T(8,128)(2,1)S(1)} %get-tuple-element.95), channel_id=1, source_target_pairs={{0,4},{4,0},{8,12},{12,8},{1,5},{5,1},{9,13},{13,9},{2,6},{6,2},{1... | collective-permute-start | bytes 2555912 | tf_op jit(solution)/shard_map/ppermute | solution.py:172
  67.7 42.7 %collective-permute-start.18 = (bf16[64,3328]{1,0:T(8,128)(2,1)S(1)}, bf16[64,3328]{1,0:T(8,128)(2,1)S(1)}, u32[]{:S(2)}, u32[]{:S(2)}) collective-permute-start(bf16[64,3328]{1,0:T(8,128)(2,1)S(1)} %fusion.16.own_x), channel_id=1, source_target_pairs={{0,8},{4,12},{8,0},{12,4},{1,9},{5,13},{9,1},{13,5},{2,10},{6,14},... | collective-permute-start | bytes 1277960 | tf_op jit(solution)/shard_map/ppermute | solution.py:172
  69.3 24.8 %collective-permute-start.15 = (bf16[256,512]{1,0:T(8,128)(2,1)S(1)}, bf16[256,512]{1,0:T(8,128)(2,1)S(1)}, u32[]{:S(2)}, u32[]{:S(2)}) collective-permute-start(bf16[256,512]{1,0:T(8,128)(2,1)S(1)} %get-tuple-element.100.refs_0_), channel_id=1, source_target_pairs={{0,1},{1,2},{2,3},{3,0},{4,5},{5,6},{6,7},{7,4},{8,9},{9,10},{10,1... | collective-permute-start | bytes 786440 | tf_op jit(solution)/shard_map/ppermute | solution.py:168
  73.8 20.3 %collective-permute-start.16 = (bf16[256,512]{1,0:T(8,128)(2,1)S(1)}, bf16[256,512]{1,0:T(8,128)(2,1)S(1)}, u32[]{:S(2)}, u32[]{:S(2)}) collective-permute-start(bf16[256,512]{1,0:T(8,128)(2,1)S(1)} %get-tuple-element.100.refs_0_), channel_id=1, source_target_pairs={{0,2},{1,3},{2,0},{3,1},{4,6},{5,7},{6,4},{7,5},{8,10},{9,11},{10,... | collective-permute-start | bytes 786440 | tf_op jit(solution)/shard_map/ppermute | solution.py:168
  75.0 19.1 %collective-permute-start.17 = (bf16[256,512]{1,0:T(8,128)(2,1)S(1)}, bf16[256,512]{1,0:T(8,128)(2,1)S(1)}, u32[]{:S(2)}, u32[]{:S(2)}) collective-permute-start(bf16[256,512]{1,0:T(8,128)(2,1)S(1)} %get-tuple-element.100.refs_0_), channel_id=1, source_target_pairs={{0,3},{1,0},{2,1},{3,2},{4,7},{5,4},{6,5},{7,6},{8,11},{9,8},{10,9... | collective-permute-start | bytes 786440 | tf_op jit(solution)/shard_map/ppermute | solution.py:168
  92.6 50.9 %collective-permute-start.25 = (bf16[2,128,3328]{2,1,0:T(8,128)(2,1)}, bf16[2,128,3328]{2,1,0:T(8,128)(2,1)}, u32[]{:S(2)}, u32[]{:S(2)}) collective-permute-start(bf16[2,128,3328]{2,1,0:T(8,128)(2,1)} %get-tuple-element.98), channel_id=1, source_target_pairs={{0,8},{4,12},{8,0},{12,4},{1,9},{5,13},{9,1},{13,5},{2,10},{6,14},... | collective-permute-start | bytes 5111816 | tf_op jit(solution)/shard_map/ppermute | solution.py:172
  94.1 17.4 %collective-permute-start.19 = (bf16[64,3328]{1,0:T(8,128)(2,1)S(1)}, bf16[64,3328]{1,0:T(8,128)(2,1)S(1)}, u32[]{:S(2)}, u32[]{:S(2)}) collective-permute-start(bf16[64,3328]{1,0:T(8,128)(2,1)S(1)} %fusion.16.own_x), channel_id=1, source_target_pairs={{0,4},{4,0},{8,12},{12,8},{1,5},{5,1},{9,13},{13,9},{2,6},{6,2},{1... | collective-permute-start | bytes 1277960 | tf_op jit(solution)/shard_map/ppermute | solution.py:172
  111.0 11.3 %collective-permute-start.21 = (bf16[1,128,3328]{2,1,0:T(8,128)(2,1)S(1)}, bf16[1,128,3328]{2,1,0:T(8,128)(2,1)S(1)}, u32[]{:S(2)}, u32[]{:S(2)}) collective-permute-start(bf16[1,128,3328]{2,1,0:T(8,128)(2,1)S(1)} %get-tuple-element.101), channel_id=1, source_target_pairs={{0,4},{4,0},{8,12},{12,8},{1,5},{5,1},{9,13},{13,9},{2,6},{6,2},{1... | collective-permute-start | bytes 2555912 | tf_op jit(solution)/shard_map/ppermute | solution.py:172
  111.1 14.1 %collective-permute-start.22 = (bf16[1,128,3328]{2,1,0:T(8,128)(2,1)}, bf16[1,128,3328]{2,1,0:T(8,128)(2,1)S(1)}, u32[]{:S(2)}, u32[]{:S(2)}) collective-permute-start(bf16[1,128,3328]{2,1,0:T(8,128)(2,1)} %get-tuple-element.102), channel_id=1, source_target_pairs={{0,4},{4,0},{8,12},{12,8},{1,5},{5,1},{9,13},{13,9},{2,6},{6,2},{1... | collective-permute-start | bytes 2555912 | tf_op jit(solution)/shard_map/ppermute | solution.py:172
  111.5 15.3 %collective-permute-start.23 = (bf16[1,128,3328]{2,1,0:T(8,128)(2,1)}, bf16[1,128,3328]{2,1,0:T(8,128)(2,1)S(1)}, u32[]{:S(2)}, u32[]{:S(2)}) collective-permute-start(bf16[1,128,3328]{2,1,0:T(8,128)(2,1)} %get-tuple-element.103), channel_id=1, source_target_pairs={{0,4},{4,0},{8,12},{12,8},{1,5},{5,1},{9,13},{13,9},{2,6},{6,2},{1... | collective-permute-start | bytes 2555912 | tf_op jit(solution)/shard_map/ppermute | solution.py:172
  113.1 14.8 %collective-permute-start.24 = (bf16[1,128,3328]{2,1,0:T(8,128)(2,1)S(1)}, bf16[1,128,3328]{2,1,0:T(8,128)(2,1)S(1)}, u32[]{:S(2)}, u32[]{:S(2)}) collective-permute-start(bf16[1,128,3328]{2,1,0:T(8,128)(2,1)S(1)} %get-tuple-element.104), channel_id=1, source_target_pairs={{0,4},{4,0},{8,12},{12,8},{1,5},{5,1},{9,13},{13,9},{2,6},{6,2},{1... | collective-permute-start | bytes 2555912 | tf_op jit(solution)/shard_map/ppermute | solution.py:172
  122.3 25.5 %collective-permute-start.26 = (bf16[384,512]{1,0:T(8,128)(2,1)S(1)}, bf16[384,512]{1,0:T(8,128)(2,1)S(1)}, u32[]{:S(2)}, u32[]{:S(2)}) collective-permute-start(bf16[384,512]{1,0:T(8,128)(2,1)S(1)} %slice.145.refs_0_), channel_id=1, source_target_pairs={{0,1},{1,2},{2,3},{3,0},{4,5},{5,6},{6,7},{7,4},{8,9},{9,10},{10,1... | collective-permute-start | bytes 1179656 | tf_op jit(solution)/shard_map/ppermute | solution.py:168
  125.2 27.7 %collective-permute-start.27 = (bf16[384,512]{1,0:T(8,128)(2,1)S(1)}, bf16[384,512]{1,0:T(8,128)(2,1)S(1)}, u32[]{:S(2)}, u32[]{:S(2)}) collective-permute-start(bf16[384,512]{1,0:T(8,128)(2,1)S(1)} %slice.145.refs_0_), channel_id=1, source_target_pairs={{0,2},{1,3},{2,0},{3,1},{4,6},{5,7},{6,4},{7,5},{8,10},{9,11},{10,... | collective-permute-start | bytes 1179656 | tf_op jit(solution)/shard_map/ppermute | solution.py:168
  126.8 26.1 %collective-permute-start.28 = (bf16[384,512]{1,0:T(8,128)(2,1)S(1)}, bf16[384,512]{1,0:T(8,128)(2,1)S(1)}, u32[]{:S(2)}, u32[]{:S(2)}) collective-permute-start(bf16[384,512]{1,0:T(8,128)(2,1)S(1)} %slice.145.refs_0_), channel_id=1, source_target_pairs={{0,3},{1,0},{2,1},{3,2},{4,7},{5,4},{6,5},{7,6},{8,11},{9,8},{10,9... | collective-permute-start | bytes 1179656 | tf_op jit(solution)/shard_map/ppermute | solution.py:168
  127.9 39.1 %collective-permute-start.29 = (bf16[128,1024]{1,0:T(8,128)(2,1)}, bf16[128,1024]{1,0:T(8,128)(2,1)S(1)}, u32[]{:S(2)}, u32[]{:S(2)}) collective-permute-start(bf16[128,1024]{1,0:T(8,128)(2,1)} %get-tuple-element.109), channel_id=1, source_target_pairs={{0,1},{1,0},{2,3},{3,2},{4,5},{5,4},{6,7},{7,6},{8,9},{9,8},{10,11... | collective-permute-start | bytes 786440 | tf_op jit(solution)/shard_map/ppermute | solution.py:231
  143.4 43.4 %collective-permute-start.34 = (bf16[2,128,3328]{2,1,0:T(8,128)(2,1)S(1)}, bf16[2,128,3328]{2,1,0:T(8,128)(2,1)S(1)}, u32[]{:S(2)}, u32[]{:S(2)}) collective-permute-start(bf16[2,128,3328]{2,1,0:T(8,128)(2,1)S(1)} %get-tuple-element.111), channel_id=1, source_target_pairs={{0,8},{4,12},{8,0},{12,4},{1,9},{5,13},{9,1},{13,5},{2,10},{6,14},... | collective-permute-start | bytes 5111816 | tf_op jit(solution)/shard_map/ppermute | solution.py:172
  168.8 32.9 %collective-permute-start.36 = (bf16[128,3328]{1,0:T(8,128)(2,1)}, bf16[128,3328]{1,0:T(8,128)(2,1)}, u32[]{:S(2)}, u32[]{:S(2)}) collective-permute-start(bf16[128,3328]{1,0:T(8,128)(2,1)} %fusion.8.own_x), channel_id=1, source_target_pairs={{0,8},{4,12},{8,0},{12,4},{1,9},{5,13},{9,1},{13,5},{2,10},{6,14},... | collective-permute-start | bytes 2555912 | tf_op jit(solution)/shard_map/ppermute | solution.py:172
  201.1 30.7 %collective-permute-start.39 = (bf16[2,128,3328]{2,1,0:T(8,128)(2,1)S(1)}, bf16[2,128,3328]{2,1,0:T(8,128)(2,1)S(1)}, u32[]{:S(2)}, u32[]{:S(2)}) collective-permute-start(bf16[2,128,3328]{2,1,0:T(8,128)(2,1)S(1)} %partner.9), channel_id=1, source_target_pairs={{0,4},{4,0},{8,12},{12,8},{1,5},{5,1},{9,13},{13,9},{2,6},{6,2},{1... | collective-permute-start | bytes 5111816 | tf_op jit(solution)/shard_map/ppermute | solution.py:172
  201.3 14.9 %collective-permute-start.37 = (bf16[128,3328]{1,0:T(8,128)(2,1)}, bf16[128,3328]{1,0:T(8,128)(2,1)}, u32[]{:S(2)}, u32[]{:S(2)}) collective-permute-start(bf16[128,3328]{1,0:T(8,128)(2,1)} %fusion.8.own_x), channel_id=1, source_target_pairs={{0,4},{4,0},{8,12},{12,8},{1,5},{5,1},{9,13},{13,9},{2,6},{6,2},{1... | collective-permute-start | bytes 2555912 | tf_op jit(solution)/shard_map/ppermute | solution.py:172
  201.7 14.5 %collective-permute-start.38 = (bf16[128,3328]{1,0:T(8,128)(2,1)}, bf16[128,3328]{1,0:T(8,128)(2,1)}, u32[]{:S(2)}, u32[]{:S(2)}) collective-permute-start(bf16[128,3328]{1,0:T(8,128)(2,1)} %collective-permute-done.36.other_x), channel_id=1, source_target_pairs={{0,4},{4,0},{8,12},{12,8},{1,5},{5,1},{9,13},{13,9},{2,6},{6,2},{1... | collective-permute-start | bytes 2555912 | tf_op jit(solution)/shard_map/ppermute | solution.py:172
  201.8 57.9 %collective-permute-start.41 = (bf16[2,128,3328]{2,1,0:T(8,128)(2,1)S(1)}, bf16[2,128,3328]{2,1,0:T(8,128)(2,1)}, u32[]{:S(2)}, u32[]{:S(2)}) collective-permute-start(bf16[2,128,3328]{2,1,0:T(8,128)(2,1)S(1)} %get-tuple-element.122), channel_id=1, source_target_pairs={{0,8},{4,12},{8,0},{12,4},{1,9},{5,13},{9,1},{13,5},{2,10},{6,14},... | collective-permute-start | bytes 5111816 | tf_op jit(solution)/shard_map/ppermute | solution.py:172
  203.1 11.6 %collective-permute-start.35 = (bf16[128,512]{1,0:T(8,128)(2,1)S(1)}, bf16[128,512]{1,0:T(8,128)(2,1)S(1)}, u32[]{:S(2)}, u32[]{:S(2)}) collective-permute-start(bf16[128,512]{1,0:T(8,128)(2,1)S(1)} %get-tuple-element.171), channel_id=1, source_target_pairs={{0,2},{1,3},{2,0},{3,1},{4,6},{5,7},{6,4},{7,5},{8,10},{9,11},{10,... | collective-permute-start | bytes 393224 | tf_op jit(solution)/shard_map/ppermute | solution.py:239
  214.8 44.9 %collective-permute-start.42 = (bf16[128,3328]{1,0:T(8,128)(2,1)}, bf16[128,3328]{1,0:T(8,128)(2,1)}, u32[]{:S(2)}, u32[]{:S(2)}) collective-permute-start(bf16[128,3328]{1,0:T(8,128)(2,1)} %fusion.4.own_x), channel_id=1, source_target_pairs={{0,8},{4,12},{8,0},{12,4},{1,9},{5,13},{9,1},{13,5},{2,10},{6,14},... | collective-permute-start | bytes 2555912 | tf_op jit(solution)/shard_map/ppermute | solution.py:172
  228.2 15.6 %collective-permute-start.40 = (bf16[256,1024]{1,0:T(8,128)(2,1)}, bf16[256,1024]{1,0:T(8,128)(2,1)S(1)}, u32[]{:S(2)}, u32[]{:S(2)}) collective-permute-start(bf16[256,1024]{1,0:T(8,128)(2,1)} %get-tuple-element.129), channel_id=1, source_target_pairs={{0,1},{1,0},{2,3},{3,2},{4,5},{5,4},{6,7},{7,6},{8,9},{9,8},{10,11... | collective-permute-start | bytes 1572872 | tf_op jit(solution)/shard_map/ppermute | solution.py:231
  231.8 40.1 %collective-permute-start.43 = (bf16[128,3328]{1,0:T(8,128)(2,1)}, bf16[128,3328]{1,0:T(8,128)(2,1)S(1)}, u32[]{:S(2)}, u32[]{:S(2)}) collective-permute-start(bf16[128,3328]{1,0:T(8,128)(2,1)} %fusion.4.own_x), channel_id=1, source_target_pairs={{0,4},{4,0},{8,12},{12,8},{1,5},{5,1},{9,13},{13,9},{2,6},{6,2},{1... | collective-permute-start | bytes 2555912 | tf_op jit(solution)/shard_map/ppermute | solution.py:172
  259.7 12.2 %collective-permute-start.44 = (bf16[128,3328]{1,0:T(8,128)(2,1)}, bf16[128,3328]{1,0:T(8,128)(2,1)S(1)}, u32[]{:S(2)}, u32[]{:S(2)}) collective-permute-start(bf16[128,3328]{1,0:T(8,128)(2,1)} %collective-permute-done.42.other_x), channel_id=1, source_target_pairs={{0,4},{4,0},{8,12},{12,8},{1,5},{5,1},{9,13},{13,9},{2,6},{6,2},{1... | collective-permute-start | bytes 2555912 | tf_op jit(solution)/shard_map/ppermute | solution.py:172
  261.9 34.8 %collective-permute-start.48 = (bf16[128,3328]{1,0:T(8,128)(2,1)S(1)}, bf16[128,3328]{1,0:T(8,128)(2,1)S(1)}, u32[]{:S(2)}, u32[]{:S(2)}) collective-permute-start(bf16[128,3328]{1,0:T(8,128)(2,1)S(1)} %fusion.own_x), channel_id=1, source_target_pairs={{0,8},{4,12},{8,0},{12,4},{1,9},{5,13},{9,1},{13,5},{2,10},{6,14},... | collective-permute-start | bytes 2555912 | tf_op jit(solution)/shard_map/ppermute | solution.py:172
  263.3 38.3 %collective-permute-start.46 = (bf16[2,64,3328]{2,1,0:T(8,128)(2,1)S(1)}, bf16[2,64,3328]{2,1,0:T(8,128)(2,1)S(1)}, u32[]{:S(2)}, u32[]{:S(2)}) collective-permute-start(bf16[2,64,3328]{2,1,0:T(8,128)(2,1)S(1)} %get-tuple-element.131), channel_id=1, source_target_pairs={{0,8},{4,12},{8,0},{12,4},{1,9},{5,13},{9,1},{13,5},{2,10},{6,14},... | collective-permute-start | bytes 2555912 | tf_op jit(solution)/shard_map/ppermute | solution.py:172
  264.0 32.6 %collective-permute-start.45 = (bf16[256,512]{1,0:T(8,128)(2,1)S(1)}, bf16[256,512]{1,0:T(8,128)(2,1)S(1)}, u32[]{:S(2)}, u32[]{:S(2)}) collective-permute-start(bf16[256,512]{1,0:T(8,128)(2,1)S(1)} %get-tuple-element.167), channel_id=1, source_target_pairs={{0,2},{1,3},{2,0},{3,1},{4,6},{5,7},{6,4},{7,5},{8,10},{9,11},{10,... | collective-permute-start | bytes 786440 | tf_op jit(solution)/shard_map/ppermute | solution.py:239
  271.9 39.5 %collective-permute-start.49 = (bf16[128,3328]{1,0:T(8,128)(2,1)S(1)}, bf16[128,3328]{1,0:T(8,128)(2,1)S(1)}, u32[]{:S(2)}, u32[]{:S(2)}) collective-permute-start(bf16[128,3328]{1,0:T(8,128)(2,1)S(1)} %fusion.own_x), channel_id=1, source_target_pairs={{0,4},{4,0},{8,12},{12,8},{1,5},{5,1},{9,13},{13,9},{2,6},{6,2},{1... | collective-permute-start | bytes 2555912 | tf_op jit(solution)/shard_map/ppermute | solution.py:172
  294.3 14.3 %collective-permute-start.47 = (bf16[256,1024]{1,0:T(8,128)(2,1)}, bf16[256,1024]{1,0:T(8,128)(2,1)S(1)}, u32[]{:S(2)}, u32[]{:S(2)}) collective-permute-start(bf16[256,1024]{1,0:T(8,128)(2,1)} %get-tuple-element.137), channel_id=1, source_target_pairs={{0,1},{1,0},{2,3},{3,2},{4,5},{5,4},{6,7},{7,6},{8,9},{9,8},{10,11... | collective-permute-start | bytes 1572872 | tf_op jit(solution)/shard_map/ppermute | solution.py:231
  296.7 14.7 %collective-permute-start.50 = (bf16[128,3328]{1,0:T(8,128)(2,1)S(1)}, bf16[128,3328]{1,0:T(8,128)(2,1)S(1)}, u32[]{:S(2)}, u32[]{:S(2)}) collective-permute-start(bf16[128,3328]{1,0:T(8,128)(2,1)S(1)} %collective-permute-done.48.other_x), channel_id=1, source_target_pairs={{0,4},{4,0},{8,12},{12,8},{1,5},{5,1},{9,13},{13,9},{2,6},{6,2},{1... | collective-permute-start | bytes 2555912 | tf_op jit(solution)/shard_map/ppermute | solution.py:172
  302.0 25.5 %collective-permute-start.52 = (bf16[64,3328]{1,0:T(8,128)(2,1)S(1)}, bf16[64,3328]{1,0:T(8,128)(2,1)S(1)}, u32[]{:S(2)}, u32[]{:S(2)}) collective-permute-start(bf16[64,3328]{1,0:T(8,128)(2,1)S(1)} %fusion.12.own_x), channel_id=1, source_target_pairs={{0,8},{4,12},{8,0},{12,4},{1,9},{5,13},{9,1},{13,5},{2,10},{6,14},... | collective-permute-start | bytes 1277960 | tf_op jit(solution)/shard_map/ppermute | solution.py:172
  308.7 19.2 %collective-permute-start.51 = (bf16[256,512]{1,0:T(8,128)(2,1)S(1)}, bf16[256,512]{1,0:T(8,128)(2,1)S(1)}, u32[]{:S(2)}, u32[]{:S(2)}) collective-permute-start(bf16[256,512]{1,0:T(8,128)(2,1)S(1)} %get-tuple-element.165), channel_id=1, source_target_pairs={{0,2},{1,3},{2,0},{3,1},{4,6},{5,7},{6,4},{7,5},{8,10},{9,11},{10,... | collective-permute-start | bytes 786440 | tf_op jit(solution)/shard_map/ppermute | solution.py:239
  325.0 17.7 %collective-permute-start.55 = (bf16[256,1024]{1,0:T(8,128)(2,1)}, bf16[256,1024]{1,0:T(8,128)(2,1)S(1)}, u32[]{:S(2)}, u32[]{:S(2)}) collective-permute-start(bf16[256,1024]{1,0:T(8,128)(2,1)} %get-tuple-element.145), channel_id=1, source_target_pairs={{0,1},{1,0},{2,3},{3,2},{4,5},{5,4},{6,7},{7,6},{8,9},{9,8},{10,11... | collective-permute-start | bytes 1572872 | tf_op jit(solution)/shard_map/ppermute | solution.py:231
  338.3 8.5 %collective-permute-start.56 = (bf16[128,512]{1,0:T(8,128)(2,1)}, bf16[128,512]{1,0:T(8,128)(2,1)S(1)}, u32[]{:S(2)}, u32[]{:S(2)}) collective-permute-start(bf16[128,512]{1,0:T(8,128)(2,1)} %get-tuple-element.150), channel_id=1, source_target_pairs={{0,1},{1,2},{2,3},{3,0},{4,5},{5,6},{6,7},{7,4},{8,9},{9,10},{10,1... | collective-permute-start | bytes 393224 | tf_op jit(solution)/shard_map/ppermute | solution.py:168
  338.3 13.9 %collective-permute-start.57 = (bf16[128,512]{1,0:T(8,128)(2,1)}, bf16[128,512]{1,0:T(8,128)(2,1)S(1)}, u32[]{:S(2)}, u32[]{:S(2)}) collective-permute-start(bf16[128,512]{1,0:T(8,128)(2,1)} %get-tuple-element.151), channel_id=1, source_target_pairs={{0,2},{1,3},{2,0},{3,1},{4,6},{5,7},{6,4},{7,5},{8,10},{9,11},{10,... | collective-permute-start | bytes 393224 | tf_op jit(solution)/shard_map/ppermute | solution.py:168
  339.9 12.3 %collective-permute-start.58 = (bf16[128,512]{1,0:T(8,128)(2,1)}, bf16[128,512]{1,0:T(8,128)(2,1)S(1)}, u32[]{:S(2)}, u32[]{:S(2)}) collective-permute-start(bf16[128,512]{1,0:T(8,128)(2,1)} %get-tuple-element.152), channel_id=1, source_target_pairs={{0,3},{1,0},{2,1},{3,2},{4,7},{5,4},{6,5},{7,6},{8,11},{9,8},{10,9... | collective-permute-start | bytes 393224 | tf_op jit(solution)/shard_map/ppermute | solution.py:168
  342.9 21.8 %collective-permute-start.59 = (bf16[256,512]{1,0:T(8,128)(2,1)S(1)}, bf16[256,512]{1,0:T(8,128)(2,1)S(1)}, u32[]{:S(2)}, u32[]{:S(2)}) collective-permute-start(bf16[256,512]{1,0:T(8,128)(2,1)S(1)} %get-tuple-element.163), channel_id=1, source_target_pairs={{0,2},{1,3},{2,0},{3,1},{4,6},{5,7},{6,4},{7,5},{8,10},{9,11},{10,... | collective-permute-start | bytes 786440 | tf_op jit(solution)/shard_map/ppermute | solution.py:239
  (52 other events, 779.3 us)

commit v7 on v6

--- a/solution.py
+++ b/solution.py
@@ -284,15 +284,15 @@
     h2 = relay(h2)
     h3 = gated(p3)
     d2 = down(h2)
+    h3 = relay(h3)
+    d3 = down(h3)
+    h4 = gated(p4)
     o1 = finish(z1)
-    h3 = relay(h3)
-    h4 = gated(p4)
     z2 = halve(d2)
-    d3 = down(h3)
     h4 = relay(h4)
+    z3 = halve(d3)
     o2 = finish(z2)
     d4 = down_direct(h4)
-    z3 = halve(d3)
     o4 = sum_direct(d4)
     o3 = finish(z3)
     return jnp.concatenate([o0, o1, o2, o3, o4], axis=0)

time: 373 us -> 374 us (level)
    ppermute x4, waiting for transfers between devices: 16.2 us -> 11.1 us  [halve(): lax.ppermute(send, 'col', [(c, c ^ 2) for c in range(n_col)])]
    ppermute x15, waiting for transfers between devices: 23 us -> 27.2 us  [shifted(): return lax.ppermute(x, 'col', [(i, (i + shift) % n) for i in range(n)])]
    unnamed x80 -> x78, local copies, waits for them, and re-layouts: 15.6 us -> 15.8 us
  transfers between devices with their start and end apart: 60 -> 60, of which waited for: 19 -> 18; matrix products, arithmetic and copies ran while one was open for 3% -> 3% of each run, Pallas kernels for 48% -> 45%
where the time goes in v7:
time: 374 us; the launch traced here: 368 us
  Pallas kernels  186 us (50%)
  starting transfers between devices  79.1 us (21%)
  waiting for transfers between devices  72.3 us (19%)
  local copies, waits for them, and re-layouts  19.7 us (5%)
  other arithmetic  9.79 us (3%)
    pallas_call x10, Pallas kernels, gate_up_call(): pl.pallas_call(functools.partial(body, len(tokens), split), out_shape=out...  135 us
    pallas_call x5, Pallas kernels, down_call(): pl.pallas_call(functools.partial(down_kernel, n_col, direct), out_shape=o...  50.8 us
    ppermute x15, starting transfers between devices, shifted(): return lax.ppermute(x, 'col', [(i, (i + shift) % n) for i in range(n)])  32.1 us
    ppermute x15, waiting for transfers between devices, shifted(): return lax.ppermute(x, 'col', [(i, (i + shift) % n) for i in range(n)])  27.2 us
    ppermute x37, waiting for transfers between devices, swapped(): return lax.ppermute(x, 'row', [(i, i ^ mask) for i in range(4)])  26.4 us
    ppermute x4, starting transfers between devices, halve(): lax.ppermute(send, 'col', [(c, c ^ 2) for c in range(n_col)])  21.1 us
    ppermute x37, starting transfers between devices, swapped(): return lax.ppermute(x, 'row', [(i, i ^ mask) for i in range(4)])  18.8 us
    unnamed x78, local copies, waits for them, and re-layouts  15.8 us
  transfers between devices with their start and end apart: 60, of which 18 were waited for; matrix products, arithmetic and copies ran while one was open for 3% of the time, Pallas kernels for 45%

profile of v7, /device:TPU:0, one launch (start us, length us, event | category | flops | bytes accessed | tf_op | source)
XLA Modules:
  0.0 367.7 jit_solution(14863278577647089552)
XLA Ops:
  2.2 3.1 collective-permute-start
  5.3 2.6 collective-permute-start.1
  9.2 2.5 collective-permute-done.refs_1_
  11.7 4.8 %collective-permute-done.1.refs_2_ = bf16[128,512]{1,0:T(8,128)(2,1)S(1)} collective-permute-done((bf16[128,512]{1,0:T(8,128)(2,1)S(1)}, bf16[128,512]{1,0:T(8,128)(2,1)S(1)}, u32[]{:S(2)}, u32[]{:S(2)}) %collective-permute-start.1) | collective-permute-done | bytes 131104 | tf_op jit(solution)/shard_map/ppermute | solution.py:168
  16.5 11.3 %partner.5 = (bf16[1,64,3328]{2,1,0:T(8,128)(2,1)S(1)}, bf16[1,64,3328]{2,1,0:T(8,128)(2,1)S(1)}, bf16[1,64,3328]{2,1,0:T(8,128)(2,1)S(1)}, bf16[1,64,3328]{2,1,0:T(8,128)(2,1)S(1)}) custom-call(s32[8]{0:T(128)S(1)} %get-tuple-element.149.place, bf16[128,512]{1,0:T(8,128)(2,1)S(1)} %slice.133.refs_0_, bf16[128,512]{1,0:T(8,128)(2,1)S(1)} %collective-permute-done.refs_1_, ...), custom_call_target="tpu_custom_call" | custom-call | flops 3489660928 | bytes 28966912 | tf_op jit(solution)/shard_map/partner/pallas_call | solution.py:123
  28.9 3.3 collective-permute-start.7
  32.2 1.7 collective-permute-start.8
  35.3 11.7 %own.5 = (bf16[2,64,3328]{2,1,0:T(8,128)(2,1)S(1)}, bf16[2,64,3328]{2,1,0:T(8,128)(2,1)S(1)}) custom-call(s32[8]{0:T(128)S(1)} %get-tuple-element.149.place, bf16[128,512]{1,0:T(8,128)(2,1)S(1)} %slice.133.refs_0_, bf16[128,512]{1,0:T(8,128)(2,1)S(1)} %collective-permute-done.refs_1_, bf16[128,512]{1,0:T(8,128)(2,1)S(1)} %collective-permute-done.1.refs_2_, ...), custom_call_target="tpu_custom_call" | custom-call | flops 3489660928 | bytes 28966912 | tf_op jit(solution)/shard_map/own/pallas_call | solution.py:123
  46.9 1.6 collective-permute-start.10
  48.5 2.7 collective-permute-done.8.refs_2_
  51.3 13.5 %partner.6 = (bf16[1,128,3328]{2,1,0:T(8,128)(2,1)S(1)}, bf16[1,128,3328]{2,1,0:T(8,128)(2,1)S(1)}, bf16[1,128,3328]{2,1,0:T(8,128)(2,1)S(1)}, bf16[1,128,3328]{2,1,0:T(8,128)(2,1)S(1)}) custom-call(s32[8]{0:T(128)S(1)} %get-tuple-element.149.place, bf16[256,512]{1,0:T(8,128)(2,1)S(1)} %get-tuple-element.91.refs_0_, ...), custom_call_target="tpu_custom_call" | custom-call | flops 6979321856 | bytes 30670848 | tf_op jit(solution)/shard_map/partner/pallas_call | solution.py:123
  65.8 1.6 collective-permute-done.10
  67.8 1.6 collective-permute-start.18
  69.4 4.5 %collective-permute-start.15 = (bf16[256,512]{1,0:T(8,128)(2,1)S(1)}, bf16[256,512]{1,0:T(8,128)(2,1)S(1)}, u32[]{:S(2)}, u32[]{:S(2)}) collective-permute-start(bf16[256,512]{1,0:T(8,128)(2,1)S(1)} %get-tuple-element.100.refs_0_), channel_id=1, source_target_pairs={{0,1},{1,2},{2,3},{3,0},{4,5},{5,6},{6,7},{7,4},{8,9},{9,10},{10,1... | collective-permute-start | bytes 786440 | tf_op jit(solution)/shard_map/ppermute | solution.py:168
  75.1 1.9 collective-permute-start.17
  77.0 15.5 %own.6 = (bf16[2,128,3328]{2,1,0:T(8,128)(2,1)}, bf16[2,128,3328]{2,1,0:T(8,128)(2,1)S(1)}) custom-call(s32[8]{0:T(128)S(1)} %get-tuple-element.149.place, bf16[256,512]{1,0:T(8,128)(2,1)S(1)} %get-tuple-element.91.refs_0_, bf16[256,512]{1,0:T(8,128)(2,1)S(1)} %collective-permute-done.7.refs_1_, bf16[256,512]{1,0:T(8,128)(2,1)S(1)} %collective-permute-done.8.refs_2_, ...), custom_call_target="tpu_custom_call" | custom-call | flops 1395864320 | bytes 6134169 | tf_op jit(solution)/shard_map/own/pallas_call | solution.py:123
  94.2 16.3 %partner.7 = (bf16[1,128,3328]{2,1,0:T(8,128)(2,1)S(1)}, bf16[1,128,3328]{2,1,0:T(8,128)(2,1)}, bf16[1,128,3328]{2,1,0:T(8,128)(2,1)}, bf16[1,128,3328]{2,1,0:T(8,128)(2,1)S(1)}) custom-call(s32[8]{0:T(128)S(1)} %get-tuple-element.149.place, bf16[256,512]{1,0:T(8,128)(2,1)S(1)} %get-tuple-element.100.refs_0_, ...), custom_call_target="tpu_custom_call" | custom-call | flops 1395864320 | bytes 6134169 | tf_op jit(solution)/shard_map/partner/pallas_call | solution.py:123
  114.7 7.7 %down.5 = (bf16[128,1024]{1,0:T(8,128)(2,1)}, bf16[128,1024]{1,0:T(8,128)(2,1)}) custom-call(s32[8]{0:T(128)} %copy-done.1, s32[8]{0:T(128)} %get-tuple-element.174.order, bf16[64,3328]{1,0:T(8,128)(2,1)} %copy-done.5, bf16[64,3328]{1,0:T(8,128)(2,1)} %copy-done.16, bf16[64,3328]{1,0:T(8,128)(2,1)} %copy-done.18, bf16[64,3328]{1,0:T(8,128)(2,1)} %copy-done.21, ...), custom_call_target="tpu_custom_call" | custom-call | flops 697932160 | bytes 340787 | tf_op jit(solution)/shard_map/down/pallas_call | solution.py:151
  122.4 2.9 collective-permute-start.26
  125.3 1.7 collective-permute-start.27
  129.1 14.4 %own.7 = (bf16[2,128,3328]{2,1,0:T(8,128)(2,1)S(1)}, bf16[2,128,3328]{2,1,0:T(8,128)(2,1)S(1)}) custom-call(s32[8]{0:T(128)S(1)} %copy-done.2, bf16[256,512]{1,0:T(8,128)(2,1)S(1)} %get-tuple-element.100.refs_0_, bf16[256,512]{1,0:T(8,128)(2,1)S(1)} %collective-permute-done.15.refs_1_, bf16[256,512]{1,0:T(8,128)(2,1)S(1)} %collective-permute-done.16.refs_2_, ...), custom_call_target="tpu_custom_call" | custom-call | flops 1395864320 | bytes 6134169 | tf_op jit(solution)/shard_map/own/pallas_call | solution.py:123
  144.9 3.0 fusion.8.own_x
  147.9 5.1 %collective-permute-done.27.refs_2_ = bf16[384,512]{1,0:T(8,128)(2,1)S(1)} collective-permute-done((bf16[384,512]{1,0:T(8,128)(2,1)S(1)}, bf16[384,512]{1,0:T(8,128)(2,1)S(1)}, u32[]{:S(2)}, u32[]{:S(2)}) %collective-permute-start.27) | collective-permute-done | bytes 393248 | tf_op jit(solution)/shard_map/ppermute | solution.py:168
  153.0 13.5 %partner.8 = (bf16[1,128,3328]{2,1,0:T(8,128)(2,1)S(1)}, bf16[1,128,3328]{2,1,0:T(8,128)(2,1)S(1)}, bf16[1,128,3328]{2,1,0:T(8,128)(2,1)S(1)}, bf16[1,128,3328]{2,1,0:T(8,128)(2,1)S(1)}) custom-call(s32[8]{0:T(128)S(1)} %copy-done.2, bf16[384,512]{1,0:T(8,128)(2,1)S(1)} %slice.145.refs_0_, bf16[384,512]{1,0:T(8,128)(2,1)S(1)} %collective-permute-done.26.refs_1_, ...), custom_call_target="tpu_custom_call" | custom-call | flops 1395864320 | bytes 6134169 | tf_op jit(solution)/shard_map/partner/pallas_call | solution.py:123
  172.6 14.4 %own.8 = (bf16[2,128,3328]{2,1,0:T(8,128)(2,1)S(1)}, bf16[2,128,3328]{2,1,0:T(8,128)(2,1)S(1)}) custom-call(s32[8]{0:T(128)S(1)} %copy-done.2, bf16[384,512]{1,0:T(8,128)(2,1)S(1)} %slice.145.refs_0_, bf16[384,512]{1,0:T(8,128)(2,1)S(1)} %collective-permute-done.26.refs_1_, bf16[384,512]{1,0:T(8,128)(2,1)S(1)} %collective-permute-done.27.refs_2_, ...), custom_call_target="tpu_custom_call" | custom-call | flops 1395864320 | bytes 6134169 | tf_op jit(solution)/shard_map/own/pallas_call | solution.py:123
  187.0 1.6 fusion.4.own_x
  188.6 12.6 %partner.9 = bf16[2,128,3328]{2,1,0:T(8,128)(2,1)S(1)} custom-call(s32[8]{0:T(128)S(1)} %copy-done.2, bf16[384,512]{1,0:T(8,128)(2,1)S(1)} %slice.145.refs_0_, bf16[384,512]{1,0:T(8,128)(2,1)S(1)} %collective-permute-done.26.refs_1_, bf16[384,512]{1,0:T(8,128)(2,1)S(1)} %collective-permute-done.27.refs_2_, ...), custom_call_target="tpu_custom_call" | custom-call | flops 697932160 | bytes 5793382 | tf_op jit(solution)/shard_map/partner/pallas_call | solution.py:123
  203.2 7.9 %collective-permute-start.35 = (bf16[128,512]{1,0:T(8,128)(2,1)S(1)}, bf16[128,512]{1,0:T(8,128)(2,1)S(1)}, u32[]{:S(2)}, u32[]{:S(2)}) collective-permute-start(bf16[128,512]{1,0:T(8,128)(2,1)S(1)} %get-tuple-element.171), channel_id=1, source_target_pairs={{0,2},{1,3},{2,0},{3,1},{4,6},{5,7},{6,4},{7,5},{8,10},{9,11},{10,... | collective-permute-start | bytes 393224 | tf_op jit(solution)/shard_map/ppermute | solution.py:239
  211.1 3.7 %collective-permute-done.35 = bf16[128,512]{1,0:T(8,128)(2,1)S(1)} collective-permute-done((bf16[128,512]{1,0:T(8,128)(2,1)S(1)}, bf16[128,512]{1,0:T(8,128)(2,1)S(1)}, u32[]{:S(2)}, u32[]{:S(2)}) %collective-permute-start.35) | collective-permute-done | bytes 131104 | tf_op jit(solution)/shard_map/ppermute | solution.py:239
  216.4 11.9 %down.6 = (bf16[256,1024]{1,0:T(8,128)(2,1)}, bf16[256,1024]{1,0:T(8,128)(2,1)}) custom-call(s32[8]{0:T(128)} %copy-done.1, s32[8]{0:T(128)} %get-tuple-element.174.order, bf16[128,3328]{1,0:T(8,128)(2,1)} %fusion.8.own_x, bf16[128,3328]{1,0:T(8,128)(2,1)} %collective-permute-done.36.other_x, bf16[128,3328]{1,0:T(8,128)(2,1)} %collective-permute-done.37.own_x_core, ...), custom_call_target="tpu_custom_call" | custom-call | flops 1395864320 | bytes 681574 | tf_op jit(solution)/shard_map/down/pallas_call | solution.py:151
  228.3 3.7 collective-permute-start.40
  231.9 11.7 %own.9 = (bf16[2,64,3328]{2,1,0:T(8,128)(2,1)S(1)}, bf16[2,64,3328]{2,1,0:T(8,128)(2,1)S(1)}) custom-call(s32[8]{0:T(128)S(1)} %copy-done.3, bf16[384,512]{1,0:T(8,128)(2,1)S(1)} %slice.145.refs_0_, bf16[384,512]{1,0:T(8,128)(2,1)S(1)} %collective-permute-done.26.refs_1_, bf16[384,512]{1,0:T(8,128)(2,1)S(1)} %collective-permute-done.27.refs_2_, ...), custom_call_target="tpu_custom_call" | custom-call | flops 697932160 | bytes 5793382 | tf_op jit(solution)/shard_map/own/pallas_call | solution.py:123
  244.0 15.8 %collective-permute-done.42.other_x = bf16[128,3328]{1,0:T(8,128)(2,1)} collective-permute-done((bf16[128,3328]{1,0:T(8,128)(2,1)}, bf16[128,3328]{1,0:T(8,128)(2,1)}, u32[]{:S(2)}, u32[]{:S(2)}) %collective-permute-start.42) | collective-permute-done | bytes 852000 | tf_op jit(solution)/shard_map/ppermute | solution.py:172
  259.8 2.1 fusion.own_x
  265.3 8.8 %copy-done = bf16[6656,2048]{1,0:T(8,128)(2,1)S(1)} copy-done((bf16[6656,2048]{1,0:T(8,128)(2,1)S(1)}, bf16[6656,2048]{1,0:T(8,128)(2,1)}, u32[]{:S(2)}) %copy-start) | copy-done | bytes 27263000
  274.1 11.8 %down.7 = (bf16[256,1024]{1,0:T(8,128)(2,1)}, bf16[256,1024]{1,0:T(8,128)(2,1)}) custom-call(s32[8]{0:T(128)} %copy-done.1, s32[8]{0:T(128)} %get-tuple-element.174.order, bf16[128,3328]{1,0:T(8,128)(2,1)} %fusion.4.own_x, bf16[128,3328]{1,0:T(8,128)(2,1)} %collective-permute-done.42.other_x, bf16[128,3328]{1,0:T(8,128)(2,1)} %copy-done.8, ...), custom_call_target="tpu_custom_call" | custom-call | flops 1395864320 | bytes 681574 | tf_op jit(solution)/shard_map/down/pallas_call | solution.py:151
  287.1 7.9 %collective-permute-start.49 = (bf16[256,512]{1,0:T(8,128)(2,1)S(1)}, bf16[256,512]{1,0:T(8,128)(2,1)S(1)}, u32[]{:S(2)}, u32[]{:S(2)}) collective-permute-start(bf16[256,512]{1,0:T(8,128)(2,1)S(1)} %get-tuple-element.167), channel_id=1, source_target_pairs={{0,2},{1,3},{2,0},{3,1},{4,6},{5,7},{6,4},{7,5},{8,10},{9,11},{10,... | collective-permute-start | bytes 786440 | tf_op jit(solution)/shard_map/ppermute | solution.py:239
  295.0 2.2 collective-permute-start.50
  299.0 11.9 %down.8 = (bf16[256,1024]{1,0:T(8,128)(2,1)}, bf16[256,1024]{1,0:T(8,128)(2,1)}) custom-call(s32[8]{0:T(128)} %copy-done.1, s32[8]{0:T(128)} %get-tuple-element.174.order, bf16[128,3328]{1,0:T(8,128)(2,1)} %copy-done.4, bf16[128,3328]{1,0:T(8,128)(2,1)} %copy-done.9, bf16[128,3328]{1,0:T(8,128)(2,1)} %copy-done.10, bf16[128,3328]{1,0:T(8,128)(2,1)} %copy-done.12, ...), custom_call_target="tpu_custom_call" | custom-call | flops 1395864320 | bytes 681574 | tf_op jit(solution)/shard_map/down/pallas_call | solution.py:151
  313.1 4.4 %collective-permute-start.52 = (bf16[256,512]{1,0:T(8,128)(2,1)S(1)}, bf16[256,512]{1,0:T(8,128)(2,1)S(1)}, u32[]{:S(2)}, u32[]{:S(2)}) collective-permute-start(bf16[256,512]{1,0:T(8,128)(2,1)S(1)} %get-tuple-element.165), channel_id=1, source_target_pairs={{0,2},{1,3},{2,0},{3,1},{4,6},{5,7},{6,4},{7,5},{8,10},{9,11},{10,... | collective-permute-start | bytes 786440 | tf_op jit(solution)/shard_map/ppermute | solution.py:239
  317.5 5.0 %collective-permute-done.53.other_x = bf16[64,3328]{1,0:T(8,128)(2,1)S(1)} collective-permute-done((bf16[64,3328]{1,0:T(8,128)(2,1)S(1)}, bf16[64,3328]{1,0:T(8,128)(2,1)S(1)}, u32[]{:S(2)}, u32[]{:S(2)}) %collective-permute-start.53) | collective-permute-done | bytes 426016 | tf_op jit(solution)/shard_map/ppermute | solution.py:172
  322.5 7.5 %collective-permute-done.51 = bf16[256,1024]{1,0:T(8,128)(2,1)S(1)} collective-permute-done((bf16[256,1024]{1,0:T(8,128)(2,1)}, bf16[256,1024]{1,0:T(8,128)(2,1)S(1)}, u32[]{:S(2)}, u32[]{:S(2)}) %collective-permute-start.51) | collective-permute-done | bytes 524320 | tf_op jit(solution)/shard_map/ppermute | solution.py:231
  331.1 7.5 %down.9 = (bf16[128,512]{1,0:T(8,128)(2,1)}, bf16[128,512]{1,0:T(8,128)(2,1)}, bf16[128,512]{1,0:T(8,128)(2,1)}, bf16[128,512]{1,0:T(8,128)(2,1)}) custom-call(s32[8]{0:T(128)} %copy-done.1, s32[8]{0:T(128)} %get-tuple-element.173.order, bf16[64,3328]{1,0:T(8,128)(2,1)} %copy-done.6, bf16[64,3328]{1,0:T(8,128)(2,1)} %copy-done.17, ...), custom_call_target="tpu_custom_call" | custom-call | flops 697932160 | bytes 340787 | tf_op jit(solution)/shard_map/down/pallas_call | solution.py:151
  338.7 3.1 collective-permute-start.56
  341.7 2.0 collective-permute-start.57
  345.2 2.7 collective-permute-done.56
  347.8 9.3 %collective-permute-done.57 = bf16[128,512]{1,0:T(8,128)(2,1)S(1)} collective-permute-done((bf16[128,512]{1,0:T(8,128)(2,1)}, bf16[128,512]{1,0:T(8,128)(2,1)S(1)}, u32[]{:S(2)}, u32[]{:S(2)}) %collective-permute-start.57) | collective-permute-done | bytes 131104 | tf_op jit(solution)/shard_map/ppermute | solution.py:168
  358.2 7.4 %collective-permute-done.59 = bf16[256,512]{1,0:T(8,128)(2,1)S(1)} collective-permute-done((bf16[256,512]{1,0:T(8,128)(2,1)S(1)}, bf16[256,512]{1,0:T(8,128)(2,1)S(1)}, u32[]{:S(2)}, u32[]{:S(2)}) %collective-permute-start.59) | collective-permute-done | bytes 262176 | tf_op jit(solution)/shard_map/ppermute | solution.py:239
  (187 shorter events, 41.6 us)
Async XLA Ops:
  2.2 9.5 %collective-permute-start = (bf16[128,512]{1,0:T(8,128)(2,1)S(1)}, bf16[128,512]{1,0:T(8,128)(2,1)S(1)}, u32[]{:S(2)}, u32[]{:S(2)}) collective-permute-start(bf16[128,512]{1,0:T(8,128)(2,1)S(1)} %slice.133.refs_0_), channel_id=1, source_target_pairs={{0,1},{1,2},{2,3},{3,0},{4,5},{5,6},{6,7},{7,4},{8,9},{9,10},{10,1... | collective-permute-start | bytes 393224 | tf_op jit(solution)/shard_map/ppermute | solution.py:168
  5.3 11.2 %collective-permute-start.1 = (bf16[128,512]{1,0:T(8,128)(2,1)S(1)}, bf16[128,512]{1,0:T(8,128)(2,1)S(1)}, u32[]{:S(2)}, u32[]{:S(2)}) collective-permute-start(bf16[128,512]{1,0:T(8,128)(2,1)S(1)} %slice.133.refs_0_), channel_id=1, source_target_pairs={{0,2},{1,3},{2,0},{3,1},{4,6},{5,7},{6,4},{7,5},{8,10},{9,11},{10,... | collective-permute-start | bytes 393224 | tf_op jit(solution)/shard_map/ppermute | solution.py:168
  7.9 8.6 %collective-permute-start.2 = (bf16[128,512]{1,0:T(8,128)(2,1)S(1)}, bf16[128,512]{1,0:T(8,128)(2,1)S(1)}, u32[]{:S(2)}, u32[]{:S(2)}) collective-permute-start(bf16[128,512]{1,0:T(8,128)(2,1)S(1)} %slice.133.refs_0_), channel_id=1, source_target_pairs={{0,3},{1,0},{2,1},{3,2},{4,7},{5,4},{6,5},{7,6},{8,11},{9,8},{10,9... | collective-permute-start | bytes 393224 | tf_op jit(solution)/shard_map/ppermute | solution.py:168
  28.9 19.6 %collective-permute-start.7 = (bf16[256,512]{1,0:T(8,128)(2,1)S(1)}, bf16[256,512]{1,0:T(8,128)(2,1)S(1)}, u32[]{:S(2)}, u32[]{:S(2)}) collective-permute-start(bf16[256,512]{1,0:T(8,128)(2,1)S(1)} %get-tuple-element.91.refs_0_), channel_id=1, source_target_pairs={{0,1},{1,2},{2,3},{3,0},{4,5},{5,6},{6,7},{7,4},{8,9},{9,10},{10,1... | collective-permute-start | bytes 786440 | tf_op jit(solution)/shard_map/ppermute | solution.py:168
  32.2 19.0 %collective-permute-start.8 = (bf16[256,512]{1,0:T(8,128)(2,1)S(1)}, bf16[256,512]{1,0:T(8,128)(2,1)S(1)}, u32[]{:S(2)}, u32[]{:S(2)}) collective-permute-start(bf16[256,512]{1,0:T(8,128)(2,1)S(1)} %get-tuple-element.91.refs_0_), channel_id=1, source_target_pairs={{0,2},{1,3},{2,0},{3,1},{4,6},{5,7},{6,4},{7,5},{8,10},{9,11},{10,... | collective-permute-start | bytes 786440 | tf_op jit(solution)/shard_map/ppermute | solution.py:168
  33.9 17.4 %collective-permute-start.9 = (bf16[256,512]{1,0:T(8,128)(2,1)S(1)}, bf16[256,512]{1,0:T(8,128)(2,1)S(1)}, u32[]{:S(2)}, u32[]{:S(2)}) collective-permute-start(bf16[256,512]{1,0:T(8,128)(2,1)S(1)} %get-tuple-element.91.refs_0_), channel_id=1, source_target_pairs={{0,3},{1,0},{2,1},{3,2},{4,7},{5,4},{6,5},{7,6},{8,11},{9,8},{10,9... | collective-permute-start | bytes 786440 | tf_op jit(solution)/shard_map/ppermute | solution.py:168
  46.9 20.5 %collective-permute-start.10 = (bf16[2,64,3328]{2,1,0:T(8,128)(2,1)S(1)}, bf16[2,64,3328]{2,1,0:T(8,128)(2,1)S(1)}, u32[]{:S(2)}, u32[]{:S(2)}) collective-permute-start(bf16[2,64,3328]{2,1,0:T(8,128)(2,1)S(1)} %get-tuple-element.89), channel_id=1, source_target_pairs={{0,8},{4,12},{8,0},{12,4},{1,9},{5,13},{9,1},{13,5},{2,10},{6,14},... | collective-permute-start | bytes 2555912 | tf_op jit(solution)/shard_map/ppermute | solution.py:172
  64.8 9.0 %collective-permute-start.12 = (bf16[1,128,3328]{2,1,0:T(8,128)(2,1)S(1)}, bf16[1,128,3328]{2,1,0:T(8,128)(2,1)S(1)}, u32[]{:S(2)}, u32[]{:S(2)}) collective-permute-start(bf16[1,128,3328]{2,1,0:T(8,128)(2,1)S(1)} %get-tuple-element.93), channel_id=1, source_target_pairs={{0,4},{4,0},{8,12},{12,8},{1,5},{5,1},{9,13},{13,9},{2,6},{6,2},{1... | collective-permute-start | bytes 2555912 | tf_op jit(solution)/shard_map/ppermute | solution.py:172
  65.3 9.8 %collective-permute-start.13 = (bf16[1,128,3328]{2,1,0:T(8,128)(2,1)S(1)}, bf16[1,128,3328]{2,1,0:T(8,128)(2,1)S(1)}, u32[]{:S(2)}, u32[]{:S(2)}) collective-permute-start(bf16[1,128,3328]{2,1,0:T(8,128)(2,1)S(1)} %get-tuple-element.94), channel_id=1, source_target_pairs={{0,4},{4,0},{8,12},{12,8},{1,5},{5,1},{9,13},{13,9},{2,6},{6,2},{1... | collective-permute-start | bytes 2555912 | tf_op jit(solution)/shard_map/ppermute | solution.py:172
  65.4 11.6 %collective-permute-start.14 = (bf16[1,128,3328]{2,1,0:T(8,128)(2,1)S(1)}, bf16[1,128,3328]{2,1,0:T(8,128)(2,1)S(1)}, u32[]{:S(2)}, u32[]{:S(2)}) collective-permute-start(bf16[1,128,3328]{2,1,0:T(8,128)(2,1)S(1)} %get-tuple-element.95), channel_id=1, source_target_pairs={{0,4},{4,0},{8,12},{12,8},{1,5},{5,1},{9,13},{13,9},{2,6},{6,2},{1... | collective-permute-start | bytes 2555912 | tf_op jit(solution)/shard_map/ppermute | solution.py:172
  67.8 42.7 %collective-permute-start.18 = (bf16[64,3328]{1,0:T(8,128)(2,1)S(1)}, bf16[64,3328]{1,0:T(8,128)(2,1)S(1)}, u32[]{:S(2)}, u32[]{:S(2)}) collective-permute-start(bf16[64,3328]{1,0:T(8,128)(2,1)S(1)} %fusion.16.own_x), channel_id=1, source_target_pairs={{0,8},{4,12},{8,0},{12,4},{1,9},{5,13},{9,1},{13,5},{2,10},{6,14},... | collective-permute-start | bytes 1277960 | tf_op jit(solution)/shard_map/ppermute | solution.py:172
  69.4 24.8 %collective-permute-start.15 = (bf16[256,512]{1,0:T(8,128)(2,1)S(1)}, bf16[256,512]{1,0:T(8,128)(2,1)S(1)}, u32[]{:S(2)}, u32[]{:S(2)}) collective-permute-start(bf16[256,512]{1,0:T(8,128)(2,1)S(1)} %get-tuple-element.100.refs_0_), channel_id=1, source_target_pairs={{0,1},{1,2},{2,3},{3,0},{4,5},{5,6},{6,7},{7,4},{8,9},{9,10},{10,1... | collective-permute-start | bytes 786440 | tf_op jit(solution)/shard_map/ppermute | solution.py:168
  73.8 20.3 %collective-permute-start.16 = (bf16[256,512]{1,0:T(8,128)(2,1)S(1)}, bf16[256,512]{1,0:T(8,128)(2,1)S(1)}, u32[]{:S(2)}, u32[]{:S(2)}) collective-permute-start(bf16[256,512]{1,0:T(8,128)(2,1)S(1)} %get-tuple-element.100.refs_0_), channel_id=1, source_target_pairs={{0,2},{1,3},{2,0},{3,1},{4,6},{5,7},{6,4},{7,5},{8,10},{9,11},{10,... | collective-permute-start | bytes 786440 | tf_op jit(solution)/shard_map/ppermute | solution.py:168
  75.1 19.1 %collective-permute-start.17 = (bf16[256,512]{1,0:T(8,128)(2,1)S(1)}, bf16[256,512]{1,0:T(8,128)(2,1)S(1)}, u32[]{:S(2)}, u32[]{:S(2)}) collective-permute-start(bf16[256,512]{1,0:T(8,128)(2,1)S(1)} %get-tuple-element.100.refs_0_), channel_id=1, source_target_pairs={{0,3},{1,0},{2,1},{3,2},{4,7},{5,4},{6,5},{7,6},{8,11},{9,8},{10,9... | collective-permute-start | bytes 786440 | tf_op jit(solution)/shard_map/ppermute | solution.py:168
  92.6 50.9 %collective-permute-start.25 = (bf16[2,128,3328]{2,1,0:T(8,128)(2,1)}, bf16[2,128,3328]{2,1,0:T(8,128)(2,1)}, u32[]{:S(2)}, u32[]{:S(2)}) collective-permute-start(bf16[2,128,3328]{2,1,0:T(8,128)(2,1)} %get-tuple-element.98), channel_id=1, source_target_pairs={{0,8},{4,12},{8,0},{12,4},{1,9},{5,13},{9,1},{13,5},{2,10},{6,14},... | collective-permute-start | bytes 5111816 | tf_op jit(solution)/shard_map/ppermute | solution.py:172
  94.2 17.4 %collective-permute-start.19 = (bf16[64,3328]{1,0:T(8,128)(2,1)S(1)}, bf16[64,3328]{1,0:T(8,128)(2,1)S(1)}, u32[]{:S(2)}, u32[]{:S(2)}) collective-permute-start(bf16[64,3328]{1,0:T(8,128)(2,1)S(1)} %fusion.16.own_x), channel_id=1, source_target_pairs={{0,4},{4,0},{8,12},{12,8},{1,5},{5,1},{9,13},{13,9},{2,6},{6,2},{1... | collective-permute-start | bytes 1277960 | tf_op jit(solution)/shard_map/ppermute | solution.py:172
  111.1 11.3 %collective-permute-start.21 = (bf16[1,128,3328]{2,1,0:T(8,128)(2,1)S(1)}, bf16[1,128,3328]{2,1,0:T(8,128)(2,1)S(1)}, u32[]{:S(2)}, u32[]{:S(2)}) collective-permute-start(bf16[1,128,3328]{2,1,0:T(8,128)(2,1)S(1)} %get-tuple-element.101), channel_id=1, source_target_pairs={{0,4},{4,0},{8,12},{12,8},{1,5},{5,1},{9,13},{13,9},{2,6},{6,2},{1... | collective-permute-start | bytes 2555912 | tf_op jit(solution)/shard_map/ppermute | solution.py:172
  111.1 14.1 %collective-permute-start.22 = (bf16[1,128,3328]{2,1,0:T(8,128)(2,1)}, bf16[1,128,3328]{2,1,0:T(8,128)(2,1)S(1)}, u32[]{:S(2)}, u32[]{:S(2)}) collective-permute-start(bf16[1,128,3328]{2,1,0:T(8,128)(2,1)} %get-tuple-element.102), channel_id=1, source_target_pairs={{0,4},{4,0},{8,12},{12,8},{1,5},{5,1},{9,13},{13,9},{2,6},{6,2},{1... | collective-permute-start | bytes 2555912 | tf_op jit(solution)/shard_map/ppermute | solution.py:172
  111.6 15.3 %collective-permute-start.23 = (bf16[1,128,3328]{2,1,0:T(8,128)(2,1)}, bf16[1,128,3328]{2,1,0:T(8,128)(2,1)S(1)}, u32[]{:S(2)}, u32[]{:S(2)}) collective-permute-start(bf16[1,128,3328]{2,1,0:T(8,128)(2,1)} %get-tuple-element.103), channel_id=1, source_target_pairs={{0,4},{4,0},{8,12},{12,8},{1,5},{5,1},{9,13},{13,9},{2,6},{6,2},{1... | collective-permute-start | bytes 2555912 | tf_op jit(solution)/shard_map/ppermute | solution.py:172
  113.2 14.8 %collective-permute-start.24 = (bf16[1,128,3328]{2,1,0:T(8,128)(2,1)S(1)}, bf16[1,128,3328]{2,1,0:T(8,128)(2,1)S(1)}, u32[]{:S(2)}, u32[]{:S(2)}) collective-permute-start(bf16[1,128,3328]{2,1,0:T(8,128)(2,1)S(1)} %get-tuple-element.104), channel_id=1, source_target_pairs={{0,4},{4,0},{8,12},{12,8},{1,5},{5,1},{9,13},{13,9},{2,6},{6,2},{1... | collective-permute-start | bytes 2555912 | tf_op jit(solution)/shard_map/ppermute | solution.py:172
  122.4 25.5 %collective-permute-start.26 = (bf16[384,512]{1,0:T(8,128)(2,1)S(1)}, bf16[384,512]{1,0:T(8,128)(2,1)S(1)}, u32[]{:S(2)}, u32[]{:S(2)}) collective-permute-start(bf16[384,512]{1,0:T(8,128)(2,1)S(1)} %slice.145.refs_0_), channel_id=1, source_target_pairs={{0,1},{1,2},{2,3},{3,0},{4,5},{5,6},{6,7},{7,4},{8,9},{9,10},{10,1... | collective-permute-start | bytes 1179656 | tf_op jit(solution)/shard_map/ppermute | solution.py:168
  125.3 27.8 %collective-permute-start.27 = (bf16[384,512]{1,0:T(8,128)(2,1)S(1)}, bf16[384,512]{1,0:T(8,128)(2,1)S(1)}, u32[]{:S(2)}, u32[]{:S(2)}) collective-permute-start(bf16[384,512]{1,0:T(8,128)(2,1)S(1)} %slice.145.refs_0_), channel_id=1, source_target_pairs={{0,2},{1,3},{2,0},{3,1},{4,6},{5,7},{6,4},{7,5},{8,10},{9,11},{10,... | collective-permute-start | bytes 1179656 | tf_op jit(solution)/shard_map/ppermute | solution.py:168
  126.9 26.1 %collective-permute-start.28 = (bf16[384,512]{1,0:T(8,128)(2,1)S(1)}, bf16[384,512]{1,0:T(8,128)(2,1)S(1)}, u32[]{:S(2)}, u32[]{:S(2)}) collective-permute-start(bf16[384,512]{1,0:T(8,128)(2,1)S(1)} %slice.145.refs_0_), channel_id=1, source_target_pairs={{0,3},{1,0},{2,1},{3,2},{4,7},{5,4},{6,5},{7,6},{8,11},{9,8},{10,9... | collective-permute-start | bytes 1179656 | tf_op jit(solution)/shard_map/ppermute | solution.py:168
  128.0 39.2 %collective-permute-start.29 = (bf16[128,1024]{1,0:T(8,128)(2,1)}, bf16[128,1024]{1,0:T(8,128)(2,1)S(1)}, u32[]{:S(2)}, u32[]{:S(2)}) collective-permute-start(bf16[128,1024]{1,0:T(8,128)(2,1)} %get-tuple-element.109), channel_id=1, source_target_pairs={{0,1},{1,0},{2,3},{3,2},{4,5},{5,4},{6,7},{7,6},{8,9},{9,8},{10,11... | collective-permute-start | bytes 786440 | tf_op jit(solution)/shard_map/ppermute | solution.py:231
  143.5 43.5 %collective-permute-start.34 = (bf16[2,128,3328]{2,1,0:T(8,128)(2,1)S(1)}, bf16[2,128,3328]{2,1,0:T(8,128)(2,1)S(1)}, u32[]{:S(2)}, u32[]{:S(2)}) collective-permute-start(bf16[2,128,3328]{2,1,0:T(8,128)(2,1)S(1)} %get-tuple-element.111), channel_id=1, source_target_pairs={{0,8},{4,12},{8,0},{12,4},{1,9},{5,13},{9,1},{13,5},{2,10},{6,14},... | collective-permute-start | bytes 5111816 | tf_op jit(solution)/shard_map/ppermute | solution.py:172
  168.9 32.9 %collective-permute-start.36 = (bf16[128,3328]{1,0:T(8,128)(2,1)}, bf16[128,3328]{1,0:T(8,128)(2,1)}, u32[]{:S(2)}, u32[]{:S(2)}) collective-permute-start(bf16[128,3328]{1,0:T(8,128)(2,1)} %fusion.8.own_x), channel_id=1, source_target_pairs={{0,8},{4,12},{8,0},{12,4},{1,9},{5,13},{9,1},{13,5},{2,10},{6,14},... | collective-permute-start | bytes 2555912 | tf_op jit(solution)/shard_map/ppermute | solution.py:172
  201.2 30.7 %collective-permute-start.39 = (bf16[2,128,3328]{2,1,0:T(8,128)(2,1)S(1)}, bf16[2,128,3328]{2,1,0:T(8,128)(2,1)S(1)}, u32[]{:S(2)}, u32[]{:S(2)}) collective-permute-start(bf16[2,128,3328]{2,1,0:T(8,128)(2,1)S(1)} %partner.9), channel_id=1, source_target_pairs={{0,4},{4,0},{8,12},{12,8},{1,5},{5,1},{9,13},{13,9},{2,6},{6,2},{1... | collective-permute-start | bytes 5111816 | tf_op jit(solution)/shard_map/ppermute | solution.py:172
  201.4 14.9 %collective-permute-start.37 = (bf16[128,3328]{1,0:T(8,128)(2,1)}, bf16[128,3328]{1,0:T(8,128)(2,1)}, u32[]{:S(2)}, u32[]{:S(2)}) collective-permute-start(bf16[128,3328]{1,0:T(8,128)(2,1)} %fusion.8.own_x), channel_id=1, source_target_pairs={{0,4},{4,0},{8,12},{12,8},{1,5},{5,1},{9,13},{13,9},{2,6},{6,2},{1... | collective-permute-start | bytes 2555912 | tf_op jit(solution)/shard_map/ppermute | solution.py:172
  201.8 14.5 %collective-permute-start.38 = (bf16[128,3328]{1,0:T(8,128)(2,1)}, bf16[128,3328]{1,0:T(8,128)(2,1)}, u32[]{:S(2)}, u32[]{:S(2)}) collective-permute-start(bf16[128,3328]{1,0:T(8,128)(2,1)} %collective-permute-done.36.other_x), channel_id=1, source_target_pairs={{0,4},{4,0},{8,12},{12,8},{1,5},{5,1},{9,13},{13,9},{2,6},{6,2},{1... | collective-permute-start | bytes 2555912 | tf_op jit(solution)/shard_map/ppermute | solution.py:172
  202.0 57.8 %collective-permute-start.41 = (bf16[2,128,3328]{2,1,0:T(8,128)(2,1)S(1)}, bf16[2,128,3328]{2,1,0:T(8,128)(2,1)}, u32[]{:S(2)}, u32[]{:S(2)}) collective-permute-start(bf16[2,128,3328]{2,1,0:T(8,128)(2,1)S(1)} %get-tuple-element.122), channel_id=1, source_target_pairs={{0,8},{4,12},{8,0},{12,4},{1,9},{5,13},{9,1},{13,5},{2,10},{6,14},... | collective-permute-start | bytes 5111816 | tf_op jit(solution)/shard_map/ppermute | solution.py:172
  203.2 11.6 %collective-permute-start.35 = (bf16[128,512]{1,0:T(8,128)(2,1)S(1)}, bf16[128,512]{1,0:T(8,128)(2,1)S(1)}, u32[]{:S(2)}, u32[]{:S(2)}) collective-permute-start(bf16[128,512]{1,0:T(8,128)(2,1)S(1)} %get-tuple-element.171), channel_id=1, source_target_pairs={{0,2},{1,3},{2,0},{3,1},{4,6},{5,7},{6,4},{7,5},{8,10},{9,11},{10,... | collective-permute-start | bytes 393224 | tf_op jit(solution)/shard_map/ppermute | solution.py:239
  214.8 45.0 %collective-permute-start.42 = (bf16[128,3328]{1,0:T(8,128)(2,1)}, bf16[128,3328]{1,0:T(8,128)(2,1)}, u32[]{:S(2)}, u32[]{:S(2)}) collective-permute-start(bf16[128,3328]{1,0:T(8,128)(2,1)} %fusion.4.own_x), channel_id=1, source_target_pairs={{0,8},{4,12},{8,0},{12,4},{1,9},{5,13},{9,1},{13,5},{2,10},{6,14},... | collective-permute-start | bytes 2555912 | tf_op jit(solution)/shard_map/ppermute | solution.py:172
  228.3 15.6 %collective-permute-start.40 = (bf16[256,1024]{1,0:T(8,128)(2,1)}, bf16[256,1024]{1,0:T(8,128)(2,1)S(1)}, u32[]{:S(2)}, u32[]{:S(2)}) collective-permute-start(bf16[256,1024]{1,0:T(8,128)(2,1)} %get-tuple-element.129), channel_id=1, source_target_pairs={{0,1},{1,0},{2,3},{3,2},{4,5},{5,4},{6,7},{7,6},{8,9},{9,8},{10,11... | collective-permute-start | bytes 1572872 | tf_op jit(solution)/shard_map/ppermute | solution.py:231
  231.9 31.5 %collective-permute-start.43 = (bf16[128,3328]{1,0:T(8,128)(2,1)}, bf16[128,3328]{1,0:T(8,128)(2,1)S(1)}, u32[]{:S(2)}, u32[]{:S(2)}) collective-permute-start(bf16[128,3328]{1,0:T(8,128)(2,1)} %fusion.4.own_x), channel_id=1, source_target_pairs={{0,4},{4,0},{8,12},{12,8},{1,5},{5,1},{9,13},{13,9},{2,6},{6,2},{1... | collective-permute-start | bytes 2555912 | tf_op jit(solution)/shard_map/ppermute | solution.py:172
  261.9 23.9 %collective-permute-start.45 = (bf16[128,3328]{1,0:T(8,128)(2,1)S(1)}, bf16[128,3328]{1,0:T(8,128)(2,1)S(1)}, u32[]{:S(2)}, u32[]{:S(2)}) collective-permute-start(bf16[128,3328]{1,0:T(8,128)(2,1)S(1)} %fusion.own_x), channel_id=1, source_target_pairs={{0,8},{4,12},{8,0},{12,4},{1,9},{5,13},{9,1},{13,5},{2,10},{6,14},... | collective-permute-start | bytes 2555912 | tf_op jit(solution)/shard_map/ppermute | solution.py:172
  263.2 34.0 %collective-permute-start.46 = (bf16[128,3328]{1,0:T(8,128)(2,1)S(1)}, bf16[128,3328]{1,0:T(8,128)(2,1)S(1)}, u32[]{:S(2)}, u32[]{:S(2)}) collective-permute-start(bf16[128,3328]{1,0:T(8,128)(2,1)S(1)} %fusion.own_x), channel_id=1, source_target_pairs={{0,4},{4,0},{8,12},{12,8},{1,5},{5,1},{9,13},{13,9},{2,6},{6,2},{1... | collective-permute-start | bytes 2555912 | tf_op jit(solution)/shard_map/ppermute | solution.py:172
  285.9 11.3 %collective-permute-start.47 = (bf16[128,3328]{1,0:T(8,128)(2,1)S(1)}, bf16[128,3328]{1,0:T(8,128)(2,1)S(1)}, u32[]{:S(2)}, u32[]{:S(2)}) collective-permute-start(bf16[128,3328]{1,0:T(8,128)(2,1)S(1)} %collective-permute-done.45.other_x), channel_id=1, source_target_pairs={{0,4},{4,0},{8,12},{12,8},{1,5},{5,1},{9,13},{13,9},{2,6},{6,2},{1... | collective-permute-start | bytes 2555912 | tf_op jit(solution)/shard_map/ppermute | solution.py:172
  286.3 24.7 %collective-permute-start.48 = (bf16[2,64,3328]{2,1,0:T(8,128)(2,1)S(1)}, bf16[2,64,3328]{2,1,0:T(8,128)(2,1)S(1)}, u32[]{:S(2)}, u32[]{:S(2)}) collective-permute-start(bf16[2,64,3328]{2,1,0:T(8,128)(2,1)S(1)} %get-tuple-element.131), channel_id=1, source_target_pairs={{0,8},{4,12},{8,0},{12,4},{1,9},{5,13},{9,1},{13,5},{2,10},{6,14},... | collective-permute-start | bytes 2555912 | tf_op jit(solution)/shard_map/ppermute | solution.py:172
  287.1 25.7 %collective-permute-start.49 = (bf16[256,512]{1,0:T(8,128)(2,1)S(1)}, bf16[256,512]{1,0:T(8,128)(2,1)S(1)}, u32[]{:S(2)}, u32[]{:S(2)}) collective-permute-start(bf16[256,512]{1,0:T(8,128)(2,1)S(1)} %get-tuple-element.167), channel_id=1, source_target_pairs={{0,2},{1,3},{2,0},{3,1},{4,6},{5,7},{6,4},{7,5},{8,10},{9,11},{10,... | collective-permute-start | bytes 786440 | tf_op jit(solution)/shard_map/ppermute | solution.py:239
  295.0 18.0 %collective-permute-start.50 = (bf16[256,1024]{1,0:T(8,128)(2,1)}, bf16[256,1024]{1,0:T(8,128)(2,1)S(1)}, u32[]{:S(2)}, u32[]{:S(2)}) collective-permute-start(bf16[256,1024]{1,0:T(8,128)(2,1)} %get-tuple-element.138), channel_id=1, source_target_pairs={{0,1},{1,0},{2,3},{3,2},{4,5},{5,4},{6,7},{7,6},{8,9},{9,8},{10,11... | collective-permute-start | bytes 1572872 | tf_op jit(solution)/shard_map/ppermute | solution.py:231
  310.9 19.1 %collective-permute-start.51 = (bf16[256,1024]{1,0:T(8,128)(2,1)}, bf16[256,1024]{1,0:T(8,128)(2,1)S(1)}, u32[]{:S(2)}, u32[]{:S(2)}) collective-permute-start(bf16[256,1024]{1,0:T(8,128)(2,1)} %get-tuple-element.141), channel_id=1, source_target_pairs={{0,1},{1,0},{2,3},{3,2},{4,5},{5,4},{6,7},{7,6},{8,9},{9,8},{10,11... | collective-permute-start | bytes 1572872 | tf_op jit(solution)/shard_map/ppermute | solution.py:231
  311.3 11.2 %collective-permute-start.53 = (bf16[64,3328]{1,0:T(8,128)(2,1)S(1)}, bf16[64,3328]{1,0:T(8,128)(2,1)S(1)}, u32[]{:S(2)}, u32[]{:S(2)}) collective-permute-start(bf16[64,3328]{1,0:T(8,128)(2,1)S(1)} %fusion.12.own_x), channel_id=1, source_target_pairs={{0,8},{4,12},{8,0},{12,4},{1,9},{5,13},{9,1},{13,5},{2,10},{6,14},... | collective-permute-start | bytes 1277960 | tf_op jit(solution)/shard_map/ppermute | solution.py:172
  313.1 17.1 %collective-permute-start.52 = (bf16[256,512]{1,0:T(8,128)(2,1)S(1)}, bf16[256,512]{1,0:T(8,128)(2,1)S(1)}, u32[]{:S(2)}, u32[]{:S(2)}) collective-permute-start(bf16[256,512]{1,0:T(8,128)(2,1)S(1)} %get-tuple-element.165), channel_id=1, source_target_pairs={{0,2},{1,3},{2,0},{3,1},{4,6},{5,7},{6,4},{7,5},{8,10},{9,11},{10,... | collective-permute-start | bytes 786440 | tf_op jit(solution)/shard_map/ppermute | solution.py:239
  317.5 12.7 %collective-permute-start.54 = (bf16[64,3328]{1,0:T(8,128)(2,1)S(1)}, bf16[64,3328]{1,0:T(8,128)(2,1)S(1)}, u32[]{:S(2)}, u32[]{:S(2)}) collective-permute-start(bf16[64,3328]{1,0:T(8,128)(2,1)S(1)} %fusion.12.own_x), channel_id=1, source_target_pairs={{0,4},{4,0},{8,12},{12,8},{1,5},{5,1},{9,13},{13,9},{2,6},{6,2},{1... | collective-permute-start | bytes 1277960 | tf_op jit(solution)/shard_map/ppermute | solution.py:172
  338.7 9.2 %collective-permute-start.56 = (bf16[128,512]{1,0:T(8,128)(2,1)}, bf16[128,512]{1,0:T(8,128)(2,1)S(1)}, u32[]{:S(2)}, u32[]{:S(2)}) collective-permute-start(bf16[128,512]{1,0:T(8,128)(2,1)} %get-tuple-element.152), channel_id=1, source_target_pairs={{0,1},{1,2},{2,3},{3,0},{4,5},{5,6},{6,7},{7,4},{8,9},{9,10},{10,1... | collective-permute-start | bytes 393224 | tf_op jit(solution)/shard_map/ppermute | solution.py:168
  341.7 15.4 %collective-permute-start.57 = (bf16[128,512]{1,0:T(8,128)(2,1)}, bf16[128,512]{1,0:T(8,128)(2,1)S(1)}, u32[]{:S(2)}, u32[]{:S(2)}) collective-permute-start(bf16[128,512]{1,0:T(8,128)(2,1)} %get-tuple-element.153), channel_id=1, source_target_pairs={{0,2},{1,3},{2,0},{3,1},{4,6},{5,7},{6,4},{7,5},{8,10},{9,11},{10,... | collective-permute-start | bytes 393224 | tf_op jit(solution)/shard_map/ppermute | solution.py:168
  343.7 13.5 %collective-permute-start.58 = (bf16[128,512]{1,0:T(8,128)(2,1)}, bf16[128,512]{1,0:T(8,128)(2,1)S(1)}, u32[]{:S(2)}, u32[]{:S(2)}) collective-permute-start(bf16[128,512]{1,0:T(8,128)(2,1)} %get-tuple-element.154), channel_id=1, source_target_pairs={{0,3},{1,0},{2,1},{3,2},{4,7},{5,4},{6,5},{7,6},{8,11},{9,8},{10,9... | collective-permute-start | bytes 393224 | tf_op jit(solution)/shard_map/ppermute | solution.py:168
  344.2 21.3 %collective-permute-start.59 = (bf16[256,512]{1,0:T(8,128)(2,1)S(1)}, bf16[256,512]{1,0:T(8,128)(2,1)S(1)}, u32[]{:S(2)}, u32[]{:S(2)}) collective-permute-start(bf16[256,512]{1,0:T(8,128)(2,1)S(1)} %get-tuple-element.164), channel_id=1, source_target_pairs={{0,2},{1,3},{2,0},{3,1},{4,6},{5,7},{6,4},{7,5},{8,10},{9,11},{10,... | collective-permute-start | bytes 786440 | tf_op jit(solution)/shard_map/ppermute | solution.py:239
  (51 other events, 721.7 us)
